TPU v7x, 32 devices: a whole 2x2x4 slice. The times are simulated.
32 devices in a mesh: grp: 2 (over x), tm: 16 (over z, y, core).
Axes of the slice: x: 2, y: 2, z: 4, core: 2. Of those that a mesh axis runs over, the one named last changes fastest.
Arguments:
- noise: float32 [32, 256, 256], P(('grp', 'tm')), parts along dimension 0, may hold values from -6 to 6
- phonon_level: int32 [32, 256, 256], P(('grp', 'tm')), parts along dimension 0, may hold values from 0 to 16
- hop_x: float32 [256, 256], replicated, as said below
- hop_y: float32 [256, 256], replicated, as said below
Outputs:
- solution: float32 [32, 256, 256], P(('grp', 'tm')), parts along dimension 0
- residual: float32 [32, 256, 256], P(('grp', 'tm')), parts along dimension 0
There are 2 independent parts, one for each index of `grp`. A program takes and returns all parts, laid end to end along the dimension named above; an argument that names none is the same for every part. Nothing has to cross between parts.
Inputs may be any that keep to these rules, and one draw needn't show every extreme that they name: hop_x is symmetric. hop_y is symmetric.
All inputs are finite; a program needn't handle non-finite values.
Results may differ from a plain program's by a relative error of at most 0.0003.
Values sent between devices are 32-bit elements; how exact they have to be, the bound alone decides.
No kernel may reach another device: no remote copies, remote signals or barrier semaphores. Data moves between devices by JAX's collectives and lax.ppermute only.
A program may use at most 64 MiB of HBM per device.

v0:
```python
import math

import jax
import jax.numpy as jnp
import numpy as np
from jax import lax
from jax.experimental import pallas as pl
from jax.experimental.pallas import tpu as pltpu
from jax.sharding import PartitionSpec as P

ORDER = 10
LEVELS = 17
MIDDLE = (LEVELS - 1) // 2
BF16 = jnp.bfloat16
F32 = jnp.float32
VMEM = pl.BlockSpec(memory_space=pltpu.VMEM)


def call(kernel, out_shape, count, scratch=()):
    return pl.pallas_call(
        kernel,
        out_shape=out_shape,
        in_specs=[VMEM] * count,
        out_specs=jax.tree.map(lambda _: VMEM, out_shape),
        scratch_shapes=list(scratch),
        compiler_params=pltpu.CompilerParams(vmem_limit_bytes=16 << 20),
    )


def shape(rows, columns, kind=F32):
    return jax.ShapeDtypeStruct((rows, columns), kind)


def split(value):
    high = value.astype(BF16)
    return high, (value - high.astype(F32)).astype(BF16)


def dot3(left, right):
    def dot(a, b):
        return jnp.dot(a, b, preferred_element_type=F32)

    return dot(left[0], right[0]) + (dot(left[1], right[0]) + dot(left[0], right[1]))


def prepare_kernel(hop_x_ref, hop_y_ref, xh_ref, xl_ref, yh_ref, yl_ref):
    for ref, high_ref, low_ref in ((hop_x_ref, xh_ref, xl_ref), (hop_y_ref, yh_ref, yl_ref)):
        side = ref.shape[0]
        hop = ref[...]
        square = jnp.dot(hop, hop, precision=lax.Precision.HIGHEST, preferred_element_type=F32)
        high_ref[:side], low_ref[:side] = split(hop)
        high_ref[side:], low_ref[side:] = split(square)


def transform_kernel(block_ref, th_ref, tl_ref, out_ref):
    rows, columns = block_ref.shape
    block = split(block_ref[...])
    result = dot3((th_ref[...], tl_ref[...]), block)
    for part in range(th_ref.shape[0] // rows):
        out_ref[:, part * columns : (part + 1) * columns] = result[part * rows : (part + 1) * rows]


def chebyshev_kernel(*refs):
    field_ref, xh_ref, xl_ref, yh_ref, yl_ref, sum_ref, cos_ref = refs[:7]
    add_ref = refs[7] if len(refs) == 10 else None
    out_ref, weight_ref = refs[-2:]
    side_x = field_ref.shape[0]
    side_y = field_ref.shape[1]
    cbar = jnp.exp(-0.05 * (sum_ref[...] - MIDDLE))
    lower = 0.05
    root_lower = math.sqrt(lower)
    root_upper = 1.0 + 3.0 * cbar
    upper = root_upper * root_upper
    spread = upper - lower
    ratio = (root_upper - root_lower) / (root_upper + root_lower)
    keep = 2.0 * (2.0 - (upper + lower)) / spread
    once = -8.0 * cos_ref[...] * cbar / spread
    twice = 4.0 * cbar * cbar / spread
    weight = 2.0 / (root_upper * root_lower)
    for degree in range(ORDER + 1):
        weight_ref[degree : degree + 1, :] = weight
        weight = weight * -ratio
    field = field_ref[...]
    x_pair = (xh_ref[...], xl_ref[...])

    def step(index, carry):
        ahead, second = carry
        inner = dot3(x_pair, split(ahead))
        first_h, first_l = split(inner[:side_x] * once)
        second_h, second_l = split(inner[side_x:] * twice)
        hops = dot3((first_h, first_l), (yh_ref[:side_y], yl_ref[:side_y])) + dot3(
            (second_h, second_l), (yh_ref[side_y:], yl_ref[side_y:])
        )
        row = weight_ref[pl.ds(ORDER - 1 - index, 1), :]
        return (row * field + keep * ahead - second) + hops, ahead

    last = weight_ref[ORDER : ORDER + 1, :] * field
    ahead, before = last, last - last

    def body(index, carry):
        first, second, _ = carry
        result, first_out = step(index, (first, second))
        return result, first_out, second

    result, _, second = lax.fori_loop(0, ORDER, body, (ahead, before, before))
    total = 0.5 * (result - second)
    out_ref[...] = total if add_ref is None else total + add_ref[...]


def normal_kernel(
    even_ref, slices_ref, other_ref, damp_ref, damp_next_ref, noise_ref, xh_ref, xl_ref, yh_ref, yl_ref, out_ref
):
    side_x, side_y = other_ref.shape
    x_pair = (xh_ref[:side_x], xl_ref[:side_x])
    y_pair = (yh_ref[:side_y], yl_ref[:side_y])
    even = even_ref[...] > 0.5
    far = slices_ref[:, :side_y]
    here = slices_ref[:, side_y:]
    near = other_ref[...]
    before = jnp.where(even, far, near)
    after = jnp.where(even, near, far)
    damp_next = damp_next_ref[...]

    def propagate(value):
        return dot3(split(dot3(x_pair, split(value))), y_pair)

    forward = here - propagate(damp_ref[...] * before)
    forward_next = after - propagate(damp_next * here)
    out_ref[...] = noise_ref[...] - (forward - damp_next * propagate(forward_next))


def tables(length, rows):
    times = np.arange(length)
    phase = (2 * (times // 2)[:, None] + 1) * times[None, :] % (2 * length)
    angles = phase * (math.pi / length)
    basis = np.where((times % 2 == 0)[:, None], np.cos(angles), np.sin(angles))
    inverse = basis.T * (2.0 / length)
    far = np.where(times % 2 == 0, times - 1, times + 1)
    wrapped = np.where((far < 0) | (far >= length), -1.0, 1.0)
    inverse_far = inverse[far % length] * wrapped[:, None]

    def parts(matrix):
        matrix = np.kron(matrix, np.eye(rows))
        high = matrix.astype(BF16)
        return jnp.asarray(high), jnp.asarray((matrix - high.astype(np.float64)).astype(BF16))

    forward = parts(basis)
    back_far, back = parts(inverse_far), parts(inverse)
    both = tuple(jnp.concatenate([a, b], axis=0) for a, b in zip(back_far, back))
    return forward, both


def total_over(value, axis):
    count = lax.axis_size(axis)
    if count & (count - 1):
        return lax.psum(value, axis)
    step = 1
    while step < count:
        value = value + lax.ppermute(value, axis, [(i, i ^ step) for i in range(count)])
        step *= 2
    return value


def exchange(value, axis):
    count = lax.axis_size(axis)
    rows, columns = value.shape
    blocks = value.reshape(count, rows // count, columns)
    return lax.all_to_all(blocks, axis, split_axis=0, concat_axis=0, tiled=True).reshape(rows, columns)


def per_device(noise, phonon_level, hop_x, hop_y):
    _, side_x, side_y = noise.shape
    length = lax.axis_size("tm")
    position = lax.axis_index("tm")
    noise = noise[0]
    levels = phonon_level[0].astype(F32)
    damp = jnp.exp(-0.05 * (levels - MIDDLE))
    damp_next = lax.ppermute(damp, "tm", [(i, (i - 1) % length) for i in range(length)])
    level_sum = total_over(jnp.full((1, side_y), jnp.sum(levels), F32), "tm")
    mean_level = level_sum / (length * side_x * side_y)
    cosine = jnp.cos((2 * (position // 2) + 1).astype(F32) * (math.pi / length))
    cosine = jnp.full((1, side_y), cosine, F32)
    even = jnp.full((1, side_y), (position % 2 == 0).astype(F32), F32)
    forward, back = tables(length, side_x // length)

    hops = call(prepare_kernel, (shape(2 * side_x, side_x, BF16),) * 2 + (shape(2 * side_y, side_y, BF16),) * 2, 2)(
        hop_x, hop_y
    )
    field_shape = shape(side_x, side_y)
    to_spectrum = call(transform_kernel, field_shape, 3)
    to_times = call(transform_kernel, shape(side_x, 2 * side_y), 3)

    def chebyshev(*operands):
        return call(chebyshev_kernel, field_shape, len(operands), [pltpu.VMEM((16, side_y), F32)])(*operands)

    def spectrum(field):
        return exchange(to_spectrum(exchange(field, "tm"), *forward), "tm")

    def slices_of(components):
        slices = exchange(to_times(exchange(components, "tm"), *back), "tm")
        here = slices[:, side_y:]
        other = lax.ppermute(here, "tm", [(i, i ^ 1) for i in range(length)])
        return slices, here, other

    def residual_of(slices, other):
        return call(normal_kernel, field_shape, 10)(even, slices, other, damp, damp_next, noise, *hops)

    first = chebyshev(spectrum(noise), *hops, mean_level, cosine)
    slices, _, other = slices_of(first)
    second_residual = residual_of(slices, other)
    total = chebyshev(spectrum(second_residual), *hops, mean_level, cosine, first)
    slices, result, other = slices_of(total)
    residual = residual_of(slices, other)
    return result[None], residual[None]


def solution(mesh):
    return jax.shard_map(
        per_device,
        mesh=mesh,
        in_specs=(P(("grp", "tm"), None, None), P(("grp", "tm"), None, None), P(), P()),
        out_specs=(P(("grp", "tm"), None, None), P(("grp", "tm"), None, None)),
        check_vma=False,
    )
```

profile of v0, /device:TPU:0, one launch (start us, length us, event | category | flops | bytes accessed | tf_op | source)
XLA Modules:
  0.0 160.3 jit_solution(6896491883234102178)
XLA Ops:
  0.6 0.0 copy-start.7
  0.6 7.6 %all-to-all-start = ((f32[16,16,256]{2,1,0:T(8,128)}), f32[16,16,256]{2,1,0:T(8,128)S(1)}, u32[]{:S(2)}, u32[]{:S(2)}) async-start(f32[16,16,256]{2,1,0:T(8,128)} %bitcast.27), calls=%async_computation | async-start | bytes 524288 | tf_op jit(solution)/shard_map/all_to_all | solution.py:168
  8.2 0.0 copy-start.3
  8.2 0.0 copy-start.4
  8.2 0.7 exponential_bitcast_fusion
  8.9 0.6 broadcast_in_dim.16
  9.6 0.5 collective-permute-start
  10.0 8.2 %all-to-all-done = f32[16,16,256]{2,1,0:T(8,128)S(1)} async-done(((f32[16,16,256]{2,1,0:T(8,128)}), f32[16,16,256]{2,1,0:T(8,128)S(1)}, u32[]{:S(2)}, u32[]{:S(2)}) %all-to-all-start) | async-done | bytes 262176 | tf_op jit(solution)/shard_map/all_to_all | solution.py:168
  18.2 0.0 copy-done.3
  18.2 1.0 shard_map.113
  19.2 3.7 %all-to-all-start.1 = ((f32[16,16,256]{2,1,0:T(8,128)}), f32[16,16,256]{2,1,0:T(8,128)S(1)}, u32[]{:S(2)}, u32[]{:S(2)}) async-start(f32[16,16,256]{2,1,0:T(8,128)} %bitcast.2), calls=%async_computation.1 | async-start | bytes 524288 | tf_op jit(solution)/shard_map/all_to_all | solution.py:168
  22.9 0.0 collective-permute-done
  22.9 0.7 broadcast_add_fusion
  23.5 1.9 %collective-permute-start.1 = (f32[1,256]{1,0:T(1,128)S(1)}, f32[1,256]{1,0:T(1,128)S(1)}, u32[]{:S(2)}, u32[]{:S(2)}) collective-permute-start(f32[1,256]{1,0:T(1,128)S(1)} %broadcast_add_fusion), channel_id=1, source_target_pairs={{0,2},{1,3},{2,0},{3,1},{4,6},{5,7},{6,4},{7,5},{8,10},{9,11},{10,... | collective-permute-start | bytes 3080 | tf_op jit(solution)/shard_map/ppermute | solution.py:159
  25.4 1.9 %collective-permute-done.1 = f32[1,256]{1,0:T(1,128)S(1)} collective-permute-done((f32[1,256]{1,0:T(1,128)S(1)}, f32[1,256]{1,0:T(1,128)S(1)}, u32[]{:S(2)}, u32[]{:S(2)}) %collective-permute-start.1) | collective-permute-done | bytes 1056 | tf_op jit(solution)/shard_map/ppermute | solution.py:159
  27.3 0.6 fusion.1
  27.9 1.8 %collective-permute-start.2 = (f32[1,256]{1,0:T(1,128)S(1)}, f32[1,256]{1,0:T(1,128)S(1)}, u32[]{:S(2)}, u32[]{:S(2)}) collective-permute-start(f32[1,256]{1,0:T(1,128)S(1)} %fusion.1), channel_id=1, source_target_pairs={{0,4},{1,5},{2,6},{3,7},{4,0},{5,1},{6,2},{7,3},{8,12},{9,13},{10,... | collective-permute-start | bytes 3080 | tf_op jit(solution)/shard_map/ppermute | solution.py:159
  29.7 1.9 %collective-permute-done.2 = f32[1,256]{1,0:T(1,128)S(1)} collective-permute-done((f32[1,256]{1,0:T(1,128)S(1)}, f32[1,256]{1,0:T(1,128)S(1)}, u32[]{:S(2)}, u32[]{:S(2)}) %collective-permute-start.2) | collective-permute-done | bytes 1056 | tf_op jit(solution)/shard_map/ppermute | solution.py:159
  31.6 2.6 %collective-permute-start.3 = (f32[1,256]{1,0:T(1,128)S(1)}, f32[1,256]{1,0:T(1,128)S(1)}, u32[]{:S(2)}, u32[]{:S(2)}) collective-permute-start(f32[1,256]{1,0:T(1,128)S(1)} %add.25), channel_id=1, source_target_pairs={{0,8},{1,9},{2,10},{3,11},{4,12},{5,13},{6,14},{7,15},{8,0},{9,1},... | collective-permute-start | bytes 3080 | tf_op jit(solution)/shard_map/ppermute | solution.py:159
  34.3 0.0 copy-done.5
  34.3 0.0 copy-done.6
  34.3 0.6 shard_map.114
  35.0 1.1 collective-permute-done.3
  36.1 0.0 all-to-all-done.1
  36.1 10.1 %shard_map.115.refs_7_ = f32[256,256]{1,0:T(8,128)S(1)} custom-call(f32[256,256]{1,0:T(8,128)S(1)} %bitcast.36, bf16[512,256]{1,0:T(8,128)(2,1)S(1)} %get-tuple-element.6.refs_1_.xh_ref, bf16[512,256]{1,0:T(8,128)(2,1)S(1)} %get-tuple-element.7.refs_2_.xl_ref, bf16[512,256]{1,0:T(8,128)(2,1)S(1)} %get-tuple-element.8.refs_3_.yh_ref, ...), custom_call_target="tpu_custom_call" | custom-call | tf_op jit(solution)/shard_map/pallas_call | solution.py:194
  46.2 0.0 copy-start.1
  46.2 0.0 copy-start.2
  46.2 15.8 %all_to_all.40 = f32[16,16,256]{2,1,0:T(8,128)S(1)} all-to-all(f32[16,16,256]{2,1,0:T(8,128)S(1)} %bitcast.26), channel_id=1, replica_groups=mesh['grp'=2,'tm'=16] {'tm'}, dimensions={0} | all-to-all | bytes 524288 | tf_op jit(solution)/shard_map/all_to_all | solution.py:168
  62.1 1.2 shard_map.116
  63.2 3.6 %all-to-all-start.3 = ((f32[16,16,512]{2,1,0:T(8,128)}), f32[16,16,512]{2,1,0:T(8,128)S(1)}, u32[]{:S(2)}, u32[]{:S(2)}) async-start(f32[16,16,512]{2,1,0:T(8,128)} %bitcast.6), calls=%async_computation.3 | async-start | bytes 1048576 | tf_op jit(solution)/shard_map/all_to_all | solution.py:168
  66.8 4.3 %collective-permute-start.5 = (f32[256,256]{1,0:T(8,128)S(1)}, f32[256,256]{1,0:T(8,128)S(1)}, u32[]{:S(2)}, u32[]{:S(2)}) collective-permute-start(f32[256,256]{1,0:T(8,128)S(1)} %get-tuple-element.12.damp_ref), channel_id=1, source_target_pairs={{0,15},{1,0},{2,1},{3,2},{4,3},{5,4},{6,5},{7,6},{8,7},{9,8},{10,9... | collective-permute-start | bytes 786440 | tf_op jit(solution)/shard_map/ppermute | solution.py:178
  71.1 9.9 %all-to-all-done.3 = f32[16,16,512]{2,1,0:T(8,128)S(1)} async-done(((f32[16,16,512]{2,1,0:T(8,128)}), f32[16,16,512]{2,1,0:T(8,128)S(1)}, u32[]{:S(2)}, u32[]{:S(2)}) %all-to-all-start.3) | async-done | bytes 524320 | tf_op jit(solution)/shard_map/all_to_all | solution.py:168
  81.1 0.7 slice.8
  81.8 0.1 collective-permute-start.4
  81.9 0.0 collective-permute-done.5.damp_next_ref
  81.9 1.8 %collective-permute-done.4.other_ref = f32[256,256]{1,0:T(8,128)} collective-permute-done((f32[256,256]{1,0:T(8,128)}, f32[256,256]{1,0:T(8,128)}, u32[]{:S(2)}, u32[]{:S(2)}) %collective-permute-start.4) | collective-permute-done | bytes 262176 | tf_op jit(solution)/shard_map/ppermute | solution.py:202
  83.7 2.4 %shard_map.117 = f32[256,256]{1,0:T(8,128)S(1)} custom-call(f32[1,256]{1,0:T(1,128)S(1)} %broadcast_in_dim.15.even_ref, f32[256,512]{1,0:T(8,128)S(1)} %bitcast.25, f32[256,256]{1,0:T(8,128)} %collective-permute-done.4.other_ref, f32[256,256]{1,0:T(8,128)S(1)} %get-tuple-element.12.damp_ref, f32[256,256]{1,0:T(8,128)S(1)} %collective-permute-done.5.damp_next_ref, ...), custom_call_target="tpu_custom_call" | custom-call | tf_op jit(solution)/shard_map/pallas_call | solution.py:206
  86.0 16.7 %all_to_all.41 = f32[16,16,256]{2,1,0:T(8,128)S(1)} all-to-all(f32[16,16,256]{2,1,0:T(8,128)S(1)} %bitcast.39), channel_id=1, replica_groups=mesh['grp'=2,'tm'=16] {'tm'}, dimensions={0} | all-to-all | bytes 524288 | tf_op jit(solution)/shard_map/all_to_all | solution.py:168
  102.8 0.3 shard_map.118
  103.0 12.7 %all_to_all.42 = f32[16,16,256]{2,1,0:T(8,128)S(1)} all-to-all(f32[16,16,256]{2,1,0:T(8,128)S(1)} %bitcast.33), channel_id=1, replica_groups=mesh['grp'=2,'tm'=16] {'tm'}, dimensions={0} | all-to-all | bytes 524288 | tf_op jit(solution)/shard_map/all_to_all | solution.py:168
  115.7 10.1 %shard_map.119 = f32[256,256]{1,0:T(8,128)S(1)} custom-call(f32[256,256]{1,0:T(8,128)S(1)} %bitcast.37, bf16[512,256]{1,0:T(8,128)(2,1)S(1)} %get-tuple-element.6.refs_1_.xh_ref, bf16[512,256]{1,0:T(8,128)(2,1)S(1)} %get-tuple-element.7.refs_2_.xl_ref, bf16[512,256]{1,0:T(8,128)(2,1)S(1)} %get-tuple-element.8.refs_3_.yh_ref, ...), custom_call_target="tpu_custom_call" | custom-call | tf_op jit(solution)/shard_map/pallas_call | solution.py:194
  125.9 12.7 %all_to_all.43 = f32[16,16,256]{2,1,0:T(8,128)S(1)} all-to-all(f32[16,16,256]{2,1,0:T(8,128)S(1)} %bitcast.38), channel_id=1, replica_groups=mesh['grp'=2,'tm'=16] {'tm'}, dimensions={0} | all-to-all | bytes 524288 | tf_op jit(solution)/shard_map/all_to_all | solution.py:168
  138.6 0.4 shard_map.120
  138.9 16.9 %all_to_all.44 = f32[16,16,512]{2,1,0:T(8,128)S(1)} all-to-all(f32[16,16,512]{2,1,0:T(8,128)S(1)} %bitcast.30), channel_id=1, replica_groups=mesh['grp'=2,'tm'=16] {'tm'}, dimensions={0} | all-to-all | bytes 1048576 | tf_op jit(solution)/shard_map/all_to_all | solution.py:168
  155.9 0.7 fusion
  156.6 0.1 collective-permute-start.6
  156.8 1.4 collective-permute-done.6.other_ref
  158.2 2.1 %shard_map.121 = f32[256,256]{1,0:T(8,128)} custom-call(f32[1,256]{1,0:T(1,128)S(1)} %broadcast_in_dim.15.even_ref, f32[256,512]{1,0:T(8,128)S(1)} %bitcast.23, f32[256,256]{1,0:T(8,128)S(1)} %collective-permute-done.6.other_ref, f32[256,256]{1,0:T(8,128)S(1)} %get-tuple-element.12.damp_ref, f32[256,256]{1,0:T(8,128)S(1)} %collective-permute-done.5.damp_next_ref, ...), custom_call_target="tpu_custom_call" | custom-call | tf_op jit(solution)/shard_map/pallas_call | solution.py:206
  (12 shorter events, 0.0 us)
Async XLA Ops:
  0.6 7.6 %copy-start.7 = (s32[1,256,256]{2,1,0:T(8,128)S(1)}, s32[1,256,256]{2,1,0:T(8,128)}, u32[]{:S(2)}) copy-start(s32[1,256,256]{2,1,0:T(8,128)} %param.11) | copy-start | bytes 786436
  0.6 17.6 %all-to-all-start = ((f32[16,16,256]{2,1,0:T(8,128)}), f32[16,16,256]{2,1,0:T(8,128)S(1)}, u32[]{:S(2)}, u32[]{:S(2)}) async-start(f32[16,16,256]{2,1,0:T(8,128)} %bitcast.27), calls=%async_computation | async-start | bytes 524288 | tf_op jit(solution)/shard_map/all_to_all | solution.py:168
  8.2 10.0 %copy-start.3 = (bf16[256,256]{1,0:T(8,128)(2,1)S(1)}, bf16[256,256]{1,0:T(8,128)(2,1)}, u32[]{:S(2)}) copy-start(bf16[256,256]{1,0:T(8,128)(2,1)} %constant.54.clone.th_ref) | copy-start | bytes 393220
  8.2 10.0 %copy-start.4 = (bf16[256,256]{1,0:T(8,128)(2,1)S(1)}, bf16[256,256]{1,0:T(8,128)(2,1)}, u32[]{:S(2)}) copy-start(bf16[256,256]{1,0:T(8,128)(2,1)} %constant.55.clone.tl_ref) | copy-start | bytes 393220
  9.6 13.3 %collective-permute-start = (f32[1,256]{1,0:T(1,128)S(1)}, f32[1,256]{1,0:T(1,128)S(1)}, u32[]{:S(2)}, u32[]{:S(2)}) collective-permute-start(f32[1,256]{1,0:T(1,128)S(1)} %broadcast_in_dim.16), channel_id=1, source_target_pairs={{0,1},{1,0},{2,3},{3,2},{4,5},{5,4},{6,7},{7,6},{8,9},{9,8},{10,11... | collective-permute-start | bytes 3080 | tf_op jit(solution)/shard_map/ppermute | solution.py:159
  19.2 15.1 %copy-start.5 = (f32[256,256]{1,0:T(8,128)S(1)}, f32[256,256]{1,0:T(8,128)}, u32[]{:S(2)}) copy-start(f32[256,256]{1,0:T(8,128)} %hop_x_ref.1) | copy-start | bytes 786436
  19.2 15.1 %copy-start.6 = (f32[256,256]{1,0:T(8,128)S(1)}, f32[256,256]{1,0:T(8,128)}, u32[]{:S(2)}) copy-start(f32[256,256]{1,0:T(8,128)} %hop_y_ref.1) | copy-start | bytes 786436
  19.2 16.9 %all-to-all-start.1 = ((f32[16,16,256]{2,1,0:T(8,128)}), f32[16,16,256]{2,1,0:T(8,128)S(1)}, u32[]{:S(2)}, u32[]{:S(2)}) async-start(f32[16,16,256]{2,1,0:T(8,128)} %bitcast.2), calls=%async_computation.1 | async-start | bytes 524288 | tf_op jit(solution)/shard_map/all_to_all | solution.py:168
  23.5 3.7 %collective-permute-start.1 = (f32[1,256]{1,0:T(1,128)S(1)}, f32[1,256]{1,0:T(1,128)S(1)}, u32[]{:S(2)}, u32[]{:S(2)}) collective-permute-start(f32[1,256]{1,0:T(1,128)S(1)} %broadcast_add_fusion), channel_id=1, source_target_pairs={{0,2},{1,3},{2,0},{3,1},{4,6},{5,7},{6,4},{7,5},{8,10},{9,11},{10,... | collective-permute-start | bytes 3080 | tf_op jit(solution)/shard_map/ppermute | solution.py:159
  27.9 3.6 %collective-permute-start.2 = (f32[1,256]{1,0:T(1,128)S(1)}, f32[1,256]{1,0:T(1,128)S(1)}, u32[]{:S(2)}, u32[]{:S(2)}) collective-permute-start(f32[1,256]{1,0:T(1,128)S(1)} %fusion.1), channel_id=1, source_target_pairs={{0,4},{1,5},{2,6},{3,7},{4,0},{5,1},{6,2},{7,3},{8,12},{9,13},{10,... | collective-permute-start | bytes 3080 | tf_op jit(solution)/shard_map/ppermute | solution.py:159
  31.6 4.5 %collective-permute-start.3 = (f32[1,256]{1,0:T(1,128)S(1)}, f32[1,256]{1,0:T(1,128)S(1)}, u32[]{:S(2)}, u32[]{:S(2)}) collective-permute-start(f32[1,256]{1,0:T(1,128)S(1)} %add.25), channel_id=1, source_target_pairs={{0,8},{1,9},{2,10},{3,11},{4,12},{5,13},{6,14},{7,15},{8,0},{9,1},... | collective-permute-start | bytes 3080 | tf_op jit(solution)/shard_map/ppermute | solution.py:159
  46.2 15.8 %copy-start.1 = (bf16[512,256]{1,0:T(8,128)(2,1)S(1)}, bf16[512,256]{1,0:T(8,128)(2,1)}, u32[]{:S(2)}) copy-start(bf16[512,256]{1,0:T(8,128)(2,1)} %constant.62.th_ref) | copy-start | bytes 786436
  46.2 15.8 %copy-start.2 = (bf16[512,256]{1,0:T(8,128)(2,1)S(1)}, bf16[512,256]{1,0:T(8,128)(2,1)}, u32[]{:S(2)}) copy-start(bf16[512,256]{1,0:T(8,128)(2,1)} %constant.63.tl_ref) | copy-start | bytes 786436
  63.2 17.8 %all-to-all-start.3 = ((f32[16,16,512]{2,1,0:T(8,128)}), f32[16,16,512]{2,1,0:T(8,128)S(1)}, u32[]{:S(2)}, u32[]{:S(2)}) async-start(f32[16,16,512]{2,1,0:T(8,128)} %bitcast.6), calls=%async_computation.3 | async-start | bytes 1048576 | tf_op jit(solution)/shard_map/all_to_all | solution.py:168
  66.8 15.1 %collective-permute-start.5 = (f32[256,256]{1,0:T(8,128)S(1)}, f32[256,256]{1,0:T(8,128)S(1)}, u32[]{:S(2)}, u32[]{:S(2)}) collective-permute-start(f32[256,256]{1,0:T(8,128)S(1)} %get-tuple-element.12.damp_ref), channel_id=1, source_target_pairs={{0,15},{1,0},{2,1},{3,2},{4,3},{5,4},{6,5},{7,6},{8,7},{9,8},{10,9... | collective-permute-start | bytes 786440 | tf_op jit(solution)/shard_map/ppermute | solution.py:178
  81.1 2.6 %copy-start = (f32[1,256,256]{2,1,0:T(8,128)S(1)}, f32[1,256,256]{2,1,0:T(8,128)}, u32[]{:S(2)}) copy-start(f32[1,256,256]{2,1,0:T(8,128)} %param.10) | copy-start | bytes 786436
  81.8 1.9 %collective-permute-start.4 = (f32[256,256]{1,0:T(8,128)}, f32[256,256]{1,0:T(8,128)}, u32[]{:S(2)}, u32[]{:S(2)}) collective-permute-start(f32[256,256]{1,0:T(8,128)} %slice.8), channel_id=1, source_target_pairs={{0,1},{1,0},{2,3},{3,2},{4,5},{5,4},{6,7},{7,6},{8,9},{9,8},{10,11... | collective-permute-start | bytes 786440 | tf_op jit(solution)/shard_map/ppermute | solution.py:202
  156.6 1.5 collective-permute-start.6
where the time goes:
time: 161 us; the launch traced here: 160 us
  blocking collectives  74.9 us (47%)
  Pallas kernels  28.2 us (18%)
  starting transfers between devices  26.1 us (16%)
  waiting for transfers between devices  26.1 us (16%)
  local copies, waits for them, and re-layouts  2.15 us (1%)
  other arithmetic  1.97 us (1%)
    all_to_all x5, blocking collectives, exchange(): lax.all_to_all(blocks, axis, split_axis=0, concat_axis=0, tiled=True)  74.9 us
    pallas_call x2, Pallas kernels, chebyshev(): call(chebyshev_kernel, field_shape, len(operands), [pltpu.VMEM((16, side_...  20.3 us
    all_to_all x3, waiting for transfers between devices, exchange(): lax.all_to_all(blocks, axis, split_axis=0, concat_axis=0, tiled=True)  18.1 us
    all_to_all x3, starting transfers between devices, exchange(): lax.all_to_all(blocks, axis, split_axis=0, concat_axis=0, tiled=True)  14.8 us
    ppermute x4, starting transfers between devices, total_over(): lax.ppermute(value, axis, [(i, i ^ step) for i in range(count)])  6.78 us
    ppermute x4, waiting for transfers between devices, total_over(): lax.ppermute(value, axis, [(i, i ^ step) for i in range(count)])  4.8 us
    pallas_call x2, Pallas kernels, residual_of(): call(normal_kernel, field_shape, 10)  4.47 us
    ppermute x1, starting transfers between devices, per_device(): lax.ppermute(damp, 'tm', [(i, (i - 1) % length) for i in range(length)])  4.32 us
  transfers between devices with their start and end apart: 10, of which 7 were waited for; matrix products, arithmetic and copies ran while one was open for 2% of the time, Pallas kernels for 1%

commit v1 on v0

--- a/solution.py
+++ b/solution.py
@@ -16,7 +16,7 @@
 VMEM = pl.BlockSpec(memory_space=pltpu.VMEM)
 
 
-def call(kernel, out_shape, count, scratch=()):
+def call(kernel, out_shape, count, scratch=(), passes=0):
     return pl.pallas_call(
         kernel,
         out_shape=out_shape,
@@ -24,6 +24,7 @@
         out_specs=jax.tree.map(lambda _: VMEM, out_shape),
         scratch_shapes=list(scratch),
         compiler_params=pltpu.CompilerParams(vmem_limit_bytes=16 << 20),
+        cost_estimate=pl.CostEstimate(flops=passes, transcendentals=0, bytes_accessed=0) if passes else None,
     )
 
 
@@ -66,7 +67,8 @@
     out_ref, weight_ref = refs[-2:]
     side_x = field_ref.shape[0]
     side_y = field_ref.shape[1]
-    cbar = jnp.exp(-0.05 * (sum_ref[...] - MIDDLE))
+    mean_level = jnp.sum(sum_ref[...], axis=0, keepdims=True)
+    cbar = jnp.exp(-0.05 * (mean_level - MIDDLE))
     lower = 0.05
     root_lower = math.sqrt(lower)
     root_upper = 1.0 + 3.0 * cbar
@@ -81,28 +83,29 @@
         weight_ref[degree : degree + 1, :] = weight
         weight = weight * -ratio
     field = field_ref[...]
-    x_pair = (xh_ref[...], xl_ref[...])
-
-    def step(index, carry):
-        ahead, second = carry
-        inner = dot3(x_pair, split(ahead))
-        first_h, first_l = split(inner[:side_x] * once)
-        second_h, second_l = split(inner[side_x:] * twice)
-        hops = dot3((first_h, first_l), (yh_ref[:side_y], yl_ref[:side_y])) + dot3(
-            (second_h, second_l), (yh_ref[side_y:], yl_ref[side_y:])
-        )
+    half = side_x // 2
+
+    def left(start, value):
+        window = slice(start, start + half)
+        return dot3((xh_ref[window], xl_ref[window]), value)
+
+    def body(index, carry):
+        ahead, second, _ = carry
+        value = split(ahead)
         row = weight_ref[pl.ds(ORDER - 1 - index, 1), :]
-        return (row * field + keep * ahead - second) + hops, ahead
-
-    last = weight_ref[ORDER : ORDER + 1, :] * field
-    ahead, before = last, last - last
-
-    def body(index, carry):
-        first, second, _ = carry
-        result, first_out = step(index, (first, second))
-        return result, first_out, second
-
-    result, _, second = lax.fori_loop(0, ORDER, body, (ahead, before, before))
+        inner = [
+            (split(left(start, value) * once), split(left(side_x + start, value) * twice)) for start in (0, half)
+        ]
+        parts = []
+        for start, (single, double) in zip((0, half), inner):
+            window = slice(start, start + half)
+            hops = dot3(single, (yh_ref[:side_y], yl_ref[:side_y])) + dot3(double, (yh_ref[side_y:], yl_ref[side_y:]))
+            parts.append((row * field[window] + keep * ahead[window] - second[window]) + hops)
+        return jnp.concatenate(parts, axis=0), ahead, second
+
+    ahead = weight_ref[ORDER : ORDER + 1, :] * field
+    before = ahead - ahead
+    result, _, second = lax.fori_loop(0, ORDER, body, (ahead, before, before), unroll=ORDER // 2)
     total = 0.5 * (result - second)
     out_ref[...] = total if add_ref is None else total + add_ref[...]
 
@@ -111,7 +114,8 @@
     even_ref, slices_ref, other_ref, damp_ref, damp_next_ref, noise_ref, xh_ref, xl_ref, yh_ref, yl_ref, out_ref
 ):
     side_x, side_y = other_ref.shape
-    x_pair = (xh_ref[:side_x], xl_ref[:side_x])
+    half = side_x // 2
+    windows = (slice(0, half), slice(half, side_x))
     y_pair = (yh_ref[:side_y], yl_ref[:side_y])
     even = even_ref[...] > 0.5
     far = slices_ref[:, :side_y]
@@ -122,11 +126,17 @@
     damp_next = damp_next_ref[...]
 
     def propagate(value):
-        return dot3(split(dot3(x_pair, split(value))), y_pair)
-
-    forward = here - propagate(damp_ref[...] * before)
-    forward_next = after - propagate(damp_next * here)
-    out_ref[...] = noise_ref[...] - (forward - damp_next * propagate(forward_next))
+        value = split(value)
+        inner = [split(dot3((xh_ref[window], xl_ref[window]), value)) for window in windows]
+        return [dot3(part, y_pair) for part in inner]
+
+    moved = propagate(damp_next * here)
+    forward_next = jnp.concatenate([after[window] - part for window, part in zip(windows, moved)], axis=0)
+    moved = propagate(damp_ref[...] * before)
+    carried = propagate(forward_next)
+    for window, part, back in zip(windows, moved, carried):
+        forward = here[window] - part
+        out_ref[window] = noise_ref[window] - (forward - damp_next[window] * back)
 
 
 def tables(length, rows):
@@ -150,15 +160,12 @@
     return forward, both
 
 
-def total_over(value, axis):
+def add_partners(value, axis, step):
     count = lax.axis_size(axis)
-    if count & (count - 1):
-        return lax.psum(value, axis)
-    step = 1
-    while step < count:
-        value = value + lax.ppermute(value, axis, [(i, i ^ step) for i in range(count)])
-        step *= 2
-    return value
+    value = jnp.sum(value, axis=0, keepdims=True)
+    shifts = range(1, min(4, count // step))
+    others = [lax.ppermute(value, axis, [(i, i ^ (step * shift)) for i in range(count)]) for shift in shifts]
+    return jnp.concatenate([value] + others, axis=0)
 
 
 def exchange(value, axis):
@@ -175,9 +182,7 @@
     noise = noise[0]
     levels = phonon_level[0].astype(F32)
     damp = jnp.exp(-0.05 * (levels - MIDDLE))
-    damp_next = lax.ppermute(damp, "tm", [(i, (i - 1) % length) for i in range(length)])
-    level_sum = total_over(jnp.full((1, side_y), jnp.sum(levels), F32), "tm")
-    mean_level = level_sum / (length * side_x * side_y)
+    mean_rows = jnp.full((1, side_y), jnp.sum(levels) / (length * side_x * side_y), F32)
     cosine = jnp.cos((2 * (position // 2) + 1).astype(F32) * (math.pi / length))
     cosine = jnp.full((1, side_y), cosine, F32)
     even = jnp.full((1, side_y), (position % 2 == 0).astype(F32), F32)
@@ -190,11 +195,15 @@
     to_spectrum = call(transform_kernel, field_shape, 3)
     to_times = call(transform_kernel, shape(side_x, 2 * side_y), 3)
 
+    work = 12 * ORDER * 2 * side_x * side_y * max(side_x, side_y)
+
     def chebyshev(*operands):
-        return call(chebyshev_kernel, field_shape, len(operands), [pltpu.VMEM((16, side_y), F32)])(*operands)
-
-    def spectrum(field):
-        return exchange(to_spectrum(exchange(field, "tm"), *forward), "tm")
+        return call(chebyshev_kernel, field_shape, len(operands), [pltpu.VMEM((16, side_y), F32)], work)(*operands)
+
+    def spectrum(field, beside):
+        block = to_spectrum(exchange(field, "tm"), *forward)
+        block, beside = lax.optimization_barrier((block, beside))
+        return exchange(block, "tm"), beside
 
     def slices_of(components):
         slices = exchange(to_times(exchange(components, "tm"), *back), "tm")
@@ -205,10 +214,22 @@
     def residual_of(slices, other):
         return call(normal_kernel, field_shape, 10)(even, slices, other, damp, damp_next, noise, *hops)
 
-    first = chebyshev(spectrum(noise), *hops, mean_level, cosine)
+    power_of_two = length & (length - 1) == 0
+    mean_rows = add_partners(mean_rows, "tm", 1) if power_of_two else lax.psum(mean_rows, "tm")
+    field, mean_rows = spectrum(noise, mean_rows)
+    step = 4
+    while power_of_two and step < length:
+        mean_rows = add_partners(mean_rows, "tm", step)
+        step *= 4
+    field, damp = lax.optimization_barrier((field, damp))
+    damp_next = lax.ppermute(damp, "tm", [(i, (i - 1) % length) for i in range(length)])
+    first = chebyshev(field, *hops, mean_rows, cosine)
+    first, damp_next = lax.optimization_barrier((first, damp_next))
+
     slices, _, other = slices_of(first)
     second_residual = residual_of(slices, other)
-    total = chebyshev(spectrum(second_residual), *hops, mean_level, cosine, first)
+    field, _ = spectrum(second_residual, cosine)
+    total = chebyshev(field, *hops, mean_rows, cosine, first)
     slices, result, other = slices_of(total)
     residual = residual_of(slices, other)
     return result[None], residual[None]

time: 161 us -> 145 us (0.901)
  waiting for transfers between devices: 26.1 us -> 14.4 us
  blocking collectives: 74.9 us -> 86.3 us
  Pallas kernels: 28.2 us -> 20 us
  starting transfers between devices: 26.1 us -> 19.4 us
    all_to_all x3 -> x2, waiting for transfers between devices: 18.1 us -> 3.71 us  [exchange(): lax.all_to_all(blocks, axis, split_axis=0, concat_axis=0, tiled=True)]
    all_to_all x5 -> x6, blocking collectives: 74.9 us -> 86.3 us  [exchange(): lax.all_to_all(blocks, axis, split_axis=0, concat_axis=0, tiled=True)]
    pallas_call x2, Pallas kernels: 20.3 us -> 13.4 us  [chebyshev(): call(chebyshev_kernel, field_shape, len(operands), [pltpu.VMEM((16, side_...]
    all_to_all x3 -> x2, starting transfers between devices: 14.8 us -> 11.2 us  [exchange(): lax.all_to_all(blocks, axis, split_axis=0, concat_axis=0, tiled=True)]
    ppermute x1, starting transfers between devices: 4.32 us -> 1.36 us  [per_device(): lax.ppermute(damp, 'tm', [(i, (i - 1) % length) for i in range(length)])]
    ppermute x4 -> x6, waiting for transfers between devices: 4.8 us -> 7.58 us  [add_partners(): lax.ppermute(value, axis, [(i, i ^ step * shift) for i in range(count)])]
    ppermute x4 -> x6, starting transfers between devices: 6.78 us -> 6.55 us  [add_partners(): lax.ppermute(value, axis, [(i, i ^ step * shift) for i in range(count)])]
  transfers between devices with their start and end apart: 10 -> 11, of which waited for: 7 -> 8; matrix products, arithmetic and copies ran while one was open for 2% -> 0% of each run, Pallas kernels for 1% -> 5%
where the time goes in v1:
time: 145 us; the launch traced here: 144 us
  blocking collectives  86.3 us (60%)
  Pallas kernels  20 us (14%)
  starting transfers between devices  19.4 us (13%)
  waiting for transfers between devices  14.4 us (10%)
  between operations  1.55 us (1%)
  local copies, waits for them, and re-layouts  1.51 us (1%)
    all_to_all x6, blocking collectives, exchange(): lax.all_to_all(blocks, axis, split_axis=0, concat_axis=0, tiled=True)  86.3 us
    pallas_call x2, Pallas kernels, chebyshev(): call(chebyshev_kernel, field_shape, len(operands), [pltpu.VMEM((16, side_...  13.4 us
    all_to_all x2, starting transfers between devices, exchange(): lax.all_to_all(blocks, axis, split_axis=0, concat_axis=0, tiled=True)  11.2 us
    ppermute x6, waiting for transfers between devices, add_partners(): lax.ppermute(value, axis, [(i, i ^ step * shift) for i in range(count)])  7.58 us
    ppermute x6, starting transfers between devices, add_partners(): lax.ppermute(value, axis, [(i, i ^ step * shift) for i in range(count)])  6.55 us
    pallas_call x2, Pallas kernels, residual_of(): call(normal_kernel, field_shape, 10)  3.97 us
    all_to_all x2, waiting for transfers between devices, exchange(): lax.all_to_all(blocks, axis, split_axis=0, concat_axis=0, tiled=True)  3.71 us
    ppermute x2, waiting for transfers between devices, slices_of(): other = lax.ppermute(here, 'tm', [(i, i ^ 1) for i in range(length)])  3.12 us
  transfers between devices with their start and end apart: 11, of which 8 were waited for; matrix products, arithmetic and copies ran while one was open for 0% of the time, Pallas kernels for 5%

profile of v1, /device:TPU:0, one launch (start us, length us, event | category | flops | bytes accessed | tf_op | source)
XLA Modules:
  0.0 144.0 jit_solution(9539435715966282291)
XLA Ops:
  0.6 0.0 copy-start.7
  0.6 7.6 %all-to-all-start = ((f32[16,16,256]{2,1,0:T(8,128)}), f32[16,16,256]{2,1,0:T(8,128)S(1)}, u32[]{:S(2)}, u32[]{:S(2)}) async-start(f32[16,16,256]{2,1,0:T(8,128)} %bitcast.27), calls=%async_computation | async-start | bytes 524288 | tf_op jit(solution)/shard_map/all_to_all | solution.py:175
  8.2 0.0 copy-done.7
  8.2 0.0 copy-start.3
  8.2 0.0 copy-start.4
  8.2 0.7 exponential_bitcast_fusion
  9.6 1.7 %collective-permute-start.2 = (f32[1,256]{1,0:T(1,128)S(1)}, f32[1,256]{1,0:T(1,128)S(1)}, u32[]{:S(2)}, u32[]{:S(2)}) collective-permute-start(f32[1,256]{1,0:T(1,128)S(1)} %broadcast_in_dim.20), channel_id=1, source_target_pairs={{0,3},{1,2},{2,1},{3,0},{4,7},{5,6},{6,5},{7,4},{8,11},{9,10},{10,... | collective-permute-start | bytes 3080 | tf_op jit(solution)/shard_map/ppermute | solution.py:167
  11.3 0.4 collective-permute-start.1
  11.7 0.0 collective-permute-start
  11.7 1.1 collective-permute-done.2
  12.7 2.1 %collective-permute-done.1 = f32[1,256]{1,0:T(1,128)S(1)} collective-permute-done((f32[1,256]{1,0:T(1,128)S(1)}, f32[1,256]{1,0:T(1,128)S(1)}, u32[]{:S(2)}, u32[]{:S(2)}) %collective-permute-start.1) | collective-permute-done | bytes 1056 | tf_op jit(solution)/shard_map/ppermute | solution.py:167
  14.9 0.0 collective-permute-done
  14.9 3.3 %all-to-all-done = f32[16,16,256]{2,1,0:T(8,128)S(1)} async-done(((f32[16,16,256]{2,1,0:T(8,128)}), f32[16,16,256]{2,1,0:T(8,128)S(1)}, u32[]{:S(2)}, u32[]{:S(2)}) %all-to-all-start) | async-done | bytes 262176 | tf_op jit(solution)/shard_map/all_to_all | solution.py:175
  18.2 1.0 shard_map.113
  19.2 3.7 %all-to-all-start.1 = ((f32[16,16,256]{2,1,0:T(8,128)}), f32[16,16,256]{2,1,0:T(8,128)S(1)}, u32[]{:S(2)}, u32[]{:S(2)}) async-start(f32[16,16,256]{2,1,0:T(8,128)} %bitcast.2), calls=%async_computation.1 | async-start | bytes 524288 | tf_op jit(solution)/shard_map/all_to_all | solution.py:175
  22.9 3.7 %collective-permute-start.5 = (f32[1,256]{1,0:T(1,128)S(1)}, f32[1,256]{1,0:T(1,128)S(1)}, u32[]{:S(2)}, u32[]{:S(2)}) collective-permute-start(f32[1,256]{1,0:T(1,128)S(1)} %bitcast.43), channel_id=1, source_target_pairs={{0,12},{1,13},{2,14},{3,15},{4,8},{5,9},{6,10},{7,11},{8,4},{9,5},... | collective-permute-start | bytes 3080 | tf_op jit(solution)/shard_map/ppermute | solution.py:167
  26.6 0.0 collective-permute-start.4
  26.6 0.7 collective-permute-start.3
  27.5 0.6 shard_map.114
  28.1 3.9 %collective-permute-done.5 = f32[1,256]{1,0:T(1,128)S(1)} collective-permute-done((f32[1,256]{1,0:T(1,128)S(1)}, f32[1,256]{1,0:T(1,128)S(1)}, u32[]{:S(2)}, u32[]{:S(2)}) %collective-permute-start.5) | collective-permute-done | bytes 1056 | tf_op jit(solution)/shard_map/ppermute | solution.py:167
  32.0 0.5 collective-permute-done.4
  32.5 0.0 collective-permute-done.3
  32.5 0.4 all-to-all-done.1
  32.9 1.4 collective-permute-start.6
  34.2 6.7 %shard_map.115.refs_7_ = f32[256,256]{1,0:T(8,128)S(1)} custom-call(f32[256,256]{1,0:T(8,128)S(1)} %bitcast.38, bf16[512,256]{1,0:T(8,128)(2,1)S(1)} %get-tuple-element.15.refs_1_.xh_ref, bf16[512,256]{1,0:T(8,128)(2,1)S(1)} %get-tuple-element.16.refs_2_.xl_ref, bf16[512,256]{1,0:T(8,128)(2,1)S(1)} %get-tuple-element.17.refs_3_.yh_ref, ...), custom_call_target="tpu_custom_call" | custom-call | flops 4026531840 | tf_op jit(solution)/shard_map/pallas_call | solution.py:201
  41.0 0.0 collective-permute-done.6.damp_next_ref
  41.0 0.0 copy-start.1
  41.0 0.0 copy-start.2
  41.0 13.1 %all_to_all.40 = f32[16,16,256]{2,1,0:T(8,128)S(1)} all-to-all(f32[16,16,256]{2,1,0:T(8,128)S(1)} %bitcast.39), channel_id=1, replica_groups=mesh['grp'=2,'tm'=16] {'tm'}, dimensions={0} | all-to-all | bytes 524288 | tf_op jit(solution)/shard_map/all_to_all | solution.py:175
  54.1 0.0 copy-done.1
  54.1 0.4 shard_map.116
  54.4 16.9 %all_to_all.41 = f32[16,16,512]{2,1,0:T(8,128)S(1)} all-to-all(f32[16,16,512]{2,1,0:T(8,128)S(1)} %bitcast.31), channel_id=1, replica_groups=mesh['grp'=2,'tm'=16] {'tm'}, dimensions={0} | all-to-all | bytes 1048576 | tf_op jit(solution)/shard_map/all_to_all | solution.py:175
  71.4 0.7 slice.8
  72.1 0.1 collective-permute-start.7
  72.3 1.7 %collective-permute-done.7.other_ref = f32[256,256]{1,0:T(8,128)} collective-permute-done((f32[256,256]{1,0:T(8,128)}, f32[256,256]{1,0:T(8,128)}, u32[]{:S(2)}, u32[]{:S(2)}) %collective-permute-start.7) | collective-permute-done | bytes 262176 | tf_op jit(solution)/shard_map/ppermute | solution.py:211
  74.0 0.0 copy-done
  74.0 2.1 %shard_map.117 = f32[256,256]{1,0:T(8,128)S(1)} custom-call(f32[1,256]{1,0:T(1,128)S(1)} %broadcast_in_dim.19.even_ref, f32[256,512]{1,0:T(8,128)S(1)} %bitcast.26, f32[256,256]{1,0:T(8,128)} %collective-permute-done.7.other_ref, f32[256,256]{1,0:T(8,128)S(1)} %get-tuple-element.20.damp_ref, f32[256,256]{1,0:T(8,128)S(1)} %collective-permute-done.6.damp_next_ref, ...), custom_call_target="tpu_custom_call" | custom-call | tf_op jit(solution)/shard_map/pallas_call | solution.py:215
  76.1 14.0 %all_to_all.42 = f32[16,16,256]{2,1,0:T(8,128)S(1)} all-to-all(f32[16,16,256]{2,1,0:T(8,128)S(1)} %bitcast.37), channel_id=1, replica_groups=mesh['grp'=2,'tm'=16] {'tm'}, dimensions={0} | all-to-all | bytes 524288 | tf_op jit(solution)/shard_map/all_to_all | solution.py:175
  90.1 0.3 shard_map.118
  90.4 12.7 %all_to_all.43 = f32[16,16,256]{2,1,0:T(8,128)S(1)} all-to-all(f32[16,16,256]{2,1,0:T(8,128)S(1)} %bitcast.34), channel_id=1, replica_groups=mesh['grp'=2,'tm'=16] {'tm'}, dimensions={0} | all-to-all | bytes 524288 | tf_op jit(solution)/shard_map/all_to_all | solution.py:175
  103.1 6.7 %shard_map.119 = f32[256,256]{1,0:T(8,128)S(1)} custom-call(f32[256,256]{1,0:T(8,128)S(1)} %bitcast.40, bf16[512,256]{1,0:T(8,128)(2,1)S(1)} %get-tuple-element.15.refs_1_.xh_ref, bf16[512,256]{1,0:T(8,128)(2,1)S(1)} %get-tuple-element.16.refs_2_.xl_ref, bf16[512,256]{1,0:T(8,128)(2,1)S(1)} %get-tuple-element.17.refs_3_.yh_ref, ...), custom_call_target="tpu_custom_call" | custom-call | flops 4026531840 | tf_op jit(solution)/shard_map/pallas_call | solution.py:201
  109.8 12.7 %all_to_all.44 = f32[16,16,256]{2,1,0:T(8,128)S(1)} all-to-all(f32[16,16,256]{2,1,0:T(8,128)S(1)} %bitcast.41), channel_id=1, replica_groups=mesh['grp'=2,'tm'=16] {'tm'}, dimensions={0} | all-to-all | bytes 524288 | tf_op jit(solution)/shard_map/all_to_all | solution.py:175
  122.5 0.4 shard_map.120
  122.9 16.9 %all_to_all.45 = f32[16,16,512]{2,1,0:T(8,128)S(1)} all-to-all(f32[16,16,512]{2,1,0:T(8,128)S(1)} %bitcast.30), channel_id=1, replica_groups=mesh['grp'=2,'tm'=16] {'tm'}, dimensions={0} | all-to-all | bytes 1048576 | tf_op jit(solution)/shard_map/all_to_all | solution.py:175
  139.8 0.7 fusion
  140.6 0.1 collective-permute-start.8
  140.7 1.4 collective-permute-done.8.other_ref
  142.1 1.9 %shard_map.121 = f32[256,256]{1,0:T(8,128)} custom-call(f32[1,256]{1,0:T(1,128)S(1)} %broadcast_in_dim.19.even_ref, f32[256,512]{1,0:T(8,128)S(1)} %bitcast.24, f32[256,256]{1,0:T(8,128)S(1)} %collective-permute-done.8.other_ref, f32[256,256]{1,0:T(8,128)S(1)} %get-tuple-element.20.damp_ref, f32[256,256]{1,0:T(8,128)S(1)} %collective-permute-done.6.damp_next_ref, ...), custom_call_target="tpu_custom_call" | custom-call | tf_op jit(solution)/shard_map/pallas_call | solution.py:215
  (14 shorter events, 0.1 us)
Async XLA Ops:
  0.6 7.6 %copy-start.7 = (s32[1,256,256]{2,1,0:T(8,128)S(1)}, s32[1,256,256]{2,1,0:T(8,128)}, u32[]{:S(2)}) copy-start(s32[1,256,256]{2,1,0:T(8,128)} %param.11) | copy-start | bytes 786436
  0.6 17.6 %all-to-all-start = ((f32[16,16,256]{2,1,0:T(8,128)}), f32[16,16,256]{2,1,0:T(8,128)S(1)}, u32[]{:S(2)}, u32[]{:S(2)}) async-start(f32[16,16,256]{2,1,0:T(8,128)} %bitcast.27), calls=%async_computation | async-start | bytes 524288 | tf_op jit(solution)/shard_map/all_to_all | solution.py:175
  8.2 10.0 %copy-start.3 = (bf16[256,256]{1,0:T(8,128)(2,1)S(1)}, bf16[256,256]{1,0:T(8,128)(2,1)}, u32[]{:S(2)}) copy-start(bf16[256,256]{1,0:T(8,128)(2,1)} %constant.55.clone.tl_ref) | copy-start | bytes 393220
  8.2 10.0 %copy-start.4 = (bf16[256,256]{1,0:T(8,128)(2,1)S(1)}, bf16[256,256]{1,0:T(8,128)(2,1)}, u32[]{:S(2)}) copy-start(bf16[256,256]{1,0:T(8,128)(2,1)} %constant.54.clone.th_ref) | copy-start | bytes 393220
  9.6 3.2 %collective-permute-start.2 = (f32[1,256]{1,0:T(1,128)S(1)}, f32[1,256]{1,0:T(1,128)S(1)}, u32[]{:S(2)}, u32[]{:S(2)}) collective-permute-start(f32[1,256]{1,0:T(1,128)S(1)} %broadcast_in_dim.20), channel_id=1, source_target_pairs={{0,3},{1,2},{2,1},{3,0},{4,7},{5,6},{6,5},{7,4},{8,11},{9,10},{10,... | collective-permute-start | bytes 3080 | tf_op jit(solution)/shard_map/ppermute | solution.py:167
  11.3 3.6 %collective-permute-start.1 = (f32[1,256]{1,0:T(1,128)S(1)}, f32[1,256]{1,0:T(1,128)S(1)}, u32[]{:S(2)}, u32[]{:S(2)}) collective-permute-start(f32[1,256]{1,0:T(1,128)S(1)} %broadcast_in_dim.20), channel_id=1, source_target_pairs={{0,2},{1,3},{2,0},{3,1},{4,6},{5,7},{6,4},{7,5},{8,10},{9,11},{10,... | collective-permute-start | bytes 3080 | tf_op jit(solution)/shard_map/ppermute | solution.py:167
  11.7 3.2 %collective-permute-start = (f32[1,256]{1,0:T(1,128)S(1)}, f32[1,256]{1,0:T(1,128)S(1)}, u32[]{:S(2)}, u32[]{:S(2)}) collective-permute-start(f32[1,256]{1,0:T(1,128)S(1)} %broadcast_in_dim.20), channel_id=1, source_target_pairs={{0,1},{1,0},{2,3},{3,2},{4,5},{5,4},{6,7},{7,6},{8,9},{9,8},{10,11... | collective-permute-start | bytes 3080 | tf_op jit(solution)/shard_map/ppermute | solution.py:167
  19.2 8.2 %copy-start.5 = (f32[256,256]{1,0:T(8,128)S(1)}, f32[256,256]{1,0:T(8,128)}, u32[]{:S(2)}) copy-start(f32[256,256]{1,0:T(8,128)} %hop_x_ref.1) | copy-start | bytes 786436
  19.2 8.3 %copy-start.6 = (f32[256,256]{1,0:T(8,128)S(1)}, f32[256,256]{1,0:T(8,128)}, u32[]{:S(2)}) copy-start(f32[256,256]{1,0:T(8,128)} %hop_y_ref.1) | copy-start | bytes 786436
  19.2 13.7 %all-to-all-start.1 = ((f32[16,16,256]{2,1,0:T(8,128)}), f32[16,16,256]{2,1,0:T(8,128)S(1)}, u32[]{:S(2)}, u32[]{:S(2)}) async-start(f32[16,16,256]{2,1,0:T(8,128)} %bitcast.2), calls=%async_computation.1 | async-start | bytes 524288 | tf_op jit(solution)/shard_map/all_to_all | solution.py:175
  22.9 9.1 %collective-permute-start.5 = (f32[1,256]{1,0:T(1,128)S(1)}, f32[1,256]{1,0:T(1,128)S(1)}, u32[]{:S(2)}, u32[]{:S(2)}) collective-permute-start(f32[1,256]{1,0:T(1,128)S(1)} %bitcast.43), channel_id=1, source_target_pairs={{0,12},{1,13},{2,14},{3,15},{4,8},{5,9},{6,10},{7,11},{8,4},{9,5},... | collective-permute-start | bytes 3080 | tf_op jit(solution)/shard_map/ppermute | solution.py:167
  26.6 5.9 %collective-permute-start.4 = (f32[1,256]{1,0:T(1,128)S(1)}, f32[1,256]{1,0:T(1,128)S(1)}, u32[]{:S(2)}, u32[]{:S(2)}) collective-permute-start(f32[1,256]{1,0:T(1,128)S(1)} %bitcast.44), channel_id=1, source_target_pairs={{0,8},{1,9},{2,10},{3,11},{4,12},{5,13},{6,14},{7,15},{8,0},{9,1},... | collective-permute-start | bytes 3080 | tf_op jit(solution)/shard_map/ppermute | solution.py:167
  26.6 5.9 %collective-permute-start.3 = (f32[1,256]{1,0:T(1,128)S(1)}, f32[1,256]{1,0:T(1,128)S(1)}, u32[]{:S(2)}, u32[]{:S(2)}) collective-permute-start(f32[1,256]{1,0:T(1,128)S(1)} %bitcast.45), channel_id=1, source_target_pairs={{0,4},{1,5},{2,6},{3,7},{4,0},{5,1},{6,2},{7,3},{8,12},{9,13},{10,... | collective-permute-start | bytes 3080 | tf_op jit(solution)/shard_map/ppermute | solution.py:167
  32.9 8.1 %collective-permute-start.6 = (f32[256,256]{1,0:T(8,128)S(1)}, f32[256,256]{1,0:T(8,128)S(1)}, u32[]{:S(2)}, u32[]{:S(2)}) collective-permute-start(f32[256,256]{1,0:T(8,128)S(1)} %get-tuple-element.20.damp_ref), channel_id=1, source_target_pairs={{0,15},{1,0},{2,1},{3,2},{4,3},{5,4},{6,5},{7,6},{8,7},{9,8},{10,9... | collective-permute-start | bytes 786440 | tf_op jit(solution)/shard_map/ppermute | solution.py:225
  41.0 13.1 %copy-start.1 = (bf16[512,256]{1,0:T(8,128)(2,1)S(1)}, bf16[512,256]{1,0:T(8,128)(2,1)}, u32[]{:S(2)}) copy-start(bf16[512,256]{1,0:T(8,128)(2,1)} %constant.63.tl_ref) | copy-start | bytes 786436
  41.0 13.1 %copy-start.2 = (bf16[512,256]{1,0:T(8,128)(2,1)S(1)}, bf16[512,256]{1,0:T(8,128)(2,1)}, u32[]{:S(2)}) copy-start(bf16[512,256]{1,0:T(8,128)(2,1)} %constant.62.th_ref) | copy-start | bytes 786436
  71.4 2.6 %copy-start = (f32[1,256,256]{2,1,0:T(8,128)S(1)}, f32[1,256,256]{2,1,0:T(8,128)}, u32[]{:S(2)}) copy-start(f32[1,256,256]{2,1,0:T(8,128)} %param.10) | copy-start | bytes 786436
  72.1 1.9 %collective-permute-start.7 = (f32[256,256]{1,0:T(8,128)}, f32[256,256]{1,0:T(8,128)}, u32[]{:S(2)}, u32[]{:S(2)}) collective-permute-start(f32[256,256]{1,0:T(8,128)} %slice.8), channel_id=1, source_target_pairs={{0,1},{1,0},{2,3},{3,2},{4,5},{5,4},{6,7},{7,6},{8,9},{9,8},{10,11... | collective-permute-start | bytes 786440 | tf_op jit(solution)/shard_map/ppermute | solution.py:211
  140.6 1.5 %collective-permute-start.8 = (f32[256,256]{1,0:T(8,128)S(1)}, f32[256,256]{1,0:T(8,128)S(1)}, u32[]{:S(2)}, u32[]{:S(2)}) collective-permute-start(f32[256,256]{1,0:T(8,128)S(1)} %get-tuple-element.24), channel_id=1, source_target_pairs={{0,1},{1,0},{2,3},{3,2},{4,5},{5,4},{6,7},{7,6},{8,9},{9,8},{10,11... | collective-permute-start | bytes 786440 | tf_op jit(solution)/shard_map/ppermute | solution.py:211

commit v2 on v1

--- a/solution.py
+++ b/solution.py
@@ -8,6 +8,7 @@
 from jax.experimental.pallas import tpu as pltpu
 from jax.sharding import PartitionSpec as P
 
+
 ORDER = 10
 LEVELS = 17
 MIDDLE = (LEVELS - 1) // 2
@@ -16,11 +17,11 @@
 VMEM = pl.BlockSpec(memory_space=pltpu.VMEM)
 
 
-def call(kernel, out_shape, count, scratch=(), passes=0):
+def call(kernel, out_shape, count, scratch=(), passes=0, scalars=0):
     return pl.pallas_call(
         kernel,
         out_shape=out_shape,
-        in_specs=[VMEM] * count,
+        in_specs=[pl.BlockSpec(memory_space=pltpu.SMEM)] * scalars + [VMEM] * count,
         out_specs=jax.tree.map(lambda _: VMEM, out_shape),
         scratch_shapes=list(scratch),
         compiler_params=pltpu.CompilerParams(vmem_limit_bytes=16 << 20),
@@ -110,54 +111,130 @@
     out_ref[...] = total if add_ref is None else total + add_ref[...]
 
 
+def residual_parts(before, here, after, damp, damp_next, noise_ref, x_refs, y_refs, out_ref):
+    side_x, side_y = here.shape
+    half = side_x // 2
+    windows = (slice(0, half), slice(half, side_x))
+    y_pair = tuple(ref[:side_y] for ref in y_refs)
+
+    def propagate(value):
+        value = split(value)
+        inner = [split(dot3((x_refs[0][window], x_refs[1][window]), value)) for window in windows]
+        return [dot3(part, y_pair) for part in inner]
+
+    moved = propagate(damp_next * here)
+    forward_next = jnp.concatenate([after[window] - part for window, part in zip(windows, moved)], axis=0)
+    moved = propagate(damp * before)
+    carried = propagate(forward_next)
+    for window, part, back in zip(windows, moved, carried):
+        forward = here[window] - part
+        out_ref[window] = noise_ref[window] - (forward - damp_next[window] * back)
+
+
 def normal_kernel(
     even_ref, slices_ref, other_ref, damp_ref, damp_next_ref, noise_ref, xh_ref, xl_ref, yh_ref, yl_ref, out_ref
 ):
-    side_x, side_y = other_ref.shape
-    half = side_x // 2
-    windows = (slice(0, half), slice(half, side_x))
-    y_pair = (yh_ref[:side_y], yl_ref[:side_y])
+    side_y = other_ref.shape[1]
     even = even_ref[...] > 0.5
     far = slices_ref[:, :side_y]
     here = slices_ref[:, side_y:]
     near = other_ref[...]
     before = jnp.where(even, far, near)
     after = jnp.where(even, near, far)
-    damp_next = damp_next_ref[...]
-
-    def propagate(value):
-        value = split(value)
-        inner = [split(dot3((xh_ref[window], xl_ref[window]), value)) for window in windows]
-        return [dot3(part, y_pair) for part in inner]
-
-    moved = propagate(damp_next * here)
-    forward_next = jnp.concatenate([after[window] - part for window, part in zip(windows, moved)], axis=0)
-    moved = propagate(damp_ref[...] * before)
-    carried = propagate(forward_next)
-    for window, part, back in zip(windows, moved, carried):
-        forward = here[window] - part
-        out_ref[window] = noise_ref[window] - (forward - damp_next[window] * back)
-
-
-def tables(length, rows):
+    damps = damp_ref[...], damp_next_ref[...]
+    residual_parts(before, here, after, *damps, noise_ref, (xh_ref, xl_ref), (yh_ref, yl_ref), out_ref)
+
+
+def gather_kernel(*refs):
+    weight_ref, keep_ref, send_ref = refs[0], refs[-2], refs[-1]
+    field_refs = refs[1:-2]
+    side_x, side_y = field_refs[0].shape
+    count = len(field_refs)
+    rows = 16
+
+    def body(index, carry):
+        window = pl.ds(pl.multiple_of(index * rows, rows), rows)
+        fields = [ref[window, :] for ref in field_refs]
+        for part in range(6):
+            total = weight_ref[part * count] * fields[0]
+            for place in range(1, count):
+                total = total + weight_ref[part * count + place] * fields[place]
+            target = keep_ref if part < 3 else send_ref
+            target[window, (part % 3) * side_y : (part % 3 + 1) * side_y] = total
+        return carry
+
+    lax.fori_loop(0, side_x // rows, body, 0, unroll=4)
+
+
+def finish_kernel(*refs):
+    weight_ref, keep_ref, other_ref = refs[:3]
+    low_ref, high_ref, low_other_ref, high_other_ref = refs[3:7]
+    damp_ref, damp_next_ref, noise_ref, xh_ref, xl_ref, yh_ref, yl_ref = refs[7:14]
+    out_refs = refs[14:]
+    side_y = damp_ref.shape[1]
+    last = jnp.concatenate([low_ref[...], high_ref[...]], axis=0)
+    last_other = jnp.concatenate([low_other_ref[...], high_other_ref[...]], axis=0)
+    slices = []
+    for part in range(3):
+        window = slice(part * side_y, (part + 1) * side_y)
+        total = keep_ref[:, window] + other_ref[:, window]
+        slices.append(total + (weight_ref[2 * part] * last + weight_ref[2 * part + 1] * last_other))
+    if len(out_refs) == 2:
+        out_refs[1][...] = slices[1]
+    damps = damp_ref[...], damp_next_ref[...]
+    residual_parts(*slices, *damps, noise_ref, (xh_ref, xl_ref), (yh_ref, yl_ref), out_refs[0])
+
+
+def basis_of(length):
     times = np.arange(length)
     phase = (2 * (times // 2)[:, None] + 1) * times[None, :] % (2 * length)
     angles = phase * (math.pi / length)
     basis = np.where((times % 2 == 0)[:, None], np.cos(angles), np.sin(angles))
-    inverse = basis.T * (2.0 / length)
-    far = np.where(times % 2 == 0, times - 1, times + 1)
-    wrapped = np.where((far < 0) | (far >= length), -1.0, 1.0)
-    inverse_far = inverse[far % length] * wrapped[:, None]
-
-    def parts(matrix):
-        matrix = np.kron(matrix, np.eye(rows))
-        high = matrix.astype(BF16)
-        return jnp.asarray(high), jnp.asarray((matrix - high.astype(np.float64)).astype(BF16))
-
-    forward = parts(basis)
-    back_far, back = parts(inverse_far), parts(inverse)
-    both = tuple(jnp.concatenate([a, b], axis=0) for a, b in zip(back_far, back))
-    return forward, both
+    return basis, basis.T * (2.0 / length)
+
+
+def times_of(inverse, slices):
+    length = inverse.shape[0]
+    outside = (slices < 0) | (slices >= length)
+    return inverse[slices % length] * np.where(outside, -1.0, 1.0)[:, None]
+
+
+def table_parts(matrix, rows):
+    matrix = np.kron(matrix, np.eye(rows))
+    high = matrix.astype(BF16)
+    return jnp.asarray(high), jnp.asarray((matrix - high.astype(np.float64)).astype(BF16))
+
+
+def ring_of(length):
+    chips = length // 2
+    return [*range(0, chips, 2), *reversed(range(1, chips, 2))]
+
+
+def ring_pairs(length, direction):
+    path = ring_of(length)
+    chips = len(path)
+    return [
+        (2 * path[i] + core, 2 * path[(i + direction) % chips] + core) for i in range(chips) for core in range(2)
+    ]
+
+
+def ring_weights(length):
+    _, inverse = basis_of(length)
+    path = ring_of(length)
+    chips = len(path)
+    reach = chips // 2
+    offsets = [0] + [sign * hop for hop in range(1, reach) for sign in (-1, 1)]
+    gathers, finishes = [], []
+    for device in range(length):
+        core = device % 2
+        place = path.index(device // 2)
+        arrivals = [2 * path[(place + offset) % chips] + core for offset in offsets]
+        own = times_of(inverse, np.arange(device - 1, device + 2))
+        partner = times_of(inverse, np.arange((device ^ 1) - 1, (device ^ 1) + 2))
+        far = 2 * path[(place + reach) % chips]
+        gathers.append(np.concatenate([own[:, arrivals].ravel(), partner[:, arrivals].ravel()]))
+        finishes.append(own[:, [far + core, far + 1 - core]].ravel())
+    return np.stack(gathers).astype(np.float32), np.stack(finishes).astype(np.float32)
 
 
 def add_partners(value, axis, step):
@@ -185,16 +262,16 @@
     mean_rows = jnp.full((1, side_y), jnp.sum(levels) / (length * side_x * side_y), F32)
     cosine = jnp.cos((2 * (position // 2) + 1).astype(F32) * (math.pi / length))
     cosine = jnp.full((1, side_y), cosine, F32)
-    even = jnp.full((1, side_y), (position % 2 == 0).astype(F32), F32)
-    forward, back = tables(length, side_x // length)
+    basis, inverse = basis_of(length)
+    forward = table_parts(basis, side_x // length)
+    chips = length // 2
+    ring = length % 4 == 0 and 4 <= chips <= 8 and side_x % 16 == 0
 
     hops = call(prepare_kernel, (shape(2 * side_x, side_x, BF16),) * 2 + (shape(2 * side_y, side_y, BF16),) * 2, 2)(
         hop_x, hop_y
     )
     field_shape = shape(side_x, side_y)
     to_spectrum = call(transform_kernel, field_shape, 3)
-    to_times = call(transform_kernel, shape(side_x, 2 * side_y), 3)
-
     work = 12 * ORDER * 2 * side_x * side_y * max(side_x, side_y)
 
     def chebyshev(*operands):
@@ -205,14 +282,49 @@
         block, beside = lax.optimization_barrier((block, beside))
         return exchange(block, "tm"), beside
 
-    def slices_of(components):
-        slices = exchange(to_times(exchange(components, "tm"), *back), "tm")
+    def by_exchange(components, turn):
+        times = np.arange(length)
+        far = times_of(inverse, np.where(times % 2 == 0, times - 1, times + 1))
+        back = [
+            jnp.concatenate(pair, axis=0)
+            for pair in zip(table_parts(far, side_x // length), table_parts(inverse, side_x // length))
+        ]
+        block = exchange(components, "tm")
+        slices = exchange(call(transform_kernel, shape(side_x, 2 * side_y), 3)(block, *back), "tm")
         here = slices[:, side_y:]
-        other = lax.ppermute(here, "tm", [(i, i ^ 1) for i in range(length)])
-        return slices, here, other
-
-    def residual_of(slices, other):
-        return call(normal_kernel, field_shape, 10)(even, slices, other, damp, damp_next, noise, *hops)
+        other = lax.ppermute(here, "tm", swap)
+        even = jnp.full((1, side_y), (position % 2 == 0).astype(F32), F32)
+        residual = call(normal_kernel, field_shape, 10)(even, slices, other, damp, damp_next, noise, *hops)
+        return (residual, here) if turn else (residual,)
+
+    def by_ring(components, turn):
+        gather_weights, finish_weights = (
+            lax.dynamic_index_in_dim(jnp.asarray(table), position, 0, keepdims=False) for table in ring_weights(length)
+        )
+        up, down = ring_pairs(length, 1), ring_pairs(length, -1)
+        going_up = going_down = components
+        arrived = [components]
+        for _ in range(chips // 2 - 1):
+            going_up = lax.ppermute(going_up, "tm", up)
+            going_down = lax.ppermute(going_down, "tm", down)
+            arrived += [going_up, going_down]
+        half = side_x // 2
+        low = lax.ppermute(going_up[:half], "tm", up)
+        high = lax.ppermute(going_down[half:], "tm", down)
+        wide = shape(side_x, 3 * side_y)
+        adds = 2 * 6 * len(arrived) * side_x * side_y
+        gather = call(gather_kernel, (wide, wide), len(arrived), passes=adds, scalars=1)
+        keep, send = gather(gather_weights, *arrived)
+        other = lax.ppermute(send, "tm", swap)
+        low_other = lax.ppermute(low, "tm", swap)
+        high_other = lax.ppermute(high, "tm", swap)
+        outs = (field_shape,) * (2 if turn else 1)
+        return call(finish_kernel, outs, 13, scalars=1)(
+            finish_weights, keep, other, low, high, low_other, high_other, damp, damp_next, noise, *hops
+        )
+
+    swap = [(i, i ^ 1) for i in range(length)]
+    residual_of = by_ring if ring else by_exchange
 
     power_of_two = length & (length - 1) == 0
     mean_rows = add_partners(mean_rows, "tm", 1) if power_of_two else lax.psum(mean_rows, "tm")
@@ -226,12 +338,10 @@
     first = chebyshev(field, *hops, mean_rows, cosine)
     first, damp_next = lax.optimization_barrier((first, damp_next))
 
-    slices, _, other = slices_of(first)
-    second_residual = residual_of(slices, other)
+    (second_residual,) = residual_of(first, 0)
     field, _ = spectrum(second_residual, cosine)
     total = chebyshev(field, *hops, mean_rows, cosine, first)
-    slices, result, other = slices_of(total)
-    residual = residual_of(slices, other)
+    residual, result = residual_of(total, 1)
     return result[None], residual[None]
 
 

time: 145 us -> 146 us (level)
  blocking collectives: 86.3 us -> 26.8 us
  waiting for transfers between devices: 14.4 us -> 55 us
  starting transfers between devices: 19.4 us -> 37 us
  Pallas kernels: 20 us -> 22.7 us
    all_to_all x6 -> x2, blocking collectives: 86.3 us -> 26.8 us  [exchange(): lax.all_to_all(blocks, axis, split_axis=0, concat_axis=0, tiled=True)]
    ppermute x2 -> x22, waiting for transfers between devices: 3.12 us -> 43.7 us  [the longest x6 31.2 us: by_ring(): going_up = lax.ppermute(going_up, 'tm', up)]
    ppermute x2 -> x22, starting transfers between devices: 0.29 us -> 17.9 us  [the longest x6 8.95 us: by_ring(): going_down = lax.ppermute(going_down, 'tm', down)]
    pallas_call x4, Pallas kernels: 4.71 us -> 7.38 us  [the longest x2 4.28 us: by_ring(): call(finish_kernel, outs, 13, scalars=1)]
  transfers between devices with their start and end apart: 11 -> 31, of which waited for: 8 -> 21; matrix products, arithmetic and copies ran while one was open for 0% -> 1% of each run, Pallas kernels for 5% -> 5%
where the time goes in v2:
time: 146 us; the launch traced here: 145 us
  waiting for transfers between devices  55 us (38%)
  starting transfers between devices  37 us (25%)
  blocking collectives  26.8 us (18%)
  Pallas kernels  22.7 us (16%)
  between operations  1.61 us (1%)
  local copies, waits for them, and re-layouts  1.46 us (1%)
    ppermute x6, waiting for transfers between devices, by_ring(): going_up = lax.ppermute(going_up, 'tm', up)  31.2 us
    all_to_all x2, blocking collectives, exchange(): lax.all_to_all(blocks, axis, split_axis=0, concat_axis=0, tiled=True)  26.8 us
    pallas_call x2, Pallas kernels, chebyshev(): call(chebyshev_kernel, field_shape, len(operands), [pltpu.VMEM((16, side_...  13.4 us
    all_to_all x2, starting transfers between devices, exchange(): lax.all_to_all(blocks, axis, split_axis=0, concat_axis=0, tiled=True)  11.2 us
    ppermute x6, starting transfers between devices, by_ring(): going_down = lax.ppermute(going_down, 'tm', down)  8.95 us
    ppermute x6, waiting for transfers between devices, add_partners(): lax.ppermute(value, axis, [(i, i ^ step * shift) for i in range(count)])  7.46 us
    ppermute x2, waiting for transfers between devices, by_ring(): low = lax.ppermute(going_up[:half], 'tm', up)  7.13 us
    ppermute x6, starting transfers between devices, add_partners(): lax.ppermute(value, axis, [(i, i ^ step * shift) for i in range(count)])  6.55 us
  transfers between devices with their start and end apart: 31, of which 21 were waited for; matrix products, arithmetic and copies ran while one was open for 1% of the time, Pallas kernels for 5%

profile of v2, /device:TPU:0, one launch (start us, length us, event | category | flops | bytes accessed | tf_op | source)
XLA Modules:
  0.0 145.3 jit_solution(111386345193936558)
XLA Ops:
  0.6 7.6 %all-to-all-start = ((f32[16,16,256]{2,1,0:T(8,128)}), f32[16,16,256]{2,1,0:T(8,128)S(1)}, u32[]{:S(2)}, u32[]{:S(2)}) async-start(f32[16,16,256]{2,1,0:T(8,128)} %bitcast.18), calls=%async_computation | async-start | bytes 524288 | tf_op jit(solution)/shard_map/all_to_all | solution.py:252
  8.2 0.7 exponential_bitcast_fusion
  9.6 0.5 collective-permute-start
  10.0 1.6 %collective-permute-start.1 = (f32[1,256]{1,0:T(1,128)S(1)}, f32[1,256]{1,0:T(1,128)S(1)}, u32[]{:S(2)}, u32[]{:S(2)}) collective-permute-start(f32[1,256]{1,0:T(1,128)S(1)} %broadcast_in_dim.16), channel_id=1, source_target_pairs={{0,2},{1,3},{2,0},{3,1},{4,6},{5,7},{6,4},{7,5},{8,10},{9,11},{10,... | collective-permute-start | bytes 3080 | tf_op jit(solution)/shard_map/ppermute | solution.py:244
  11.7 2.0 %collective-permute-done.1 = f32[1,256]{1,0:T(1,128)S(1)} collective-permute-done((f32[1,256]{1,0:T(1,128)S(1)}, f32[1,256]{1,0:T(1,128)S(1)}, u32[]{:S(2)}, u32[]{:S(2)}) %collective-permute-start.1) | collective-permute-done | bytes 1056 | tf_op jit(solution)/shard_map/ppermute | solution.py:244
  13.7 1.0 collective-permute-done.2
  14.7 3.5 %all-to-all-done = f32[16,16,256]{2,1,0:T(8,128)S(1)} async-done(((f32[16,16,256]{2,1,0:T(8,128)}), f32[16,16,256]{2,1,0:T(8,128)S(1)}, u32[]{:S(2)}, u32[]{:S(2)}) %all-to-all-start) | async-done | bytes 262176 | tf_op jit(solution)/shard_map/all_to_all | solution.py:252
  18.2 1.0 shard_map.113
  19.2 3.7 %all-to-all-start.1 = ((f32[16,16,256]{2,1,0:T(8,128)}), f32[16,16,256]{2,1,0:T(8,128)S(1)}, u32[]{:S(2)}, u32[]{:S(2)}) async-start(f32[16,16,256]{2,1,0:T(8,128)} %bitcast.4), calls=%async_computation.1 | async-start | bytes 524288 | tf_op jit(solution)/shard_map/all_to_all | solution.py:252
  22.9 1.9 %collective-permute-start.3 = (f32[1,256]{1,0:T(1,128)S(1)}, f32[1,256]{1,0:T(1,128)S(1)}, u32[]{:S(2)}, u32[]{:S(2)}) collective-permute-start(f32[1,256]{1,0:T(1,128)S(1)} %bitcast.27), channel_id=1, source_target_pairs={{0,4},{1,5},{2,6},{3,7},{4,0},{5,1},{6,2},{7,3},{8,12},{9,13},{10,... | collective-permute-start | bytes 3080 | tf_op jit(solution)/shard_map/ppermute | solution.py:244
  24.8 2.4 %collective-permute-start.4 = (f32[1,256]{1,0:T(1,128)S(1)}, f32[1,256]{1,0:T(1,128)S(1)}, u32[]{:S(2)}, u32[]{:S(2)}) collective-permute-start(f32[1,256]{1,0:T(1,128)S(1)} %bitcast.28), channel_id=1, source_target_pairs={{0,8},{1,9},{2,10},{3,11},{4,12},{5,13},{6,14},{7,15},{8,0},{9,1},... | collective-permute-start | bytes 3080 | tf_op jit(solution)/shard_map/ppermute | solution.py:244
  27.5 0.6 shard_map.114
  28.3 4.2 %collective-permute-done.4 = f32[1,256]{1,0:T(1,128)S(1)} collective-permute-done((f32[1,256]{1,0:T(1,128)S(1)}, f32[1,256]{1,0:T(1,128)S(1)}, u32[]{:S(2)}, u32[]{:S(2)}) %collective-permute-start.4) | collective-permute-done | bytes 1056 | tf_op jit(solution)/shard_map/ppermute | solution.py:244
  32.9 1.4 collective-permute-start.6
  34.2 6.7 %shard_map.115.refs_1_.refs_7_ = f32[256,256]{1,0:T(8,128)S(1)} custom-call(f32[256,256]{1,0:T(8,128)S(1)} %bitcast.25, bf16[512,256]{1,0:T(8,128)(2,1)S(1)} %get-tuple-element.21.refs_1_.refs_10_, bf16[512,256]{1,0:T(8,128)(2,1)S(1)} %get-tuple-element.22.refs_2_.refs_11_, bf16[512,256]{1,0:T(8,128)(2,1)S(1)} %get-tuple-element.23.refs_3_.refs_12_, ...), custom_call_target="tpu_custom_call" | custom-call | flops 4026531840 | tf_op jit(solution)/shard_map/pallas_call | solution.py:278
  41.0 0.6 collective-permute-start.7
  41.6 1.5 %collective-permute-start.8 = (f32[256,256]{1,0:T(8,128)S(1)}, f32[256,256]{1,0:T(8,128)S(1)}, u32[]{:S(2)}, u32[]{:S(2)}) collective-permute-start(f32[256,256]{1,0:T(8,128)S(1)} %shard_map.115.refs_1_.refs_7_), channel_id=1, source_target_pairs={{0,2},{1,3},{4,0},{5,1},{8,4},{9,5},{12,8},{13,9},{14,12},{15,13},... | collective-permute-start | bytes 786440 | tf_op jit(solution)/shard_map/ppermute | solution.py:309
  43.1 5.3 %collective-permute-done.7.refs_2_ = f32[256,256]{1,0:T(8,128)S(1)} collective-permute-done((f32[256,256]{1,0:T(8,128)S(1)}, f32[256,256]{1,0:T(8,128)S(1)}, u32[]{:S(2)}, u32[]{:S(2)}) %collective-permute-start.7) | collective-permute-done | bytes 262176 | tf_op jit(solution)/shard_map/ppermute | solution.py:308
  48.7 1.7 %collective-permute-start.10 = (f32[256,256]{1,0:T(8,128)S(1)}, f32[256,256]{1,0:T(8,128)}, u32[]{:S(2)}, u32[]{:S(2)}) collective-permute-start(f32[256,256]{1,0:T(8,128)S(1)} %collective-permute-done.8.refs_3_), channel_id=1, source_target_pairs={{0,2},{1,3},{4,0},{5,1},{8,4},{9,5},{12,8},{13,9},{14,12},{15,13},... | collective-permute-start | bytes 786440 | tf_op jit(solution)/shard_map/ppermute | solution.py:309
  50.4 5.0 %collective-permute-done.9.refs_4_ = f32[256,256]{1,0:T(8,128)S(1)} collective-permute-done((f32[256,256]{1,0:T(8,128)S(1)}, f32[256,256]{1,0:T(8,128)S(1)}, u32[]{:S(2)}, u32[]{:S(2)}) %collective-permute-start.9) | collective-permute-done | bytes 262176 | tf_op jit(solution)/shard_map/ppermute | solution.py:308
  55.5 2.0 %collective-permute-start.12 = (f32[256,256]{1,0:T(8,128)}, f32[256,256]{1,0:T(8,128)S(1)}, u32[]{:S(2)}, u32[]{:S(2)}) collective-permute-start(f32[256,256]{1,0:T(8,128)} %collective-permute-done.10.refs_5_), channel_id=1, source_target_pairs={{0,2},{1,3},{4,0},{5,1},{8,4},{9,5},{12,8},{13,9},{14,12},{15,13},... | collective-permute-start | bytes 786440 | tf_op jit(solution)/shard_map/ppermute | solution.py:309
  57.5 0.7 dynamic-slice_bitcast_fusion.refs_0_
  58.2 4.1 %collective-permute-done.11.refs_6_ = f32[256,256]{1,0:T(8,128)S(1)} collective-permute-done((f32[256,256]{1,0:T(8,128)S(1)}, f32[256,256]{1,0:T(8,128)S(1)}, u32[]{:S(2)}, u32[]{:S(2)}) %collective-permute-start.11) | collective-permute-done | bytes 262176 | tf_op jit(solution)/shard_map/ppermute | solution.py:308
  62.3 1.8 %shard_map.116 = (f32[256,768]{1,0:T(8,128)S(1)}, f32[256,768]{1,0:T(8,128)S(1)}) custom-call(f32[42]{0:T(128)S(1)} %dynamic-slice_bitcast_fusion.refs_0_, f32[256,256]{1,0:T(8,128)S(1)} %shard_map.115.refs_1_.refs_7_, f32[256,256]{1,0:T(8,128)S(1)} %collective-permute-done.7.refs_2_, f32[256,256]{1,0:T(8,128)S(1)} %collective-permute-done.8.refs_3_, ...), custom_call_target="tpu_custom_call" | custom-call | flops 5505024 | tf_op jit(solution)/shard_map/pallas_call | solution.py:317
  64.2 2.9 %collective-permute-start.14 = (f32[128,256]{1,0:T(8,128)S(1)}, f32[128,256]{1,0:T(8,128)S(1)}, u32[]{:S(2)}, u32[]{:S(2)}) collective-permute-start(f32[128,256]{1,0:T(8,128)S(1)} %slice.16), channel_id=1, source_target_pairs={{0,4},{1,5},{4,8},{5,9},{8,12},{9,13},{12,14},{13,15},{14,10},{15,... | collective-permute-start | bytes 393224 | tf_op jit(solution)/shard_map/ppermute | solution.py:312
  67.1 3.3 %collective-permute-done.14.refs_3_ = f32[128,256]{1,0:T(8,128)S(1)} collective-permute-done((f32[128,256]{1,0:T(8,128)S(1)}, f32[128,256]{1,0:T(8,128)S(1)}, u32[]{:S(2)}, u32[]{:S(2)}) %collective-permute-start.14) | collective-permute-done | bytes 131104 | tf_op jit(solution)/shard_map/ppermute | solution.py:312
  70.5 2.5 %collective-permute-done.15.refs_4_ = f32[128,256]{1,0:T(8,128)S(1)} collective-permute-done((f32[128,256]{1,0:T(8,128)S(1)}, f32[128,256]{1,0:T(8,128)S(1)}, u32[]{:S(2)}, u32[]{:S(2)}) %collective-permute-start.15) | collective-permute-done | bytes 131104 | tf_op jit(solution)/shard_map/ppermute | solution.py:313
  73.0 0.7 dynamic-slice_bitcast_fusion.1.refs_0_
  73.7 0.6 collective-permute-done.17.refs_6_
  74.3 1.8 %shard_map.117 = f32[256,256]{1,0:T(8,128)S(1)} custom-call(f32[6]{0:T(128)S(1)} %dynamic-slice_bitcast_fusion.1.refs_0_, f32[256,768]{1,0:T(8,128)S(1)} %get-tuple-element.28.refs_1_, f32[256,768]{1,0:T(8,128)S(1)} %collective-permute-done.13.refs_2_, f32[128,256]{1,0:T(8,128)S(1)} %collective-permute-done.14.refs_3_, ...), custom_call_target="tpu_custom_call" | custom-call | tf_op jit(solution)/shard_map/pallas_call | solution.py:322
  76.1 14.1 %all_to_all.20 = f32[16,16,256]{2,1,0:T(8,128)S(1)} all-to-all(f32[16,16,256]{2,1,0:T(8,128)S(1)} %bitcast.22), channel_id=1, replica_groups=mesh['grp'=2,'tm'=16] {'tm'}, dimensions={0} | all-to-all | bytes 524288 | tf_op jit(solution)/shard_map/all_to_all | solution.py:252
  90.5 12.7 %all_to_all.21 = f32[16,16,256]{2,1,0:T(8,128)S(1)} all-to-all(f32[16,16,256]{2,1,0:T(8,128)S(1)} %bitcast.24), channel_id=1, replica_groups=mesh['grp'=2,'tm'=16] {'tm'}, dimensions={0} | all-to-all | bytes 524288 | tf_op jit(solution)/shard_map/all_to_all | solution.py:252
  103.2 6.7 %shard_map.119.refs_1_ = f32[256,256]{1,0:T(8,128)S(1)} custom-call(f32[256,256]{1,0:T(8,128)S(1)} %bitcast.26, bf16[512,256]{1,0:T(8,128)(2,1)S(1)} %get-tuple-element.21.refs_1_.refs_10_, bf16[512,256]{1,0:T(8,128)(2,1)S(1)} %get-tuple-element.22.refs_2_.refs_11_, bf16[512,256]{1,0:T(8,128)(2,1)S(1)} %get-tuple-element.23.refs_3_.refs_12_, ...), custom_call_target="tpu_custom_call" | custom-call | flops 4026531840 | tf_op jit(solution)/shard_map/pallas_call | solution.py:278
  110.0 2.0 %collective-permute-start.19 = (f32[256,256]{1,0:T(8,128)S(1)}, f32[256,256]{1,0:T(8,128)S(1)}, u32[]{:S(2)}, u32[]{:S(2)}) collective-permute-start(f32[256,256]{1,0:T(8,128)S(1)} %shard_map.119.refs_1_), channel_id=1, source_target_pairs={{0,2},{1,3},{4,0},{5,1},{8,4},{9,5},{12,8},{13,9},{14,12},{15,13},... | collective-permute-start | bytes 786440 | tf_op jit(solution)/shard_map/ppermute | solution.py:309
  112.0 6.1 %collective-permute-done.18.refs_2_ = f32[256,256]{1,0:T(8,128)S(1)} collective-permute-done((f32[256,256]{1,0:T(8,128)S(1)}, f32[256,256]{1,0:T(8,128)S(1)}, u32[]{:S(2)}, u32[]{:S(2)}) %collective-permute-start.18) | collective-permute-done | bytes 262176 | tf_op jit(solution)/shard_map/ppermute | solution.py:308
  118.1 0.8 collective-permute-start.20
  118.9 1.2 collective-permute-start.21
  120.1 5.2 %collective-permute-done.20.refs_4_ = f32[256,256]{1,0:T(8,128)S(1)} collective-permute-done((f32[256,256]{1,0:T(8,128)S(1)}, f32[256,256]{1,0:T(8,128)S(1)}, u32[]{:S(2)}, u32[]{:S(2)}) %collective-permute-start.20) | collective-permute-done | bytes 262176 | tf_op jit(solution)/shard_map/ppermute | solution.py:308
  125.4 1.6 %collective-permute-start.22 = (f32[256,256]{1,0:T(8,128)S(1)}, f32[256,256]{1,0:T(8,128)S(1)}, u32[]{:S(2)}, u32[]{:S(2)}) collective-permute-start(f32[256,256]{1,0:T(8,128)S(1)} %collective-permute-done.20.refs_4_), channel_id=1, source_target_pairs={{0,4},{1,5},{4,8},{5,9},{8,12},{9,13},{12,14},{13,15},{14,10},{15,... | collective-permute-start | bytes 786440 | tf_op jit(solution)/shard_map/ppermute | solution.py:308
  127.0 0.5 collective-permute-start.23
  127.4 5.4 %collective-permute-done.22.refs_6_ = f32[256,256]{1,0:T(8,128)S(1)} collective-permute-done((f32[256,256]{1,0:T(8,128)S(1)}, f32[256,256]{1,0:T(8,128)S(1)}, u32[]{:S(2)}, u32[]{:S(2)}) %collective-permute-start.22) | collective-permute-done | bytes 262176 | tf_op jit(solution)/shard_map/ppermute | solution.py:308
  132.8 1.1 collective-permute-done.23.refs_7_
  133.9 1.3 shard_map.120
  135.7 1.8 %collective-permute-start.26 = (f32[128,256]{1,0:T(8,128)S(1)}, f32[128,256]{1,0:T(8,128)S(1)}, u32[]{:S(2)}, u32[]{:S(2)}) collective-permute-start(f32[128,256]{1,0:T(8,128)S(1)} %slice.19), channel_id=1, source_target_pairs={{0,2},{1,3},{4,0},{5,1},{8,4},{9,5},{12,8},{13,9},{14,12},{15,13},... | collective-permute-start | bytes 393224 | tf_op jit(solution)/shard_map/ppermute | solution.py:313
  137.5 3.8 %collective-permute-done.25.refs_3_ = f32[128,256]{1,0:T(8,128)S(1)} collective-permute-done((f32[128,256]{1,0:T(8,128)S(1)}, f32[128,256]{1,0:T(8,128)S(1)}, u32[]{:S(2)}, u32[]{:S(2)}) %collective-permute-start.25) | collective-permute-done | bytes 131104 | tf_op jit(solution)/shard_map/ppermute | solution.py:312
  141.4 0.4 collective-permute-start.28
  141.8 0.8 collective-permute-done.27.refs_5_
  142.8 2.5 %shard_map.121 = (f32[256,256]{1,0:T(8,128)}, f32[256,256]{1,0:T(8,128)}) custom-call(f32[6]{0:T(128)S(1)} %dynamic-slice_bitcast_fusion.1.refs_0_, f32[256,768]{1,0:T(8,128)S(1)} %get-tuple-element.32.refs_1_, f32[256,768]{1,0:T(8,128)S(1)} %collective-permute-done.24.refs_2_, f32[128,256]{1,0:T(8,128)S(1)} %collective-permute-done.25.refs_3_, ...), custom_call_target="tpu_custom_call" | custom-call | tf_op jit(solution)/shard_map/pallas_call | solution.py:322
  (49 shorter events, 2.3 us)
Async XLA Ops:
  0.6 7.6 %copy-start.5 = (s32[1,256,256]{2,1,0:T(8,128)S(1)}, s32[1,256,256]{2,1,0:T(8,128)}, u32[]{:S(2)}) copy-start(s32[1,256,256]{2,1,0:T(8,128)} %param.11) | copy-start | bytes 786436
  0.6 17.6 %all-to-all-start = ((f32[16,16,256]{2,1,0:T(8,128)}), f32[16,16,256]{2,1,0:T(8,128)S(1)}, u32[]{:S(2)}, u32[]{:S(2)}) async-start(f32[16,16,256]{2,1,0:T(8,128)} %bitcast.18), calls=%async_computation | async-start | bytes 524288 | tf_op jit(solution)/shard_map/all_to_all | solution.py:252
  8.2 10.0 %copy-start.1 = (bf16[256,256]{1,0:T(8,128)(2,1)S(1)}, bf16[256,256]{1,0:T(8,128)(2,1)}, u32[]{:S(2)}) copy-start(bf16[256,256]{1,0:T(8,128)(2,1)} %constant.53.clone.th_ref) | copy-start | bytes 393220
  8.2 10.0 %copy-start.2 = (bf16[256,256]{1,0:T(8,128)(2,1)S(1)}, bf16[256,256]{1,0:T(8,128)(2,1)}, u32[]{:S(2)}) copy-start(bf16[256,256]{1,0:T(8,128)(2,1)} %constant.54.clone.tl_ref) | copy-start | bytes 393220
  9.6 2.1 %collective-permute-start = (f32[1,256]{1,0:T(1,128)S(1)}, f32[1,256]{1,0:T(1,128)S(1)}, u32[]{:S(2)}, u32[]{:S(2)}) collective-permute-start(f32[1,256]{1,0:T(1,128)S(1)} %broadcast_in_dim.16), channel_id=1, source_target_pairs={{0,1},{1,0},{2,3},{3,2},{4,5},{5,4},{6,7},{7,6},{8,9},{9,8},{10,11... | collective-permute-start | bytes 3080 | tf_op jit(solution)/shard_map/ppermute | solution.py:244
  10.0 3.6 %collective-permute-start.1 = (f32[1,256]{1,0:T(1,128)S(1)}, f32[1,256]{1,0:T(1,128)S(1)}, u32[]{:S(2)}, u32[]{:S(2)}) collective-permute-start(f32[1,256]{1,0:T(1,128)S(1)} %broadcast_in_dim.16), channel_id=1, source_target_pairs={{0,2},{1,3},{2,0},{3,1},{4,6},{5,7},{6,4},{7,5},{8,10},{9,11},{10,... | collective-permute-start | bytes 3080 | tf_op jit(solution)/shard_map/ppermute | solution.py:244
  11.7 3.0 %collective-permute-start.2 = (f32[1,256]{1,0:T(1,128)S(1)}, f32[1,256]{1,0:T(1,128)S(1)}, u32[]{:S(2)}, u32[]{:S(2)}) collective-permute-start(f32[1,256]{1,0:T(1,128)S(1)} %broadcast_in_dim.16), channel_id=1, source_target_pairs={{0,3},{1,2},{2,1},{3,0},{4,7},{5,6},{6,5},{7,4},{8,11},{9,10},{10,... | collective-permute-start | bytes 3080 | tf_op jit(solution)/shard_map/ppermute | solution.py:244
  19.2 8.2 %copy-start.3 = (f32[256,256]{1,0:T(8,128)S(1)}, f32[256,256]{1,0:T(8,128)}, u32[]{:S(2)}) copy-start(f32[256,256]{1,0:T(8,128)} %hop_x_ref.1) | copy-start | bytes 786436
  19.2 8.2 %copy-start.4 = (f32[256,256]{1,0:T(8,128)S(1)}, f32[256,256]{1,0:T(8,128)}, u32[]{:S(2)}) copy-start(f32[256,256]{1,0:T(8,128)} %hop_y_ref.1) | copy-start | bytes 786436
  19.2 13.7 %all-to-all-start.1 = ((f32[16,16,256]{2,1,0:T(8,128)}), f32[16,16,256]{2,1,0:T(8,128)S(1)}, u32[]{:S(2)}, u32[]{:S(2)}) async-start(f32[16,16,256]{2,1,0:T(8,128)} %bitcast.4), calls=%async_computation.1 | async-start | bytes 524288 | tf_op jit(solution)/shard_map/all_to_all | solution.py:252
  22.9 5.4 %collective-permute-start.3 = (f32[1,256]{1,0:T(1,128)S(1)}, f32[1,256]{1,0:T(1,128)S(1)}, u32[]{:S(2)}, u32[]{:S(2)}) collective-permute-start(f32[1,256]{1,0:T(1,128)S(1)} %bitcast.27), channel_id=1, source_target_pairs={{0,4},{1,5},{2,6},{3,7},{4,0},{5,1},{6,2},{7,3},{8,12},{9,13},{10,... | collective-permute-start | bytes 3080 | tf_op jit(solution)/shard_map/ppermute | solution.py:244
  24.8 7.7 %collective-permute-start.4 = (f32[1,256]{1,0:T(1,128)S(1)}, f32[1,256]{1,0:T(1,128)S(1)}, u32[]{:S(2)}, u32[]{:S(2)}) collective-permute-start(f32[1,256]{1,0:T(1,128)S(1)} %bitcast.28), channel_id=1, source_target_pairs={{0,8},{1,9},{2,10},{3,11},{4,12},{5,13},{6,14},{7,15},{8,0},{9,1},... | collective-permute-start | bytes 3080 | tf_op jit(solution)/shard_map/ppermute | solution.py:244
  27.2 5.4 %collective-permute-start.5 = (f32[1,256]{1,0:T(1,128)S(1)}, f32[1,256]{1,0:T(1,128)S(1)}, u32[]{:S(2)}, u32[]{:S(2)}) collective-permute-start(f32[1,256]{1,0:T(1,128)S(1)} %bitcast.29), channel_id=1, source_target_pairs={{0,12},{1,13},{2,14},{3,15},{4,8},{5,9},{6,10},{7,11},{8,4},{9,5},... | collective-permute-start | bytes 3080 | tf_op jit(solution)/shard_map/ppermute | solution.py:244
  32.9 8.1 %collective-permute-start.6 = (f32[256,256]{1,0:T(8,128)S(1)}, f32[256,256]{1,0:T(8,128)S(1)}, u32[]{:S(2)}, u32[]{:S(2)}) collective-permute-start(f32[256,256]{1,0:T(8,128)S(1)} %get-tuple-element.26.refs_7_), channel_id=1, source_target_pairs={{0,15},{1,0},{2,1},{3,2},{4,3},{5,4},{6,5},{7,6},{8,7},{9,8},{10,9... | collective-permute-start | bytes 786440 | tf_op jit(solution)/shard_map/ppermute | solution.py:337
  41.0 7.4 %collective-permute-start.7 = (f32[256,256]{1,0:T(8,128)S(1)}, f32[256,256]{1,0:T(8,128)S(1)}, u32[]{:S(2)}, u32[]{:S(2)}) collective-permute-start(f32[256,256]{1,0:T(8,128)S(1)} %shard_map.115.refs_1_.refs_7_), channel_id=1, source_target_pairs={{0,4},{1,5},{4,8},{5,9},{8,12},{9,13},{12,14},{13,15},{14,10},{15,... | collective-permute-start | bytes 786440 | tf_op jit(solution)/shard_map/ppermute | solution.py:308
  41.6 7.1 %collective-permute-start.8 = (f32[256,256]{1,0:T(8,128)S(1)}, f32[256,256]{1,0:T(8,128)S(1)}, u32[]{:S(2)}, u32[]{:S(2)}) collective-permute-start(f32[256,256]{1,0:T(8,128)S(1)} %shard_map.115.refs_1_.refs_7_), channel_id=1, source_target_pairs={{0,2},{1,3},{4,0},{5,1},{8,4},{9,5},{12,8},{13,9},{14,12},{15,13},... | collective-permute-start | bytes 786440 | tf_op jit(solution)/shard_map/ppermute | solution.py:309
  48.4 7.1 %collective-permute-start.9 = (f32[256,256]{1,0:T(8,128)S(1)}, f32[256,256]{1,0:T(8,128)S(1)}, u32[]{:S(2)}, u32[]{:S(2)}) collective-permute-start(f32[256,256]{1,0:T(8,128)S(1)} %collective-permute-done.7.refs_2_), channel_id=1, source_target_pairs={{0,4},{1,5},{4,8},{5,9},{8,12},{9,13},{12,14},{13,15},{14,10},{15,... | collective-permute-start | bytes 786440 | tf_op jit(solution)/shard_map/ppermute | solution.py:308
  48.7 6.8 %collective-permute-start.10 = (f32[256,256]{1,0:T(8,128)S(1)}, f32[256,256]{1,0:T(8,128)}, u32[]{:S(2)}, u32[]{:S(2)}) collective-permute-start(f32[256,256]{1,0:T(8,128)S(1)} %collective-permute-done.8.refs_3_), channel_id=1, source_target_pairs={{0,2},{1,3},{4,0},{5,1},{8,4},{9,5},{12,8},{13,9},{14,12},{15,13},... | collective-permute-start | bytes 786440 | tf_op jit(solution)/shard_map/ppermute | solution.py:309
  55.5 6.8 %collective-permute-start.11 = (f32[256,256]{1,0:T(8,128)S(1)}, f32[256,256]{1,0:T(8,128)S(1)}, u32[]{:S(2)}, u32[]{:S(2)}) collective-permute-start(f32[256,256]{1,0:T(8,128)S(1)} %collective-permute-done.9.refs_4_), channel_id=1, source_target_pairs={{0,4},{1,5},{4,8},{5,9},{8,12},{9,13},{12,14},{13,15},{14,10},{15,... | collective-permute-start | bytes 786440 | tf_op jit(solution)/shard_map/ppermute | solution.py:308
  55.5 6.8 %collective-permute-start.12 = (f32[256,256]{1,0:T(8,128)}, f32[256,256]{1,0:T(8,128)S(1)}, u32[]{:S(2)}, u32[]{:S(2)}) collective-permute-start(f32[256,256]{1,0:T(8,128)} %collective-permute-done.10.refs_5_), channel_id=1, source_target_pairs={{0,2},{1,3},{4,0},{5,1},{8,4},{9,5},{12,8},{13,9},{14,12},{15,13},... | collective-permute-start | bytes 786440 | tf_op jit(solution)/shard_map/ppermute | solution.py:309
  64.1 10.3 %copy-start = (f32[1,256,256]{2,1,0:T(8,128)S(1)}, f32[1,256,256]{2,1,0:T(8,128)}, u32[]{:S(2)}) copy-start(f32[1,256,256]{2,1,0:T(8,128)} %param.10) | copy-start | bytes 786436
  64.1 10.3 %collective-permute-start.13 = (f32[256,768]{1,0:T(8,128)S(1)}, f32[256,768]{1,0:T(8,128)S(1)}, u32[]{:S(2)}, u32[]{:S(2)}) collective-permute-start(f32[256,768]{1,0:T(8,128)S(1)} %get-tuple-element.29), channel_id=1, source_target_pairs={{0,1},{1,0},{2,3},{3,2},{4,5},{5,4},{6,7},{7,6},{8,9},{9,8},{10,11... | collective-permute-start | bytes 2359304 | tf_op jit(solution)/shard_map/ppermute | solution.py:318
  64.2 6.3 %collective-permute-start.14 = (f32[128,256]{1,0:T(8,128)S(1)}, f32[128,256]{1,0:T(8,128)S(1)}, u32[]{:S(2)}, u32[]{:S(2)}) collective-permute-start(f32[128,256]{1,0:T(8,128)S(1)} %slice.16), channel_id=1, source_target_pairs={{0,4},{1,5},{4,8},{5,9},{8,12},{9,13},{12,14},{13,15},{14,10},{15,... | collective-permute-start | bytes 393224 | tf_op jit(solution)/shard_map/ppermute | solution.py:312
  67.1 5.9 %collective-permute-start.15 = (f32[128,256]{1,0:T(8,128)S(1)}, f32[128,256]{1,0:T(8,128)S(1)}, u32[]{:S(2)}, u32[]{:S(2)}) collective-permute-start(f32[128,256]{1,0:T(8,128)S(1)} %slice.17), channel_id=1, source_target_pairs={{0,2},{1,3},{4,0},{5,1},{8,4},{9,5},{12,8},{13,9},{14,12},{15,13},... | collective-permute-start | bytes 393224 | tf_op jit(solution)/shard_map/ppermute | solution.py:313
  70.5 3.2 %collective-permute-start.16 = (f32[128,256]{1,0:T(8,128)S(1)}, f32[128,256]{1,0:T(8,128)S(1)}, u32[]{:S(2)}, u32[]{:S(2)}) collective-permute-start(f32[128,256]{1,0:T(8,128)S(1)} %collective-permute-done.14.refs_3_), channel_id=1, source_target_pairs={{0,1},{1,0},{2,3},{3,2},{4,5},{5,4},{6,7},{7,6},{8,9},{9,8},{10,11... | collective-permute-start | bytes 393224 | tf_op jit(solution)/shard_map/ppermute | solution.py:319
  73.0 1.3 collective-permute-start.17
  109.9 8.2 %collective-permute-start.18 = (f32[256,256]{1,0:T(8,128)S(1)}, f32[256,256]{1,0:T(8,128)S(1)}, u32[]{:S(2)}, u32[]{:S(2)}) collective-permute-start(f32[256,256]{1,0:T(8,128)S(1)} %shard_map.119.refs_1_), channel_id=1, source_target_pairs={{0,4},{1,5},{4,8},{5,9},{8,12},{9,13},{12,14},{13,15},{14,10},{15,... | collective-permute-start | bytes 786440 | tf_op jit(solution)/shard_map/ppermute | solution.py:308
  110.0 8.9 %collective-permute-start.19 = (f32[256,256]{1,0:T(8,128)S(1)}, f32[256,256]{1,0:T(8,128)S(1)}, u32[]{:S(2)}, u32[]{:S(2)}) collective-permute-start(f32[256,256]{1,0:T(8,128)S(1)} %shard_map.119.refs_1_), channel_id=1, source_target_pairs={{0,2},{1,3},{4,0},{5,1},{8,4},{9,5},{12,8},{13,9},{14,12},{15,13},... | collective-permute-start | bytes 786440 | tf_op jit(solution)/shard_map/ppermute | solution.py:309
  118.1 7.3 %collective-permute-start.20 = (f32[256,256]{1,0:T(8,128)S(1)}, f32[256,256]{1,0:T(8,128)S(1)}, u32[]{:S(2)}, u32[]{:S(2)}) collective-permute-start(f32[256,256]{1,0:T(8,128)S(1)} %collective-permute-done.18.refs_2_), channel_id=1, source_target_pairs={{0,4},{1,5},{4,8},{5,9},{8,12},{9,13},{12,14},{13,15},{14,10},{15,... | collective-permute-start | bytes 786440 | tf_op jit(solution)/shard_map/ppermute | solution.py:308
  118.9 8.1 %collective-permute-start.21 = (f32[256,256]{1,0:T(8,128)S(1)}, f32[256,256]{1,0:T(8,128)S(1)}, u32[]{:S(2)}, u32[]{:S(2)}) collective-permute-start(f32[256,256]{1,0:T(8,128)S(1)} %collective-permute-done.19.refs_3_), channel_id=1, source_target_pairs={{0,2},{1,3},{4,0},{5,1},{8,4},{9,5},{12,8},{13,9},{14,12},{15,13},... | collective-permute-start | bytes 786440 | tf_op jit(solution)/shard_map/ppermute | solution.py:309
  125.4 7.4 %collective-permute-start.22 = (f32[256,256]{1,0:T(8,128)S(1)}, f32[256,256]{1,0:T(8,128)S(1)}, u32[]{:S(2)}, u32[]{:S(2)}) collective-permute-start(f32[256,256]{1,0:T(8,128)S(1)} %collective-permute-done.20.refs_4_), channel_id=1, source_target_pairs={{0,4},{1,5},{4,8},{5,9},{8,12},{9,13},{12,14},{13,15},{14,10},{15,... | collective-permute-start | bytes 786440 | tf_op jit(solution)/shard_map/ppermute | solution.py:308
  127.0 6.9 %collective-permute-start.23 = (f32[256,256]{1,0:T(8,128)S(1)}, f32[256,256]{1,0:T(8,128)S(1)}, u32[]{:S(2)}, u32[]{:S(2)}) collective-permute-start(f32[256,256]{1,0:T(8,128)S(1)} %collective-permute-done.21.refs_5_), channel_id=1, source_target_pairs={{0,2},{1,3},{4,0},{5,1},{8,4},{9,5},{12,8},{13,9},{14,12},{15,13},... | collective-permute-start | bytes 786440 | tf_op jit(solution)/shard_map/ppermute | solution.py:309
  135.2 7.6 %collective-permute-start.24 = (f32[256,768]{1,0:T(8,128)S(1)}, f32[256,768]{1,0:T(8,128)S(1)}, u32[]{:S(2)}, u32[]{:S(2)}) collective-permute-start(f32[256,768]{1,0:T(8,128)S(1)} %get-tuple-element.33), channel_id=1, source_target_pairs={{0,1},{1,0},{2,3},{3,2},{4,5},{5,4},{6,7},{7,6},{8,9},{9,8},{10,11... | collective-permute-start | bytes 2359304 | tf_op jit(solution)/shard_map/ppermute | solution.py:318
  135.3 5.9 %collective-permute-start.25 = (f32[128,256]{1,0:T(8,128)S(1)}, f32[128,256]{1,0:T(8,128)S(1)}, u32[]{:S(2)}, u32[]{:S(2)}) collective-permute-start(f32[128,256]{1,0:T(8,128)S(1)} %slice.18), channel_id=1, source_target_pairs={{0,4},{1,5},{4,8},{5,9},{8,12},{9,13},{12,14},{13,15},{14,10},{15,... | collective-permute-start | bytes 393224 | tf_op jit(solution)/shard_map/ppermute | solution.py:312
  135.7 5.7 %collective-permute-start.26 = (f32[128,256]{1,0:T(8,128)S(1)}, f32[128,256]{1,0:T(8,128)S(1)}, u32[]{:S(2)}, u32[]{:S(2)}) collective-permute-start(f32[128,256]{1,0:T(8,128)S(1)} %slice.19), channel_id=1, source_target_pairs={{0,2},{1,3},{4,0},{5,1},{8,4},{9,5},{12,8},{13,9},{14,12},{15,13},... | collective-permute-start | bytes 393224 | tf_op jit(solution)/shard_map/ppermute | solution.py:313
  141.3 1.3 collective-permute-start.27
  141.4 1.5 collective-permute-start.28

commit v3 on v2

v3 whole, which is shorter than its diff:
```python
import math

import jax
import jax.numpy as jnp
import numpy as np
from jax import lax
from jax.experimental import pallas as pl
from jax.experimental.pallas import tpu as pltpu
from jax.sharding import PartitionSpec as P


ORDER = 10
LEVELS = 17
MIDDLE = (LEVELS - 1) // 2
BF16 = jnp.bfloat16
F32 = jnp.float32
VMEM = pl.BlockSpec(memory_space=pltpu.VMEM)


def call(kernel, out_shape, count, scratch=(), passes=0, scalars=0):
    return pl.pallas_call(
        kernel,
        out_shape=out_shape,
        in_specs=[pl.BlockSpec(memory_space=pltpu.SMEM)] * scalars + [VMEM] * count,
        out_specs=jax.tree.map(lambda _: VMEM, out_shape),
        scratch_shapes=list(scratch),
        compiler_params=pltpu.CompilerParams(vmem_limit_bytes=16 << 20),
        cost_estimate=pl.CostEstimate(flops=passes, transcendentals=0, bytes_accessed=0) if passes else None,
    )


def shape(rows, columns, kind=F32):
    return jax.ShapeDtypeStruct((rows, columns), kind)


def split(value):
    high = value.astype(BF16)
    return high, (value - high.astype(F32)).astype(BF16)


def dot3(left, right):
    def dot(a, b):
        return jnp.dot(a, b, preferred_element_type=F32)

    return dot(left[0], right[0]) + (dot(left[1], right[0]) + dot(left[0], right[1]))


def prepare_kernel(hop_x_ref, hop_y_ref, xh_ref, xl_ref, yh_ref, yl_ref):
    for ref, high_ref, low_ref in ((hop_x_ref, xh_ref, xl_ref), (hop_y_ref, yh_ref, yl_ref)):
        side = ref.shape[0]
        hop = ref[...]
        square = jnp.dot(hop, hop, precision=lax.Precision.HIGHEST, preferred_element_type=F32)
        high_ref[:side], low_ref[:side] = split(hop)
        high_ref[side:], low_ref[side:] = split(square)


def transform_kernel(block_ref, th_ref, tl_ref, out_ref):
    rows, columns = block_ref.shape
    block = split(block_ref[...])
    result = dot3((th_ref[...], tl_ref[...]), block)
    for part in range(th_ref.shape[0] // rows):
        out_ref[:, part * columns : (part + 1) * columns] = result[part * rows : (part + 1) * rows]


def chebyshev_sum(field, mean_level, cos_ref, hop_refs, weight_ref):
    xh_ref, xl_ref, yh_ref, yl_ref = hop_refs
    side_x, side_y = field.shape
    cbar = jnp.exp(-0.05 * (mean_level - MIDDLE))
    lower = 0.05
    root_lower = math.sqrt(lower)
    root_upper = 1.0 + 3.0 * cbar
    upper = root_upper * root_upper
    spread = upper - lower
    ratio = (root_upper - root_lower) / (root_upper + root_lower)
    keep = 2.0 * (2.0 - (upper + lower)) / spread
    once = -8.0 * cos_ref[...] * cbar / spread
    twice = 4.0 * cbar * cbar / spread
    weight = 2.0 / (root_upper * root_lower)
    for degree in range(ORDER + 1):
        weight_ref[degree : degree + 1, :] = weight
        weight = weight * -ratio
    half = side_x // 2

    def left(start, value):
        window = slice(start, start + half)
        return dot3((xh_ref[window], xl_ref[window]), value)

    def body(index, carry):
        ahead, second, _ = carry
        value = split(ahead)
        row = weight_ref[pl.ds(ORDER - 1 - index, 1), :]
        inner = [
            (split(left(start, value) * once), split(left(side_x + start, value) * twice)) for start in (0, half)
        ]
        parts = []
        for start, (single, double) in zip((0, half), inner):
            window = slice(start, start + half)
            hops = dot3(single, (yh_ref[:side_y], yl_ref[:side_y])) + dot3(double, (yh_ref[side_y:], yl_ref[side_y:]))
            parts.append((row * field[window] + keep * ahead[window] - second[window]) + hops)
        return jnp.concatenate(parts, axis=0), ahead, second

    ahead = weight_ref[ORDER : ORDER + 1, :] * field
    before = ahead - ahead
    result, _, second = lax.fori_loop(0, ORDER, body, (ahead, before, before), unroll=ORDER // 2)
    return 0.5 * (result - second)


def chebyshev_kernel(*refs):
    field_ref, sum_ref, cos_ref = refs[:3]
    out_ref, weight_ref = refs[-2:]
    mean_level = jnp.sum(sum_ref[...], axis=0, keepdims=True)
    total = chebyshev_sum(field_ref[...], mean_level, cos_ref, refs[3:7], weight_ref)
    out_ref[...] = total if len(refs) == 9 else total + refs[7][...]


def joined(weight_ref, part, refs, window):
    keep_ref, other_ref, last_ref, last_other_ref = refs
    side_y = last_ref.shape[1]
    columns = slice(part * side_y, (part + 1) * side_y)
    total = keep_ref[window, columns] + other_ref[window, columns]
    return total + (weight_ref[2 * part] * last_ref[window] + weight_ref[2 * part + 1] * last_other_ref[window])


def first_spectral_kernel(weight_ref, keep_ref, other_ref, last_ref, last_other_ref, cos_ref, *refs):
    hop_refs, (out_ref, mean_ref, row_ref) = refs[:4], refs[4:]
    side_x = out_ref.shape[0]
    sources = keep_ref, other_ref, last_ref, last_other_ref
    row = sum(ref[side_x : side_x + 1, :] for ref in sources)
    mean_level = jnp.broadcast_to(jnp.sum(row, axis=1, keepdims=True), row.shape)
    mean_ref[...] = mean_level
    field = joined(weight_ref, 0, sources, slice(0, side_x))
    out_ref[...] = chebyshev_sum(field, mean_level, cos_ref, hop_refs, row_ref)


def next_spectral_kernel(weight_ref, keep_ref, other_ref, last_ref, last_other_ref, cos_ref, *refs):
    hop_refs, (mean_ref, add_ref, out_ref, row_ref) = refs[:4], refs[4:]
    field = joined(weight_ref, 0, (keep_ref, other_ref, last_ref, last_other_ref), slice(None))
    out_ref[...] = chebyshev_sum(field, mean_ref[...], cos_ref, hop_refs, row_ref) + add_ref[...]


def pack_kernel(noise_ref, level_ref, packed_ref, damp_ref, *, scale):
    side_x = noise_ref.shape[0]
    levels = level_ref[...].astype(F32)
    damp_ref[...] = jnp.exp(-0.05 * (levels - MIDDLE))
    packed_ref[:side_x] = noise_ref[...]
    share = jnp.sum(levels, axis=0, keepdims=True) * scale
    packed_ref[side_x:] = jnp.broadcast_to(share, (packed_ref.shape[0] - side_x, share.shape[1]))


def residual_parts(before, here, after, damp, damp_next, noise_ref, x_refs, y_refs, out_ref):
    side_x, side_y = here.shape
    half = side_x // 2
    windows = (slice(0, half), slice(half, side_x))
    y_pair = tuple(ref[:side_y] for ref in y_refs)

    def propagate(value):
        value = split(value)
        inner = [split(dot3((x_refs[0][window], x_refs[1][window]), value)) for window in windows]
        return [dot3(part, y_pair) for part in inner]

    moved = propagate(damp_next * here)
    forward_next = jnp.concatenate([after[window] - part for window, part in zip(windows, moved)], axis=0)
    moved = propagate(damp * before)
    carried = propagate(forward_next)
    for window, part, back in zip(windows, moved, carried):
        forward = here[window] - part
        out_ref[window] = noise_ref[window] - (forward - damp_next[window] * back)


def normal_kernel(
    even_ref, slices_ref, other_ref, damp_ref, damp_next_ref, noise_ref, xh_ref, xl_ref, yh_ref, yl_ref, out_ref
):
    side_y = other_ref.shape[1]
    even = even_ref[...] > 0.5
    far = slices_ref[:, :side_y]
    here = slices_ref[:, side_y:]
    near = other_ref[...]
    before = jnp.where(even, far, near)
    after = jnp.where(even, near, far)
    damps = damp_ref[...], damp_next_ref[...]
    residual_parts(before, here, after, *damps, noise_ref, (xh_ref, xl_ref), (yh_ref, yl_ref), out_ref)


def gather_kernel(*refs, outs, side_x):
    weight_ref, keep_ref, send_ref = refs[0], refs[-2], refs[-1]
    field_refs = refs[1:-2]
    rows_in, side_y = field_refs[0].shape
    count = len(field_refs)
    rows = 16

    def body(index, carry):
        window = pl.ds(pl.multiple_of(index * rows, rows), rows)
        fields = [ref[window, :] for ref in field_refs]
        for target, start, base in ((keep_ref, 0, 0), (send_ref, 2, outs * count)):
            for part in range(outs):
                place = base + part * (count - start) - start
                total = weight_ref[place + start] * fields[start]
                for index_in in range(start + 1, count):
                    total = total + weight_ref[place + index_in] * fields[index_in]
                target[window, part * side_y : (part + 1) * side_y] = total
        return carry

    lax.fori_loop(0, side_x // rows, body, 0, unroll=4)
    if rows_in > side_x:
        extra = [ref[side_x:, :] for ref in field_refs]
        keep_ref[side_x:, :] = sum(extra)
        send_ref[side_x:, :] = sum(extra[2:])


def finish_kernel(weight_ref, keep_ref, other_ref, last_ref, last_other_ref, *refs):
    damp_ref, damp_next_ref, noise_ref, xh_ref, xl_ref, yh_ref, yl_ref = refs[:7]
    out_refs = refs[7:]
    sources = keep_ref, other_ref, last_ref, last_other_ref
    slices = [joined(weight_ref, part, sources, slice(None)) for part in range(3)]
    if len(out_refs) == 2:
        out_refs[1][...] = slices[1]
    damps = damp_ref[...], damp_next_ref[...]
    residual_parts(*slices, *damps, noise_ref, (xh_ref, xl_ref), (yh_ref, yl_ref), out_refs[0])


def basis_of(length):
    times = np.arange(length)
    phase = (2 * (times // 2)[:, None] + 1) * times[None, :] % (2 * length)
    angles = phase * (math.pi / length)
    basis = np.where((times % 2 == 0)[:, None], np.cos(angles), np.sin(angles))
    return basis, basis.T * (2.0 / length)


def times_of(inverse, slices):
    length = inverse.shape[0]
    outside = (slices < 0) | (slices >= length)
    return inverse[slices % length] * np.where(outside, -1.0, 1.0)[:, None]


def table_parts(matrix, rows):
    matrix = np.kron(matrix, np.eye(rows))
    high = matrix.astype(BF16)
    return jnp.asarray(high), jnp.asarray((matrix - high.astype(np.float64)).astype(BF16))


def ring_of(length):
    chips = length // 2
    return [*range(0, chips, 2), *reversed(range(1, chips, 2))]


def ring_pairs(length):
    path = ring_of(length)
    chips = len(path)
    pairs = []
    for place, chip in enumerate(path):
        pairs += [(2 * chip, 2 * path[(place + 1) % chips]), (2 * chip + 1, 2 * path[place - 1] + 1)]
    return pairs


def ring_weights(length, rows_of):
    path = ring_of(length)
    chips = len(path)
    reach = chips // 2
    gathers, finishes = [], []
    for device in range(length):
        core = device % 2
        place = path.index(device // 2)
        way = 1 - 2 * core
        own, partner = rows_of(device), rows_of(device ^ 1)
        arrivals = [
            2 * path[(place - way * hop) % chips] + side for hop in range(reach) for side in (core, 1 - core)
        ]
        far = 2 * path[(place + reach) % chips]
        gathers.append(np.concatenate([own[:, arrivals].ravel(), partner[:, arrivals[2:]].ravel()]))
        finishes.append(own[:, [far + core, far + 1 - core]].ravel())
    return np.stack(gathers).astype(np.float32), np.stack(finishes).astype(np.float32)


def add_partners(value, axis, step):
    count = lax.axis_size(axis)
    value = jnp.sum(value, axis=0, keepdims=True)
    shifts = range(1, min(4, count // step))
    others = [lax.ppermute(value, axis, [(i, i ^ (step * shift)) for i in range(count)]) for shift in shifts]
    return jnp.concatenate([value] + others, axis=0)


def exchange(value, axis):
    count = lax.axis_size(axis)
    rows, columns = value.shape
    blocks = value.reshape(count, rows // count, columns)
    return lax.all_to_all(blocks, axis, split_axis=0, concat_axis=0, tiled=True).reshape(rows, columns)


def by_exchange(noise, phonon_level, hops, cosine):
    side_x, side_y = noise.shape
    length = lax.axis_size("tm")
    position = lax.axis_index("tm")
    rows = side_x // length
    field_shape = shape(side_x, side_y)
    levels = phonon_level.astype(F32)
    damp = jnp.exp(-0.05 * (levels - MIDDLE))
    mean_rows = jnp.full((1, side_y), jnp.sum(levels) / (length * side_x * side_y), F32)
    basis, inverse = basis_of(length)
    forward = table_parts(basis, rows)
    times = np.arange(length)
    far = times_of(inverse, np.where(times % 2 == 0, times - 1, times + 1))
    back = [jnp.concatenate(pair, axis=0) for pair in zip(table_parts(far, rows), table_parts(inverse, rows))]

    def chebyshev(field, *operands):
        scratch = [pltpu.VMEM((16, side_y), F32)]
        return call(chebyshev_kernel, field_shape, 7 + len(operands), scratch)(field, mean_rows, cosine, *hops, *operands)

    def spectrum(field, beside):
        block = call(transform_kernel, field_shape, 3)(exchange(field, "tm"), *forward)
        block, beside = lax.optimization_barrier((block, beside))
        return exchange(block, "tm"), beside

    def residual_of(components):
        block = exchange(components, "tm")
        slices = exchange(call(transform_kernel, shape(side_x, 2 * side_y), 3)(block, *back), "tm")
        here = slices[:, side_y:]
        other = lax.ppermute(here, "tm", [(i, i ^ 1) for i in range(length)])
        even = jnp.full((1, side_y), (position % 2 == 0).astype(F32), F32)
        return here, call(normal_kernel, field_shape, 10)(even, slices, other, damp, damp_next, noise, *hops)

    power_of_two = length & (length - 1) == 0
    mean_rows = add_partners(mean_rows, "tm", 1) if power_of_two else lax.psum(mean_rows, "tm")
    field, mean_rows = spectrum(noise, mean_rows)
    step = 4
    while power_of_two and step < length:
        mean_rows = add_partners(mean_rows, "tm", step)
        step *= 4
    damp_next = lax.ppermute(damp, "tm", [(i, (i - 1) % length) for i in range(length)])
    first = chebyshev(field)
    _, second_residual = residual_of(first)
    field, _ = spectrum(second_residual, cosine)
    return residual_of(chebyshev(field, first))


def by_ring(noise, phonon_level, hops, cosine):
    side_x, side_y = noise.shape
    length = lax.axis_size("tm")
    position = lax.axis_index("tm")
    reach = length // 4
    extra = 8
    field_shape = shape(side_x, side_y)
    basis, inverse = basis_of(length)
    hop = ring_pairs(length)
    swap = [(i, i ^ 1) for i in range(length)]

    def weights_of(rows_of):
        tables = ring_weights(length, rows_of)
        return [lax.dynamic_index_in_dim(jnp.asarray(table), position, 0, keepdims=False) for table in tables]

    forward = weights_of(lambda device: basis[device : device + 1])
    back = weights_of(lambda device: times_of(inverse, np.arange(device - 1, device + 2)))

    def around(own, weights, outs):
        partner = lax.ppermute(own, "tm", swap)
        fields = [own, partner]
        for _ in range(reach - 1):
            own = lax.ppermute(own, "tm", hop)
            partner = lax.ppermute(partner, "tm", hop)
            fields += [own, partner]
        last = lax.ppermute(own, "tm", hop)

        def kernel(*refs):
            gather_kernel(*refs, outs=outs, side_x=side_x)

        wide = shape(own.shape[0], outs * side_y)
        adds = 4 * outs * len(fields) * side_x * side_y
        keep, send = call(kernel, (wide, wide), len(fields), passes=adds, scalars=1)(weights[0], *fields)
        other = lax.ppermute(send, "tm", swap)
        last_other = lax.ppermute(last, "tm", swap)
        return weights[1], keep, other, last, last_other

    scratch = [pltpu.VMEM((16, side_y), F32)]
    work = 12 * ORDER * 2 * side_x * side_y * max(side_x, side_y)

    def pack(*refs):
        pack_kernel(*refs, scale=1.0 / (length * side_x * side_y))

    packed, damp = call(pack, (shape(side_x + extra, side_y), field_shape), 2)(noise, phonon_level)
    parts = around(packed, forward, 1)
    parts, damp_late = lax.optimization_barrier((parts, damp))
    damp_next = lax.ppermute(damp_late, "tm", [(i, (i - 1) % length) for i in range(length)])
    first_outs = (field_shape, shape(1, side_y))
    first, mean_level = call(first_spectral_kernel, first_outs, 9, scratch, work, 1)(*parts, cosine, *hops)
    first, damp_next = lax.optimization_barrier((first, damp_next))
    parts = around(first, back, 3)
    (second_residual,) = call(finish_kernel, (field_shape,), 11, scalars=1)(*parts, damp, damp_next, noise, *hops)
    parts = around(second_residual, forward, 1)
    total = call(next_spectral_kernel, field_shape, 11, scratch, work, 1)(*parts, cosine, *hops, mean_level, first)
    parts = around(total, back, 3)
    residual, result = call(finish_kernel, (field_shape,) * 2, 11, scalars=1)(*parts, damp, damp_next, noise, *hops)
    return result, residual


def per_device(noise, phonon_level, hop_x, hop_y):
    _, side_x, side_y = noise.shape
    length = lax.axis_size("tm")
    position = lax.axis_index("tm")
    cosine = jnp.cos((2 * (position // 2) + 1).astype(F32) * (math.pi / length))
    cosine = jnp.full((1, side_y), cosine, F32)
    hop_parts = (shape(2 * side_x, side_x, BF16),) * 2 + (shape(2 * side_y, side_y, BF16),) * 2
    hops = call(prepare_kernel, hop_parts, 2)(hop_x, hop_y)
    ring = length % 4 == 0 and 8 <= length <= 16 and side_x % 64 == 0
    result, residual = (by_ring if ring else by_exchange)(noise[0], phonon_level[0], hops, cosine)
    return result[None], residual[None]


def solution(mesh):
    return jax.shard_map(
        per_device,
        mesh=mesh,
        in_specs=(P(("grp", "tm"), None, None), P(("grp", "tm"), None, None), P(), P()),
        out_specs=(P(("grp", "tm"), None, None), P(("grp", "tm"), None, None)),
        check_vma=False,
    )
```

time: 146 us -> 146 us (level)
  waiting for transfers between devices: 55 us -> 93.9 us
  blocking collectives: 26.8 us -> 0 us
  starting transfers between devices: 37 us -> 21.3 us
  local copies, waits for them, and re-layouts: 1.46 us -> 4.68 us
  Pallas kernels: 22.7 us -> 24.9 us
    ppermute x29 -> x41, waiting for transfers between devices: 51.2 us -> 93.9 us  [the longest x12 41.3 us: around(): own = lax.ppermute(own, 'tm', hop)]
    all_to_all x2 -> x0, blocking collectives: 26.8 us -> none  [exchange(): lax.all_to_all(blocks, axis, split_axis=0, concat_axis=0, tiled=True)]
    all_to_all x2 -> x0, starting transfers between devices: 11.2 us -> none  [exchange(): lax.all_to_all(blocks, axis, split_axis=0, concat_axis=0, tiled=True)]
    ppermute x29 -> x41, starting transfers between devices: 25.8 us -> 21.3 us  [the longest x12 6.87 us: around(): own = lax.ppermute(own, 'tm', hop)]
    all_to_all x2 -> x0, waiting for transfers between devices: 3.83 us -> none  [exchange(): lax.all_to_all(blocks, axis, split_axis=0, concat_axis=0, tiled=True)]
    pallas_call x9 -> x10, Pallas kernels: 22.7 us -> 24.9 us  [the longest x1 7.41 us: by_ring(): call(first_spectral_kernel, first_outs, 9, scratch, work, 1)]
    unnamed x12 -> x10, local copies, waits for them, and re-layouts: 0.03 us -> 1.91 us
  transfers between devices with their start and end apart: 31 -> 41, of which waited for: 21 -> 35; matrix products, arithmetic and copies ran while one was open for 1% -> 2% of each run, Pallas kernels for 5% -> 7%
where the time goes in v3:
time: 146 us
  waiting for transfers between devices  93.9 us (64%)
  Pallas kernels  24.9 us (17%)
  starting transfers between devices  21.3 us (15%)
  local copies, waits for them, and re-layouts  4.68 us (3%)
    ppermute x12, waiting for transfers between devices, around(): own = lax.ppermute(own, 'tm', hop)  41.3 us
    ppermute x12, waiting for transfers between devices, around(): partner = lax.ppermute(partner, 'tm', hop)  27 us
    ppermute x4, waiting for transfers between devices, around(): last = lax.ppermute(own, 'tm', hop)  17.4 us
    pallas_call x1, Pallas kernels, by_ring(): call(first_spectral_kernel, first_outs, 9, scratch, work, 1)  7.41 us
    pallas_call x1, Pallas kernels, by_ring(): call(next_spectral_kernel, field_shape, 11, scratch, work, 1)  7.38 us
    ppermute x12, starting transfers between devices, around(): own = lax.ppermute(own, 'tm', hop)  6.87 us
    ppermute x12, starting transfers between devices, around(): partner = lax.ppermute(partner, 'tm', hop)  5.78 us
    ppermute x1, starting transfers between devices, by_ring(): lax.ppermute(damp_late, 'tm', [(i, (i - 1) % length) for i in range(lengt...  5.14 us
  transfers between devices with their start and end apart: 41, of which 35 were waited for; matrix products, arithmetic and copies ran while one was open for 2% of the time, Pallas kernels for 7%

profile of v3, /device:TPU:0, one launch (start us, length us, event | category | flops | bytes accessed | tf_op | source)
XLA Modules:
  0.0 145.6 jit_solution(8525096994767010518)
XLA Ops:
  0.6 0.9 copy-done
  1.6 0.9 copy-done.2
  3.2 2.6 %collective-permute-start.1 = (f32[264,256]{1,0:T(8,128)S(1)}, f32[264,256]{1,0:T(8,128)S(1)}, u32[]{:S(2)}, u32[]{:S(2)}) collective-permute-start(f32[264,256]{1,0:T(8,128)S(1)} %get-tuple-element.28.refs_1_), channel_id=1, source_target_pairs={{0,4},{1,3},{4,8},{5,1},{8,12},{9,5},{12,14},{13,9},{14,10},{15,13... | collective-permute-start | bytes 811016 | tf_op jit(solution)/shard_map/ppermute | solution.py:357
  5.8 1.6 %collective-permute-start.2 = (f32[264,256]{1,0:T(8,128)S(1)}, f32[264,256]{1,0:T(8,128)S(1)}, u32[]{:S(2)}, u32[]{:S(2)}) collective-permute-start(f32[264,256]{1,0:T(8,128)S(1)} %collective-permute-done.refs_2_), channel_id=1, source_target_pairs={{0,4},{1,3},{4,8},{5,1},{8,12},{9,5},{12,14},{13,9},{14,10},{15,13... | collective-permute-start | bytes 811016 | tf_op jit(solution)/shard_map/ppermute | solution.py:358
  7.4 2.8 %collective-permute-done.1.refs_3_ = f32[264,256]{1,0:T(8,128)S(1)} collective-permute-done((f32[264,256]{1,0:T(8,128)S(1)}, f32[264,256]{1,0:T(8,128)S(1)}, u32[]{:S(2)}, u32[]{:S(2)}) %collective-permute-start.1) | collective-permute-done | bytes 270368 | tf_op jit(solution)/shard_map/ppermute | solution.py:357
  10.2 2.1 %collective-permute-start.3 = (f32[264,256]{1,0:T(8,128)S(1)}, f32[264,256]{1,0:T(8,128)S(1)}, u32[]{:S(2)}, u32[]{:S(2)}) collective-permute-start(f32[264,256]{1,0:T(8,128)S(1)} %collective-permute-done.1.refs_3_), channel_id=1, source_target_pairs={{0,4},{1,3},{4,8},{5,1},{8,12},{9,5},{12,14},{13,9},{14,10},{15,13... | collective-permute-start | bytes 811016 | tf_op jit(solution)/shard_map/ppermute | solution.py:357
  13.1 2.1 %collective-permute-start.4 = (f32[264,256]{1,0:T(8,128)S(1)}, f32[264,256]{1,0:T(8,128)S(1)}, u32[]{:S(2)}, u32[]{:S(2)}) collective-permute-start(f32[264,256]{1,0:T(8,128)S(1)} %collective-permute-done.2.refs_4_), channel_id=1, source_target_pairs={{0,4},{1,3},{4,8},{5,1},{8,12},{9,5},{12,14},{13,9},{14,10},{15,13... | collective-permute-start | bytes 811016 | tf_op jit(solution)/shard_map/ppermute | solution.py:358
  15.1 1.5 %collective-permute-done.3.refs_5_ = f32[264,256]{1,0:T(8,128)S(1)} collective-permute-done((f32[264,256]{1,0:T(8,128)S(1)}, f32[264,256]{1,0:T(8,128)S(1)}, u32[]{:S(2)}, u32[]{:S(2)}) %collective-permute-start.3) | collective-permute-done | bytes 270368 | tf_op jit(solution)/shard_map/ppermute | solution.py:357
  16.6 2.1 %collective-permute-start.5 = (f32[264,256]{1,0:T(8,128)S(1)}, f32[264,256]{1,0:T(8,128)S(1)}, u32[]{:S(2)}, u32[]{:S(2)}) collective-permute-start(f32[264,256]{1,0:T(8,128)S(1)} %collective-permute-done.3.refs_5_), channel_id=1, source_target_pairs={{0,4},{1,3},{4,8},{5,1},{8,12},{9,5},{12,14},{13,9},{14,10},{15,13... | collective-permute-start | bytes 811016 | tf_op jit(solution)/shard_map/ppermute | solution.py:357
  19.5 2.1 %collective-permute-start.6 = (f32[264,256]{1,0:T(8,128)S(1)}, f32[264,256]{1,0:T(8,128)S(1)}, u32[]{:S(2)}, u32[]{:S(2)}) collective-permute-start(f32[264,256]{1,0:T(8,128)S(1)} %collective-permute-done.4.refs_6_), channel_id=1, source_target_pairs={{0,4},{1,3},{4,8},{5,1},{8,12},{9,5},{12,14},{13,9},{14,10},{15,13... | collective-permute-start | bytes 811016 | tf_op jit(solution)/shard_map/ppermute | solution.py:358
  21.6 1.5 %collective-permute-done.5.refs_7_ = f32[264,256]{1,0:T(8,128)S(1)} collective-permute-done((f32[264,256]{1,0:T(8,128)S(1)}, f32[264,256]{1,0:T(8,128)S(1)}, u32[]{:S(2)}, u32[]{:S(2)}) %collective-permute-start.5) | collective-permute-done | bytes 270368 | tf_op jit(solution)/shard_map/ppermute | solution.py:357
  23.1 2.1 %collective-permute-start.8 = (f32[264,256]{1,0:T(8,128)S(1)}, f32[264,256]{1,0:T(8,128)S(1)}, u32[]{:S(2)}, u32[]{:S(2)}) collective-permute-start(f32[264,256]{1,0:T(8,128)S(1)} %collective-permute-done.5.refs_7_), channel_id=1, source_target_pairs={{0,4},{1,3},{4,8},{5,1},{8,12},{9,5},{12,14},{13,9},{14,10},{15,13... | collective-permute-start | bytes 811016 | tf_op jit(solution)/shard_map/ppermute | solution.py:360
  26.0 1.5 %shard_map.96 = (f32[264,256]{1,0:T(8,128)S(1)}, f32[264,256]{1,0:T(8,128)}) custom-call(f32[14]{0:T(128)S(1)} %fusion.3.refs_0_, f32[264,256]{1,0:T(8,128)S(1)} %get-tuple-element.28.refs_1_, f32[264,256]{1,0:T(8,128)S(1)} %collective-permute-done.refs_2_, f32[264,256]{1,0:T(8,128)S(1)} %collective-permute-done.1.refs_3_, ...), custom_call_target="tpu_custom_call" | custom-call | flops 2097152 | tf_op jit(solution)/shard_map/pallas_call | solution.py:367
  27.5 2.0 %collective-permute-done.8.last_ref = f32[264,256]{1,0:T(8,128)S(1)} collective-permute-done((f32[264,256]{1,0:T(8,128)S(1)}, f32[264,256]{1,0:T(8,128)S(1)}, u32[]{:S(2)}, u32[]{:S(2)}) %collective-permute-start.8) | collective-permute-done | bytes 270368 | tf_op jit(solution)/shard_map/ppermute | solution.py:360
  31.1 5.1 %collective-permute-start.10 = (f32[256,256]{1,0:T(8,128)S(1)}, f32[256,256]{1,0:T(8,128)S(1)}, u32[]{:S(2)}, u32[]{:S(2)}) collective-permute-start(f32[256,256]{1,0:T(8,128)S(1)} %get-tuple-element.42.refs_0_), channel_id=1, source_target_pairs={{0,15},{1,0},{2,1},{3,2},{4,3},{5,4},{6,5},{7,6},{8,7},{9,8},{10,9... | collective-permute-start | bytes 786440 | tf_op jit(solution)/shard_map/ppermute | solution.py:381
  36.2 7.4 %shard_map.98 = (f32[256,256]{1,0:T(8,128)S(1)}, f32[1,256]{1,0:T(1,128)S(1)}) custom-call(f32[2]{0:T(128)S(1)} %fusion.2.weight_ref, f32[264,256]{1,0:T(8,128)S(1)} %get-tuple-element.33.keep_ref, f32[264,256]{1,0:T(8,128)S(1)} %collective-permute-done.7.other_ref, f32[264,256]{1,0:T(8,128)S(1)} %collective-permute-done.8.last_ref, ...), custom_call_target="tpu_custom_call" | custom-call | flops 4026531840 | tf_op jit(solution)/shard_map/pallas_call | solution.py:383
  43.8 1.5 collective-permute-done.11.refs_2_
  45.3 4.9 %collective-permute-done.12.refs_3_ = f32[256,256]{1,0:T(8,128)S(1)} collective-permute-done((f32[256,256]{1,0:T(8,128)S(1)}, f32[256,256]{1,0:T(8,128)S(1)}, u32[]{:S(2)}, u32[]{:S(2)}) %collective-permute-start.12) | collective-permute-done | bytes 262176 | tf_op jit(solution)/shard_map/ppermute | solution.py:357
  50.2 2.8 %collective-permute-done.13.refs_4_ = f32[256,256]{1,0:T(8,128)S(1)} collective-permute-done((f32[256,256]{1,0:T(8,128)S(1)}, f32[256,256]{1,0:T(8,128)S(1)}, u32[]{:S(2)}, u32[]{:S(2)}) %collective-permute-start.13) | collective-permute-done | bytes 262176 | tf_op jit(solution)/shard_map/ppermute | solution.py:358
  53.0 3.6 %collective-permute-done.14.refs_5_ = f32[256,256]{1,0:T(8,128)S(1)} collective-permute-done((f32[256,256]{1,0:T(8,128)S(1)}, f32[256,256]{1,0:T(8,128)S(1)}, u32[]{:S(2)}, u32[]{:S(2)}) %collective-permute-start.14) | collective-permute-done | bytes 262176 | tf_op jit(solution)/shard_map/ppermute | solution.py:357
  56.6 2.8 %collective-permute-done.15.refs_6_ = f32[256,256]{1,0:T(8,128)S(1)} collective-permute-done((f32[256,256]{1,0:T(8,128)S(1)}, f32[256,256]{1,0:T(8,128)S(1)}, u32[]{:S(2)}, u32[]{:S(2)}) %collective-permute-start.15) | collective-permute-done | bytes 262176 | tf_op jit(solution)/shard_map/ppermute | solution.py:358
  60.1 2.9 %collective-permute-done.16.refs_7_ = f32[256,256]{1,0:T(8,128)S(1)} collective-permute-done((f32[256,256]{1,0:T(8,128)S(1)}, f32[256,256]{1,0:T(8,128)S(1)}, u32[]{:S(2)}, u32[]{:S(2)}) %collective-permute-start.16) | collective-permute-done | bytes 262176 | tf_op jit(solution)/shard_map/ppermute | solution.py:357
  62.9 2.8 %collective-permute-done.17.refs_8_ = f32[256,256]{1,0:T(8,128)S(1)} collective-permute-done((f32[256,256]{1,0:T(8,128)S(1)}, f32[256,256]{1,0:T(8,128)S(1)}, u32[]{:S(2)}, u32[]{:S(2)}) %collective-permute-start.17) | collective-permute-done | bytes 262176 | tf_op jit(solution)/shard_map/ppermute | solution.py:358
  65.7 1.4 shard_map.99
  67.2 6.4 %collective-permute-done.19.last_ref = f32[256,256]{1,0:T(8,128)S(1)} collective-permute-done((f32[256,256]{1,0:T(8,128)S(1)}, f32[256,256]{1,0:T(8,128)S(1)}, u32[]{:S(2)}, u32[]{:S(2)}) %collective-permute-start.19) | collective-permute-done | bytes 262176 | tf_op jit(solution)/shard_map/ppermute | solution.py:360
  74.3 0.8 collective-permute-done.20.last_other_ref
  75.1 1.8 %shard_map.100.refs_1_ = f32[256,256]{1,0:T(8,128)S(1)} custom-call(f32[6]{0:T(128)S(1)} %fusion.weight_ref, f32[256,768]{1,0:T(8,128)S(1)} %get-tuple-element.44.keep_ref, f32[256,768]{1,0:T(8,128)S(1)} %collective-permute-done.18.other_ref, f32[256,256]{1,0:T(8,128)S(1)} %collective-permute-done.19.last_ref, ...), custom_call_target="tpu_custom_call" | custom-call | tf_op jit(solution)/shard_map/pallas_call | solution.py:386
  77.2 1.4 collective-permute-done.21.refs_2_
  78.6 5.0 %collective-permute-done.22.refs_3_ = f32[256,256]{1,0:T(8,128)S(1)} collective-permute-done((f32[256,256]{1,0:T(8,128)S(1)}, f32[256,256]{1,0:T(8,128)S(1)}, u32[]{:S(2)}, u32[]{:S(2)}) %collective-permute-start.22) | collective-permute-done | bytes 262176 | tf_op jit(solution)/shard_map/ppermute | solution.py:357
  83.6 2.8 %collective-permute-done.23.refs_4_ = f32[256,256]{1,0:T(8,128)S(1)} collective-permute-done((f32[256,256]{1,0:T(8,128)S(1)}, f32[256,256]{1,0:T(8,128)S(1)}, u32[]{:S(2)}, u32[]{:S(2)}) %collective-permute-start.23) | collective-permute-done | bytes 262176 | tf_op jit(solution)/shard_map/ppermute | solution.py:358
  86.4 3.6 %collective-permute-done.24.refs_5_ = f32[256,256]{1,0:T(8,128)S(1)} collective-permute-done((f32[256,256]{1,0:T(8,128)S(1)}, f32[256,256]{1,0:T(8,128)S(1)}, u32[]{:S(2)}, u32[]{:S(2)}) %collective-permute-start.24) | collective-permute-done | bytes 262176 | tf_op jit(solution)/shard_map/ppermute | solution.py:357
  89.9 2.8 %collective-permute-done.25.refs_6_ = f32[256,256]{1,0:T(8,128)S(1)} collective-permute-done((f32[256,256]{1,0:T(8,128)S(1)}, f32[256,256]{1,0:T(8,128)S(1)}, u32[]{:S(2)}, u32[]{:S(2)}) %collective-permute-start.25) | collective-permute-done | bytes 262176 | tf_op jit(solution)/shard_map/ppermute | solution.py:358
  92.7 3.6 %collective-permute-done.26.refs_7_ = f32[256,256]{1,0:T(8,128)S(1)} collective-permute-done((f32[256,256]{1,0:T(8,128)S(1)}, f32[256,256]{1,0:T(8,128)S(1)}, u32[]{:S(2)}, u32[]{:S(2)}) %collective-permute-start.26) | collective-permute-done | bytes 262176 | tf_op jit(solution)/shard_map/ppermute | solution.py:357
  96.3 2.8 %collective-permute-done.27.refs_8_ = f32[256,256]{1,0:T(8,128)S(1)} collective-permute-done((f32[256,256]{1,0:T(8,128)S(1)}, f32[256,256]{1,0:T(8,128)S(1)}, u32[]{:S(2)}, u32[]{:S(2)}) %collective-permute-start.27) | collective-permute-done | bytes 262176 | tf_op jit(solution)/shard_map/ppermute | solution.py:358
  100.0 2.7 %collective-permute-done.29.last_ref = f32[256,256]{1,0:T(8,128)S(1)} collective-permute-done((f32[256,256]{1,0:T(8,128)S(1)}, f32[256,256]{1,0:T(8,128)S(1)}, u32[]{:S(2)}, u32[]{:S(2)}) %collective-permute-start.29) | collective-permute-done | bytes 262176 | tf_op jit(solution)/shard_map/ppermute | solution.py:360
  102.7 1.5 %collective-permute-done.30.last_other_ref = f32[256,256]{1,0:T(8,128)S(1)} collective-permute-done((f32[256,256]{1,0:T(8,128)S(1)}, f32[256,256]{1,0:T(8,128)S(1)}, u32[]{:S(2)}, u32[]{:S(2)}) %collective-permute-start.30) | collective-permute-done | bytes 262176 | tf_op jit(solution)/shard_map/ppermute | solution.py:369
  104.2 7.4 %shard_map.102.refs_1_ = f32[256,256]{1,0:T(8,128)S(1)} custom-call(f32[2]{0:T(128)S(1)} %fusion.2.weight_ref, f32[256,256]{1,0:T(8,128)S(1)} %get-tuple-element.47.keep_ref, f32[256,256]{1,0:T(8,128)S(1)} %collective-permute-done.28.other_ref, f32[256,256]{1,0:T(8,128)S(1)} %collective-permute-done.29.last_ref, ...), custom_call_target="tpu_custom_call" | custom-call | flops 4026531840 | tf_op jit(solution)/shard_map/pallas_call | solution.py:388
  111.8 1.4 collective-permute-done.31.refs_2_
  113.2 5.0 %collective-permute-done.32.refs_3_ = f32[256,256]{1,0:T(8,128)S(1)} collective-permute-done((f32[256,256]{1,0:T(8,128)S(1)}, f32[256,256]{1,0:T(8,128)S(1)}, u32[]{:S(2)}, u32[]{:S(2)}) %collective-permute-start.32) | collective-permute-done | bytes 262176 | tf_op jit(solution)/shard_map/ppermute | solution.py:357
  118.2 2.8 %collective-permute-done.33.refs_4_ = f32[256,256]{1,0:T(8,128)S(1)} collective-permute-done((f32[256,256]{1,0:T(8,128)S(1)}, f32[256,256]{1,0:T(8,128)S(1)}, u32[]{:S(2)}, u32[]{:S(2)}) %collective-permute-start.33) | collective-permute-done | bytes 262176 | tf_op jit(solution)/shard_map/ppermute | solution.py:358
  121.0 3.6 %collective-permute-done.34.refs_5_ = f32[256,256]{1,0:T(8,128)S(1)} collective-permute-done((f32[256,256]{1,0:T(8,128)S(1)}, f32[256,256]{1,0:T(8,128)S(1)}, u32[]{:S(2)}, u32[]{:S(2)}) %collective-permute-start.34) | collective-permute-done | bytes 262176 | tf_op jit(solution)/shard_map/ppermute | solution.py:357
  124.6 2.8 %collective-permute-done.35.refs_6_ = f32[256,256]{1,0:T(8,128)S(1)} collective-permute-done((f32[256,256]{1,0:T(8,128)S(1)}, f32[256,256]{1,0:T(8,128)S(1)}, u32[]{:S(2)}, u32[]{:S(2)}) %collective-permute-start.35) | collective-permute-done | bytes 262176 | tf_op jit(solution)/shard_map/ppermute | solution.py:358
  127.4 3.6 %collective-permute-done.36.refs_7_ = f32[256,256]{1,0:T(8,128)S(1)} collective-permute-done((f32[256,256]{1,0:T(8,128)S(1)}, f32[256,256]{1,0:T(8,128)S(1)}, u32[]{:S(2)}, u32[]{:S(2)}) %collective-permute-start.36) | collective-permute-done | bytes 262176 | tf_op jit(solution)/shard_map/ppermute | solution.py:357
  130.9 2.8 %collective-permute-done.37.refs_8_ = f32[256,256]{1,0:T(8,128)S(1)} collective-permute-done((f32[256,256]{1,0:T(8,128)S(1)}, f32[256,256]{1,0:T(8,128)S(1)}, u32[]{:S(2)}, u32[]{:S(2)}) %collective-permute-start.37) | collective-permute-done | bytes 262176 | tf_op jit(solution)/shard_map/ppermute | solution.py:358
  133.7 1.3 shard_map.103
  135.2 6.4 %collective-permute-done.39.last_ref = f32[256,256]{1,0:T(8,128)S(1)} collective-permute-done((f32[256,256]{1,0:T(8,128)S(1)}, f32[256,256]{1,0:T(8,128)S(1)}, u32[]{:S(2)}, u32[]{:S(2)}) %collective-permute-start.39) | collective-permute-done | bytes 262176 | tf_op jit(solution)/shard_map/ppermute | solution.py:360
  141.6 1.5 %collective-permute-done.40.last_other_ref = f32[256,256]{1,0:T(8,128)S(1)} collective-permute-done((f32[256,256]{1,0:T(8,128)S(1)}, f32[256,256]{1,0:T(8,128)S(1)}, u32[]{:S(2)}, u32[]{:S(2)}) %collective-permute-start.40) | collective-permute-done | bytes 262176 | tf_op jit(solution)/shard_map/ppermute | solution.py:369
  143.1 2.5 %shard_map.104 = (f32[256,256]{1,0:T(8,128)}, f32[256,256]{1,0:T(8,128)}) custom-call(f32[6]{0:T(128)S(1)} %fusion.weight_ref, f32[256,768]{1,0:T(8,128)S(1)} %get-tuple-element.50.keep_ref, f32[256,768]{1,0:T(8,128)S(1)} %collective-permute-done.38.other_ref, f32[256,256]{1,0:T(8,128)S(1)} %collective-permute-done.39.last_ref, ...), custom_call_target="tpu_custom_call" | custom-call | tf_op jit(solution)/shard_map/pallas_call | solution.py:390
  (59 shorter events, 7.7 us)
Async XLA Ops:
  0.6 1.0 copy-start
  1.6 0.9 copy-start.2
  2.6 3.2 %collective-permute-start = (f32[264,256]{1,0:T(8,128)S(1)}, f32[264,256]{1,0:T(8,128)S(1)}, u32[]{:S(2)}, u32[]{:S(2)}) collective-permute-start(f32[264,256]{1,0:T(8,128)S(1)} %get-tuple-element.28.refs_1_), channel_id=1, source_target_pairs={{0,1},{1,0},{2,3},{3,2},{4,5},{5,4},{6,7},{7,6},{8,9},{9,8},{10,11... | collective-permute-start | bytes 811016 | tf_op jit(solution)/shard_map/ppermute | solution.py:354
  3.2 7.0 %collective-permute-start.1 = (f32[264,256]{1,0:T(8,128)S(1)}, f32[264,256]{1,0:T(8,128)S(1)}, u32[]{:S(2)}, u32[]{:S(2)}) collective-permute-start(f32[264,256]{1,0:T(8,128)S(1)} %get-tuple-element.28.refs_1_), channel_id=1, source_target_pairs={{0,4},{1,3},{4,8},{5,1},{8,12},{9,5},{12,14},{13,9},{14,10},{15,13... | collective-permute-start | bytes 811016 | tf_op jit(solution)/shard_map/ppermute | solution.py:357
  5.8 7.3 %collective-permute-start.2 = (f32[264,256]{1,0:T(8,128)S(1)}, f32[264,256]{1,0:T(8,128)S(1)}, u32[]{:S(2)}, u32[]{:S(2)}) collective-permute-start(f32[264,256]{1,0:T(8,128)S(1)} %collective-permute-done.refs_2_), channel_id=1, source_target_pairs={{0,4},{1,3},{4,8},{5,1},{8,12},{9,5},{12,14},{13,9},{14,10},{15,13... | collective-permute-start | bytes 811016 | tf_op jit(solution)/shard_map/ppermute | solution.py:358
  10.2 6.5 %collective-permute-start.3 = (f32[264,256]{1,0:T(8,128)S(1)}, f32[264,256]{1,0:T(8,128)S(1)}, u32[]{:S(2)}, u32[]{:S(2)}) collective-permute-start(f32[264,256]{1,0:T(8,128)S(1)} %collective-permute-done.1.refs_3_), channel_id=1, source_target_pairs={{0,4},{1,3},{4,8},{5,1},{8,12},{9,5},{12,14},{13,9},{14,10},{15,13... | collective-permute-start | bytes 811016 | tf_op jit(solution)/shard_map/ppermute | solution.py:357
  13.1 6.5 %collective-permute-start.4 = (f32[264,256]{1,0:T(8,128)S(1)}, f32[264,256]{1,0:T(8,128)S(1)}, u32[]{:S(2)}, u32[]{:S(2)}) collective-permute-start(f32[264,256]{1,0:T(8,128)S(1)} %collective-permute-done.2.refs_4_), channel_id=1, source_target_pairs={{0,4},{1,3},{4,8},{5,1},{8,12},{9,5},{12,14},{13,9},{14,10},{15,13... | collective-permute-start | bytes 811016 | tf_op jit(solution)/shard_map/ppermute | solution.py:358
  16.6 6.5 %collective-permute-start.5 = (f32[264,256]{1,0:T(8,128)S(1)}, f32[264,256]{1,0:T(8,128)S(1)}, u32[]{:S(2)}, u32[]{:S(2)}) collective-permute-start(f32[264,256]{1,0:T(8,128)S(1)} %collective-permute-done.3.refs_5_), channel_id=1, source_target_pairs={{0,4},{1,3},{4,8},{5,1},{8,12},{9,5},{12,14},{13,9},{14,10},{15,13... | collective-permute-start | bytes 811016 | tf_op jit(solution)/shard_map/ppermute | solution.py:357
  19.5 6.5 %collective-permute-start.6 = (f32[264,256]{1,0:T(8,128)S(1)}, f32[264,256]{1,0:T(8,128)S(1)}, u32[]{:S(2)}, u32[]{:S(2)}) collective-permute-start(f32[264,256]{1,0:T(8,128)S(1)} %collective-permute-done.4.refs_6_), channel_id=1, source_target_pairs={{0,4},{1,3},{4,8},{5,1},{8,12},{9,5},{12,14},{13,9},{14,10},{15,13... | collective-permute-start | bytes 811016 | tf_op jit(solution)/shard_map/ppermute | solution.py:358
  23.1 6.5 %collective-permute-start.8 = (f32[264,256]{1,0:T(8,128)S(1)}, f32[264,256]{1,0:T(8,128)S(1)}, u32[]{:S(2)}, u32[]{:S(2)}) collective-permute-start(f32[264,256]{1,0:T(8,128)S(1)} %collective-permute-done.5.refs_7_), channel_id=1, source_target_pairs={{0,4},{1,3},{4,8},{5,1},{8,12},{9,5},{12,14},{13,9},{14,10},{15,13... | collective-permute-start | bytes 811016 | tf_op jit(solution)/shard_map/ppermute | solution.py:360
  25.9 3.8 %copy-start.3 = (f32[256,256]{1,0:T(8,128)S(1)}, f32[256,256]{1,0:T(8,128)}, u32[]{:S(2)}) copy-start(f32[256,256]{1,0:T(8,128)} %hop_x_ref.1) | copy-start | bytes 786436
  25.9 3.8 %copy-start.4 = (f32[256,256]{1,0:T(8,128)S(1)}, f32[256,256]{1,0:T(8,128)}, u32[]{:S(2)}) copy-start(f32[256,256]{1,0:T(8,128)} %hop_y_ref.1) | copy-start | bytes 786436
  27.5 3.5 %collective-permute-start.7 = (f32[264,256]{1,0:T(8,128)}, f32[264,256]{1,0:T(8,128)S(1)}, u32[]{:S(2)}, u32[]{:S(2)}) collective-permute-start(f32[264,256]{1,0:T(8,128)} %get-tuple-element.30), channel_id=1, source_target_pairs={{0,1},{1,0},{2,3},{3,2},{4,5},{5,4},{6,7},{7,6},{8,9},{9,8},{10,11... | collective-permute-start | bytes 811016 | tf_op jit(solution)/shard_map/ppermute | solution.py:368
  29.6 1.5 %collective-permute-start.9 = (f32[264,256]{1,0:T(8,128)S(1)}, f32[264,256]{1,0:T(8,128)S(1)}, u32[]{:S(2)}, u32[]{:S(2)}) collective-permute-start(f32[264,256]{1,0:T(8,128)S(1)} %collective-permute-done.8.last_ref), channel_id=1, source_target_pairs={{0,1},{1,0},{2,3},{3,2},{4,5},{5,4},{6,7},{7,6},{8,9},{9,8},{10,11... | collective-permute-start | bytes 811016 | tf_op jit(solution)/shard_map/ppermute | solution.py:369
  31.1 12.6 %collective-permute-start.10 = (f32[256,256]{1,0:T(8,128)S(1)}, f32[256,256]{1,0:T(8,128)S(1)}, u32[]{:S(2)}, u32[]{:S(2)}) collective-permute-start(f32[256,256]{1,0:T(8,128)S(1)} %get-tuple-element.42.refs_0_), channel_id=1, source_target_pairs={{0,15},{1,0},{2,1},{3,2},{4,3},{5,4},{6,5},{7,6},{8,7},{9,8},{10,9... | collective-permute-start | bytes 786440 | tf_op jit(solution)/shard_map/ppermute | solution.py:381
  43.7 1.6 %collective-permute-start.11 = (f32[256,256]{1,0:T(8,128)S(1)}, f32[256,256]{1,0:T(8,128)S(1)}, u32[]{:S(2)}, u32[]{:S(2)}) collective-permute-start(f32[256,256]{1,0:T(8,128)S(1)} %get-tuple-element.43.refs_1_.refs_5_), channel_id=1, source_target_pairs={{0,1},{1,0},{2,3},{3,2},{4,5},{5,4},{6,7},{7,6},{8,9},{9,8},{10,11... | collective-permute-start | bytes 786440 | tf_op jit(solution)/shard_map/ppermute | solution.py:354
  43.8 6.4 %collective-permute-start.12 = (f32[256,256]{1,0:T(8,128)S(1)}, f32[256,256]{1,0:T(8,128)S(1)}, u32[]{:S(2)}, u32[]{:S(2)}) collective-permute-start(f32[256,256]{1,0:T(8,128)S(1)} %get-tuple-element.43.refs_1_.refs_5_), channel_id=1, source_target_pairs={{0,4},{1,3},{4,8},{5,1},{8,12},{9,5},{12,14},{13,9},{14,10},{15,13... | collective-permute-start | bytes 786440 | tf_op jit(solution)/shard_map/ppermute | solution.py:357
  45.3 7.7 %collective-permute-start.13 = (f32[256,256]{1,0:T(8,128)S(1)}, f32[256,256]{1,0:T(8,128)S(1)}, u32[]{:S(2)}, u32[]{:S(2)}) collective-permute-start(f32[256,256]{1,0:T(8,128)S(1)} %collective-permute-done.11.refs_2_), channel_id=1, source_target_pairs={{0,4},{1,3},{4,8},{5,1},{8,12},{9,5},{12,14},{13,9},{14,10},{15,13... | collective-permute-start | bytes 786440 | tf_op jit(solution)/shard_map/ppermute | solution.py:358
  50.2 6.4 %collective-permute-start.14 = (f32[256,256]{1,0:T(8,128)S(1)}, f32[256,256]{1,0:T(8,128)S(1)}, u32[]{:S(2)}, u32[]{:S(2)}) collective-permute-start(f32[256,256]{1,0:T(8,128)S(1)} %collective-permute-done.12.refs_3_), channel_id=1, source_target_pairs={{0,4},{1,3},{4,8},{5,1},{8,12},{9,5},{12,14},{13,9},{14,10},{15,13... | collective-permute-start | bytes 786440 | tf_op jit(solution)/shard_map/ppermute | solution.py:357
  53.0 6.4 %collective-permute-start.15 = (f32[256,256]{1,0:T(8,128)S(1)}, f32[256,256]{1,0:T(8,128)S(1)}, u32[]{:S(2)}, u32[]{:S(2)}) collective-permute-start(f32[256,256]{1,0:T(8,128)S(1)} %collective-permute-done.13.refs_4_), channel_id=1, source_target_pairs={{0,4},{1,3},{4,8},{5,1},{8,12},{9,5},{12,14},{13,9},{14,10},{15,13... | collective-permute-start | bytes 786440 | tf_op jit(solution)/shard_map/ppermute | solution.py:358
  56.6 6.4 %collective-permute-start.16 = (f32[256,256]{1,0:T(8,128)S(1)}, f32[256,256]{1,0:T(8,128)S(1)}, u32[]{:S(2)}, u32[]{:S(2)}) collective-permute-start(f32[256,256]{1,0:T(8,128)S(1)} %collective-permute-done.14.refs_5_), channel_id=1, source_target_pairs={{0,4},{1,3},{4,8},{5,1},{8,12},{9,5},{12,14},{13,9},{14,10},{15,13... | collective-permute-start | bytes 786440 | tf_op jit(solution)/shard_map/ppermute | solution.py:357
  59.4 6.4 %collective-permute-start.17 = (f32[256,256]{1,0:T(8,128)S(1)}, f32[256,256]{1,0:T(8,128)S(1)}, u32[]{:S(2)}, u32[]{:S(2)}) collective-permute-start(f32[256,256]{1,0:T(8,128)S(1)} %collective-permute-done.15.refs_6_), channel_id=1, source_target_pairs={{0,4},{1,3},{4,8},{5,1},{8,12},{9,5},{12,14},{13,9},{14,10},{15,13... | collective-permute-start | bytes 786440 | tf_op jit(solution)/shard_map/ppermute | solution.py:358
  60.1 15.1 %copy-start.1 = (f32[1,256,256]{2,1,0:T(8,128)S(1)}, f32[1,256,256]{2,1,0:T(8,128)}, u32[]{:S(2)}) copy-start(f32[1,256,256]{2,1,0:T(8,128)} %param.8) | copy-start | bytes 786436
  67.1 8.0 %collective-permute-start.18 = (f32[256,768]{1,0:T(8,128)S(1)}, f32[256,768]{1,0:T(8,128)S(1)}, u32[]{:S(2)}, u32[]{:S(2)}) collective-permute-start(f32[256,768]{1,0:T(8,128)S(1)} %get-tuple-element.45), channel_id=1, source_target_pairs={{0,1},{1,0},{2,3},{3,2},{4,5},{5,4},{6,7},{7,6},{8,9},{9,8},{10,11... | collective-permute-start | bytes 2359304 | tf_op jit(solution)/shard_map/ppermute | solution.py:368
  67.2 6.4 %collective-permute-start.19 = (f32[256,256]{1,0:T(8,128)S(1)}, f32[256,256]{1,0:T(8,128)S(1)}, u32[]{:S(2)}, u32[]{:S(2)}) collective-permute-start(f32[256,256]{1,0:T(8,128)S(1)} %collective-permute-done.16.refs_7_), channel_id=1, source_target_pairs={{0,4},{1,3},{4,8},{5,1},{8,12},{9,5},{12,14},{13,9},{14,10},{15,13... | collective-permute-start | bytes 786440 | tf_op jit(solution)/shard_map/ppermute | solution.py:360
  73.6 1.5 %collective-permute-start.20 = (f32[256,256]{1,0:T(8,128)S(1)}, f32[256,256]{1,0:T(8,128)S(1)}, u32[]{:S(2)}, u32[]{:S(2)}) collective-permute-start(f32[256,256]{1,0:T(8,128)S(1)} %collective-permute-done.19.last_ref), channel_id=1, source_target_pairs={{0,1},{1,0},{2,3},{3,2},{4,5},{5,4},{6,7},{7,6},{8,9},{9,8},{10,11... | collective-permute-start | bytes 786440 | tf_op jit(solution)/shard_map/ppermute | solution.py:369
  77.0 1.6 %collective-permute-start.21 = (f32[256,256]{1,0:T(8,128)S(1)}, f32[256,256]{1,0:T(8,128)S(1)}, u32[]{:S(2)}, u32[]{:S(2)}) collective-permute-start(f32[256,256]{1,0:T(8,128)S(1)} %shard_map.100.refs_1_), channel_id=1, source_target_pairs={{0,1},{1,0},{2,3},{3,2},{4,5},{5,4},{6,7},{7,6},{8,9},{9,8},{10,11... | collective-permute-start | bytes 786440 | tf_op jit(solution)/shard_map/ppermute | solution.py:354
  77.2 6.4 %collective-permute-start.22 = (f32[256,256]{1,0:T(8,128)S(1)}, f32[256,256]{1,0:T(8,128)S(1)}, u32[]{:S(2)}, u32[]{:S(2)}) collective-permute-start(f32[256,256]{1,0:T(8,128)S(1)} %shard_map.100.refs_1_), channel_id=1, source_target_pairs={{0,4},{1,3},{4,8},{5,1},{8,12},{9,5},{12,14},{13,9},{14,10},{15,13... | collective-permute-start | bytes 786440 | tf_op jit(solution)/shard_map/ppermute | solution.py:357
  78.6 7.8 %collective-permute-start.23 = (f32[256,256]{1,0:T(8,128)S(1)}, f32[256,256]{1,0:T(8,128)S(1)}, u32[]{:S(2)}, u32[]{:S(2)}) collective-permute-start(f32[256,256]{1,0:T(8,128)S(1)} %collective-permute-done.21.refs_2_), channel_id=1, source_target_pairs={{0,4},{1,3},{4,8},{5,1},{8,12},{9,5},{12,14},{13,9},{14,10},{15,13... | collective-permute-start | bytes 786440 | tf_op jit(solution)/shard_map/ppermute | solution.py:358
  83.6 6.4 %collective-permute-start.24 = (f32[256,256]{1,0:T(8,128)S(1)}, f32[256,256]{1,0:T(8,128)S(1)}, u32[]{:S(2)}, u32[]{:S(2)}) collective-permute-start(f32[256,256]{1,0:T(8,128)S(1)} %collective-permute-done.22.refs_3_), channel_id=1, source_target_pairs={{0,4},{1,3},{4,8},{5,1},{8,12},{9,5},{12,14},{13,9},{14,10},{15,13... | collective-permute-start | bytes 786440 | tf_op jit(solution)/shard_map/ppermute | solution.py:357
  86.4 6.4 %collective-permute-start.25 = (f32[256,256]{1,0:T(8,128)S(1)}, f32[256,256]{1,0:T(8,128)S(1)}, u32[]{:S(2)}, u32[]{:S(2)}) collective-permute-start(f32[256,256]{1,0:T(8,128)S(1)} %collective-permute-done.23.refs_4_), channel_id=1, source_target_pairs={{0,4},{1,3},{4,8},{5,1},{8,12},{9,5},{12,14},{13,9},{14,10},{15,13... | collective-permute-start | bytes 786440 | tf_op jit(solution)/shard_map/ppermute | solution.py:358
  89.9 6.4 %collective-permute-start.26 = (f32[256,256]{1,0:T(8,128)S(1)}, f32[256,256]{1,0:T(8,128)S(1)}, u32[]{:S(2)}, u32[]{:S(2)}) collective-permute-start(f32[256,256]{1,0:T(8,128)S(1)} %collective-permute-done.24.refs_5_), channel_id=1, source_target_pairs={{0,4},{1,3},{4,8},{5,1},{8,12},{9,5},{12,14},{13,9},{14,10},{15,13... | collective-permute-start | bytes 786440 | tf_op jit(solution)/shard_map/ppermute | solution.py:357
  92.7 6.4 %collective-permute-start.27 = (f32[256,256]{1,0:T(8,128)S(1)}, f32[256,256]{1,0:T(8,128)S(1)}, u32[]{:S(2)}, u32[]{:S(2)}) collective-permute-start(f32[256,256]{1,0:T(8,128)S(1)} %collective-permute-done.25.refs_6_), channel_id=1, source_target_pairs={{0,4},{1,3},{4,8},{5,1},{8,12},{9,5},{12,14},{13,9},{14,10},{15,13... | collective-permute-start | bytes 786440 | tf_op jit(solution)/shard_map/ppermute | solution.py:358
  96.3 6.4 %collective-permute-start.29 = (f32[256,256]{1,0:T(8,128)S(1)}, f32[256,256]{1,0:T(8,128)S(1)}, u32[]{:S(2)}, u32[]{:S(2)}) collective-permute-start(f32[256,256]{1,0:T(8,128)S(1)} %collective-permute-done.26.refs_7_), channel_id=1, source_target_pairs={{0,4},{1,3},{4,8},{5,1},{8,12},{9,5},{12,14},{13,9},{14,10},{15,13... | collective-permute-start | bytes 786440 | tf_op jit(solution)/shard_map/ppermute | solution.py:360
  99.9 2.8 %collective-permute-start.28 = (f32[256,256]{1,0:T(8,128)S(1)}, f32[256,256]{1,0:T(8,128)S(1)}, u32[]{:S(2)}, u32[]{:S(2)}) collective-permute-start(f32[256,256]{1,0:T(8,128)S(1)} %get-tuple-element.48), channel_id=1, source_target_pairs={{0,1},{1,0},{2,3},{3,2},{4,5},{5,4},{6,7},{7,6},{8,9},{9,8},{10,11... | collective-permute-start | bytes 786440 | tf_op jit(solution)/shard_map/ppermute | solution.py:368
  102.7 1.5 %collective-permute-start.30 = (f32[256,256]{1,0:T(8,128)S(1)}, f32[256,256]{1,0:T(8,128)S(1)}, u32[]{:S(2)}, u32[]{:S(2)}) collective-permute-start(f32[256,256]{1,0:T(8,128)S(1)} %collective-permute-done.29.last_ref), channel_id=1, source_target_pairs={{0,1},{1,0},{2,3},{3,2},{4,5},{5,4},{6,7},{7,6},{8,9},{9,8},{10,11... | collective-permute-start | bytes 786440 | tf_op jit(solution)/shard_map/ppermute | solution.py:369
  111.6 1.6 %collective-permute-start.31 = (f32[256,256]{1,0:T(8,128)S(1)}, f32[256,256]{1,0:T(8,128)S(1)}, u32[]{:S(2)}, u32[]{:S(2)}) collective-permute-start(f32[256,256]{1,0:T(8,128)S(1)} %shard_map.102.refs_1_), channel_id=1, source_target_pairs={{0,1},{1,0},{2,3},{3,2},{4,5},{5,4},{6,7},{7,6},{8,9},{9,8},{10,11... | collective-permute-start | bytes 786440 | tf_op jit(solution)/shard_map/ppermute | solution.py:354
  111.8 6.4 %collective-permute-start.32 = (f32[256,256]{1,0:T(8,128)S(1)}, f32[256,256]{1,0:T(8,128)S(1)}, u32[]{:S(2)}, u32[]{:S(2)}) collective-permute-start(f32[256,256]{1,0:T(8,128)S(1)} %shard_map.102.refs_1_), channel_id=1, source_target_pairs={{0,4},{1,3},{4,8},{5,1},{8,12},{9,5},{12,14},{13,9},{14,10},{15,13... | collective-permute-start | bytes 786440 | tf_op jit(solution)/shard_map/ppermute | solution.py:357
  113.2 7.8 %collective-permute-start.33 = (f32[256,256]{1,0:T(8,128)S(1)}, f32[256,256]{1,0:T(8,128)S(1)}, u32[]{:S(2)}, u32[]{:S(2)}) collective-permute-start(f32[256,256]{1,0:T(8,128)S(1)} %collective-permute-done.31.refs_2_), channel_id=1, source_target_pairs={{0,4},{1,3},{4,8},{5,1},{8,12},{9,5},{12,14},{13,9},{14,10},{15,13... | collective-permute-start | bytes 786440 | tf_op jit(solution)/shard_map/ppermute | solution.py:358
  118.2 6.4 %collective-permute-start.34 = (f32[256,256]{1,0:T(8,128)S(1)}, f32[256,256]{1,0:T(8,128)S(1)}, u32[]{:S(2)}, u32[]{:S(2)}) collective-permute-start(f32[256,256]{1,0:T(8,128)S(1)} %collective-permute-done.32.refs_3_), channel_id=1, source_target_pairs={{0,4},{1,3},{4,8},{5,1},{8,12},{9,5},{12,14},{13,9},{14,10},{15,13... | collective-permute-start | bytes 786440 | tf_op jit(solution)/shard_map/ppermute | solution.py:357
  121.0 6.4 %collective-permute-start.35 = (f32[256,256]{1,0:T(8,128)S(1)}, f32[256,256]{1,0:T(8,128)S(1)}, u32[]{:S(2)}, u32[]{:S(2)}) collective-permute-start(f32[256,256]{1,0:T(8,128)S(1)} %collective-permute-done.33.refs_4_), channel_id=1, source_target_pairs={{0,4},{1,3},{4,8},{5,1},{8,12},{9,5},{12,14},{13,9},{14,10},{15,13... | collective-permute-start | bytes 786440 | tf_op jit(solution)/shard_map/ppermute | solution.py:358
  124.6 6.4 %collective-permute-start.36 = (f32[256,256]{1,0:T(8,128)S(1)}, f32[256,256]{1,0:T(8,128)S(1)}, u32[]{:S(2)}, u32[]{:S(2)}) collective-permute-start(f32[256,256]{1,0:T(8,128)S(1)} %collective-permute-done.34.refs_5_), channel_id=1, source_target_pairs={{0,4},{1,3},{4,8},{5,1},{8,12},{9,5},{12,14},{13,9},{14,10},{15,13... | collective-permute-start | bytes 786440 | tf_op jit(solution)/shard_map/ppermute | solution.py:357
  127.4 6.4 %collective-permute-start.37 = (f32[256,256]{1,0:T(8,128)S(1)}, f32[256,256]{1,0:T(8,128)S(1)}, u32[]{:S(2)}, u32[]{:S(2)}) collective-permute-start(f32[256,256]{1,0:T(8,128)S(1)} %collective-permute-done.35.refs_6_), channel_id=1, source_target_pairs={{0,4},{1,3},{4,8},{5,1},{8,12},{9,5},{12,14},{13,9},{14,10},{15,13... | collective-permute-start | bytes 786440 | tf_op jit(solution)/shard_map/ppermute | solution.py:358
  135.1 8.0 %collective-permute-start.38 = (f32[256,768]{1,0:T(8,128)S(1)}, f32[256,768]{1,0:T(8,128)S(1)}, u32[]{:S(2)}, u32[]{:S(2)}) collective-permute-start(f32[256,768]{1,0:T(8,128)S(1)} %get-tuple-element.51), channel_id=1, source_target_pairs={{0,1},{1,0},{2,3},{3,2},{4,5},{5,4},{6,7},{7,6},{8,9},{9,8},{10,11... | collective-permute-start | bytes 2359304 | tf_op jit(solution)/shard_map/ppermute | solution.py:368
  135.2 6.4 %collective-permute-start.39 = (f32[256,256]{1,0:T(8,128)S(1)}, f32[256,256]{1,0:T(8,128)S(1)}, u32[]{:S(2)}, u32[]{:S(2)}) collective-permute-start(f32[256,256]{1,0:T(8,128)S(1)} %collective-permute-done.36.refs_7_), channel_id=1, source_target_pairs={{0,4},{1,3},{4,8},{5,1},{8,12},{9,5},{12,14},{13,9},{14,10},{15,13... | collective-permute-start | bytes 786440 | tf_op jit(solution)/shard_map/ppermute | solution.py:360
  141.6 1.5 %collective-permute-start.40 = (f32[256,256]{1,0:T(8,128)S(1)}, f32[256,256]{1,0:T(8,128)S(1)}, u32[]{:S(2)}, u32[]{:S(2)}) collective-permute-start(f32[256,256]{1,0:T(8,128)S(1)} %collective-permute-done.39.last_ref), channel_id=1, source_target_pairs={{0,1},{1,0},{2,3},{3,2},{4,5},{5,4},{6,7},{7,6},{8,9},{9,8},{10,11... | collective-permute-start | bytes 786440 | tf_op jit(solution)/shard_map/ppermute | solution.py:369

commit v4 on v3

--- a/solution.py
+++ b/solution.py
@@ -113,38 +113,43 @@
     out_ref[...] = total if len(refs) == 9 else total + refs[7][...]
 
 
-def joined(weight_ref, part, refs, window):
+def joined(weight_ref, base, part, refs, window):
     keep_ref, other_ref, last_ref, last_other_ref = refs
     side_y = last_ref.shape[1]
     columns = slice(part * side_y, (part + 1) * side_y)
     total = keep_ref[window, columns] + other_ref[window, columns]
-    return total + (weight_ref[2 * part] * last_ref[window] + weight_ref[2 * part + 1] * last_other_ref[window])
-
-
-def first_spectral_kernel(weight_ref, keep_ref, other_ref, last_ref, last_other_ref, cos_ref, *refs):
+    return total + (weight_ref[base + 2 * part] * last_ref[window] + weight_ref[base + 2 * part + 1] * last_other_ref[window])
+
+
+def first_spectral_kernel(weight_ref, base, keep_ref, other_ref, last_ref, last_other_ref, cos_ref, *refs):
     hop_refs, (out_ref, mean_ref, row_ref) = refs[:4], refs[4:]
     side_x = out_ref.shape[0]
     sources = keep_ref, other_ref, last_ref, last_other_ref
     row = sum(ref[side_x : side_x + 1, :] for ref in sources)
     mean_level = jnp.broadcast_to(jnp.sum(row, axis=1, keepdims=True), row.shape)
     mean_ref[...] = mean_level
-    field = joined(weight_ref, 0, sources, slice(0, side_x))
+    field = joined(weight_ref, base, 0, sources, slice(0, side_x))
     out_ref[...] = chebyshev_sum(field, mean_level, cos_ref, hop_refs, row_ref)
 
 
-def next_spectral_kernel(weight_ref, keep_ref, other_ref, last_ref, last_other_ref, cos_ref, *refs):
+def next_spectral_kernel(weight_ref, base, keep_ref, other_ref, last_ref, last_other_ref, cos_ref, *refs):
     hop_refs, (mean_ref, add_ref, out_ref, row_ref) = refs[:4], refs[4:]
-    field = joined(weight_ref, 0, (keep_ref, other_ref, last_ref, last_other_ref), slice(None))
+    field = joined(weight_ref, base, 0, (keep_ref, other_ref, last_ref, last_other_ref), slice(None))
     out_ref[...] = chebyshev_sum(field, mean_ref[...], cos_ref, hop_refs, row_ref) + add_ref[...]
 
 
-def pack_kernel(noise_ref, level_ref, packed_ref, damp_ref, *, scale):
+def pack_kernel(noise_ref, level_ref, packed_ref, damp_ref, held_ref, noise_sem, level_sem, *, scale):
     side_x = noise_ref.shape[0]
-    levels = level_ref[...].astype(F32)
+    noise_copy = pltpu.make_async_copy(noise_ref, packed_ref.at[pl.ds(0, side_x)], noise_sem)
+    level_copy = pltpu.make_async_copy(level_ref, held_ref, level_sem)
+    noise_copy.start()
+    level_copy.start()
+    level_copy.wait()
+    levels = held_ref[...].astype(F32)
     damp_ref[...] = jnp.exp(-0.05 * (levels - MIDDLE))
-    packed_ref[:side_x] = noise_ref[...]
     share = jnp.sum(levels, axis=0, keepdims=True) * scale
     packed_ref[side_x:] = jnp.broadcast_to(share, (packed_ref.shape[0] - side_x, share.shape[1]))
+    noise_copy.wait()
 
 
 def residual_parts(before, here, after, damp, damp_next, noise_ref, x_refs, y_refs, out_ref):
@@ -181,7 +186,7 @@
     residual_parts(before, here, after, *damps, noise_ref, (xh_ref, xl_ref), (yh_ref, yl_ref), out_ref)
 
 
-def gather_kernel(*refs, outs, side_x):
+def gather_kernel(*refs, outs, side_x, base):
     weight_ref, keep_ref, send_ref = refs[0], refs[-2], refs[-1]
     field_refs = refs[1:-2]
     rows_in, side_y = field_refs[0].shape
@@ -191,9 +196,9 @@
     def body(index, carry):
         window = pl.ds(pl.multiple_of(index * rows, rows), rows)
         fields = [ref[window, :] for ref in field_refs]
-        for target, start, base in ((keep_ref, 0, 0), (send_ref, 2, outs * count)):
+        for target, start, begin in ((keep_ref, 0, base), (send_ref, 2, base + outs * count)):
             for part in range(outs):
-                place = base + part * (count - start) - start
+                place = begin + part * (count - start) - start
                 total = weight_ref[place + start] * fields[start]
                 for index_in in range(start + 1, count):
                     total = total + weight_ref[place + index_in] * fields[index_in]
@@ -207,11 +212,11 @@
         send_ref[side_x:, :] = sum(extra[2:])
 
 
-def finish_kernel(weight_ref, keep_ref, other_ref, last_ref, last_other_ref, *refs):
+def finish_kernel(weight_ref, base, keep_ref, other_ref, last_ref, last_other_ref, *refs):
     damp_ref, damp_next_ref, noise_ref, xh_ref, xl_ref, yh_ref, yl_ref = refs[:7]
     out_refs = refs[7:]
     sources = keep_ref, other_ref, last_ref, last_other_ref
-    slices = [joined(weight_ref, part, sources, slice(None)) for part in range(3)]
+    slices = [joined(weight_ref, base, part, sources, slice(None)) for part in range(3)]
     if len(out_refs) == 2:
         out_refs[1][...] = slices[1]
     damps = damp_ref[...], damp_next_ref[...]
@@ -343,31 +348,41 @@
     hop = ring_pairs(length)
     swap = [(i, i ^ 1) for i in range(length)]
 
-    def weights_of(rows_of):
-        tables = ring_weights(length, rows_of)
-        return [lax.dynamic_index_in_dim(jnp.asarray(table), position, 0, keepdims=False) for table in tables]
-
-    forward = weights_of(lambda device: basis[device : device + 1])
-    back = weights_of(lambda device: times_of(inverse, np.arange(device - 1, device + 2)))
-
-    def around(own, weights, outs):
+    tables = [
+        *ring_weights(length, lambda device: basis[device : device + 1]),
+        *ring_weights(length, lambda device: times_of(inverse, np.arange(device - 1, device + 2))),
+    ]
+    starts = np.cumsum([0] + [table.shape[1] for table in tables]).tolist()
+    forward, back = starts[:2], starts[2:4]
+    table = jnp.asarray(np.concatenate(tables, axis=1))
+    weights = lax.dynamic_index_in_dim(table, position, 0, keepdims=False)
+
+    def around(own, base, outs, beside):
         partner = lax.ppermute(own, "tm", swap)
         fields = [own, partner]
-        for _ in range(reach - 1):
+        for step in range(1, reach):
             own = lax.ppermute(own, "tm", hop)
             partner = lax.ppermute(partner, "tm", hop)
             fields += [own, partner]
+            if step == 1:
+                own, beside = lax.optimization_barrier((own, beside))
         last = lax.ppermute(own, "tm", hop)
 
         def kernel(*refs):
-            gather_kernel(*refs, outs=outs, side_x=side_x)
+            gather_kernel(*refs, outs=outs, side_x=side_x, base=base[0])
 
         wide = shape(own.shape[0], outs * side_y)
         adds = 4 * outs * len(fields) * side_x * side_y
-        keep, send = call(kernel, (wide, wide), len(fields), passes=adds, scalars=1)(weights[0], *fields)
+        keep, send = call(kernel, (wide, wide), len(fields), passes=adds, scalars=1)(beside[0], *fields)
         other = lax.ppermute(send, "tm", swap)
         last_other = lax.ppermute(last, "tm", swap)
-        return weights[1], keep, other, last, last_other
+        return (beside[0], keep, other, last, last_other), beside
+
+    def based(kernel, base):
+        def run(weight_ref, *refs):
+            kernel(weight_ref, base[1], *refs)
+
+        return run
 
     scratch = [pltpu.VMEM((16, side_y), F32)]
     work = 12 * ORDER * 2 * side_x * side_y * max(side_x, side_y)
@@ -375,19 +390,28 @@
     def pack(*refs):
         pack_kernel(*refs, scale=1.0 / (length * side_x * side_y))
 
-    packed, damp = call(pack, (shape(side_x + extra, side_y), field_shape), 2)(noise, phonon_level)
-    parts = around(packed, forward, 1)
-    parts, damp_late = lax.optimization_barrier((parts, damp))
-    damp_next = lax.ppermute(damp_late, "tm", [(i, (i - 1) % length) for i in range(length)])
+    packed, damp = pl.pallas_call(
+        pack,
+        out_shape=(shape(side_x + extra, side_y), field_shape),
+        in_specs=[pl.BlockSpec(memory_space=pltpu.HBM)] * 2,
+        out_specs=(VMEM, VMEM),
+        scratch_shapes=[pltpu.VMEM((side_x, side_y), jnp.int32), pltpu.SemaphoreType.DMA, pltpu.SemaphoreType.DMA],
+        compiler_params=pltpu.CompilerParams(vmem_limit_bytes=60 * 1024 * 1024),
+    )(noise, phonon_level)
+    parts, (weights, hops) = around(packed, forward, 1, (weights, hops))
+    damp_next = lax.ppermute(damp, "tm", [(i, (i - 1) % length) for i in range(length)])
+    first_kernel, next_kernel = based(first_spectral_kernel, forward), based(next_spectral_kernel, forward)
+    finish = based(finish_kernel, back)
     first_outs = (field_shape, shape(1, side_y))
-    first, mean_level = call(first_spectral_kernel, first_outs, 9, scratch, work, 1)(*parts, cosine, *hops)
+    first, mean_level = call(first_kernel, first_outs, 9, scratch, work, 1)(*parts, cosine, *hops)
     first, damp_next = lax.optimization_barrier((first, damp_next))
-    parts = around(first, back, 3)
-    (second_residual,) = call(finish_kernel, (field_shape,), 11, scalars=1)(*parts, damp, damp_next, noise, *hops)
-    parts = around(second_residual, forward, 1)
-    total = call(next_spectral_kernel, field_shape, 11, scratch, work, 1)(*parts, cosine, *hops, mean_level, first)
-    parts = around(total, back, 3)
-    residual, result = call(finish_kernel, (field_shape,) * 2, 11, scalars=1)(*parts, damp, damp_next, noise, *hops)
+    beside = (weights,)
+    parts, beside = around(first, back, 3, beside)
+    (second_residual,) = call(finish, (field_shape,), 11, scalars=1)(*parts, damp, damp_next, noise, *hops)
+    parts, beside = around(second_residual, forward, 1, beside)
+    total = call(next_kernel, field_shape, 11, scratch, work, 1)(*parts, cosine, *hops, mean_level, first)
+    parts, beside = around(total, back, 3, beside)
+    residual, result = call(finish, (field_shape,) * 2, 11, scalars=1)(*parts, damp, damp_next, noise, *hops)
     return result, residual
 
 

time: 146 us -> 145 us (level)
  local copies, waits for them, and re-layouts: 4.68 us -> 0.72 us
  waiting for transfers between devices: 93.9 us -> 96 us
    squeeze x4 -> x1, local copies, waits for them, and re-layouts: 2.77 us -> 0.7 us  [by_ring(): weights = lax.dynamic_index_in_dim(table, position, 0, keepdims=False)]
    unnamed x10, local copies, waits for them, and re-layouts: 1.91 us -> 0.02 us
    pallas_call x5, Pallas kernels: 19.2 us -> 21 us  [the longest x1 7.34 us: by_ring(): call(first_kernel, first_outs, 9, scratch, work, 1)(*parts, cosine, *hops)]
    ppermute x12, waiting for transfers between devices: 27 us -> 28.7 us  [around(): partner = lax.ppermute(partner, 'tm', hop)]
  transfers between devices with their start and end apart: 41 -> 41, of which waited for: 35 -> 34; matrix products, arithmetic and copies ran while one was open for 2% -> 0% of each run, Pallas kernels for 7% -> 7%
where the time goes in v4:
time: 145 us; the launch traced here: 144 us
  waiting for transfers between devices  96 us (66%)
  Pallas kernels  26 us (18%)
  starting transfers between devices  20.8 us (14%)
    ppermute x12, waiting for transfers between devices, around(): own = lax.ppermute(own, 'tm', hop)  40.8 us
    ppermute x12, waiting for transfers between devices, around(): partner = lax.ppermute(partner, 'tm', hop)  28.7 us
    ppermute x4, waiting for transfers between devices, around(): last = lax.ppermute(own, 'tm', hop)  17.7 us
    pallas_call x1, Pallas kernels, by_ring(): call(first_kernel, first_outs, 9, scratch, work, 1)(*parts, cosine, *hops)  7.34 us
    pallas_call x1, Pallas kernels, by_ring(): call(next_kernel, field_shape, 11, scratch, work, 1)  7.33 us
    ppermute x12, starting transfers between devices, around(): own = lax.ppermute(own, 'tm', hop)  6.91 us
    ppermute x1, starting transfers between devices, by_ring(): lax.ppermute(damp, 'tm', [(i, (i - 1) % length) for i in range(length)])  5.17 us
    ppermute x12, starting transfers between devices, around(): partner = lax.ppermute(partner, 'tm', hop)  5.12 us
  transfers between devices with their start and end apart: 41, of which 34 were waited for; matrix products, arithmetic and copies ran while one was open for 0% of the time, Pallas kernels for 7%

profile of v4, /device:TPU:0, one launch (start us, length us, event | category | flops | bytes accessed | tf_op | source)
XLA Modules:
  0.0 144.4 jit_solution(10373998758002875432)
XLA Ops:
  0.7 2.0 %shard_map.68 = (f32[264,256]{1,0:T(8,128)}, f32[256,256]{1,0:T(8,128)}) custom-call(f32[256,256]{1,0:T(8,128)} %bitcast.6, s32[256,256]{1,0:T(8,128)} %bitcast.9), custom_call_target="tpu_custom_call" | custom-call | tf_op jit(solution)/shard_map/pallas_call | solution.py:393
  3.2 2.6 %collective-permute-start = (f32[264,256]{1,0:T(8,128)}, f32[264,256]{1,0:T(8,128)S(1)}, u32[]{:S(2)}, u32[]{:S(2)}) collective-permute-start(f32[264,256]{1,0:T(8,128)} %get-tuple-element.34.refs_1_), channel_id=1, source_target_pairs={{0,4},{1,3},{4,8},{5,1},{8,12},{9,5},{12,14},{13,9},{14,10},{15,13... | collective-permute-start | bytes 811016 | tf_op jit(solution)/shard_map/ppermute | solution.py:364
  7.2 1.6 %collective-permute-start.2 = (f32[264,256]{1,0:T(8,128)S(1)}, f32[264,256]{1,0:T(8,128)S(1)}, u32[]{:S(2)}, u32[]{:S(2)}) collective-permute-start(f32[264,256]{1,0:T(8,128)S(1)} %collective-permute-done.1.refs_2_), channel_id=1, source_target_pairs={{0,4},{1,3},{4,8},{5,1},{8,12},{9,5},{12,14},{13,9},{14,10},{15,13... | collective-permute-start | bytes 811016 | tf_op jit(solution)/shard_map/ppermute | solution.py:365
  8.7 1.6 %collective-permute-done.refs_3_ = f32[264,256]{1,0:T(8,128)S(1)} collective-permute-done((f32[264,256]{1,0:T(8,128)}, f32[264,256]{1,0:T(8,128)S(1)}, u32[]{:S(2)}, u32[]{:S(2)}) %collective-permute-start) | collective-permute-done | bytes 270368 | tf_op jit(solution)/shard_map/ppermute | solution.py:364
  10.4 2.1 %collective-permute-start.3 = (f32[264,256]{1,0:T(8,128)S(1)}, f32[264,256]{1,0:T(8,128)S(1)}, u32[]{:S(2)}, u32[]{:S(2)}) collective-permute-start(f32[264,256]{1,0:T(8,128)S(1)} %collective-permute-done.refs_3_), channel_id=1, source_target_pairs={{0,4},{1,3},{4,8},{5,1},{8,12},{9,5},{12,14},{13,9},{14,10},{15,13... | collective-permute-start | bytes 811016 | tf_op jit(solution)/shard_map/ppermute | solution.py:364
  12.5 1.2 collective-permute-done.2.refs_4_
  13.6 1.7 %collective-permute-start.4 = (f32[264,256]{1,0:T(8,128)S(1)}, f32[264,256]{1,0:T(8,128)S(1)}, u32[]{:S(2)}, u32[]{:S(2)}) collective-permute-start(f32[264,256]{1,0:T(8,128)S(1)} %collective-permute-done.2.refs_4_), channel_id=1, source_target_pairs={{0,4},{1,3},{4,8},{5,1},{8,12},{9,5},{12,14},{13,9},{14,10},{15,13... | collective-permute-start | bytes 811016 | tf_op jit(solution)/shard_map/ppermute | solution.py:365
  15.4 1.5 %collective-permute-done.3.refs_5_ = f32[264,256]{1,0:T(8,128)S(1)} collective-permute-done((f32[264,256]{1,0:T(8,128)S(1)}, f32[264,256]{1,0:T(8,128)S(1)}, u32[]{:S(2)}, u32[]{:S(2)}) %collective-permute-start.3) | collective-permute-done | bytes 270368 | tf_op jit(solution)/shard_map/ppermute | solution.py:364
  16.9 2.1 %collective-permute-start.5 = (f32[264,256]{1,0:T(8,128)S(1)}, f32[264,256]{1,0:T(8,128)S(1)}, u32[]{:S(2)}, u32[]{:S(2)}) collective-permute-start(f32[264,256]{1,0:T(8,128)S(1)} %collective-permute-done.3.refs_5_), channel_id=1, source_target_pairs={{0,4},{1,3},{4,8},{5,1},{8,12},{9,5},{12,14},{13,9},{14,10},{15,13... | collective-permute-start | bytes 811016 | tf_op jit(solution)/shard_map/ppermute | solution.py:364
  20.1 1.7 %collective-permute-start.6 = (f32[264,256]{1,0:T(8,128)S(1)}, f32[264,256]{1,0:T(8,128)S(1)}, u32[]{:S(2)}, u32[]{:S(2)}) collective-permute-start(f32[264,256]{1,0:T(8,128)S(1)} %collective-permute-done.4.refs_6_), channel_id=1, source_target_pairs={{0,4},{1,3},{4,8},{5,1},{8,12},{9,5},{12,14},{13,9},{14,10},{15,13... | collective-permute-start | bytes 811016 | tf_op jit(solution)/shard_map/ppermute | solution.py:365
  21.8 1.5 %collective-permute-done.5.refs_7_ = f32[264,256]{1,0:T(8,128)S(1)} collective-permute-done((f32[264,256]{1,0:T(8,128)S(1)}, f32[264,256]{1,0:T(8,128)S(1)}, u32[]{:S(2)}, u32[]{:S(2)}) %collective-permute-start.5) | collective-permute-done | bytes 270368 | tf_op jit(solution)/shard_map/ppermute | solution.py:364
  23.3 2.1 %collective-permute-start.8 = (f32[264,256]{1,0:T(8,128)S(1)}, f32[264,256]{1,0:T(8,128)S(1)}, u32[]{:S(2)}, u32[]{:S(2)}) collective-permute-start(f32[264,256]{1,0:T(8,128)S(1)} %collective-permute-done.5.refs_7_), channel_id=1, source_target_pairs={{0,4},{1,3},{4,8},{5,1},{8,12},{9,5},{12,14},{13,9},{14,10},{15,13... | collective-permute-start | bytes 811016 | tf_op jit(solution)/shard_map/ppermute | solution.py:369
  25.4 1.2 collective-permute-done.6.refs_8_
  27.5 2.3 %collective-permute-done.8.refs_2_ = f32[264,256]{1,0:T(8,128)S(1)} collective-permute-done((f32[264,256]{1,0:T(8,128)S(1)}, f32[264,256]{1,0:T(8,128)S(1)}, u32[]{:S(2)}, u32[]{:S(2)}) %collective-permute-start.8) | collective-permute-done | bytes 270368 | tf_op jit(solution)/shard_map/ppermute | solution.py:369
  29.8 5.2 %collective-permute-start.10 = (f32[256,256]{1,0:T(8,128)S(1)}, f32[256,256]{1,0:T(8,128)S(1)}, u32[]{:S(2)}, u32[]{:S(2)}) collective-permute-start(f32[256,256]{1,0:T(8,128)S(1)} %copy-done.1), channel_id=1, source_target_pairs={{0,15},{1,0},{2,1},{3,2},{4,3},{5,4},{6,5},{7,6},{8,7},{9,8},{10,9... | collective-permute-start | bytes 786440 | tf_op jit(solution)/shard_map/ppermute | solution.py:402
  35.1 7.3 %shard_map.71 = (f32[256,256]{1,0:T(8,128)S(1)}, f32[1,256]{1,0:T(1,128)S(1)}) custom-call(f32[64]{0:T(128)S(1)} %dynamic-slice_bitcast_fusion.refs_0_.weight_ref, f32[264,256]{1,0:T(8,128)S(1)} %get-tuple-element.41.refs_0_, f32[264,256]{1,0:T(8,128)S(1)} %collective-permute-done.7.refs_1_, f32[264,256]{1,0:T(8,128)S(1)} %collective-permute-done.8.refs_2_, ...), custom_call_target="tpu_custom_call" | custom-call | flops 4026531840 | tf_op jit(solution)/shard_map/pallas_call | solution.py:406
  42.6 1.5 %collective-permute-done.12.refs_2_ = f32[256,256]{1,0:T(8,128)S(1)} collective-permute-done((f32[256,256]{1,0:T(8,128)S(1)}, f32[256,256]{1,0:T(8,128)S(1)}, u32[]{:S(2)}, u32[]{:S(2)}) %collective-permute-start.12) | collective-permute-done | bytes 262176 | tf_op jit(solution)/shard_map/ppermute | solution.py:361
  44.0 4.9 %collective-permute-done.11.refs_3_ = f32[256,256]{1,0:T(8,128)S(1)} collective-permute-done((f32[256,256]{1,0:T(8,128)S(1)}, f32[256,256]{1,0:T(8,128)S(1)}, u32[]{:S(2)}, u32[]{:S(2)}) %collective-permute-start.11) | collective-permute-done | bytes 262176 | tf_op jit(solution)/shard_map/ppermute | solution.py:364
  49.0 2.8 %collective-permute-done.13.refs_4_ = f32[256,256]{1,0:T(8,128)S(1)} collective-permute-done((f32[256,256]{1,0:T(8,128)S(1)}, f32[256,256]{1,0:T(8,128)S(1)}, u32[]{:S(2)}, u32[]{:S(2)}) %collective-permute-start.13) | collective-permute-done | bytes 262176 | tf_op jit(solution)/shard_map/ppermute | solution.py:365
  51.8 3.6 %collective-permute-done.14.refs_5_ = f32[256,256]{1,0:T(8,128)S(1)} collective-permute-done((f32[256,256]{1,0:T(8,128)S(1)}, f32[256,256]{1,0:T(8,128)S(1)}, u32[]{:S(2)}, u32[]{:S(2)}) %collective-permute-start.14) | collective-permute-done | bytes 262176 | tf_op jit(solution)/shard_map/ppermute | solution.py:364
  55.3 2.8 %collective-permute-done.15.refs_6_ = f32[256,256]{1,0:T(8,128)S(1)} collective-permute-done((f32[256,256]{1,0:T(8,128)S(1)}, f32[256,256]{1,0:T(8,128)S(1)}, u32[]{:S(2)}, u32[]{:S(2)}) %collective-permute-start.15) | collective-permute-done | bytes 262176 | tf_op jit(solution)/shard_map/ppermute | solution.py:365
  58.1 3.6 %collective-permute-done.16.refs_7_ = f32[256,256]{1,0:T(8,128)S(1)} collective-permute-done((f32[256,256]{1,0:T(8,128)S(1)}, f32[256,256]{1,0:T(8,128)S(1)}, u32[]{:S(2)}, u32[]{:S(2)}) %collective-permute-start.16) | collective-permute-done | bytes 262176 | tf_op jit(solution)/shard_map/ppermute | solution.py:364
  61.7 2.8 %collective-permute-done.17.refs_8_ = f32[256,256]{1,0:T(8,128)S(1)} collective-permute-done((f32[256,256]{1,0:T(8,128)S(1)}, f32[256,256]{1,0:T(8,128)S(1)}, u32[]{:S(2)}, u32[]{:S(2)}) %collective-permute-start.17) | collective-permute-done | bytes 262176 | tf_op jit(solution)/shard_map/ppermute | solution.py:365
  64.5 1.3 shard_map.72
  66.0 6.4 %collective-permute-done.19.refs_2_ = f32[256,256]{1,0:T(8,128)S(1)} collective-permute-done((f32[256,256]{1,0:T(8,128)S(1)}, f32[256,256]{1,0:T(8,128)S(1)}, u32[]{:S(2)}, u32[]{:S(2)}) %collective-permute-start.19) | collective-permute-done | bytes 262176 | tf_op jit(solution)/shard_map/ppermute | solution.py:369
  72.4 1.5 %collective-permute-done.20.refs_3_ = f32[256,256]{1,0:T(8,128)S(1)} collective-permute-done((f32[256,256]{1,0:T(8,128)S(1)}, f32[256,256]{1,0:T(8,128)S(1)}, u32[]{:S(2)}, u32[]{:S(2)}) %collective-permute-start.20) | collective-permute-done | bytes 262176 | tf_op jit(solution)/shard_map/ppermute | solution.py:378
  73.9 1.8 %shard_map.73.refs_1_ = f32[256,256]{1,0:T(8,128)S(1)} custom-call(f32[64]{0:T(128)S(1)} %dynamic-slice_bitcast_fusion.refs_0_.weight_ref, f32[256,768]{1,0:T(8,128)S(1)} %get-tuple-element.52.refs_0_, f32[256,768]{1,0:T(8,128)S(1)} %collective-permute-done.18.refs_1_, f32[256,256]{1,0:T(8,128)S(1)} %collective-permute-done.19.refs_2_, ...), custom_call_target="tpu_custom_call" | custom-call | tf_op jit(solution)/shard_map/pallas_call | solution.py:410
  75.9 1.4 collective-permute-done.22.refs_2_
  77.3 5.0 %collective-permute-done.21.refs_3_ = f32[256,256]{1,0:T(8,128)S(1)} collective-permute-done((f32[256,256]{1,0:T(8,128)S(1)}, f32[256,256]{1,0:T(8,128)S(1)}, u32[]{:S(2)}, u32[]{:S(2)}) %collective-permute-start.21) | collective-permute-done | bytes 262176 | tf_op jit(solution)/shard_map/ppermute | solution.py:364
  82.3 2.8 %collective-permute-done.23.refs_4_ = f32[256,256]{1,0:T(8,128)S(1)} collective-permute-done((f32[256,256]{1,0:T(8,128)S(1)}, f32[256,256]{1,0:T(8,128)S(1)}, u32[]{:S(2)}, u32[]{:S(2)}) %collective-permute-start.23) | collective-permute-done | bytes 262176 | tf_op jit(solution)/shard_map/ppermute | solution.py:365
  85.1 3.6 %collective-permute-done.24.refs_5_ = f32[256,256]{1,0:T(8,128)S(1)} collective-permute-done((f32[256,256]{1,0:T(8,128)S(1)}, f32[256,256]{1,0:T(8,128)S(1)}, u32[]{:S(2)}, u32[]{:S(2)}) %collective-permute-start.24) | collective-permute-done | bytes 262176 | tf_op jit(solution)/shard_map/ppermute | solution.py:364
  88.7 2.8 %collective-permute-done.25.refs_6_ = f32[256,256]{1,0:T(8,128)S(1)} collective-permute-done((f32[256,256]{1,0:T(8,128)S(1)}, f32[256,256]{1,0:T(8,128)S(1)}, u32[]{:S(2)}, u32[]{:S(2)}) %collective-permute-start.25) | collective-permute-done | bytes 262176 | tf_op jit(solution)/shard_map/ppermute | solution.py:365
  91.5 3.6 %collective-permute-done.26.refs_7_ = f32[256,256]{1,0:T(8,128)S(1)} collective-permute-done((f32[256,256]{1,0:T(8,128)S(1)}, f32[256,256]{1,0:T(8,128)S(1)}, u32[]{:S(2)}, u32[]{:S(2)}) %collective-permute-start.26) | collective-permute-done | bytes 262176 | tf_op jit(solution)/shard_map/ppermute | solution.py:364
  95.1 2.8 %collective-permute-done.27.refs_8_ = f32[256,256]{1,0:T(8,128)S(1)} collective-permute-done((f32[256,256]{1,0:T(8,128)S(1)}, f32[256,256]{1,0:T(8,128)S(1)}, u32[]{:S(2)}, u32[]{:S(2)}) %collective-permute-start.27) | collective-permute-done | bytes 262176 | tf_op jit(solution)/shard_map/ppermute | solution.py:365
  98.8 2.7 %collective-permute-done.29.refs_2_ = f32[256,256]{1,0:T(8,128)S(1)} collective-permute-done((f32[256,256]{1,0:T(8,128)S(1)}, f32[256,256]{1,0:T(8,128)S(1)}, u32[]{:S(2)}, u32[]{:S(2)}) %collective-permute-start.29) | collective-permute-done | bytes 262176 | tf_op jit(solution)/shard_map/ppermute | solution.py:369
  101.4 1.5 %collective-permute-done.30.refs_3_ = f32[256,256]{1,0:T(8,128)S(1)} collective-permute-done((f32[256,256]{1,0:T(8,128)S(1)}, f32[256,256]{1,0:T(8,128)S(1)}, u32[]{:S(2)}, u32[]{:S(2)}) %collective-permute-start.30) | collective-permute-done | bytes 262176 | tf_op jit(solution)/shard_map/ppermute | solution.py:378
  103.0 7.3 %shard_map.75.refs_1_ = f32[256,256]{1,0:T(8,128)S(1)} custom-call(f32[64]{0:T(128)S(1)} %dynamic-slice_bitcast_fusion.refs_0_.weight_ref, f32[256,256]{1,0:T(8,128)S(1)} %get-tuple-element.57.refs_0_, f32[256,256]{1,0:T(8,128)S(1)} %collective-permute-done.28.refs_1_, f32[256,256]{1,0:T(8,128)S(1)} %collective-permute-done.29.refs_2_, ...), custom_call_target="tpu_custom_call" | custom-call | flops 4026531840 | tf_op jit(solution)/shard_map/pallas_call | solution.py:412
  110.5 1.4 collective-permute-done.32.refs_2_
  111.9 5.0 %collective-permute-done.31.refs_3_ = f32[256,256]{1,0:T(8,128)S(1)} collective-permute-done((f32[256,256]{1,0:T(8,128)S(1)}, f32[256,256]{1,0:T(8,128)S(1)}, u32[]{:S(2)}, u32[]{:S(2)}) %collective-permute-start.31) | collective-permute-done | bytes 262176 | tf_op jit(solution)/shard_map/ppermute | solution.py:364
  116.9 2.8 %collective-permute-done.33.refs_4_ = f32[256,256]{1,0:T(8,128)S(1)} collective-permute-done((f32[256,256]{1,0:T(8,128)S(1)}, f32[256,256]{1,0:T(8,128)S(1)}, u32[]{:S(2)}, u32[]{:S(2)}) %collective-permute-start.33) | collective-permute-done | bytes 262176 | tf_op jit(solution)/shard_map/ppermute | solution.py:365
  119.7 3.6 %collective-permute-done.34.refs_5_ = f32[256,256]{1,0:T(8,128)S(1)} collective-permute-done((f32[256,256]{1,0:T(8,128)S(1)}, f32[256,256]{1,0:T(8,128)S(1)}, u32[]{:S(2)}, u32[]{:S(2)}) %collective-permute-start.34) | collective-permute-done | bytes 262176 | tf_op jit(solution)/shard_map/ppermute | solution.py:364
  123.3 2.8 %collective-permute-done.35.refs_6_ = f32[256,256]{1,0:T(8,128)S(1)} collective-permute-done((f32[256,256]{1,0:T(8,128)S(1)}, f32[256,256]{1,0:T(8,128)S(1)}, u32[]{:S(2)}, u32[]{:S(2)}) %collective-permute-start.35) | collective-permute-done | bytes 262176 | tf_op jit(solution)/shard_map/ppermute | solution.py:365
  126.1 3.6 %collective-permute-done.36.refs_7_ = f32[256,256]{1,0:T(8,128)S(1)} collective-permute-done((f32[256,256]{1,0:T(8,128)S(1)}, f32[256,256]{1,0:T(8,128)S(1)}, u32[]{:S(2)}, u32[]{:S(2)}) %collective-permute-start.36) | collective-permute-done | bytes 262176 | tf_op jit(solution)/shard_map/ppermute | solution.py:364
  129.6 2.8 %collective-permute-done.37.refs_8_ = f32[256,256]{1,0:T(8,128)S(1)} collective-permute-done((f32[256,256]{1,0:T(8,128)S(1)}, f32[256,256]{1,0:T(8,128)S(1)}, u32[]{:S(2)}, u32[]{:S(2)}) %collective-permute-start.37) | collective-permute-done | bytes 262176 | tf_op jit(solution)/shard_map/ppermute | solution.py:365
  132.4 1.3 shard_map.76
  133.9 6.4 %collective-permute-done.39.refs_2_ = f32[256,256]{1,0:T(8,128)S(1)} collective-permute-done((f32[256,256]{1,0:T(8,128)S(1)}, f32[256,256]{1,0:T(8,128)S(1)}, u32[]{:S(2)}, u32[]{:S(2)}) %collective-permute-start.39) | collective-permute-done | bytes 262176 | tf_op jit(solution)/shard_map/ppermute | solution.py:369
  140.3 1.5 %collective-permute-done.40.refs_3_ = f32[256,256]{1,0:T(8,128)S(1)} collective-permute-done((f32[256,256]{1,0:T(8,128)S(1)}, f32[256,256]{1,0:T(8,128)S(1)}, u32[]{:S(2)}, u32[]{:S(2)}) %collective-permute-start.40) | collective-permute-done | bytes 262176 | tf_op jit(solution)/shard_map/ppermute | solution.py:378
  141.8 2.5 %shard_map.77 = (f32[256,256]{1,0:T(8,128)}, f32[256,256]{1,0:T(8,128)}) custom-call(f32[64]{0:T(128)S(1)} %dynamic-slice_bitcast_fusion.refs_0_.weight_ref, f32[256,768]{1,0:T(8,128)S(1)} %get-tuple-element.62.refs_0_, f32[256,768]{1,0:T(8,128)S(1)} %collective-permute-done.38.refs_1_, f32[256,256]{1,0:T(8,128)S(1)} %collective-permute-done.39.refs_2_, ...), custom_call_target="tpu_custom_call" | custom-call | tf_op jit(solution)/shard_map/pallas_call | solution.py:414
  (56 shorter events, 5.9 us)
Async XLA Ops:
  0.6 5.2 %copy-start.3 = (f32[256,256]{1,0:T(8,128)S(1)}, f32[256,256]{1,0:T(8,128)}, u32[]{:S(2)}) copy-start(f32[256,256]{1,0:T(8,128)} %hop_x_ref.1) | copy-start | bytes 786436
  0.6 5.2 %copy-start.4 = (f32[256,256]{1,0:T(8,128)S(1)}, f32[256,256]{1,0:T(8,128)}, u32[]{:S(2)}) copy-start(f32[256,256]{1,0:T(8,128)} %hop_y_ref.1) | copy-start | bytes 786436
  2.6 4.6 %collective-permute-start.1 = (f32[264,256]{1,0:T(8,128)}, f32[264,256]{1,0:T(8,128)S(1)}, u32[]{:S(2)}, u32[]{:S(2)}) collective-permute-start(f32[264,256]{1,0:T(8,128)} %get-tuple-element.34.refs_1_), channel_id=1, source_target_pairs={{0,1},{1,0},{2,3},{3,2},{4,5},{5,4},{6,7},{7,6},{8,9},{9,8},{10,11... | collective-permute-start | bytes 811016 | tf_op jit(solution)/shard_map/ppermute | solution.py:361
  3.2 7.2 %collective-permute-start = (f32[264,256]{1,0:T(8,128)}, f32[264,256]{1,0:T(8,128)S(1)}, u32[]{:S(2)}, u32[]{:S(2)}) collective-permute-start(f32[264,256]{1,0:T(8,128)} %get-tuple-element.34.refs_1_), channel_id=1, source_target_pairs={{0,4},{1,3},{4,8},{5,1},{8,12},{9,5},{12,14},{13,9},{14,10},{15,13... | collective-permute-start | bytes 811016 | tf_op jit(solution)/shard_map/ppermute | solution.py:364
  5.8 20.8 %copy-start.2 = (f32[264,256]{1,0:T(8,128)S(1)}, f32[264,256]{1,0:T(8,128)}, u32[]{:S(2)}) copy-start(f32[264,256]{1,0:T(8,128)} %get-tuple-element.34.refs_1_) | copy-start | bytes 811012
  7.2 6.5 %collective-permute-start.2 = (f32[264,256]{1,0:T(8,128)S(1)}, f32[264,256]{1,0:T(8,128)S(1)}, u32[]{:S(2)}, u32[]{:S(2)}) collective-permute-start(f32[264,256]{1,0:T(8,128)S(1)} %collective-permute-done.1.refs_2_), channel_id=1, source_target_pairs={{0,4},{1,3},{4,8},{5,1},{8,12},{9,5},{12,14},{13,9},{14,10},{15,13... | collective-permute-start | bytes 811016 | tf_op jit(solution)/shard_map/ppermute | solution.py:365
  10.4 19.4 %copy-start.1 = (f32[256,256]{1,0:T(8,128)S(1)}, f32[256,256]{1,0:T(8,128)}, u32[]{:S(2)}) copy-start(f32[256,256]{1,0:T(8,128)} %get-tuple-element.48.refs_4_) | copy-start | bytes 786436
  10.4 6.5 %collective-permute-start.3 = (f32[264,256]{1,0:T(8,128)S(1)}, f32[264,256]{1,0:T(8,128)S(1)}, u32[]{:S(2)}, u32[]{:S(2)}) collective-permute-start(f32[264,256]{1,0:T(8,128)S(1)} %collective-permute-done.refs_3_), channel_id=1, source_target_pairs={{0,4},{1,3},{4,8},{5,1},{8,12},{9,5},{12,14},{13,9},{14,10},{15,13... | collective-permute-start | bytes 811016 | tf_op jit(solution)/shard_map/ppermute | solution.py:364
  13.6 6.5 %collective-permute-start.4 = (f32[264,256]{1,0:T(8,128)S(1)}, f32[264,256]{1,0:T(8,128)S(1)}, u32[]{:S(2)}, u32[]{:S(2)}) collective-permute-start(f32[264,256]{1,0:T(8,128)S(1)} %collective-permute-done.2.refs_4_), channel_id=1, source_target_pairs={{0,4},{1,3},{4,8},{5,1},{8,12},{9,5},{12,14},{13,9},{14,10},{15,13... | collective-permute-start | bytes 811016 | tf_op jit(solution)/shard_map/ppermute | solution.py:365
  16.9 6.5 %collective-permute-start.5 = (f32[264,256]{1,0:T(8,128)S(1)}, f32[264,256]{1,0:T(8,128)S(1)}, u32[]{:S(2)}, u32[]{:S(2)}) collective-permute-start(f32[264,256]{1,0:T(8,128)S(1)} %collective-permute-done.3.refs_5_), channel_id=1, source_target_pairs={{0,4},{1,3},{4,8},{5,1},{8,12},{9,5},{12,14},{13,9},{14,10},{15,13... | collective-permute-start | bytes 811016 | tf_op jit(solution)/shard_map/ppermute | solution.py:364
  20.1 6.5 %collective-permute-start.6 = (f32[264,256]{1,0:T(8,128)S(1)}, f32[264,256]{1,0:T(8,128)S(1)}, u32[]{:S(2)}, u32[]{:S(2)}) collective-permute-start(f32[264,256]{1,0:T(8,128)S(1)} %collective-permute-done.4.refs_6_), channel_id=1, source_target_pairs={{0,4},{1,3},{4,8},{5,1},{8,12},{9,5},{12,14},{13,9},{14,10},{15,13... | collective-permute-start | bytes 811016 | tf_op jit(solution)/shard_map/ppermute | solution.py:365
  23.3 6.5 %collective-permute-start.8 = (f32[264,256]{1,0:T(8,128)S(1)}, f32[264,256]{1,0:T(8,128)S(1)}, u32[]{:S(2)}, u32[]{:S(2)}) collective-permute-start(f32[264,256]{1,0:T(8,128)S(1)} %collective-permute-done.5.refs_7_), channel_id=1, source_target_pairs={{0,4},{1,3},{4,8},{5,1},{8,12},{9,5},{12,14},{13,9},{14,10},{15,13... | collective-permute-start | bytes 811016 | tf_op jit(solution)/shard_map/ppermute | solution.py:369
  27.4 7.6 %collective-permute-start.7 = (f32[264,256]{1,0:T(8,128)S(1)}, f32[264,256]{1,0:T(8,128)S(1)}, u32[]{:S(2)}, u32[]{:S(2)}) collective-permute-start(f32[264,256]{1,0:T(8,128)S(1)} %get-tuple-element.42), channel_id=1, source_target_pairs={{0,1},{1,0},{2,3},{3,2},{4,5},{5,4},{6,7},{7,6},{8,9},{9,8},{10,11... | collective-permute-start | bytes 811016 | tf_op jit(solution)/shard_map/ppermute | solution.py:377
  29.8 5.3 %collective-permute-start.9 = (f32[264,256]{1,0:T(8,128)S(1)}, f32[264,256]{1,0:T(8,128)S(1)}, u32[]{:S(2)}, u32[]{:S(2)}) collective-permute-start(f32[264,256]{1,0:T(8,128)S(1)} %collective-permute-done.8.refs_2_), channel_id=1, source_target_pairs={{0,1},{1,0},{2,3},{3,2},{4,5},{5,4},{6,7},{7,6},{8,9},{9,8},{10,11... | collective-permute-start | bytes 811016 | tf_op jit(solution)/shard_map/ppermute | solution.py:378
  29.8 12.6 %collective-permute-start.10 = (f32[256,256]{1,0:T(8,128)S(1)}, f32[256,256]{1,0:T(8,128)S(1)}, u32[]{:S(2)}, u32[]{:S(2)}) collective-permute-start(f32[256,256]{1,0:T(8,128)S(1)} %copy-done.1), channel_id=1, source_target_pairs={{0,15},{1,0},{2,1},{3,2},{4,3},{5,4},{6,5},{7,6},{8,7},{9,8},{10,9... | collective-permute-start | bytes 786440 | tf_op jit(solution)/shard_map/ppermute | solution.py:402
  42.4 31.5 %copy-start = (f32[1,256,256]{2,1,0:T(8,128)S(1)}, f32[1,256,256]{2,1,0:T(8,128)}, u32[]{:S(2)}) copy-start(f32[1,256,256]{2,1,0:T(8,128)} %param.5) | copy-start | bytes 786436
  42.4 1.6 %collective-permute-start.12 = (f32[256,256]{1,0:T(8,128)S(1)}, f32[256,256]{1,0:T(8,128)S(1)}, u32[]{:S(2)}, u32[]{:S(2)}) collective-permute-start(f32[256,256]{1,0:T(8,128)S(1)} %get-tuple-element.49.refs_1_.refs_10_), channel_id=1, source_target_pairs={{0,1},{1,0},{2,3},{3,2},{4,5},{5,4},{6,7},{7,6},{8,9},{9,8},{10,11... | collective-permute-start | bytes 786440 | tf_op jit(solution)/shard_map/ppermute | solution.py:361
  42.5 6.4 %collective-permute-start.11 = (f32[256,256]{1,0:T(8,128)S(1)}, f32[256,256]{1,0:T(8,128)S(1)}, u32[]{:S(2)}, u32[]{:S(2)}) collective-permute-start(f32[256,256]{1,0:T(8,128)S(1)} %get-tuple-element.49.refs_1_.refs_10_), channel_id=1, source_target_pairs={{0,4},{1,3},{4,8},{5,1},{8,12},{9,5},{12,14},{13,9},{14,10},{15,13... | collective-permute-start | bytes 786440 | tf_op jit(solution)/shard_map/ppermute | solution.py:364
  44.0 7.7 %collective-permute-start.13 = (f32[256,256]{1,0:T(8,128)S(1)}, f32[256,256]{1,0:T(8,128)S(1)}, u32[]{:S(2)}, u32[]{:S(2)}) collective-permute-start(f32[256,256]{1,0:T(8,128)S(1)} %collective-permute-done.12.refs_2_), channel_id=1, source_target_pairs={{0,4},{1,3},{4,8},{5,1},{8,12},{9,5},{12,14},{13,9},{14,10},{15,13... | collective-permute-start | bytes 786440 | tf_op jit(solution)/shard_map/ppermute | solution.py:365
  48.9 6.4 %collective-permute-start.14 = (f32[256,256]{1,0:T(8,128)S(1)}, f32[256,256]{1,0:T(8,128)S(1)}, u32[]{:S(2)}, u32[]{:S(2)}) collective-permute-start(f32[256,256]{1,0:T(8,128)S(1)} %collective-permute-done.11.refs_3_), channel_id=1, source_target_pairs={{0,4},{1,3},{4,8},{5,1},{8,12},{9,5},{12,14},{13,9},{14,10},{15,13... | collective-permute-start | bytes 786440 | tf_op jit(solution)/shard_map/ppermute | solution.py:364
  51.8 6.4 %collective-permute-start.15 = (f32[256,256]{1,0:T(8,128)S(1)}, f32[256,256]{1,0:T(8,128)S(1)}, u32[]{:S(2)}, u32[]{:S(2)}) collective-permute-start(f32[256,256]{1,0:T(8,128)S(1)} %collective-permute-done.13.refs_4_), channel_id=1, source_target_pairs={{0,4},{1,3},{4,8},{5,1},{8,12},{9,5},{12,14},{13,9},{14,10},{15,13... | collective-permute-start | bytes 786440 | tf_op jit(solution)/shard_map/ppermute | solution.py:365
  55.3 6.4 %collective-permute-start.16 = (f32[256,256]{1,0:T(8,128)S(1)}, f32[256,256]{1,0:T(8,128)S(1)}, u32[]{:S(2)}, u32[]{:S(2)}) collective-permute-start(f32[256,256]{1,0:T(8,128)S(1)} %collective-permute-done.14.refs_5_), channel_id=1, source_target_pairs={{0,4},{1,3},{4,8},{5,1},{8,12},{9,5},{12,14},{13,9},{14,10},{15,13... | collective-permute-start | bytes 786440 | tf_op jit(solution)/shard_map/ppermute | solution.py:364
  58.1 6.4 %collective-permute-start.17 = (f32[256,256]{1,0:T(8,128)S(1)}, f32[256,256]{1,0:T(8,128)S(1)}, u32[]{:S(2)}, u32[]{:S(2)}) collective-permute-start(f32[256,256]{1,0:T(8,128)S(1)} %collective-permute-done.15.refs_6_), channel_id=1, source_target_pairs={{0,4},{1,3},{4,8},{5,1},{8,12},{9,5},{12,14},{13,9},{14,10},{15,13... | collective-permute-start | bytes 786440 | tf_op jit(solution)/shard_map/ppermute | solution.py:365
  65.8 8.0 %collective-permute-start.18 = (f32[256,768]{1,0:T(8,128)S(1)}, f32[256,768]{1,0:T(8,128)S(1)}, u32[]{:S(2)}, u32[]{:S(2)}) collective-permute-start(f32[256,768]{1,0:T(8,128)S(1)} %get-tuple-element.53), channel_id=1, source_target_pairs={{0,1},{1,0},{2,3},{3,2},{4,5},{5,4},{6,7},{7,6},{8,9},{9,8},{10,11... | collective-permute-start | bytes 2359304 | tf_op jit(solution)/shard_map/ppermute | solution.py:377
  65.9 6.4 %collective-permute-start.19 = (f32[256,256]{1,0:T(8,128)S(1)}, f32[256,256]{1,0:T(8,128)S(1)}, u32[]{:S(2)}, u32[]{:S(2)}) collective-permute-start(f32[256,256]{1,0:T(8,128)S(1)} %collective-permute-done.16.refs_7_), channel_id=1, source_target_pairs={{0,4},{1,3},{4,8},{5,1},{8,12},{9,5},{12,14},{13,9},{14,10},{15,13... | collective-permute-start | bytes 786440 | tf_op jit(solution)/shard_map/ppermute | solution.py:369
  72.4 1.5 %collective-permute-start.20 = (f32[256,256]{1,0:T(8,128)S(1)}, f32[256,256]{1,0:T(8,128)S(1)}, u32[]{:S(2)}, u32[]{:S(2)}) collective-permute-start(f32[256,256]{1,0:T(8,128)S(1)} %collective-permute-done.19.refs_2_), channel_id=1, source_target_pairs={{0,1},{1,0},{2,3},{3,2},{4,5},{5,4},{6,7},{7,6},{8,9},{9,8},{10,11... | collective-permute-start | bytes 786440 | tf_op jit(solution)/shard_map/ppermute | solution.py:378
  75.7 1.6 %collective-permute-start.22 = (f32[256,256]{1,0:T(8,128)S(1)}, f32[256,256]{1,0:T(8,128)S(1)}, u32[]{:S(2)}, u32[]{:S(2)}) collective-permute-start(f32[256,256]{1,0:T(8,128)S(1)} %shard_map.73.refs_1_), channel_id=1, source_target_pairs={{0,1},{1,0},{2,3},{3,2},{4,5},{5,4},{6,7},{7,6},{8,9},{9,8},{10,11... | collective-permute-start | bytes 786440 | tf_op jit(solution)/shard_map/ppermute | solution.py:361
  75.9 6.4 %collective-permute-start.21 = (f32[256,256]{1,0:T(8,128)S(1)}, f32[256,256]{1,0:T(8,128)S(1)}, u32[]{:S(2)}, u32[]{:S(2)}) collective-permute-start(f32[256,256]{1,0:T(8,128)S(1)} %shard_map.73.refs_1_), channel_id=1, source_target_pairs={{0,4},{1,3},{4,8},{5,1},{8,12},{9,5},{12,14},{13,9},{14,10},{15,13... | collective-permute-start | bytes 786440 | tf_op jit(solution)/shard_map/ppermute | solution.py:364
  77.3 7.8 %collective-permute-start.23 = (f32[256,256]{1,0:T(8,128)S(1)}, f32[256,256]{1,0:T(8,128)S(1)}, u32[]{:S(2)}, u32[]{:S(2)}) collective-permute-start(f32[256,256]{1,0:T(8,128)S(1)} %collective-permute-done.22.refs_2_), channel_id=1, source_target_pairs={{0,4},{1,3},{4,8},{5,1},{8,12},{9,5},{12,14},{13,9},{14,10},{15,13... | collective-permute-start | bytes 786440 | tf_op jit(solution)/shard_map/ppermute | solution.py:365
  82.3 6.4 %collective-permute-start.24 = (f32[256,256]{1,0:T(8,128)S(1)}, f32[256,256]{1,0:T(8,128)S(1)}, u32[]{:S(2)}, u32[]{:S(2)}) collective-permute-start(f32[256,256]{1,0:T(8,128)S(1)} %collective-permute-done.21.refs_3_), channel_id=1, source_target_pairs={{0,4},{1,3},{4,8},{5,1},{8,12},{9,5},{12,14},{13,9},{14,10},{15,13... | collective-permute-start | bytes 786440 | tf_op jit(solution)/shard_map/ppermute | solution.py:364
  85.1 6.4 %collective-permute-start.25 = (f32[256,256]{1,0:T(8,128)S(1)}, f32[256,256]{1,0:T(8,128)S(1)}, u32[]{:S(2)}, u32[]{:S(2)}) collective-permute-start(f32[256,256]{1,0:T(8,128)S(1)} %collective-permute-done.23.refs_4_), channel_id=1, source_target_pairs={{0,4},{1,3},{4,8},{5,1},{8,12},{9,5},{12,14},{13,9},{14,10},{15,13... | collective-permute-start | bytes 786440 | tf_op jit(solution)/shard_map/ppermute | solution.py:365
  88.7 6.4 %collective-permute-start.26 = (f32[256,256]{1,0:T(8,128)S(1)}, f32[256,256]{1,0:T(8,128)S(1)}, u32[]{:S(2)}, u32[]{:S(2)}) collective-permute-start(f32[256,256]{1,0:T(8,128)S(1)} %collective-permute-done.24.refs_5_), channel_id=1, source_target_pairs={{0,4},{1,3},{4,8},{5,1},{8,12},{9,5},{12,14},{13,9},{14,10},{15,13... | collective-permute-start | bytes 786440 | tf_op jit(solution)/shard_map/ppermute | solution.py:364
  91.5 6.4 %collective-permute-start.27 = (f32[256,256]{1,0:T(8,128)S(1)}, f32[256,256]{1,0:T(8,128)S(1)}, u32[]{:S(2)}, u32[]{:S(2)}) collective-permute-start(f32[256,256]{1,0:T(8,128)S(1)} %collective-permute-done.25.refs_6_), channel_id=1, source_target_pairs={{0,4},{1,3},{4,8},{5,1},{8,12},{9,5},{12,14},{13,9},{14,10},{15,13... | collective-permute-start | bytes 786440 | tf_op jit(solution)/shard_map/ppermute | solution.py:365
  95.0 6.4 %collective-permute-start.29 = (f32[256,256]{1,0:T(8,128)S(1)}, f32[256,256]{1,0:T(8,128)S(1)}, u32[]{:S(2)}, u32[]{:S(2)}) collective-permute-start(f32[256,256]{1,0:T(8,128)S(1)} %collective-permute-done.26.refs_7_), channel_id=1, source_target_pairs={{0,4},{1,3},{4,8},{5,1},{8,12},{9,5},{12,14},{13,9},{14,10},{15,13... | collective-permute-start | bytes 786440 | tf_op jit(solution)/shard_map/ppermute | solution.py:369
  98.7 2.8 %collective-permute-start.28 = (f32[256,256]{1,0:T(8,128)S(1)}, f32[256,256]{1,0:T(8,128)S(1)}, u32[]{:S(2)}, u32[]{:S(2)}) collective-permute-start(f32[256,256]{1,0:T(8,128)S(1)} %get-tuple-element.58), channel_id=1, source_target_pairs={{0,1},{1,0},{2,3},{3,2},{4,5},{5,4},{6,7},{7,6},{8,9},{9,8},{10,11... | collective-permute-start | bytes 786440 | tf_op jit(solution)/shard_map/ppermute | solution.py:377
  101.4 1.5 %collective-permute-start.30 = (f32[256,256]{1,0:T(8,128)S(1)}, f32[256,256]{1,0:T(8,128)S(1)}, u32[]{:S(2)}, u32[]{:S(2)}) collective-permute-start(f32[256,256]{1,0:T(8,128)S(1)} %collective-permute-done.29.refs_2_), channel_id=1, source_target_pairs={{0,1},{1,0},{2,3},{3,2},{4,5},{5,4},{6,7},{7,6},{8,9},{9,8},{10,11... | collective-permute-start | bytes 786440 | tf_op jit(solution)/shard_map/ppermute | solution.py:378
  110.3 1.6 %collective-permute-start.32 = (f32[256,256]{1,0:T(8,128)S(1)}, f32[256,256]{1,0:T(8,128)S(1)}, u32[]{:S(2)}, u32[]{:S(2)}) collective-permute-start(f32[256,256]{1,0:T(8,128)S(1)} %shard_map.75.refs_1_), channel_id=1, source_target_pairs={{0,1},{1,0},{2,3},{3,2},{4,5},{5,4},{6,7},{7,6},{8,9},{9,8},{10,11... | collective-permute-start | bytes 786440 | tf_op jit(solution)/shard_map/ppermute | solution.py:361
  110.5 6.4 %collective-permute-start.31 = (f32[256,256]{1,0:T(8,128)S(1)}, f32[256,256]{1,0:T(8,128)S(1)}, u32[]{:S(2)}, u32[]{:S(2)}) collective-permute-start(f32[256,256]{1,0:T(8,128)S(1)} %shard_map.75.refs_1_), channel_id=1, source_target_pairs={{0,4},{1,3},{4,8},{5,1},{8,12},{9,5},{12,14},{13,9},{14,10},{15,13... | collective-permute-start | bytes 786440 | tf_op jit(solution)/shard_map/ppermute | solution.py:364
  111.9 7.8 %collective-permute-start.33 = (f32[256,256]{1,0:T(8,128)S(1)}, f32[256,256]{1,0:T(8,128)S(1)}, u32[]{:S(2)}, u32[]{:S(2)}) collective-permute-start(f32[256,256]{1,0:T(8,128)S(1)} %collective-permute-done.32.refs_2_), channel_id=1, source_target_pairs={{0,4},{1,3},{4,8},{5,1},{8,12},{9,5},{12,14},{13,9},{14,10},{15,13... | collective-permute-start | bytes 786440 | tf_op jit(solution)/shard_map/ppermute | solution.py:365
  116.9 6.4 %collective-permute-start.34 = (f32[256,256]{1,0:T(8,128)S(1)}, f32[256,256]{1,0:T(8,128)S(1)}, u32[]{:S(2)}, u32[]{:S(2)}) collective-permute-start(f32[256,256]{1,0:T(8,128)S(1)} %collective-permute-done.31.refs_3_), channel_id=1, source_target_pairs={{0,4},{1,3},{4,8},{5,1},{8,12},{9,5},{12,14},{13,9},{14,10},{15,13... | collective-permute-start | bytes 786440 | tf_op jit(solution)/shard_map/ppermute | solution.py:364
  119.7 6.4 %collective-permute-start.35 = (f32[256,256]{1,0:T(8,128)S(1)}, f32[256,256]{1,0:T(8,128)S(1)}, u32[]{:S(2)}, u32[]{:S(2)}) collective-permute-start(f32[256,256]{1,0:T(8,128)S(1)} %collective-permute-done.33.refs_4_), channel_id=1, source_target_pairs={{0,4},{1,3},{4,8},{5,1},{8,12},{9,5},{12,14},{13,9},{14,10},{15,13... | collective-permute-start | bytes 786440 | tf_op jit(solution)/shard_map/ppermute | solution.py:365
  123.3 6.4 %collective-permute-start.36 = (f32[256,256]{1,0:T(8,128)S(1)}, f32[256,256]{1,0:T(8,128)S(1)}, u32[]{:S(2)}, u32[]{:S(2)}) collective-permute-start(f32[256,256]{1,0:T(8,128)S(1)} %collective-permute-done.34.refs_5_), channel_id=1, source_target_pairs={{0,4},{1,3},{4,8},{5,1},{8,12},{9,5},{12,14},{13,9},{14,10},{15,13... | collective-permute-start | bytes 786440 | tf_op jit(solution)/shard_map/ppermute | solution.py:364
  126.1 6.4 %collective-permute-start.37 = (f32[256,256]{1,0:T(8,128)S(1)}, f32[256,256]{1,0:T(8,128)S(1)}, u32[]{:S(2)}, u32[]{:S(2)}) collective-permute-start(f32[256,256]{1,0:T(8,128)S(1)} %collective-permute-done.35.refs_6_), channel_id=1, source_target_pairs={{0,4},{1,3},{4,8},{5,1},{8,12},{9,5},{12,14},{13,9},{14,10},{15,13... | collective-permute-start | bytes 786440 | tf_op jit(solution)/shard_map/ppermute | solution.py:365
  133.8 8.0 %collective-permute-start.38 = (f32[256,768]{1,0:T(8,128)S(1)}, f32[256,768]{1,0:T(8,128)S(1)}, u32[]{:S(2)}, u32[]{:S(2)}) collective-permute-start(f32[256,768]{1,0:T(8,128)S(1)} %get-tuple-element.63), channel_id=1, source_target_pairs={{0,1},{1,0},{2,3},{3,2},{4,5},{5,4},{6,7},{7,6},{8,9},{9,8},{10,11... | collective-permute-start | bytes 2359304 | tf_op jit(solution)/shard_map/ppermute | solution.py:377
  133.9 6.4 %collective-permute-start.39 = (f32[256,256]{1,0:T(8,128)S(1)}, f32[256,256]{1,0:T(8,128)S(1)}, u32[]{:S(2)}, u32[]{:S(2)}) collective-permute-start(f32[256,256]{1,0:T(8,128)S(1)} %collective-permute-done.36.refs_7_), channel_id=1, source_target_pairs={{0,4},{1,3},{4,8},{5,1},{8,12},{9,5},{12,14},{13,9},{14,10},{15,13... | collective-permute-start | bytes 786440 | tf_op jit(solution)/shard_map/ppermute | solution.py:369
  140.3 1.5 %collective-permute-start.40 = (f32[256,256]{1,0:T(8,128)S(1)}, f32[256,256]{1,0:T(8,128)S(1)}, u32[]{:S(2)}, u32[]{:S(2)}) collective-permute-start(f32[256,256]{1,0:T(8,128)S(1)} %collective-permute-done.39.refs_2_), channel_id=1, source_target_pairs={{0,1},{1,0},{2,3},{3,2},{4,5},{5,4},{6,7},{7,6},{8,9},{9,8},{10,11... | collective-permute-start | bytes 786440 | tf_op jit(solution)/shard_map/ppermute | solution.py:378

commit v5 on v4

--- a/solution.py
+++ b/solution.py
@@ -17,12 +17,12 @@
 VMEM = pl.BlockSpec(memory_space=pltpu.VMEM)
 
 
-def call(kernel, out_shape, count, scratch=(), passes=0, scalars=0):
+def call(kernel, out_shape, count, scratch=(), passes=0, scalars=0, out_specs=None):
     return pl.pallas_call(
         kernel,
         out_shape=out_shape,
         in_specs=[pl.BlockSpec(memory_space=pltpu.SMEM)] * scalars + [VMEM] * count,
-        out_specs=jax.tree.map(lambda _: VMEM, out_shape),
+        out_specs=out_specs or jax.tree.map(lambda _: VMEM, out_shape),
         scratch_shapes=list(scratch),
         compiler_params=pltpu.CompilerParams(vmem_limit_bytes=16 << 20),
         cost_estimate=pl.CostEstimate(flops=passes, transcendentals=0, bytes_accessed=0) if passes else None,
@@ -152,7 +152,7 @@
     noise_copy.wait()
 
 
-def residual_parts(before, here, after, damp, damp_next, noise_ref, x_refs, y_refs, out_ref):
+def residual_parts(before, here, after, damp, damp_next, noise_ref, x_refs, y_refs, out_ref, written=None):
     side_x, side_y = here.shape
     half = side_x // 2
     windows = (slice(0, half), slice(half, side_x))
@@ -170,6 +170,8 @@
     for window, part, back in zip(windows, moved, carried):
         forward = here[window] - part
         out_ref[window] = noise_ref[window] - (forward - damp_next[window] * back)
+        if written is not None:
+            written(window)
 
 
 def normal_kernel(
@@ -217,10 +219,26 @@
     out_refs = refs[7:]
     sources = keep_ref, other_ref, last_ref, last_other_ref
     slices = [joined(weight_ref, base, part, sources, slice(None)) for part in range(3)]
-    if len(out_refs) == 2:
-        out_refs[1][...] = slices[1]
+    copies = []
+    out_ref = out_refs[0]
+
+    def send(source, target, place):
+        copies.append(pltpu.make_async_copy(source, target, out_refs[-1].at[place]))
+        copies[-1].start()
+
+    written = None
+    if len(out_refs) > 1:
+        residual_ref, result_ref, out_ref, held_ref = out_refs[:4]
+        held_ref[...] = slices[1]
+        send(held_ref, result_ref, 0)
+
+        def written(window):
+            send(out_ref.at[window], residual_ref.at[window], len(copies))
+
     damps = damp_ref[...], damp_next_ref[...]
-    residual_parts(*slices, *damps, noise_ref, (xh_ref, xl_ref), (yh_ref, yl_ref), out_refs[0])
+    residual_parts(*slices, *damps, noise_ref, (xh_ref, xl_ref), (yh_ref, yl_ref), out_ref, written)
+    for copy in copies:
+        copy.wait()
 
 
 def basis_of(length):
@@ -399,19 +417,24 @@
         compiler_params=pltpu.CompilerParams(vmem_limit_bytes=60 * 1024 * 1024),
     )(noise, phonon_level)
     parts, (weights, hops) = around(packed, forward, 1, (weights, hops))
-    damp_next = lax.ppermute(damp, "tm", [(i, (i - 1) % length) for i in range(length)])
+    damp_wrap = lax.ppermute(damp, "tm", [(0, length - 1)])
+    damp_next = lax.ppermute(damp, "tm", [(i, i - 1) for i in range(1, length)])
     first_kernel, next_kernel = based(first_spectral_kernel, forward), based(next_spectral_kernel, forward)
     finish = based(finish_kernel, back)
     first_outs = (field_shape, shape(1, side_y))
     first, mean_level = call(first_kernel, first_outs, 9, scratch, work, 1)(*parts, cosine, *hops)
-    first, damp_next = lax.optimization_barrier((first, damp_next))
+    first, damp_next, damp_wrap = lax.optimization_barrier((first, damp_next, damp_wrap))
+    damp_next = damp_next + damp_wrap
     beside = (weights,)
     parts, beside = around(first, back, 3, beside)
     (second_residual,) = call(finish, (field_shape,), 11, scalars=1)(*parts, damp, damp_next, noise, *hops)
     parts, beside = around(second_residual, forward, 1, beside)
     total = call(next_kernel, field_shape, 11, scratch, work, 1)(*parts, cosine, *hops, mean_level, first)
     parts, beside = around(total, back, 3, beside)
-    residual, result = call(finish, (field_shape,) * 2, 11, scalars=1)(*parts, damp, damp_next, noise, *hops)
+    scratch = [pltpu.VMEM((side_x, side_y), F32)] * 2 + [pltpu.SemaphoreType.DMA((3,))]
+    out_specs = (pl.BlockSpec(memory_space=pltpu.HBM),) * 2
+    last_finish = call(finish, (field_shape,) * 2, 11, scratch, scalars=1, out_specs=out_specs)
+    residual, result = last_finish(*parts, damp, damp_next, noise, *hops)
     return result, residual
 
 

time: 145 us -> 149 us (1.028)
  starting transfers between devices: 20.8 us -> 24.9 us
    ppermute x1 -> x2, starting transfers between devices: 5.17 us -> 8.37 us  [the longest x1 7.08 us: by_ring(): damp_wrap = lax.ppermute(damp, 'tm', [(0, length - 1)])]
  transfers between devices with their start and end apart: 41 -> 42, of which waited for: 34 -> 34; matrix products, arithmetic and copies ran while one was open for 0% -> 0% of each run, Pallas kernels for 7% -> 6%
where the time goes in v5:
time: 149 us
  waiting for transfers between devices  96 us (64%)
  Pallas kernels  26 us (17%)
  starting transfers between devices  24.9 us (17%)
    ppermute x12, waiting for transfers between devices, around(): own = lax.ppermute(own, 'tm', hop)  41.1 us
    ppermute x12, waiting for transfers between devices, around(): partner = lax.ppermute(partner, 'tm', hop)  28.7 us
    ppermute x4, waiting for transfers between devices, around(): last = lax.ppermute(own, 'tm', hop)  17.7 us
    pallas_call x1, Pallas kernels, by_ring(): call(first_kernel, first_outs, 9, scratch, work, 1)(*parts, cosine, *hops)  7.35 us
    pallas_call x1, Pallas kernels, by_ring(): call(next_kernel, field_shape, 11, scratch, work, 1)  7.34 us
    ppermute x1, starting transfers between devices, by_ring(): damp_wrap = lax.ppermute(damp, 'tm', [(0, length - 1)])  7.08 us
    ppermute x12, starting transfers between devices, around(): own = lax.ppermute(own, 'tm', hop)  6.8 us
    ppermute x12, starting transfers between devices, around(): partner = lax.ppermute(partner, 'tm', hop)  5.1 us
  transfers between devices with their start and end apart: 42, of which 34 were waited for; matrix products, arithmetic and copies ran while one was open for 0% of the time, Pallas kernels for 6%

profile of v5, /device:TPU:0, one launch (start us, length us, event | category | flops | bytes accessed | tf_op | source)
XLA Modules:
  0.0 148.7 jit_solution(2958970497084339167)
XLA Ops:
  0.7 2.0 %shard_map.68 = (f32[264,256]{1,0:T(8,128)}, f32[256,256]{1,0:T(8,128)}) custom-call(f32[256,256]{1,0:T(8,128)} %bitcast.6, s32[256,256]{1,0:T(8,128)} %bitcast.9), custom_call_target="tpu_custom_call" | custom-call | tf_op jit(solution)/shard_map/pallas_call | solution.py:411
  3.2 2.6 %collective-permute-start = (f32[264,256]{1,0:T(8,128)}, f32[264,256]{1,0:T(8,128)S(1)}, u32[]{:S(2)}, u32[]{:S(2)}) collective-permute-start(f32[264,256]{1,0:T(8,128)} %get-tuple-element.35.refs_1_), channel_id=1, source_target_pairs={{0,4},{1,3},{4,8},{5,1},{8,12},{9,5},{12,14},{13,9},{14,10},{15,13... | collective-permute-start | bytes 811016 | tf_op jit(solution)/shard_map/ppermute | solution.py:382
  7.2 1.6 %collective-permute-start.2 = (f32[264,256]{1,0:T(8,128)S(1)}, f32[264,256]{1,0:T(8,128)S(1)}, u32[]{:S(2)}, u32[]{:S(2)}) collective-permute-start(f32[264,256]{1,0:T(8,128)S(1)} %collective-permute-done.1.refs_2_), channel_id=1, source_target_pairs={{0,4},{1,3},{4,8},{5,1},{8,12},{9,5},{12,14},{13,9},{14,10},{15,13... | collective-permute-start | bytes 811016 | tf_op jit(solution)/shard_map/ppermute | solution.py:383
  8.7 1.6 %collective-permute-done.refs_3_ = f32[264,256]{1,0:T(8,128)S(1)} collective-permute-done((f32[264,256]{1,0:T(8,128)}, f32[264,256]{1,0:T(8,128)S(1)}, u32[]{:S(2)}, u32[]{:S(2)}) %collective-permute-start) | collective-permute-done | bytes 270368 | tf_op jit(solution)/shard_map/ppermute | solution.py:382
  10.4 2.1 %collective-permute-start.3 = (f32[264,256]{1,0:T(8,128)S(1)}, f32[264,256]{1,0:T(8,128)S(1)}, u32[]{:S(2)}, u32[]{:S(2)}) collective-permute-start(f32[264,256]{1,0:T(8,128)S(1)} %collective-permute-done.refs_3_), channel_id=1, source_target_pairs={{0,4},{1,3},{4,8},{5,1},{8,12},{9,5},{12,14},{13,9},{14,10},{15,13... | collective-permute-start | bytes 811016 | tf_op jit(solution)/shard_map/ppermute | solution.py:382
  12.5 1.2 collective-permute-done.2.refs_4_
  13.6 1.7 %collective-permute-start.4 = (f32[264,256]{1,0:T(8,128)S(1)}, f32[264,256]{1,0:T(8,128)S(1)}, u32[]{:S(2)}, u32[]{:S(2)}) collective-permute-start(f32[264,256]{1,0:T(8,128)S(1)} %collective-permute-done.2.refs_4_), channel_id=1, source_target_pairs={{0,4},{1,3},{4,8},{5,1},{8,12},{9,5},{12,14},{13,9},{14,10},{15,13... | collective-permute-start | bytes 811016 | tf_op jit(solution)/shard_map/ppermute | solution.py:383
  15.4 1.5 %collective-permute-done.3.refs_5_ = f32[264,256]{1,0:T(8,128)S(1)} collective-permute-done((f32[264,256]{1,0:T(8,128)S(1)}, f32[264,256]{1,0:T(8,128)S(1)}, u32[]{:S(2)}, u32[]{:S(2)}) %collective-permute-start.3) | collective-permute-done | bytes 270368 | tf_op jit(solution)/shard_map/ppermute | solution.py:382
  16.9 2.1 %collective-permute-start.5 = (f32[264,256]{1,0:T(8,128)S(1)}, f32[264,256]{1,0:T(8,128)S(1)}, u32[]{:S(2)}, u32[]{:S(2)}) collective-permute-start(f32[264,256]{1,0:T(8,128)S(1)} %collective-permute-done.3.refs_5_), channel_id=1, source_target_pairs={{0,4},{1,3},{4,8},{5,1},{8,12},{9,5},{12,14},{13,9},{14,10},{15,13... | collective-permute-start | bytes 811016 | tf_op jit(solution)/shard_map/ppermute | solution.py:382
  20.1 1.7 %collective-permute-start.6 = (f32[264,256]{1,0:T(8,128)S(1)}, f32[264,256]{1,0:T(8,128)S(1)}, u32[]{:S(2)}, u32[]{:S(2)}) collective-permute-start(f32[264,256]{1,0:T(8,128)S(1)} %collective-permute-done.4.refs_6_), channel_id=1, source_target_pairs={{0,4},{1,3},{4,8},{5,1},{8,12},{9,5},{12,14},{13,9},{14,10},{15,13... | collective-permute-start | bytes 811016 | tf_op jit(solution)/shard_map/ppermute | solution.py:383
  21.8 1.5 collective-permute-done.5.refs_7_
  23.3 2.1 %collective-permute-start.8 = (f32[264,256]{1,0:T(8,128)S(1)}, f32[264,256]{1,0:T(8,128)S(1)}, u32[]{:S(2)}, u32[]{:S(2)}) collective-permute-start(f32[264,256]{1,0:T(8,128)S(1)} %collective-permute-done.5.refs_7_), channel_id=1, source_target_pairs={{0,4},{1,3},{4,8},{5,1},{8,12},{9,5},{12,14},{13,9},{14,10},{15,13... | collective-permute-start | bytes 811016 | tf_op jit(solution)/shard_map/ppermute | solution.py:387
  27.5 2.3 %collective-permute-done.8.refs_2_ = f32[264,256]{1,0:T(8,128)S(1)} collective-permute-done((f32[264,256]{1,0:T(8,128)S(1)}, f32[264,256]{1,0:T(8,128)S(1)}, u32[]{:S(2)}, u32[]{:S(2)}) %collective-permute-start.8) | collective-permute-done | bytes 270368 | tf_op jit(solution)/shard_map/ppermute | solution.py:387
  29.8 7.1 %collective-permute-start.11 = (f32[256,256]{1,0:T(8,128)S(1)}, f32[256,256]{1,0:T(8,128)S(1)}, u32[]{:S(2)}, u32[]{:S(2)}) collective-permute-start(f32[256,256]{1,0:T(8,128)S(1)} %copy-done.1), channel_id=1, source_target_pairs={{0,15},{16,31}} | collective-permute-start | bytes 786440 | tf_op jit(solution)/shard_map/ppermute | solution.py:420
  36.9 1.3 collective-permute-start.10
  38.3 7.4 %shard_map.71 = (f32[256,256]{1,0:T(8,128)S(1)}, f32[1,256]{1,0:T(1,128)S(1)}) custom-call(f32[64]{0:T(128)S(1)} %dynamic-slice_bitcast_fusion.refs_0_.weight_ref, f32[264,256]{1,0:T(8,128)S(1)} %get-tuple-element.42.refs_0_, f32[264,256]{1,0:T(8,128)S(1)} %collective-permute-done.7.refs_1_, f32[264,256]{1,0:T(8,128)S(1)} %collective-permute-done.8.refs_2_, ...), custom_call_target="tpu_custom_call" | custom-call | flops 4026531840 | tf_op jit(solution)/shard_map/pallas_call | solution.py:425
  45.7 1.2 collective-permute-start.13
  48.0 5.2 %collective-permute-done.12.refs_3_ = f32[256,256]{1,0:T(8,128)S(1)} collective-permute-done((f32[256,256]{1,0:T(8,128)S(1)}, f32[256,256]{1,0:T(8,128)S(1)}, u32[]{:S(2)}, u32[]{:S(2)}) %collective-permute-start.12) | collective-permute-done | bytes 262176 | tf_op jit(solution)/shard_map/ppermute | solution.py:382
  53.2 2.8 %collective-permute-done.14.refs_4_ = f32[256,256]{1,0:T(8,128)S(1)} collective-permute-done((f32[256,256]{1,0:T(8,128)S(1)}, f32[256,256]{1,0:T(8,128)S(1)}, u32[]{:S(2)}, u32[]{:S(2)}) %collective-permute-start.14) | collective-permute-done | bytes 262176 | tf_op jit(solution)/shard_map/ppermute | solution.py:383
  56.0 3.6 %collective-permute-done.15.refs_5_ = f32[256,256]{1,0:T(8,128)S(1)} collective-permute-done((f32[256,256]{1,0:T(8,128)S(1)}, f32[256,256]{1,0:T(8,128)S(1)}, u32[]{:S(2)}, u32[]{:S(2)}) %collective-permute-start.15) | collective-permute-done | bytes 262176 | tf_op jit(solution)/shard_map/ppermute | solution.py:382
  59.6 2.8 %collective-permute-done.16.refs_6_ = f32[256,256]{1,0:T(8,128)S(1)} collective-permute-done((f32[256,256]{1,0:T(8,128)S(1)}, f32[256,256]{1,0:T(8,128)S(1)}, u32[]{:S(2)}, u32[]{:S(2)}) %collective-permute-start.16) | collective-permute-done | bytes 262176 | tf_op jit(solution)/shard_map/ppermute | solution.py:383
  62.4 3.6 %collective-permute-done.17.refs_7_ = f32[256,256]{1,0:T(8,128)S(1)} collective-permute-done((f32[256,256]{1,0:T(8,128)S(1)}, f32[256,256]{1,0:T(8,128)S(1)}, u32[]{:S(2)}, u32[]{:S(2)}) %collective-permute-start.17) | collective-permute-done | bytes 262176 | tf_op jit(solution)/shard_map/ppermute | solution.py:382
  66.0 2.8 %collective-permute-done.18.refs_8_ = f32[256,256]{1,0:T(8,128)S(1)} collective-permute-done((f32[256,256]{1,0:T(8,128)S(1)}, f32[256,256]{1,0:T(8,128)S(1)}, u32[]{:S(2)}, u32[]{:S(2)}) %collective-permute-start.18) | collective-permute-done | bytes 262176 | tf_op jit(solution)/shard_map/ppermute | solution.py:383
  68.8 1.3 shard_map.72
  70.3 6.4 %collective-permute-done.20.refs_2_ = f32[256,256]{1,0:T(8,128)S(1)} collective-permute-done((f32[256,256]{1,0:T(8,128)S(1)}, f32[256,256]{1,0:T(8,128)S(1)}, u32[]{:S(2)}, u32[]{:S(2)}) %collective-permute-start.20) | collective-permute-done | bytes 262176 | tf_op jit(solution)/shard_map/ppermute | solution.py:387
  76.7 1.5 %collective-permute-done.21.refs_3_ = f32[256,256]{1,0:T(8,128)S(1)} collective-permute-done((f32[256,256]{1,0:T(8,128)S(1)}, f32[256,256]{1,0:T(8,128)S(1)}, u32[]{:S(2)}, u32[]{:S(2)}) %collective-permute-start.21) | collective-permute-done | bytes 262176 | tf_op jit(solution)/shard_map/ppermute | solution.py:396
  78.2 1.8 %shard_map.73.refs_1_ = f32[256,256]{1,0:T(8,128)S(1)} custom-call(f32[64]{0:T(128)S(1)} %dynamic-slice_bitcast_fusion.refs_0_.weight_ref, f32[256,768]{1,0:T(8,128)S(1)} %get-tuple-element.53.refs_0_, f32[256,768]{1,0:T(8,128)S(1)} %collective-permute-done.19.refs_1_, f32[256,256]{1,0:T(8,128)S(1)} %collective-permute-done.20.refs_2_, ...), custom_call_target="tpu_custom_call" | custom-call | tf_op jit(solution)/shard_map/pallas_call | solution.py:430
  80.2 1.4 collective-permute-done.23.refs_2_
  81.6 5.0 %collective-permute-done.22.refs_3_ = f32[256,256]{1,0:T(8,128)S(1)} collective-permute-done((f32[256,256]{1,0:T(8,128)S(1)}, f32[256,256]{1,0:T(8,128)S(1)}, u32[]{:S(2)}, u32[]{:S(2)}) %collective-permute-start.22) | collective-permute-done | bytes 262176 | tf_op jit(solution)/shard_map/ppermute | solution.py:382
  86.6 2.8 %collective-permute-done.24.refs_4_ = f32[256,256]{1,0:T(8,128)S(1)} collective-permute-done((f32[256,256]{1,0:T(8,128)S(1)}, f32[256,256]{1,0:T(8,128)S(1)}, u32[]{:S(2)}, u32[]{:S(2)}) %collective-permute-start.24) | collective-permute-done | bytes 262176 | tf_op jit(solution)/shard_map/ppermute | solution.py:383
  89.4 3.6 %collective-permute-done.25.refs_5_ = f32[256,256]{1,0:T(8,128)S(1)} collective-permute-done((f32[256,256]{1,0:T(8,128)S(1)}, f32[256,256]{1,0:T(8,128)S(1)}, u32[]{:S(2)}, u32[]{:S(2)}) %collective-permute-start.25) | collective-permute-done | bytes 262176 | tf_op jit(solution)/shard_map/ppermute | solution.py:382
  93.0 2.8 %collective-permute-done.26.refs_6_ = f32[256,256]{1,0:T(8,128)S(1)} collective-permute-done((f32[256,256]{1,0:T(8,128)S(1)}, f32[256,256]{1,0:T(8,128)S(1)}, u32[]{:S(2)}, u32[]{:S(2)}) %collective-permute-start.26) | collective-permute-done | bytes 262176 | tf_op jit(solution)/shard_map/ppermute | solution.py:383
  95.8 3.6 %collective-permute-done.27.refs_7_ = f32[256,256]{1,0:T(8,128)S(1)} collective-permute-done((f32[256,256]{1,0:T(8,128)S(1)}, f32[256,256]{1,0:T(8,128)S(1)}, u32[]{:S(2)}, u32[]{:S(2)}) %collective-permute-start.27) | collective-permute-done | bytes 262176 | tf_op jit(solution)/shard_map/ppermute | solution.py:382
  99.4 2.8 %collective-permute-done.28.refs_8_ = f32[256,256]{1,0:T(8,128)S(1)} collective-permute-done((f32[256,256]{1,0:T(8,128)S(1)}, f32[256,256]{1,0:T(8,128)S(1)}, u32[]{:S(2)}, u32[]{:S(2)}) %collective-permute-start.28) | collective-permute-done | bytes 262176 | tf_op jit(solution)/shard_map/ppermute | solution.py:383
  103.1 2.7 %collective-permute-done.30.refs_2_ = f32[256,256]{1,0:T(8,128)S(1)} collective-permute-done((f32[256,256]{1,0:T(8,128)S(1)}, f32[256,256]{1,0:T(8,128)S(1)}, u32[]{:S(2)}, u32[]{:S(2)}) %collective-permute-start.30) | collective-permute-done | bytes 262176 | tf_op jit(solution)/shard_map/ppermute | solution.py:387
  105.7 1.5 %collective-permute-done.31.refs_3_ = f32[256,256]{1,0:T(8,128)S(1)} collective-permute-done((f32[256,256]{1,0:T(8,128)S(1)}, f32[256,256]{1,0:T(8,128)S(1)}, u32[]{:S(2)}, u32[]{:S(2)}) %collective-permute-start.31) | collective-permute-done | bytes 262176 | tf_op jit(solution)/shard_map/ppermute | solution.py:396
  107.3 7.3 %shard_map.75.refs_1_ = f32[256,256]{1,0:T(8,128)S(1)} custom-call(f32[64]{0:T(128)S(1)} %dynamic-slice_bitcast_fusion.refs_0_.weight_ref, f32[256,256]{1,0:T(8,128)S(1)} %get-tuple-element.59.refs_0_, f32[256,256]{1,0:T(8,128)S(1)} %collective-permute-done.29.refs_1_, f32[256,256]{1,0:T(8,128)S(1)} %collective-permute-done.30.refs_2_, ...), custom_call_target="tpu_custom_call" | custom-call | flops 4026531840 | tf_op jit(solution)/shard_map/pallas_call | solution.py:432
  114.8 1.4 collective-permute-done.33.refs_2_
  116.2 4.9 %collective-permute-done.32.refs_3_ = f32[256,256]{1,0:T(8,128)S(1)} collective-permute-done((f32[256,256]{1,0:T(8,128)S(1)}, f32[256,256]{1,0:T(8,128)S(1)}, u32[]{:S(2)}, u32[]{:S(2)}) %collective-permute-start.32) | collective-permute-done | bytes 262176 | tf_op jit(solution)/shard_map/ppermute | solution.py:382
  121.2 2.8 %collective-permute-done.34.refs_4_ = f32[256,256]{1,0:T(8,128)S(1)} collective-permute-done((f32[256,256]{1,0:T(8,128)S(1)}, f32[256,256]{1,0:T(8,128)S(1)}, u32[]{:S(2)}, u32[]{:S(2)}) %collective-permute-start.34) | collective-permute-done | bytes 262176 | tf_op jit(solution)/shard_map/ppermute | solution.py:383
  124.0 3.6 %collective-permute-done.35.refs_5_ = f32[256,256]{1,0:T(8,128)S(1)} collective-permute-done((f32[256,256]{1,0:T(8,128)S(1)}, f32[256,256]{1,0:T(8,128)S(1)}, u32[]{:S(2)}, u32[]{:S(2)}) %collective-permute-start.35) | collective-permute-done | bytes 262176 | tf_op jit(solution)/shard_map/ppermute | solution.py:382
  127.5 2.8 %collective-permute-done.36.refs_6_ = f32[256,256]{1,0:T(8,128)S(1)} collective-permute-done((f32[256,256]{1,0:T(8,128)S(1)}, f32[256,256]{1,0:T(8,128)S(1)}, u32[]{:S(2)}, u32[]{:S(2)}) %collective-permute-start.36) | collective-permute-done | bytes 262176 | tf_op jit(solution)/shard_map/ppermute | solution.py:383
  130.4 3.6 %collective-permute-done.37.refs_7_ = f32[256,256]{1,0:T(8,128)S(1)} collective-permute-done((f32[256,256]{1,0:T(8,128)S(1)}, f32[256,256]{1,0:T(8,128)S(1)}, u32[]{:S(2)}, u32[]{:S(2)}) %collective-permute-start.37) | collective-permute-done | bytes 262176 | tf_op jit(solution)/shard_map/ppermute | solution.py:382
  133.9 2.8 %collective-permute-done.38.refs_8_ = f32[256,256]{1,0:T(8,128)S(1)} collective-permute-done((f32[256,256]{1,0:T(8,128)S(1)}, f32[256,256]{1,0:T(8,128)S(1)}, u32[]{:S(2)}, u32[]{:S(2)}) %collective-permute-start.38) | collective-permute-done | bytes 262176 | tf_op jit(solution)/shard_map/ppermute | solution.py:383
  136.7 1.3 shard_map.76
  138.2 6.4 %collective-permute-done.40.refs_2_ = f32[256,256]{1,0:T(8,128)S(1)} collective-permute-done((f32[256,256]{1,0:T(8,128)S(1)}, f32[256,256]{1,0:T(8,128)S(1)}, u32[]{:S(2)}, u32[]{:S(2)}) %collective-permute-start.40) | collective-permute-done | bytes 262176 | tf_op jit(solution)/shard_map/ppermute | solution.py:387
  144.6 1.5 %collective-permute-done.41.refs_3_ = f32[256,256]{1,0:T(8,128)S(1)} collective-permute-done((f32[256,256]{1,0:T(8,128)S(1)}, f32[256,256]{1,0:T(8,128)S(1)}, u32[]{:S(2)}, u32[]{:S(2)}) %collective-permute-start.41) | collective-permute-done | bytes 262176 | tf_op jit(solution)/shard_map/ppermute | solution.py:396
  146.1 2.5 %shard_map.77 = (f32[256,256]{1,0:T(8,128)}, f32[256,256]{1,0:T(8,128)}) custom-call(f32[64]{0:T(128)S(1)} %dynamic-slice_bitcast_fusion.refs_0_.weight_ref, f32[256,768]{1,0:T(8,128)S(1)} %get-tuple-element.64.refs_0_, f32[256,768]{1,0:T(8,128)S(1)} %collective-permute-done.39.refs_1_, f32[256,256]{1,0:T(8,128)S(1)} %collective-permute-done.40.refs_2_, ...), custom_call_target="tpu_custom_call" | custom-call | tf_op jit(solution)/shard_map/pallas_call | solution.py:437
  (59 shorter events, 8.0 us)
Async XLA Ops:
  0.6 5.2 %copy-start.3 = (f32[256,256]{1,0:T(8,128)S(1)}, f32[256,256]{1,0:T(8,128)}, u32[]{:S(2)}) copy-start(f32[256,256]{1,0:T(8,128)} %hop_x_ref.1) | copy-start | bytes 786436
  0.6 5.2 %copy-start.4 = (f32[256,256]{1,0:T(8,128)S(1)}, f32[256,256]{1,0:T(8,128)}, u32[]{:S(2)}) copy-start(f32[256,256]{1,0:T(8,128)} %hop_y_ref.1) | copy-start | bytes 786436
  2.6 4.6 %collective-permute-start.1 = (f32[264,256]{1,0:T(8,128)}, f32[264,256]{1,0:T(8,128)S(1)}, u32[]{:S(2)}, u32[]{:S(2)}) collective-permute-start(f32[264,256]{1,0:T(8,128)} %get-tuple-element.35.refs_1_), channel_id=1, source_target_pairs={{0,1},{1,0},{2,3},{3,2},{4,5},{5,4},{6,7},{7,6},{8,9},{9,8},{10,11... | collective-permute-start | bytes 811016 | tf_op jit(solution)/shard_map/ppermute | solution.py:379
  3.2 7.2 %collective-permute-start = (f32[264,256]{1,0:T(8,128)}, f32[264,256]{1,0:T(8,128)S(1)}, u32[]{:S(2)}, u32[]{:S(2)}) collective-permute-start(f32[264,256]{1,0:T(8,128)} %get-tuple-element.35.refs_1_), channel_id=1, source_target_pairs={{0,4},{1,3},{4,8},{5,1},{8,12},{9,5},{12,14},{13,9},{14,10},{15,13... | collective-permute-start | bytes 811016 | tf_op jit(solution)/shard_map/ppermute | solution.py:382
  5.8 20.8 %copy-start.2 = (f32[264,256]{1,0:T(8,128)S(1)}, f32[264,256]{1,0:T(8,128)}, u32[]{:S(2)}) copy-start(f32[264,256]{1,0:T(8,128)} %get-tuple-element.35.refs_1_) | copy-start | bytes 811012
  7.2 6.5 %collective-permute-start.2 = (f32[264,256]{1,0:T(8,128)S(1)}, f32[264,256]{1,0:T(8,128)S(1)}, u32[]{:S(2)}, u32[]{:S(2)}) collective-permute-start(f32[264,256]{1,0:T(8,128)S(1)} %collective-permute-done.1.refs_2_), channel_id=1, source_target_pairs={{0,4},{1,3},{4,8},{5,1},{8,12},{9,5},{12,14},{13,9},{14,10},{15,13... | collective-permute-start | bytes 811016 | tf_op jit(solution)/shard_map/ppermute | solution.py:383
  10.4 19.4 %copy-start.1 = (f32[256,256]{1,0:T(8,128)S(1)}, f32[256,256]{1,0:T(8,128)}, u32[]{:S(2)}) copy-start(f32[256,256]{1,0:T(8,128)} %get-tuple-element.49.refs_4_) | copy-start | bytes 786436
  10.4 6.5 %collective-permute-start.3 = (f32[264,256]{1,0:T(8,128)S(1)}, f32[264,256]{1,0:T(8,128)S(1)}, u32[]{:S(2)}, u32[]{:S(2)}) collective-permute-start(f32[264,256]{1,0:T(8,128)S(1)} %collective-permute-done.refs_3_), channel_id=1, source_target_pairs={{0,4},{1,3},{4,8},{5,1},{8,12},{9,5},{12,14},{13,9},{14,10},{15,13... | collective-permute-start | bytes 811016 | tf_op jit(solution)/shard_map/ppermute | solution.py:382
  13.6 6.5 %collective-permute-start.4 = (f32[264,256]{1,0:T(8,128)S(1)}, f32[264,256]{1,0:T(8,128)S(1)}, u32[]{:S(2)}, u32[]{:S(2)}) collective-permute-start(f32[264,256]{1,0:T(8,128)S(1)} %collective-permute-done.2.refs_4_), channel_id=1, source_target_pairs={{0,4},{1,3},{4,8},{5,1},{8,12},{9,5},{12,14},{13,9},{14,10},{15,13... | collective-permute-start | bytes 811016 | tf_op jit(solution)/shard_map/ppermute | solution.py:383
  16.9 6.5 %collective-permute-start.5 = (f32[264,256]{1,0:T(8,128)S(1)}, f32[264,256]{1,0:T(8,128)S(1)}, u32[]{:S(2)}, u32[]{:S(2)}) collective-permute-start(f32[264,256]{1,0:T(8,128)S(1)} %collective-permute-done.3.refs_5_), channel_id=1, source_target_pairs={{0,4},{1,3},{4,8},{5,1},{8,12},{9,5},{12,14},{13,9},{14,10},{15,13... | collective-permute-start | bytes 811016 | tf_op jit(solution)/shard_map/ppermute | solution.py:382
  20.1 6.5 %collective-permute-start.6 = (f32[264,256]{1,0:T(8,128)S(1)}, f32[264,256]{1,0:T(8,128)S(1)}, u32[]{:S(2)}, u32[]{:S(2)}) collective-permute-start(f32[264,256]{1,0:T(8,128)S(1)} %collective-permute-done.4.refs_6_), channel_id=1, source_target_pairs={{0,4},{1,3},{4,8},{5,1},{8,12},{9,5},{12,14},{13,9},{14,10},{15,13... | collective-permute-start | bytes 811016 | tf_op jit(solution)/shard_map/ppermute | solution.py:383
  23.3 6.5 %collective-permute-start.8 = (f32[264,256]{1,0:T(8,128)S(1)}, f32[264,256]{1,0:T(8,128)S(1)}, u32[]{:S(2)}, u32[]{:S(2)}) collective-permute-start(f32[264,256]{1,0:T(8,128)S(1)} %collective-permute-done.5.refs_7_), channel_id=1, source_target_pairs={{0,4},{1,3},{4,8},{5,1},{8,12},{9,5},{12,14},{13,9},{14,10},{15,13... | collective-permute-start | bytes 811016 | tf_op jit(solution)/shard_map/ppermute | solution.py:387
  27.4 10.9 %collective-permute-start.7 = (f32[264,256]{1,0:T(8,128)S(1)}, f32[264,256]{1,0:T(8,128)S(1)}, u32[]{:S(2)}, u32[]{:S(2)}) collective-permute-start(f32[264,256]{1,0:T(8,128)S(1)} %get-tuple-element.43), channel_id=1, source_target_pairs={{0,1},{1,0},{2,3},{3,2},{4,5},{5,4},{6,7},{7,6},{8,9},{9,8},{10,11... | collective-permute-start | bytes 811016 | tf_op jit(solution)/shard_map/ppermute | solution.py:395
  29.8 8.5 %collective-permute-start.9 = (f32[264,256]{1,0:T(8,128)S(1)}, f32[264,256]{1,0:T(8,128)S(1)}, u32[]{:S(2)}, u32[]{:S(2)}) collective-permute-start(f32[264,256]{1,0:T(8,128)S(1)} %collective-permute-done.8.refs_2_), channel_id=1, source_target_pairs={{0,1},{1,0},{2,3},{3,2},{4,5},{5,4},{6,7},{7,6},{8,9},{9,8},{10,11... | collective-permute-start | bytes 811016 | tf_op jit(solution)/shard_map/ppermute | solution.py:396
  29.8 15.9 %collective-permute-start.11 = (f32[256,256]{1,0:T(8,128)S(1)}, f32[256,256]{1,0:T(8,128)S(1)}, u32[]{:S(2)}, u32[]{:S(2)}) collective-permute-start(f32[256,256]{1,0:T(8,128)S(1)} %copy-done.1), channel_id=1, source_target_pairs={{0,15},{16,31}} | collective-permute-start | bytes 786440 | tf_op jit(solution)/shard_map/ppermute | solution.py:420
  36.9 8.8 %collective-permute-start.10 = (f32[256,256]{1,0:T(8,128)S(1)}, f32[256,256]{1,0:T(8,128)S(1)}, u32[]{:S(2)}, u32[]{:S(2)}) collective-permute-start(f32[256,256]{1,0:T(8,128)S(1)} %copy-done.1), channel_id=1, source_target_pairs={{1,0},{2,1},{3,2},{4,3},{5,4},{6,5},{7,6},{8,7},{9,8},{10,9},{11,1... | collective-permute-start | bytes 786440 | tf_op jit(solution)/shard_map/ppermute | solution.py:421
  45.7 2.4 %collective-permute-start.13 = (f32[256,256]{1,0:T(8,128)S(1)}, f32[256,256]{1,0:T(8,128)S(1)}, u32[]{:S(2)}, u32[]{:S(2)}) collective-permute-start(f32[256,256]{1,0:T(8,128)S(1)} %get-tuple-element.50.refs_1_.refs_10_), channel_id=1, source_target_pairs={{0,1},{1,0},{2,3},{3,2},{4,5},{5,4},{6,7},{7,6},{8,9},{9,8},{10,11... | collective-permute-start | bytes 786440 | tf_op jit(solution)/shard_map/ppermute | solution.py:379
  46.9 6.4 %collective-permute-start.12 = (f32[256,256]{1,0:T(8,128)S(1)}, f32[256,256]{1,0:T(8,128)S(1)}, u32[]{:S(2)}, u32[]{:S(2)}) collective-permute-start(f32[256,256]{1,0:T(8,128)S(1)} %get-tuple-element.50.refs_1_.refs_10_), channel_id=1, source_target_pairs={{0,4},{1,3},{4,8},{5,1},{8,12},{9,5},{12,14},{13,9},{14,10},{15,13... | collective-permute-start | bytes 786440 | tf_op jit(solution)/shard_map/ppermute | solution.py:382
  48.0 8.0 %collective-permute-start.14 = (f32[256,256]{1,0:T(8,128)S(1)}, f32[256,256]{1,0:T(8,128)S(1)}, u32[]{:S(2)}, u32[]{:S(2)}) collective-permute-start(f32[256,256]{1,0:T(8,128)S(1)} %collective-permute-done.13.refs_2_), channel_id=1, source_target_pairs={{0,4},{1,3},{4,8},{5,1},{8,12},{9,5},{12,14},{13,9},{14,10},{15,13... | collective-permute-start | bytes 786440 | tf_op jit(solution)/shard_map/ppermute | solution.py:383
  53.2 6.4 %collective-permute-start.15 = (f32[256,256]{1,0:T(8,128)S(1)}, f32[256,256]{1,0:T(8,128)S(1)}, u32[]{:S(2)}, u32[]{:S(2)}) collective-permute-start(f32[256,256]{1,0:T(8,128)S(1)} %collective-permute-done.12.refs_3_), channel_id=1, source_target_pairs={{0,4},{1,3},{4,8},{5,1},{8,12},{9,5},{12,14},{13,9},{14,10},{15,13... | collective-permute-start | bytes 786440 | tf_op jit(solution)/shard_map/ppermute | solution.py:382
  56.0 6.4 %collective-permute-start.16 = (f32[256,256]{1,0:T(8,128)S(1)}, f32[256,256]{1,0:T(8,128)S(1)}, u32[]{:S(2)}, u32[]{:S(2)}) collective-permute-start(f32[256,256]{1,0:T(8,128)S(1)} %collective-permute-done.14.refs_4_), channel_id=1, source_target_pairs={{0,4},{1,3},{4,8},{5,1},{8,12},{9,5},{12,14},{13,9},{14,10},{15,13... | collective-permute-start | bytes 786440 | tf_op jit(solution)/shard_map/ppermute | solution.py:383
  59.6 6.4 %collective-permute-start.17 = (f32[256,256]{1,0:T(8,128)S(1)}, f32[256,256]{1,0:T(8,128)S(1)}, u32[]{:S(2)}, u32[]{:S(2)}) collective-permute-start(f32[256,256]{1,0:T(8,128)S(1)} %collective-permute-done.15.refs_5_), channel_id=1, source_target_pairs={{0,4},{1,3},{4,8},{5,1},{8,12},{9,5},{12,14},{13,9},{14,10},{15,13... | collective-permute-start | bytes 786440 | tf_op jit(solution)/shard_map/ppermute | solution.py:382
  62.4 6.4 %collective-permute-start.18 = (f32[256,256]{1,0:T(8,128)S(1)}, f32[256,256]{1,0:T(8,128)S(1)}, u32[]{:S(2)}, u32[]{:S(2)}) collective-permute-start(f32[256,256]{1,0:T(8,128)S(1)} %collective-permute-done.16.refs_6_), channel_id=1, source_target_pairs={{0,4},{1,3},{4,8},{5,1},{8,12},{9,5},{12,14},{13,9},{14,10},{15,13... | collective-permute-start | bytes 786440 | tf_op jit(solution)/shard_map/ppermute | solution.py:383
  70.1 8.1 %copy-start = (f32[1,256,256]{2,1,0:T(8,128)S(1)}, f32[1,256,256]{2,1,0:T(8,128)}, u32[]{:S(2)}) copy-start(f32[1,256,256]{2,1,0:T(8,128)} %param.5) | copy-start | bytes 786436
  70.2 8.0 %collective-permute-start.19 = (f32[256,768]{1,0:T(8,128)S(1)}, f32[256,768]{1,0:T(8,128)S(1)}, u32[]{:S(2)}, u32[]{:S(2)}) collective-permute-start(f32[256,768]{1,0:T(8,128)S(1)} %get-tuple-element.54), channel_id=1, source_target_pairs={{0,1},{1,0},{2,3},{3,2},{4,5},{5,4},{6,7},{7,6},{8,9},{9,8},{10,11... | collective-permute-start | bytes 2359304 | tf_op jit(solution)/shard_map/ppermute | solution.py:395
  70.2 6.4 %collective-permute-start.20 = (f32[256,256]{1,0:T(8,128)S(1)}, f32[256,256]{1,0:T(8,128)S(1)}, u32[]{:S(2)}, u32[]{:S(2)}) collective-permute-start(f32[256,256]{1,0:T(8,128)S(1)} %collective-permute-done.17.refs_7_), channel_id=1, source_target_pairs={{0,4},{1,3},{4,8},{5,1},{8,12},{9,5},{12,14},{13,9},{14,10},{15,13... | collective-permute-start | bytes 786440 | tf_op jit(solution)/shard_map/ppermute | solution.py:387
  76.7 1.5 %collective-permute-start.21 = (f32[256,256]{1,0:T(8,128)S(1)}, f32[256,256]{1,0:T(8,128)S(1)}, u32[]{:S(2)}, u32[]{:S(2)}) collective-permute-start(f32[256,256]{1,0:T(8,128)S(1)} %collective-permute-done.20.refs_2_), channel_id=1, source_target_pairs={{0,1},{1,0},{2,3},{3,2},{4,5},{5,4},{6,7},{7,6},{8,9},{9,8},{10,11... | collective-permute-start | bytes 786440 | tf_op jit(solution)/shard_map/ppermute | solution.py:396
  80.0 1.6 %collective-permute-start.23 = (f32[256,256]{1,0:T(8,128)S(1)}, f32[256,256]{1,0:T(8,128)S(1)}, u32[]{:S(2)}, u32[]{:S(2)}) collective-permute-start(f32[256,256]{1,0:T(8,128)S(1)} %shard_map.73.refs_1_), channel_id=1, source_target_pairs={{0,1},{1,0},{2,3},{3,2},{4,5},{5,4},{6,7},{7,6},{8,9},{9,8},{10,11... | collective-permute-start | bytes 786440 | tf_op jit(solution)/shard_map/ppermute | solution.py:379
  80.2 6.4 %collective-permute-start.22 = (f32[256,256]{1,0:T(8,128)S(1)}, f32[256,256]{1,0:T(8,128)S(1)}, u32[]{:S(2)}, u32[]{:S(2)}) collective-permute-start(f32[256,256]{1,0:T(8,128)S(1)} %shard_map.73.refs_1_), channel_id=1, source_target_pairs={{0,4},{1,3},{4,8},{5,1},{8,12},{9,5},{12,14},{13,9},{14,10},{15,13... | collective-permute-start | bytes 786440 | tf_op jit(solution)/shard_map/ppermute | solution.py:382
  81.6 7.8 %collective-permute-start.24 = (f32[256,256]{1,0:T(8,128)S(1)}, f32[256,256]{1,0:T(8,128)S(1)}, u32[]{:S(2)}, u32[]{:S(2)}) collective-permute-start(f32[256,256]{1,0:T(8,128)S(1)} %collective-permute-done.23.refs_2_), channel_id=1, source_target_pairs={{0,4},{1,3},{4,8},{5,1},{8,12},{9,5},{12,14},{13,9},{14,10},{15,13... | collective-permute-start | bytes 786440 | tf_op jit(solution)/shard_map/ppermute | solution.py:383
  86.6 6.4 %collective-permute-start.25 = (f32[256,256]{1,0:T(8,128)S(1)}, f32[256,256]{1,0:T(8,128)S(1)}, u32[]{:S(2)}, u32[]{:S(2)}) collective-permute-start(f32[256,256]{1,0:T(8,128)S(1)} %collective-permute-done.22.refs_3_), channel_id=1, source_target_pairs={{0,4},{1,3},{4,8},{5,1},{8,12},{9,5},{12,14},{13,9},{14,10},{15,13... | collective-permute-start | bytes 786440 | tf_op jit(solution)/shard_map/ppermute | solution.py:382
  89.4 6.4 %collective-permute-start.26 = (f32[256,256]{1,0:T(8,128)S(1)}, f32[256,256]{1,0:T(8,128)S(1)}, u32[]{:S(2)}, u32[]{:S(2)}) collective-permute-start(f32[256,256]{1,0:T(8,128)S(1)} %collective-permute-done.24.refs_4_), channel_id=1, source_target_pairs={{0,4},{1,3},{4,8},{5,1},{8,12},{9,5},{12,14},{13,9},{14,10},{15,13... | collective-permute-start | bytes 786440 | tf_op jit(solution)/shard_map/ppermute | solution.py:383
  93.0 6.4 %collective-permute-start.27 = (f32[256,256]{1,0:T(8,128)S(1)}, f32[256,256]{1,0:T(8,128)S(1)}, u32[]{:S(2)}, u32[]{:S(2)}) collective-permute-start(f32[256,256]{1,0:T(8,128)S(1)} %collective-permute-done.25.refs_5_), channel_id=1, source_target_pairs={{0,4},{1,3},{4,8},{5,1},{8,12},{9,5},{12,14},{13,9},{14,10},{15,13... | collective-permute-start | bytes 786440 | tf_op jit(solution)/shard_map/ppermute | solution.py:382
  95.8 6.4 %collective-permute-start.28 = (f32[256,256]{1,0:T(8,128)S(1)}, f32[256,256]{1,0:T(8,128)S(1)}, u32[]{:S(2)}, u32[]{:S(2)}) collective-permute-start(f32[256,256]{1,0:T(8,128)S(1)} %collective-permute-done.26.refs_6_), channel_id=1, source_target_pairs={{0,4},{1,3},{4,8},{5,1},{8,12},{9,5},{12,14},{13,9},{14,10},{15,13... | collective-permute-start | bytes 786440 | tf_op jit(solution)/shard_map/ppermute | solution.py:383
  99.4 6.4 %collective-permute-start.30 = (f32[256,256]{1,0:T(8,128)S(1)}, f32[256,256]{1,0:T(8,128)S(1)}, u32[]{:S(2)}, u32[]{:S(2)}) collective-permute-start(f32[256,256]{1,0:T(8,128)S(1)} %collective-permute-done.27.refs_7_), channel_id=1, source_target_pairs={{0,4},{1,3},{4,8},{5,1},{8,12},{9,5},{12,14},{13,9},{14,10},{15,13... | collective-permute-start | bytes 786440 | tf_op jit(solution)/shard_map/ppermute | solution.py:387
  103.0 2.8 %collective-permute-start.29 = (f32[256,256]{1,0:T(8,128)S(1)}, f32[256,256]{1,0:T(8,128)S(1)}, u32[]{:S(2)}, u32[]{:S(2)}) collective-permute-start(f32[256,256]{1,0:T(8,128)S(1)} %get-tuple-element.60), channel_id=1, source_target_pairs={{0,1},{1,0},{2,3},{3,2},{4,5},{5,4},{6,7},{7,6},{8,9},{9,8},{10,11... | collective-permute-start | bytes 786440 | tf_op jit(solution)/shard_map/ppermute | solution.py:395
  105.7 1.5 %collective-permute-start.31 = (f32[256,256]{1,0:T(8,128)S(1)}, f32[256,256]{1,0:T(8,128)S(1)}, u32[]{:S(2)}, u32[]{:S(2)}) collective-permute-start(f32[256,256]{1,0:T(8,128)S(1)} %collective-permute-done.30.refs_2_), channel_id=1, source_target_pairs={{0,1},{1,0},{2,3},{3,2},{4,5},{5,4},{6,7},{7,6},{8,9},{9,8},{10,11... | collective-permute-start | bytes 786440 | tf_op jit(solution)/shard_map/ppermute | solution.py:396
  114.6 1.6 %collective-permute-start.33 = (f32[256,256]{1,0:T(8,128)S(1)}, f32[256,256]{1,0:T(8,128)S(1)}, u32[]{:S(2)}, u32[]{:S(2)}) collective-permute-start(f32[256,256]{1,0:T(8,128)S(1)} %shard_map.75.refs_1_), channel_id=1, source_target_pairs={{0,1},{1,0},{2,3},{3,2},{4,5},{5,4},{6,7},{7,6},{8,9},{9,8},{10,11... | collective-permute-start | bytes 786440 | tf_op jit(solution)/shard_map/ppermute | solution.py:379
  114.8 6.4 %collective-permute-start.32 = (f32[256,256]{1,0:T(8,128)S(1)}, f32[256,256]{1,0:T(8,128)S(1)}, u32[]{:S(2)}, u32[]{:S(2)}) collective-permute-start(f32[256,256]{1,0:T(8,128)S(1)} %shard_map.75.refs_1_), channel_id=1, source_target_pairs={{0,4},{1,3},{4,8},{5,1},{8,12},{9,5},{12,14},{13,9},{14,10},{15,13... | collective-permute-start | bytes 786440 | tf_op jit(solution)/shard_map/ppermute | solution.py:382
  116.2 7.8 %collective-permute-start.34 = (f32[256,256]{1,0:T(8,128)S(1)}, f32[256,256]{1,0:T(8,128)S(1)}, u32[]{:S(2)}, u32[]{:S(2)}) collective-permute-start(f32[256,256]{1,0:T(8,128)S(1)} %collective-permute-done.33.refs_2_), channel_id=1, source_target_pairs={{0,4},{1,3},{4,8},{5,1},{8,12},{9,5},{12,14},{13,9},{14,10},{15,13... | collective-permute-start | bytes 786440 | tf_op jit(solution)/shard_map/ppermute | solution.py:383
  121.2 6.4 %collective-permute-start.35 = (f32[256,256]{1,0:T(8,128)S(1)}, f32[256,256]{1,0:T(8,128)S(1)}, u32[]{:S(2)}, u32[]{:S(2)}) collective-permute-start(f32[256,256]{1,0:T(8,128)S(1)} %collective-permute-done.32.refs_3_), channel_id=1, source_target_pairs={{0,4},{1,3},{4,8},{5,1},{8,12},{9,5},{12,14},{13,9},{14,10},{15,13... | collective-permute-start | bytes 786440 | tf_op jit(solution)/shard_map/ppermute | solution.py:382
  124.0 6.4 %collective-permute-start.36 = (f32[256,256]{1,0:T(8,128)S(1)}, f32[256,256]{1,0:T(8,128)S(1)}, u32[]{:S(2)}, u32[]{:S(2)}) collective-permute-start(f32[256,256]{1,0:T(8,128)S(1)} %collective-permute-done.34.refs_4_), channel_id=1, source_target_pairs={{0,4},{1,3},{4,8},{5,1},{8,12},{9,5},{12,14},{13,9},{14,10},{15,13... | collective-permute-start | bytes 786440 | tf_op jit(solution)/shard_map/ppermute | solution.py:383
  127.5 6.4 %collective-permute-start.37 = (f32[256,256]{1,0:T(8,128)S(1)}, f32[256,256]{1,0:T(8,128)S(1)}, u32[]{:S(2)}, u32[]{:S(2)}) collective-permute-start(f32[256,256]{1,0:T(8,128)S(1)} %collective-permute-done.35.refs_5_), channel_id=1, source_target_pairs={{0,4},{1,3},{4,8},{5,1},{8,12},{9,5},{12,14},{13,9},{14,10},{15,13... | collective-permute-start | bytes 786440 | tf_op jit(solution)/shard_map/ppermute | solution.py:382
  130.3 6.4 %collective-permute-start.38 = (f32[256,256]{1,0:T(8,128)S(1)}, f32[256,256]{1,0:T(8,128)S(1)}, u32[]{:S(2)}, u32[]{:S(2)}) collective-permute-start(f32[256,256]{1,0:T(8,128)S(1)} %collective-permute-done.36.refs_6_), channel_id=1, source_target_pairs={{0,4},{1,3},{4,8},{5,1},{8,12},{9,5},{12,14},{13,9},{14,10},{15,13... | collective-permute-start | bytes 786440 | tf_op jit(solution)/shard_map/ppermute | solution.py:383
  138.1 8.0 %collective-permute-start.39 = (f32[256,768]{1,0:T(8,128)S(1)}, f32[256,768]{1,0:T(8,128)S(1)}, u32[]{:S(2)}, u32[]{:S(2)}) collective-permute-start(f32[256,768]{1,0:T(8,128)S(1)} %get-tuple-element.65), channel_id=1, source_target_pairs={{0,1},{1,0},{2,3},{3,2},{4,5},{5,4},{6,7},{7,6},{8,9},{9,8},{10,11... | collective-permute-start | bytes 2359304 | tf_op jit(solution)/shard_map/ppermute | solution.py:395
  138.2 6.4 %collective-permute-start.40 = (f32[256,256]{1,0:T(8,128)S(1)}, f32[256,256]{1,0:T(8,128)S(1)}, u32[]{:S(2)}, u32[]{:S(2)}) collective-permute-start(f32[256,256]{1,0:T(8,128)S(1)} %collective-permute-done.37.refs_7_), channel_id=1, source_target_pairs={{0,4},{1,3},{4,8},{5,1},{8,12},{9,5},{12,14},{13,9},{14,10},{15,13... | collective-permute-start | bytes 786440 | tf_op jit(solution)/shard_map/ppermute | solution.py:387
  144.6 1.5 %collective-permute-start.41 = (f32[256,256]{1,0:T(8,128)S(1)}, f32[256,256]{1,0:T(8,128)S(1)}, u32[]{:S(2)}, u32[]{:S(2)}) collective-permute-start(f32[256,256]{1,0:T(8,128)S(1)} %collective-permute-done.40.refs_2_), channel_id=1, source_target_pairs={{0,1},{1,0},{2,3},{3,2},{4,5},{5,4},{6,7},{7,6},{8,9},{9,8},{10,11... | collective-permute-start | bytes 786440 | tf_op jit(solution)/shard_map/ppermute | solution.py:396

commit v6 on v4

--- a/solution.py
+++ b/solution.py
@@ -101,7 +101,7 @@
 
     ahead = weight_ref[ORDER : ORDER + 1, :] * field
     before = ahead - ahead
-    result, _, second = lax.fori_loop(0, ORDER, body, (ahead, before, before), unroll=ORDER // 2)
+    result, _, second = lax.fori_loop(0, ORDER, body, (ahead, before, before), unroll=True)
     return 0.5 * (result - second)
 
 
@@ -130,12 +130,6 @@
     mean_ref[...] = mean_level
     field = joined(weight_ref, base, 0, sources, slice(0, side_x))
     out_ref[...] = chebyshev_sum(field, mean_level, cos_ref, hop_refs, row_ref)
-
-
-def next_spectral_kernel(weight_ref, base, keep_ref, other_ref, last_ref, last_other_ref, cos_ref, *refs):
-    hop_refs, (mean_ref, add_ref, out_ref, row_ref) = refs[:4], refs[4:]
-    field = joined(weight_ref, base, 0, (keep_ref, other_ref, last_ref, last_other_ref), slice(None))
-    out_ref[...] = chebyshev_sum(field, mean_ref[...], cos_ref, hop_refs, row_ref) + add_ref[...]
 
 
 def pack_kernel(noise_ref, level_ref, packed_ref, damp_ref, held_ref, noise_sem, level_sem, *, scale):
@@ -400,7 +394,7 @@
     )(noise, phonon_level)
     parts, (weights, hops) = around(packed, forward, 1, (weights, hops))
     damp_next = lax.ppermute(damp, "tm", [(i, (i - 1) % length) for i in range(length)])
-    first_kernel, next_kernel = based(first_spectral_kernel, forward), based(next_spectral_kernel, forward)
+    first_kernel = based(first_spectral_kernel, forward)
     finish = based(finish_kernel, back)
     first_outs = (field_shape, shape(1, side_y))
     first, mean_level = call(first_kernel, first_outs, 9, scratch, work, 1)(*parts, cosine, *hops)
@@ -408,8 +402,9 @@
     beside = (weights,)
     parts, beside = around(first, back, 3, beside)
     (second_residual,) = call(finish, (field_shape,), 11, scalars=1)(*parts, damp, damp_next, noise, *hops)
-    parts, beside = around(second_residual, forward, 1, beside)
-    total = call(next_kernel, field_shape, 11, scratch, work, 1)(*parts, cosine, *hops, mean_level, first)
+    field_table = table_parts(basis, side_x // length)
+    field = exchange(call(transform_kernel, field_shape, 3)(exchange(second_residual, "tm"), *field_table), "tm")
+    total = call(chebyshev_kernel, field_shape, 8, scratch, work)(field, mean_level, cosine, *hops, first)
     parts, beside = around(total, back, 3, beside)
     residual, result = call(finish, (field_shape,) * 2, 11, scalars=1)(*parts, damp, damp_next, noise, *hops)
     return result, residual

time: 145 us -> 142 us (0.979)
  waiting for transfers between devices: 96 us -> 65.8 us
  blocking collectives: 0 us -> 25.5 us
  starting transfers between devices: 20.8 us -> 24.4 us
  Pallas kernels: 26 us -> 24.4 us
    all_to_all x0 -> x2, blocking collectives: none -> 25.5 us  [exchange(): lax.all_to_all(blocks, axis, split_axis=0, concat_axis=0, tiled=True)]
    ppermute x12 -> x9, waiting for transfers between devices: 40.8 us -> 27 us  [around(): own = lax.ppermute(own, 'tm', hop)]
    ppermute x12 -> x9, waiting for transfers between devices: 28.7 us -> 19 us  [around(): partner = lax.ppermute(partner, 'tm', hop)]
    ppermute x4 -> x3, waiting for transfers between devices: 17.7 us -> 14.4 us  [around(): last = lax.ppermute(own, 'tm', hop)]
    ppermute x4 -> x3, waiting for transfers between devices: 4.22 us -> 2.29 us  [around(): partner = lax.ppermute(own, 'tm', swap)]
    ppermute x12 -> x9, starting transfers between devices: 6.91 us -> 8.82 us  [around(): own = lax.ppermute(own, 'tm', hop)]
    ppermute x12 -> x9, starting transfers between devices: 5.12 us -> 6.67 us  [around(): partner = lax.ppermute(partner, 'tm', hop)]
    ppermute x4 -> x3, waiting for transfers between devices: 4.6 us -> 3.07 us  [around(): last_other = lax.ppermute(last, 'tm', swap)]
  transfers between devices with their start and end apart: 41 -> 31, of which waited for: 34 -> 25; matrix products, arithmetic and copies ran while one was open for 0% -> 0% of each run, Pallas kernels for 7% -> 6%
where the time goes in v6:
time: 142 us
  waiting for transfers between devices  65.8 us (46%)
  blocking collectives  25.5 us (18%)
  Pallas kernels  24.4 us (17%)
  starting transfers between devices  24.4 us (17%)
    ppermute x9, waiting for transfers between devices, around(): own = lax.ppermute(own, 'tm', hop)  27 us
    all_to_all x2, blocking collectives, exchange(): lax.all_to_all(blocks, axis, split_axis=0, concat_axis=0, tiled=True)  25.5 us
    ppermute x9, waiting for transfers between devices, around(): partner = lax.ppermute(partner, 'tm', hop)  19 us
    ppermute x3, waiting for transfers between devices, around(): last = lax.ppermute(own, 'tm', hop)  14.4 us
    ppermute x9, starting transfers between devices, around(): own = lax.ppermute(own, 'tm', hop)  8.82 us
    pallas_call x1, Pallas kernels, by_ring(): call(first_kernel, first_outs, 9, scratch, work, 1)(*parts, cosine, *hops)  7.13 us
    ppermute x9, starting transfers between devices, around(): partner = lax.ppermute(partner, 'tm', hop)  6.67 us
    pallas_call x1, Pallas kernels, by_ring(): call(chebyshev_kernel, field_shape, 8, scratch, work)  6.49 us
  transfers between devices with their start and end apart: 31, of which 25 were waited for; matrix products, arithmetic and copies ran while one was open for 0% of the time, Pallas kernels for 6%

profile of v6, /device:TPU:0, one launch (start us, length us, event | category | flops | bytes accessed | tf_op | source)
XLA Modules:
  0.0 141.8 jit_solution(6515742367632752724)
XLA Ops:
  0.7 2.0 %shard_map.86 = (f32[264,256]{1,0:T(8,128)}, f32[256,256]{1,0:T(8,128)}) custom-call(f32[256,256]{1,0:T(8,128)} %bitcast.10, s32[256,256]{1,0:T(8,128)} %bitcast.17), custom_call_target="tpu_custom_call" | custom-call | tf_op jit(solution)/shard_map/pallas_call | solution.py:387
  3.2 2.6 %collective-permute-start = (f32[264,256]{1,0:T(8,128)}, f32[264,256]{1,0:T(8,128)S(1)}, u32[]{:S(2)}, u32[]{:S(2)}) collective-permute-start(f32[264,256]{1,0:T(8,128)} %get-tuple-element.30.refs_1_), channel_id=1, source_target_pairs={{0,4},{1,3},{4,8},{5,1},{8,12},{9,5},{12,14},{13,9},{14,10},{15,13... | collective-permute-start | bytes 811016 | tf_op jit(solution)/shard_map/ppermute | solution.py:358
  5.8 0.7 shard_map.87
  6.5 0.7 dynamic-slice_bitcast_fusion.refs_0_.weight_ref
  7.2 1.6 %collective-permute-start.2 = (f32[264,256]{1,0:T(8,128)S(1)}, f32[264,256]{1,0:T(8,128)S(1)}, u32[]{:S(2)}, u32[]{:S(2)}) collective-permute-start(f32[264,256]{1,0:T(8,128)S(1)} %collective-permute-done.1.refs_2_), channel_id=1, source_target_pairs={{0,4},{1,3},{4,8},{5,1},{8,12},{9,5},{12,14},{13,9},{14,10},{15,13... | collective-permute-start | bytes 811016 | tf_op jit(solution)/shard_map/ppermute | solution.py:359
  8.7 1.6 %collective-permute-done.refs_3_ = f32[264,256]{1,0:T(8,128)S(1)} collective-permute-done((f32[264,256]{1,0:T(8,128)}, f32[264,256]{1,0:T(8,128)S(1)}, u32[]{:S(2)}, u32[]{:S(2)}) %collective-permute-start) | collective-permute-done | bytes 270368 | tf_op jit(solution)/shard_map/ppermute | solution.py:358
  10.4 2.1 %collective-permute-start.3 = (f32[264,256]{1,0:T(8,128)S(1)}, f32[264,256]{1,0:T(8,128)S(1)}, u32[]{:S(2)}, u32[]{:S(2)}) collective-permute-start(f32[264,256]{1,0:T(8,128)S(1)} %collective-permute-done.refs_3_), channel_id=1, source_target_pairs={{0,4},{1,3},{4,8},{5,1},{8,12},{9,5},{12,14},{13,9},{14,10},{15,13... | collective-permute-start | bytes 811016 | tf_op jit(solution)/shard_map/ppermute | solution.py:358
  12.5 1.2 collective-permute-done.2.refs_4_
  13.6 1.7 %collective-permute-start.4 = (f32[264,256]{1,0:T(8,128)S(1)}, f32[264,256]{1,0:T(8,128)S(1)}, u32[]{:S(2)}, u32[]{:S(2)}) collective-permute-start(f32[264,256]{1,0:T(8,128)S(1)} %collective-permute-done.2.refs_4_), channel_id=1, source_target_pairs={{0,4},{1,3},{4,8},{5,1},{8,12},{9,5},{12,14},{13,9},{14,10},{15,13... | collective-permute-start | bytes 811016 | tf_op jit(solution)/shard_map/ppermute | solution.py:359
  15.4 1.5 %collective-permute-done.3.refs_5_ = f32[264,256]{1,0:T(8,128)S(1)} collective-permute-done((f32[264,256]{1,0:T(8,128)S(1)}, f32[264,256]{1,0:T(8,128)S(1)}, u32[]{:S(2)}, u32[]{:S(2)}) %collective-permute-start.3) | collective-permute-done | bytes 270368 | tf_op jit(solution)/shard_map/ppermute | solution.py:358
  16.9 2.1 %collective-permute-start.5 = (f32[264,256]{1,0:T(8,128)S(1)}, f32[264,256]{1,0:T(8,128)S(1)}, u32[]{:S(2)}, u32[]{:S(2)}) collective-permute-start(f32[264,256]{1,0:T(8,128)S(1)} %collective-permute-done.3.refs_5_), channel_id=1, source_target_pairs={{0,4},{1,3},{4,8},{5,1},{8,12},{9,5},{12,14},{13,9},{14,10},{15,13... | collective-permute-start | bytes 811016 | tf_op jit(solution)/shard_map/ppermute | solution.py:358
  18.9 1.2 collective-permute-done.4.refs_6_
  20.1 1.7 %collective-permute-start.6 = (f32[264,256]{1,0:T(8,128)S(1)}, f32[264,256]{1,0:T(8,128)S(1)}, u32[]{:S(2)}, u32[]{:S(2)}) collective-permute-start(f32[264,256]{1,0:T(8,128)S(1)} %collective-permute-done.4.refs_6_), channel_id=1, source_target_pairs={{0,4},{1,3},{4,8},{5,1},{8,12},{9,5},{12,14},{13,9},{14,10},{15,13... | collective-permute-start | bytes 811016 | tf_op jit(solution)/shard_map/ppermute | solution.py:359
  21.8 1.5 %collective-permute-done.5.refs_7_ = f32[264,256]{1,0:T(8,128)S(1)} collective-permute-done((f32[264,256]{1,0:T(8,128)S(1)}, f32[264,256]{1,0:T(8,128)S(1)}, u32[]{:S(2)}, u32[]{:S(2)}) %collective-permute-start.5) | collective-permute-done | bytes 270368 | tf_op jit(solution)/shard_map/ppermute | solution.py:358
  23.3 2.1 %collective-permute-start.8 = (f32[264,256]{1,0:T(8,128)S(1)}, f32[264,256]{1,0:T(8,128)S(1)}, u32[]{:S(2)}, u32[]{:S(2)}) collective-permute-start(f32[264,256]{1,0:T(8,128)S(1)} %collective-permute-done.5.refs_7_), channel_id=1, source_target_pairs={{0,4},{1,3},{4,8},{5,1},{8,12},{9,5},{12,14},{13,9},{14,10},{15,13... | collective-permute-start | bytes 811016 | tf_op jit(solution)/shard_map/ppermute | solution.py:363
  25.4 1.2 collective-permute-done.6.refs_8_
  26.6 0.8 shard_map.88
  27.5 2.3 %collective-permute-done.8.refs_2_ = f32[264,256]{1,0:T(8,128)S(1)} collective-permute-done((f32[264,256]{1,0:T(8,128)S(1)}, f32[264,256]{1,0:T(8,128)S(1)}, u32[]{:S(2)}, u32[]{:S(2)}) %collective-permute-start.8) | collective-permute-done | bytes 270368 | tf_op jit(solution)/shard_map/ppermute | solution.py:363
  29.8 5.2 %collective-permute-start.10 = (f32[256,256]{1,0:T(8,128)S(1)}, f32[256,256]{1,0:T(8,128)S(1)}, u32[]{:S(2)}, u32[]{:S(2)}) collective-permute-start(f32[256,256]{1,0:T(8,128)S(1)} %copy-done.1), channel_id=1, source_target_pairs={{0,15},{1,0},{2,1},{3,2},{4,3},{5,4},{6,5},{7,6},{8,7},{9,8},{10,9... | collective-permute-start | bytes 786440 | tf_op jit(solution)/shard_map/ppermute | solution.py:396
  35.1 7.1 %shard_map.89 = (f32[256,256]{1,0:T(8,128)S(1)}, f32[1,256]{1,0:T(1,128)S(1)}) custom-call(f32[64]{0:T(128)S(1)} %dynamic-slice_bitcast_fusion.refs_0_.weight_ref, f32[264,256]{1,0:T(8,128)S(1)} %get-tuple-element.37.refs_0_, f32[264,256]{1,0:T(8,128)S(1)} %collective-permute-done.7.refs_1_, f32[264,256]{1,0:T(8,128)S(1)} %collective-permute-done.8.refs_2_, ...), custom_call_target="tpu_custom_call" | custom-call | flops 4026531840 | tf_op jit(solution)/shard_map/pallas_call | solution.py:400
  42.4 1.5 %collective-permute-done.12.refs_2_ = f32[256,256]{1,0:T(8,128)S(1)} collective-permute-done((f32[256,256]{1,0:T(8,128)S(1)}, f32[256,256]{1,0:T(8,128)S(1)}, u32[]{:S(2)}, u32[]{:S(2)}) %collective-permute-start.12) | collective-permute-done | bytes 262176 | tf_op jit(solution)/shard_map/ppermute | solution.py:355
  43.8 4.9 %collective-permute-done.11.refs_3_ = f32[256,256]{1,0:T(8,128)S(1)} collective-permute-done((f32[256,256]{1,0:T(8,128)S(1)}, f32[256,256]{1,0:T(8,128)S(1)}, u32[]{:S(2)}, u32[]{:S(2)}) %collective-permute-start.11) | collective-permute-done | bytes 262176 | tf_op jit(solution)/shard_map/ppermute | solution.py:358
  48.7 2.8 %collective-permute-done.13.refs_4_ = f32[256,256]{1,0:T(8,128)S(1)} collective-permute-done((f32[256,256]{1,0:T(8,128)S(1)}, f32[256,256]{1,0:T(8,128)S(1)}, u32[]{:S(2)}, u32[]{:S(2)}) %collective-permute-start.13) | collective-permute-done | bytes 262176 | tf_op jit(solution)/shard_map/ppermute | solution.py:359
  51.5 3.6 %collective-permute-done.14.refs_5_ = f32[256,256]{1,0:T(8,128)S(1)} collective-permute-done((f32[256,256]{1,0:T(8,128)S(1)}, f32[256,256]{1,0:T(8,128)S(1)}, u32[]{:S(2)}, u32[]{:S(2)}) %collective-permute-start.14) | collective-permute-done | bytes 262176 | tf_op jit(solution)/shard_map/ppermute | solution.py:358
  55.1 2.8 %collective-permute-done.15.refs_6_ = f32[256,256]{1,0:T(8,128)S(1)} collective-permute-done((f32[256,256]{1,0:T(8,128)S(1)}, f32[256,256]{1,0:T(8,128)S(1)}, u32[]{:S(2)}, u32[]{:S(2)}) %collective-permute-start.15) | collective-permute-done | bytes 262176 | tf_op jit(solution)/shard_map/ppermute | solution.py:359
  57.9 3.6 %collective-permute-done.16.refs_7_ = f32[256,256]{1,0:T(8,128)S(1)} collective-permute-done((f32[256,256]{1,0:T(8,128)S(1)}, f32[256,256]{1,0:T(8,128)S(1)}, u32[]{:S(2)}, u32[]{:S(2)}) %collective-permute-start.16) | collective-permute-done | bytes 262176 | tf_op jit(solution)/shard_map/ppermute | solution.py:358
  61.5 2.8 %collective-permute-done.17.refs_8_ = f32[256,256]{1,0:T(8,128)S(1)} collective-permute-done((f32[256,256]{1,0:T(8,128)S(1)}, f32[256,256]{1,0:T(8,128)S(1)}, u32[]{:S(2)}, u32[]{:S(2)}) %collective-permute-start.17) | collective-permute-done | bytes 262176 | tf_op jit(solution)/shard_map/ppermute | solution.py:359
  64.3 1.4 shard_map.90
  65.8 6.4 %collective-permute-done.19.refs_2_ = f32[256,256]{1,0:T(8,128)S(1)} collective-permute-done((f32[256,256]{1,0:T(8,128)S(1)}, f32[256,256]{1,0:T(8,128)S(1)}, u32[]{:S(2)}, u32[]{:S(2)}) %collective-permute-start.19) | collective-permute-done | bytes 262176 | tf_op jit(solution)/shard_map/ppermute | solution.py:363
  72.1 1.5 %collective-permute-done.20.refs_3_ = f32[256,256]{1,0:T(8,128)S(1)} collective-permute-done((f32[256,256]{1,0:T(8,128)S(1)}, f32[256,256]{1,0:T(8,128)S(1)}, u32[]{:S(2)}, u32[]{:S(2)}) %collective-permute-start.20) | collective-permute-done | bytes 262176 | tf_op jit(solution)/shard_map/ppermute | solution.py:372
  73.7 1.8 %shard_map.91 = f32[256,256]{1,0:T(8,128)S(1)} custom-call(f32[64]{0:T(128)S(1)} %dynamic-slice_bitcast_fusion.refs_0_.weight_ref, f32[256,768]{1,0:T(8,128)S(1)} %get-tuple-element.48.refs_0_, f32[256,768]{1,0:T(8,128)S(1)} %collective-permute-done.18.refs_1_, f32[256,256]{1,0:T(8,128)S(1)} %collective-permute-done.19.refs_2_, ...), custom_call_target="tpu_custom_call" | custom-call | tf_op jit(solution)/shard_map/pallas_call | solution.py:404
  75.5 12.8 %all_to_all.10 = f32[16,16,256]{2,1,0:T(8,128)S(1)} all-to-all(f32[16,16,256]{2,1,0:T(8,128)S(1)} %bitcast.13), channel_id=1, replica_groups=mesh['grp'=2,'tm'=16] {'tm'}, dimensions={0} | all-to-all | bytes 524288 | tf_op jit(solution)/shard_map/all_to_all | solution.py:285
  88.6 12.7 %all_to_all.11 = f32[16,16,256]{2,1,0:T(8,128)S(1)} all-to-all(f32[16,16,256]{2,1,0:T(8,128)S(1)} %bitcast.15), channel_id=1, replica_groups=mesh['grp'=2,'tm'=16] {'tm'}, dimensions={0} | all-to-all | bytes 524288 | tf_op jit(solution)/shard_map/all_to_all | solution.py:285
  101.3 6.5 %shard_map.93.refs_1_ = f32[256,256]{1,0:T(8,128)S(1)} custom-call(f32[256,256]{1,0:T(8,128)S(1)} %bitcast.16, f32[1,256]{1,0:T(1,128)S(1)} %get-tuple-element.51.refs_1_, f32[1,256]{1,0:T(1,128)S(1)} %broadcast_in_dim.9.refs_4_.refs_2_, bf16[512,256]{1,0:T(8,128)(2,1)S(1)} %get-tuple-element.39.refs_5_.refs_7_.refs_3_, ...), custom_call_target="tpu_custom_call" | custom-call | flops 4026531840 | tf_op jit(solution)/shard_map/pallas_call | solution.py:407
  107.9 0.7 collective-permute-start.21
  108.6 0.8 collective-permute-done.22.refs_2_
  109.8 4.6 %collective-permute-done.21.refs_3_ = f32[256,256]{1,0:T(8,128)S(1)} collective-permute-done((f32[256,256]{1,0:T(8,128)S(1)}, f32[256,256]{1,0:T(8,128)S(1)}, u32[]{:S(2)}, u32[]{:S(2)}) %collective-permute-start.21) | collective-permute-done | bytes 262176 | tf_op jit(solution)/shard_map/ppermute | solution.py:358
  114.3 0.6 collective-permute-start.24
  115.0 2.2 %collective-permute-done.23.refs_4_ = f32[256,256]{1,0:T(8,128)S(1)} collective-permute-done((f32[256,256]{1,0:T(8,128)S(1)}, f32[256,256]{1,0:T(8,128)S(1)}, u32[]{:S(2)}, u32[]{:S(2)}) %collective-permute-start.23) | collective-permute-done | bytes 262176 | tf_op jit(solution)/shard_map/ppermute | solution.py:359
  117.8 2.9 %collective-permute-done.24.refs_5_ = f32[256,256]{1,0:T(8,128)S(1)} collective-permute-done((f32[256,256]{1,0:T(8,128)S(1)}, f32[256,256]{1,0:T(8,128)S(1)}, u32[]{:S(2)}, u32[]{:S(2)}) %collective-permute-start.24) | collective-permute-done | bytes 262176 | tf_op jit(solution)/shard_map/ppermute | solution.py:358
  121.4 2.2 %collective-permute-done.25.refs_6_ = f32[256,256]{1,0:T(8,128)S(1)} collective-permute-done((f32[256,256]{1,0:T(8,128)S(1)}, f32[256,256]{1,0:T(8,128)S(1)}, u32[]{:S(2)}, u32[]{:S(2)}) %collective-permute-start.25) | collective-permute-done | bytes 262176 | tf_op jit(solution)/shard_map/ppermute | solution.py:359
  124.2 2.9 %collective-permute-done.26.refs_7_ = f32[256,256]{1,0:T(8,128)S(1)} collective-permute-done((f32[256,256]{1,0:T(8,128)S(1)}, f32[256,256]{1,0:T(8,128)S(1)}, u32[]{:S(2)}, u32[]{:S(2)}) %collective-permute-start.26) | collective-permute-done | bytes 262176 | tf_op jit(solution)/shard_map/ppermute | solution.py:358
  127.1 2.8 %collective-permute-done.27.refs_8_ = f32[256,256]{1,0:T(8,128)S(1)} collective-permute-done((f32[256,256]{1,0:T(8,128)S(1)}, f32[256,256]{1,0:T(8,128)S(1)}, u32[]{:S(2)}, u32[]{:S(2)}) %collective-permute-start.27) | collective-permute-done | bytes 262176 | tf_op jit(solution)/shard_map/ppermute | solution.py:359
  129.9 1.4 shard_map.94
  131.3 0.7 collective-permute-start.29
  132.0 5.7 %collective-permute-done.29.refs_2_ = f32[256,256]{1,0:T(8,128)S(1)} collective-permute-done((f32[256,256]{1,0:T(8,128)S(1)}, f32[256,256]{1,0:T(8,128)S(1)}, u32[]{:S(2)}, u32[]{:S(2)}) %collective-permute-start.29) | collective-permute-done | bytes 262176 | tf_op jit(solution)/shard_map/ppermute | solution.py:363
  137.8 1.5 %collective-permute-done.30.refs_3_ = f32[256,256]{1,0:T(8,128)S(1)} collective-permute-done((f32[256,256]{1,0:T(8,128)S(1)}, f32[256,256]{1,0:T(8,128)S(1)}, u32[]{:S(2)}, u32[]{:S(2)}) %collective-permute-start.30) | collective-permute-done | bytes 262176 | tf_op jit(solution)/shard_map/ppermute | solution.py:372
  139.3 2.5 %shard_map.95 = (f32[256,256]{1,0:T(8,128)}, f32[256,256]{1,0:T(8,128)}) custom-call(f32[64]{0:T(128)S(1)} %dynamic-slice_bitcast_fusion.refs_0_.weight_ref, f32[256,768]{1,0:T(8,128)S(1)} %get-tuple-element.54.refs_0_, f32[256,768]{1,0:T(8,128)S(1)} %collective-permute-done.28.refs_1_, f32[256,256]{1,0:T(8,128)S(1)} %collective-permute-done.29.refs_2_, ...), custom_call_target="tpu_custom_call" | custom-call | tf_op jit(solution)/shard_map/pallas_call | solution.py:409
  (42 shorter events, 3.6 us)
Async XLA Ops:
  0.6 5.2 %copy-start.3 = (f32[256,256]{1,0:T(8,128)S(1)}, f32[256,256]{1,0:T(8,128)}, u32[]{:S(2)}) copy-start(f32[256,256]{1,0:T(8,128)} %hop_x_ref.1) | copy-start | bytes 786436
  0.6 5.2 %copy-start.4 = (f32[256,256]{1,0:T(8,128)S(1)}, f32[256,256]{1,0:T(8,128)}, u32[]{:S(2)}) copy-start(f32[256,256]{1,0:T(8,128)} %hop_y_ref.1) | copy-start | bytes 786436
  2.6 4.6 %collective-permute-start.1 = (f32[264,256]{1,0:T(8,128)}, f32[264,256]{1,0:T(8,128)S(1)}, u32[]{:S(2)}, u32[]{:S(2)}) collective-permute-start(f32[264,256]{1,0:T(8,128)} %get-tuple-element.30.refs_1_), channel_id=1, source_target_pairs={{0,1},{1,0},{2,3},{3,2},{4,5},{5,4},{6,7},{7,6},{8,9},{9,8},{10,11... | collective-permute-start | bytes 811016 | tf_op jit(solution)/shard_map/ppermute | solution.py:355
  3.2 7.2 %collective-permute-start = (f32[264,256]{1,0:T(8,128)}, f32[264,256]{1,0:T(8,128)S(1)}, u32[]{:S(2)}, u32[]{:S(2)}) collective-permute-start(f32[264,256]{1,0:T(8,128)} %get-tuple-element.30.refs_1_), channel_id=1, source_target_pairs={{0,4},{1,3},{4,8},{5,1},{8,12},{9,5},{12,14},{13,9},{14,10},{15,13... | collective-permute-start | bytes 811016 | tf_op jit(solution)/shard_map/ppermute | solution.py:358
  5.8 20.8 %copy-start.2 = (f32[264,256]{1,0:T(8,128)S(1)}, f32[264,256]{1,0:T(8,128)}, u32[]{:S(2)}) copy-start(f32[264,256]{1,0:T(8,128)} %get-tuple-element.30.refs_1_) | copy-start | bytes 811012
  7.2 6.5 %collective-permute-start.2 = (f32[264,256]{1,0:T(8,128)S(1)}, f32[264,256]{1,0:T(8,128)S(1)}, u32[]{:S(2)}, u32[]{:S(2)}) collective-permute-start(f32[264,256]{1,0:T(8,128)S(1)} %collective-permute-done.1.refs_2_), channel_id=1, source_target_pairs={{0,4},{1,3},{4,8},{5,1},{8,12},{9,5},{12,14},{13,9},{14,10},{15,13... | collective-permute-start | bytes 811016 | tf_op jit(solution)/shard_map/ppermute | solution.py:359
  10.4 19.4 %copy-start.1 = (f32[256,256]{1,0:T(8,128)S(1)}, f32[256,256]{1,0:T(8,128)}, u32[]{:S(2)}) copy-start(f32[256,256]{1,0:T(8,128)} %get-tuple-element.44.refs_4_) | copy-start | bytes 786436
  10.4 6.5 %collective-permute-start.3 = (f32[264,256]{1,0:T(8,128)S(1)}, f32[264,256]{1,0:T(8,128)S(1)}, u32[]{:S(2)}, u32[]{:S(2)}) collective-permute-start(f32[264,256]{1,0:T(8,128)S(1)} %collective-permute-done.refs_3_), channel_id=1, source_target_pairs={{0,4},{1,3},{4,8},{5,1},{8,12},{9,5},{12,14},{13,9},{14,10},{15,13... | collective-permute-start | bytes 811016 | tf_op jit(solution)/shard_map/ppermute | solution.py:358
  13.6 6.5 %collective-permute-start.4 = (f32[264,256]{1,0:T(8,128)S(1)}, f32[264,256]{1,0:T(8,128)S(1)}, u32[]{:S(2)}, u32[]{:S(2)}) collective-permute-start(f32[264,256]{1,0:T(8,128)S(1)} %collective-permute-done.2.refs_4_), channel_id=1, source_target_pairs={{0,4},{1,3},{4,8},{5,1},{8,12},{9,5},{12,14},{13,9},{14,10},{15,13... | collective-permute-start | bytes 811016 | tf_op jit(solution)/shard_map/ppermute | solution.py:359
  16.9 6.5 %collective-permute-start.5 = (f32[264,256]{1,0:T(8,128)S(1)}, f32[264,256]{1,0:T(8,128)S(1)}, u32[]{:S(2)}, u32[]{:S(2)}) collective-permute-start(f32[264,256]{1,0:T(8,128)S(1)} %collective-permute-done.3.refs_5_), channel_id=1, source_target_pairs={{0,4},{1,3},{4,8},{5,1},{8,12},{9,5},{12,14},{13,9},{14,10},{15,13... | collective-permute-start | bytes 811016 | tf_op jit(solution)/shard_map/ppermute | solution.py:358
  20.1 6.5 %collective-permute-start.6 = (f32[264,256]{1,0:T(8,128)S(1)}, f32[264,256]{1,0:T(8,128)S(1)}, u32[]{:S(2)}, u32[]{:S(2)}) collective-permute-start(f32[264,256]{1,0:T(8,128)S(1)} %collective-permute-done.4.refs_6_), channel_id=1, source_target_pairs={{0,4},{1,3},{4,8},{5,1},{8,12},{9,5},{12,14},{13,9},{14,10},{15,13... | collective-permute-start | bytes 811016 | tf_op jit(solution)/shard_map/ppermute | solution.py:359
  23.3 6.5 %collective-permute-start.8 = (f32[264,256]{1,0:T(8,128)S(1)}, f32[264,256]{1,0:T(8,128)S(1)}, u32[]{:S(2)}, u32[]{:S(2)}) collective-permute-start(f32[264,256]{1,0:T(8,128)S(1)} %collective-permute-done.5.refs_7_), channel_id=1, source_target_pairs={{0,4},{1,3},{4,8},{5,1},{8,12},{9,5},{12,14},{13,9},{14,10},{15,13... | collective-permute-start | bytes 811016 | tf_op jit(solution)/shard_map/ppermute | solution.py:363
  27.4 7.6 %collective-permute-start.7 = (f32[264,256]{1,0:T(8,128)S(1)}, f32[264,256]{1,0:T(8,128)S(1)}, u32[]{:S(2)}, u32[]{:S(2)}) collective-permute-start(f32[264,256]{1,0:T(8,128)S(1)} %get-tuple-element.38), channel_id=1, source_target_pairs={{0,1},{1,0},{2,3},{3,2},{4,5},{5,4},{6,7},{7,6},{8,9},{9,8},{10,11... | collective-permute-start | bytes 811016 | tf_op jit(solution)/shard_map/ppermute | solution.py:371
  29.8 5.3 %collective-permute-start.9 = (f32[264,256]{1,0:T(8,128)S(1)}, f32[264,256]{1,0:T(8,128)S(1)}, u32[]{:S(2)}, u32[]{:S(2)}) collective-permute-start(f32[264,256]{1,0:T(8,128)S(1)} %collective-permute-done.8.refs_2_), channel_id=1, source_target_pairs={{0,1},{1,0},{2,3},{3,2},{4,5},{5,4},{6,7},{7,6},{8,9},{9,8},{10,11... | collective-permute-start | bytes 811016 | tf_op jit(solution)/shard_map/ppermute | solution.py:372
  29.8 12.4 %collective-permute-start.10 = (f32[256,256]{1,0:T(8,128)S(1)}, f32[256,256]{1,0:T(8,128)S(1)}, u32[]{:S(2)}, u32[]{:S(2)}) collective-permute-start(f32[256,256]{1,0:T(8,128)S(1)} %copy-done.1), channel_id=1, source_target_pairs={{0,15},{1,0},{2,1},{3,2},{4,3},{5,4},{6,5},{7,6},{8,7},{9,8},{10,9... | collective-permute-start | bytes 786440 | tf_op jit(solution)/shard_map/ppermute | solution.py:396
  42.2 31.5 %copy-start = (f32[1,256,256]{2,1,0:T(8,128)S(1)}, f32[1,256,256]{2,1,0:T(8,128)}, u32[]{:S(2)}) copy-start(f32[1,256,256]{2,1,0:T(8,128)} %param.7) | copy-start | bytes 786436
  42.2 1.6 %collective-permute-start.12 = (f32[256,256]{1,0:T(8,128)S(1)}, f32[256,256]{1,0:T(8,128)S(1)}, u32[]{:S(2)}, u32[]{:S(2)}) collective-permute-start(f32[256,256]{1,0:T(8,128)S(1)} %get-tuple-element.45.refs_1_.refs_7_), channel_id=1, source_target_pairs={{0,1},{1,0},{2,3},{3,2},{4,5},{5,4},{6,7},{7,6},{8,9},{9,8},{10,11... | collective-permute-start | bytes 786440 | tf_op jit(solution)/shard_map/ppermute | solution.py:355
  42.3 6.4 %collective-permute-start.11 = (f32[256,256]{1,0:T(8,128)S(1)}, f32[256,256]{1,0:T(8,128)S(1)}, u32[]{:S(2)}, u32[]{:S(2)}) collective-permute-start(f32[256,256]{1,0:T(8,128)S(1)} %get-tuple-element.45.refs_1_.refs_7_), channel_id=1, source_target_pairs={{0,4},{1,3},{4,8},{5,1},{8,12},{9,5},{12,14},{13,9},{14,10},{15,13... | collective-permute-start | bytes 786440 | tf_op jit(solution)/shard_map/ppermute | solution.py:358
  43.8 7.7 %collective-permute-start.13 = (f32[256,256]{1,0:T(8,128)S(1)}, f32[256,256]{1,0:T(8,128)S(1)}, u32[]{:S(2)}, u32[]{:S(2)}) collective-permute-start(f32[256,256]{1,0:T(8,128)S(1)} %collective-permute-done.12.refs_2_), channel_id=1, source_target_pairs={{0,4},{1,3},{4,8},{5,1},{8,12},{9,5},{12,14},{13,9},{14,10},{15,13... | collective-permute-start | bytes 786440 | tf_op jit(solution)/shard_map/ppermute | solution.py:359
  48.7 6.4 %collective-permute-start.14 = (f32[256,256]{1,0:T(8,128)S(1)}, f32[256,256]{1,0:T(8,128)S(1)}, u32[]{:S(2)}, u32[]{:S(2)}) collective-permute-start(f32[256,256]{1,0:T(8,128)S(1)} %collective-permute-done.11.refs_3_), channel_id=1, source_target_pairs={{0,4},{1,3},{4,8},{5,1},{8,12},{9,5},{12,14},{13,9},{14,10},{15,13... | collective-permute-start | bytes 786440 | tf_op jit(solution)/shard_map/ppermute | solution.py:358
  51.5 6.4 %collective-permute-start.15 = (f32[256,256]{1,0:T(8,128)S(1)}, f32[256,256]{1,0:T(8,128)S(1)}, u32[]{:S(2)}, u32[]{:S(2)}) collective-permute-start(f32[256,256]{1,0:T(8,128)S(1)} %collective-permute-done.13.refs_4_), channel_id=1, source_target_pairs={{0,4},{1,3},{4,8},{5,1},{8,12},{9,5},{12,14},{13,9},{14,10},{15,13... | collective-permute-start | bytes 786440 | tf_op jit(solution)/shard_map/ppermute | solution.py:359
  55.1 6.4 %collective-permute-start.16 = (f32[256,256]{1,0:T(8,128)S(1)}, f32[256,256]{1,0:T(8,128)S(1)}, u32[]{:S(2)}, u32[]{:S(2)}) collective-permute-start(f32[256,256]{1,0:T(8,128)S(1)} %collective-permute-done.14.refs_5_), channel_id=1, source_target_pairs={{0,4},{1,3},{4,8},{5,1},{8,12},{9,5},{12,14},{13,9},{14,10},{15,13... | collective-permute-start | bytes 786440 | tf_op jit(solution)/shard_map/ppermute | solution.py:358
  57.9 6.4 %collective-permute-start.17 = (f32[256,256]{1,0:T(8,128)S(1)}, f32[256,256]{1,0:T(8,128)S(1)}, u32[]{:S(2)}, u32[]{:S(2)}) collective-permute-start(f32[256,256]{1,0:T(8,128)S(1)} %collective-permute-done.15.refs_6_), channel_id=1, source_target_pairs={{0,4},{1,3},{4,8},{5,1},{8,12},{9,5},{12,14},{13,9},{14,10},{15,13... | collective-permute-start | bytes 786440 | tf_op jit(solution)/shard_map/ppermute | solution.py:359
  65.6 8.0 %collective-permute-start.18 = (f32[256,768]{1,0:T(8,128)S(1)}, f32[256,768]{1,0:T(8,128)S(1)}, u32[]{:S(2)}, u32[]{:S(2)}) collective-permute-start(f32[256,768]{1,0:T(8,128)S(1)} %get-tuple-element.49), channel_id=1, source_target_pairs={{0,1},{1,0},{2,3},{3,2},{4,5},{5,4},{6,7},{7,6},{8,9},{9,8},{10,11... | collective-permute-start | bytes 2359304 | tf_op jit(solution)/shard_map/ppermute | solution.py:371
  65.7 6.4 %collective-permute-start.19 = (f32[256,256]{1,0:T(8,128)S(1)}, f32[256,256]{1,0:T(8,128)S(1)}, u32[]{:S(2)}, u32[]{:S(2)}) collective-permute-start(f32[256,256]{1,0:T(8,128)S(1)} %collective-permute-done.16.refs_7_), channel_id=1, source_target_pairs={{0,4},{1,3},{4,8},{5,1},{8,12},{9,5},{12,14},{13,9},{14,10},{15,13... | collective-permute-start | bytes 786440 | tf_op jit(solution)/shard_map/ppermute | solution.py:363
  72.1 1.5 %collective-permute-start.20 = (f32[256,256]{1,0:T(8,128)S(1)}, f32[256,256]{1,0:T(8,128)S(1)}, u32[]{:S(2)}, u32[]{:S(2)}) collective-permute-start(f32[256,256]{1,0:T(8,128)S(1)} %collective-permute-done.19.refs_2_), channel_id=1, source_target_pairs={{0,1},{1,0},{2,3},{3,2},{4,5},{5,4},{6,7},{7,6},{8,9},{9,8},{10,11... | collective-permute-start | bytes 786440 | tf_op jit(solution)/shard_map/ppermute | solution.py:372
  75.5 12.8 %copy-start.5 = (bf16[256,256]{1,0:T(8,128)(2,1)S(1)}, bf16[256,256]{1,0:T(8,128)(2,1)}, u32[]{:S(2)}) copy-start(bf16[256,256]{1,0:T(8,128)(2,1)} %constant.35.clone.tl_ref) | copy-start | bytes 393220
  75.5 12.8 %copy-start.6 = (bf16[256,256]{1,0:T(8,128)(2,1)S(1)}, bf16[256,256]{1,0:T(8,128)(2,1)}, u32[]{:S(2)}) copy-start(bf16[256,256]{1,0:T(8,128)(2,1)} %constant.34.clone.th_ref) | copy-start | bytes 393220
  107.8 1.6 %collective-permute-start.22 = (f32[256,256]{1,0:T(8,128)S(1)}, f32[256,256]{1,0:T(8,128)S(1)}, u32[]{:S(2)}, u32[]{:S(2)}) collective-permute-start(f32[256,256]{1,0:T(8,128)S(1)} %shard_map.93.refs_1_), channel_id=1, source_target_pairs={{0,1},{1,0},{2,3},{3,2},{4,5},{5,4},{6,7},{7,6},{8,9},{9,8},{10,11... | collective-permute-start | bytes 786440 | tf_op jit(solution)/shard_map/ppermute | solution.py:355
  107.9 6.4 %collective-permute-start.21 = (f32[256,256]{1,0:T(8,128)S(1)}, f32[256,256]{1,0:T(8,128)S(1)}, u32[]{:S(2)}, u32[]{:S(2)}) collective-permute-start(f32[256,256]{1,0:T(8,128)S(1)} %shard_map.93.refs_1_), channel_id=1, source_target_pairs={{0,4},{1,3},{4,8},{5,1},{8,12},{9,5},{12,14},{13,9},{14,10},{15,13... | collective-permute-start | bytes 786440 | tf_op jit(solution)/shard_map/ppermute | solution.py:358
  109.4 7.7 %collective-permute-start.23 = (f32[256,256]{1,0:T(8,128)S(1)}, f32[256,256]{1,0:T(8,128)S(1)}, u32[]{:S(2)}, u32[]{:S(2)}) collective-permute-start(f32[256,256]{1,0:T(8,128)S(1)} %collective-permute-done.22.refs_2_), channel_id=1, source_target_pairs={{0,4},{1,3},{4,8},{5,1},{8,12},{9,5},{12,14},{13,9},{14,10},{15,13... | collective-permute-start | bytes 786440 | tf_op jit(solution)/shard_map/ppermute | solution.py:359
  114.3 6.4 %collective-permute-start.24 = (f32[256,256]{1,0:T(8,128)S(1)}, f32[256,256]{1,0:T(8,128)S(1)}, u32[]{:S(2)}, u32[]{:S(2)}) collective-permute-start(f32[256,256]{1,0:T(8,128)S(1)} %collective-permute-done.21.refs_3_), channel_id=1, source_target_pairs={{0,4},{1,3},{4,8},{5,1},{8,12},{9,5},{12,14},{13,9},{14,10},{15,13... | collective-permute-start | bytes 786440 | tf_op jit(solution)/shard_map/ppermute | solution.py:358
  117.1 6.4 %collective-permute-start.25 = (f32[256,256]{1,0:T(8,128)S(1)}, f32[256,256]{1,0:T(8,128)S(1)}, u32[]{:S(2)}, u32[]{:S(2)}) collective-permute-start(f32[256,256]{1,0:T(8,128)S(1)} %collective-permute-done.23.refs_4_), channel_id=1, source_target_pairs={{0,4},{1,3},{4,8},{5,1},{8,12},{9,5},{12,14},{13,9},{14,10},{15,13... | collective-permute-start | bytes 786440 | tf_op jit(solution)/shard_map/ppermute | solution.py:359
  120.7 6.4 %collective-permute-start.26 = (f32[256,256]{1,0:T(8,128)S(1)}, f32[256,256]{1,0:T(8,128)S(1)}, u32[]{:S(2)}, u32[]{:S(2)}) collective-permute-start(f32[256,256]{1,0:T(8,128)S(1)} %collective-permute-done.24.refs_5_), channel_id=1, source_target_pairs={{0,4},{1,3},{4,8},{5,1},{8,12},{9,5},{12,14},{13,9},{14,10},{15,13... | collective-permute-start | bytes 786440 | tf_op jit(solution)/shard_map/ppermute | solution.py:358
  123.5 6.4 %collective-permute-start.27 = (f32[256,256]{1,0:T(8,128)S(1)}, f32[256,256]{1,0:T(8,128)S(1)}, u32[]{:S(2)}, u32[]{:S(2)}) collective-permute-start(f32[256,256]{1,0:T(8,128)S(1)} %collective-permute-done.25.refs_6_), channel_id=1, source_target_pairs={{0,4},{1,3},{4,8},{5,1},{8,12},{9,5},{12,14},{13,9},{14,10},{15,13... | collective-permute-start | bytes 786440 | tf_op jit(solution)/shard_map/ppermute | solution.py:359
  131.3 8.0 %collective-permute-start.28 = (f32[256,768]{1,0:T(8,128)S(1)}, f32[256,768]{1,0:T(8,128)S(1)}, u32[]{:S(2)}, u32[]{:S(2)}) collective-permute-start(f32[256,768]{1,0:T(8,128)S(1)} %get-tuple-element.55), channel_id=1, source_target_pairs={{0,1},{1,0},{2,3},{3,2},{4,5},{5,4},{6,7},{7,6},{8,9},{9,8},{10,11... | collective-permute-start | bytes 2359304 | tf_op jit(solution)/shard_map/ppermute | solution.py:371
  131.3 6.4 %collective-permute-start.29 = (f32[256,256]{1,0:T(8,128)S(1)}, f32[256,256]{1,0:T(8,128)S(1)}, u32[]{:S(2)}, u32[]{:S(2)}) collective-permute-start(f32[256,256]{1,0:T(8,128)S(1)} %collective-permute-done.26.refs_7_), channel_id=1, source_target_pairs={{0,4},{1,3},{4,8},{5,1},{8,12},{9,5},{12,14},{13,9},{14,10},{15,13... | collective-permute-start | bytes 786440 | tf_op jit(solution)/shard_map/ppermute | solution.py:363
  137.8 1.5 %collective-permute-start.30 = (f32[256,256]{1,0:T(8,128)S(1)}, f32[256,256]{1,0:T(8,128)S(1)}, u32[]{:S(2)}, u32[]{:S(2)}) collective-permute-start(f32[256,256]{1,0:T(8,128)S(1)} %collective-permute-done.29.refs_2_), channel_id=1, source_target_pairs={{0,1},{1,0},{2,3},{3,2},{4,5},{5,4},{6,7},{7,6},{8,9},{9,8},{10,11... | collective-permute-start | bytes 786440 | tf_op jit(solution)/shard_map/ppermute | solution.py:372

commit v7 on v4

--- a/solution.py
+++ b/solution.py
@@ -101,7 +101,7 @@
 
     ahead = weight_ref[ORDER : ORDER + 1, :] * field
     before = ahead - ahead
-    result, _, second = lax.fori_loop(0, ORDER, body, (ahead, before, before), unroll=ORDER // 2)
+    result, _, second = lax.fori_loop(0, ORDER, body, (ahead, before, before), unroll=True)
     return 0.5 * (result - second)
 
 
@@ -253,7 +253,7 @@
     chips = len(path)
     pairs = []
     for place, chip in enumerate(path):
-        pairs += [(2 * chip, 2 * path[(place + 1) % chips]), (2 * chip + 1, 2 * path[place - 1] + 1)]
+        pairs += [(2 * chip, 2 * path[place - 1]), (2 * chip + 1, 2 * path[(place + 1) % chips] + 1)]
     return pairs
 
 
@@ -265,7 +265,7 @@
     for device in range(length):
         core = device % 2
         place = path.index(device // 2)
-        way = 1 - 2 * core
+        way = 2 * core - 1
         own, partner = rows_of(device), rows_of(device ^ 1)
         arrivals = [
             2 * path[(place - way * hop) % chips] + side for hop in range(reach) for side in (core, 1 - core)
@@ -396,15 +396,17 @@
         in_specs=[pl.BlockSpec(memory_space=pltpu.HBM)] * 2,
         out_specs=(VMEM, VMEM),
         scratch_shapes=[pltpu.VMEM((side_x, side_y), jnp.int32), pltpu.SemaphoreType.DMA, pltpu.SemaphoreType.DMA],
-        compiler_params=pltpu.CompilerParams(vmem_limit_bytes=60 * 1024 * 1024),
-    )(noise, phonon_level)
+        compiler_params=pltpu.CompilerParams(vmem_limit_bytes=16 << 20),
+    )(*(pltpu.with_memory_space_constraint(array, pltpu.HBM) for array in (noise, phonon_level)))
     parts, (weights, hops) = around(packed, forward, 1, (weights, hops))
-    damp_next = lax.ppermute(damp, "tm", [(i, (i - 1) % length) for i in range(length)])
+    damp_wrap = lax.ppermute(damp, "tm", [(0, length - 1)])
+    damp_next = lax.ppermute(damp, "tm", [(i, i - 1) for i in range(1, length)])
     first_kernel, next_kernel = based(first_spectral_kernel, forward), based(next_spectral_kernel, forward)
     finish = based(finish_kernel, back)
     first_outs = (field_shape, shape(1, side_y))
     first, mean_level = call(first_kernel, first_outs, 9, scratch, work, 1)(*parts, cosine, *hops)
-    first, damp_next = lax.optimization_barrier((first, damp_next))
+    first, damp_next, damp_wrap = lax.optimization_barrier((first, damp_next, damp_wrap))
+    damp_next = damp_next + damp_wrap
     beside = (weights,)
     parts, beside = around(first, back, 3, beside)
     (second_residual,) = call(finish, (field_shape,), 11, scalars=1)(*parts, damp, damp_next, noise, *hops)

time: 145 us -> 147 us (1.014)
  starting transfers between devices: 20.8 us -> 24.5 us
    ppermute x1 -> x2, starting transfers between devices: 5.17 us -> 8.31 us  [the longest x1 7.02 us: by_ring(): damp_wrap = lax.ppermute(damp, 'tm', [(0, length - 1)])]
  transfers between devices with their start and end apart: 41 -> 42, of which waited for: 34 -> 34; matrix products, arithmetic and copies ran while one was open for 0% -> 0% of each run, Pallas kernels for 7% -> 6%
where the time goes in v7:
time: 147 us
  waiting for transfers between devices  96.2 us (65%)
  Pallas kernels  24.8 us (17%)
  starting transfers between devices  24.5 us (17%)
    ppermute x12, waiting for transfers between devices, around(): own = lax.ppermute(own, 'tm', hop)  40.9 us
    ppermute x12, waiting for transfers between devices, around(): partner = lax.ppermute(partner, 'tm', hop)  29.2 us
    ppermute x4, waiting for transfers between devices, around(): last = lax.ppermute(own, 'tm', hop)  17.5 us
    pallas_call x1, Pallas kernels, by_ring(): call(next_kernel, field_shape, 11, scratch, work, 1)  7.13 us
    pallas_call x1, Pallas kernels, by_ring(): call(first_kernel, first_outs, 9, scratch, work, 1)(*parts, cosine, *hops)  7.11 us
    ppermute x1, starting transfers between devices, by_ring(): damp_wrap = lax.ppermute(damp, 'tm', [(0, length - 1)])  7.02 us
    ppermute x12, starting transfers between devices, around(): own = lax.ppermute(own, 'tm', hop)  6.74 us
    ppermute x12, starting transfers between devices, around(): partner = lax.ppermute(partner, 'tm', hop)  4.9 us
  transfers between devices with their start and end apart: 42, of which 34 were waited for; matrix products, arithmetic and copies ran while one was open for 0% of the time, Pallas kernels for 6%

profile of v7, /device:TPU:0, one launch (start us, length us, event | category | flops | bytes accessed | tf_op | source)
XLA Modules:
  0.0 147.2 jit_solution(4303459535257828757)
XLA Ops:
  2.4 2.6 %collective-permute-start = (f32[264,256]{1,0:T(8,128)S(1)}, f32[264,256]{1,0:T(8,128)S(1)}, u32[]{:S(2)}, u32[]{:S(2)}) collective-permute-start(f32[264,256]{1,0:T(8,128)S(1)} %get-tuple-element.35.refs_1_), channel_id=1, source_target_pairs={{0,2},{1,5},{4,0},{5,9},{8,4},{9,13},{12,8},{13,15},{14,12},{15,11... | collective-permute-start | bytes 811016 | tf_op jit(solution)/shard_map/ppermute | solution.py:364
  6.3 1.6 %collective-permute-start.2 = (f32[264,256]{1,0:T(8,128)S(1)}, f32[264,256]{1,0:T(8,128)S(1)}, u32[]{:S(2)}, u32[]{:S(2)}) collective-permute-start(f32[264,256]{1,0:T(8,128)S(1)} %collective-permute-done.1.refs_2_), channel_id=1, source_target_pairs={{0,2},{1,5},{4,0},{5,9},{8,4},{9,13},{12,8},{13,15},{14,12},{15,11... | collective-permute-start | bytes 811016 | tf_op jit(solution)/shard_map/ppermute | solution.py:365
  7.9 1.6 %collective-permute-done.refs_3_ = f32[264,256]{1,0:T(8,128)S(1)} collective-permute-done((f32[264,256]{1,0:T(8,128)S(1)}, f32[264,256]{1,0:T(8,128)S(1)}, u32[]{:S(2)}, u32[]{:S(2)}) %collective-permute-start) | collective-permute-done | bytes 270368 | tf_op jit(solution)/shard_map/ppermute | solution.py:364
  9.4 2.0 %collective-permute-start.3 = (f32[264,256]{1,0:T(8,128)S(1)}, f32[264,256]{1,0:T(8,128)S(1)}, u32[]{:S(2)}, u32[]{:S(2)}) collective-permute-start(f32[264,256]{1,0:T(8,128)S(1)} %collective-permute-done.refs_3_), channel_id=1, source_target_pairs={{0,2},{1,5},{4,0},{5,9},{8,4},{9,13},{12,8},{13,15},{14,12},{15,11... | collective-permute-start | bytes 811016 | tf_op jit(solution)/shard_map/ppermute | solution.py:364
  11.4 1.4 collective-permute-done.2.refs_4_
  12.8 1.6 %collective-permute-start.4 = (f32[264,256]{1,0:T(8,128)S(1)}, f32[264,256]{1,0:T(8,128)S(1)}, u32[]{:S(2)}, u32[]{:S(2)}) collective-permute-start(f32[264,256]{1,0:T(8,128)S(1)} %collective-permute-done.2.refs_4_), channel_id=1, source_target_pairs={{0,2},{1,5},{4,0},{5,9},{8,4},{9,13},{12,8},{13,15},{14,12},{15,11... | collective-permute-start | bytes 811016 | tf_op jit(solution)/shard_map/ppermute | solution.py:365
  14.4 1.6 %collective-permute-done.3.refs_5_ = f32[264,256]{1,0:T(8,128)S(1)} collective-permute-done((f32[264,256]{1,0:T(8,128)S(1)}, f32[264,256]{1,0:T(8,128)S(1)}, u32[]{:S(2)}, u32[]{:S(2)}) %collective-permute-start.3) | collective-permute-done | bytes 270368 | tf_op jit(solution)/shard_map/ppermute | solution.py:364
  15.9 2.0 %collective-permute-start.5 = (f32[264,256]{1,0:T(8,128)S(1)}, f32[264,256]{1,0:T(8,128)S(1)}, u32[]{:S(2)}, u32[]{:S(2)}) collective-permute-start(f32[264,256]{1,0:T(8,128)S(1)} %collective-permute-done.3.refs_5_), channel_id=1, source_target_pairs={{0,2},{1,5},{4,0},{5,9},{8,4},{9,13},{12,8},{13,15},{14,12},{15,11... | collective-permute-start | bytes 811016 | tf_op jit(solution)/shard_map/ppermute | solution.py:364
  17.9 1.4 collective-permute-done.4.refs_6_
  19.2 1.6 %collective-permute-start.6 = (f32[264,256]{1,0:T(8,128)S(1)}, f32[264,256]{1,0:T(8,128)S(1)}, u32[]{:S(2)}, u32[]{:S(2)}) collective-permute-start(f32[264,256]{1,0:T(8,128)S(1)} %collective-permute-done.4.refs_6_), channel_id=1, source_target_pairs={{0,2},{1,5},{4,0},{5,9},{8,4},{9,13},{12,8},{13,15},{14,12},{15,11... | collective-permute-start | bytes 811016 | tf_op jit(solution)/shard_map/ppermute | solution.py:365
  20.8 1.6 %collective-permute-done.5.refs_7_ = f32[264,256]{1,0:T(8,128)S(1)} collective-permute-done((f32[264,256]{1,0:T(8,128)S(1)}, f32[264,256]{1,0:T(8,128)S(1)}, u32[]{:S(2)}, u32[]{:S(2)}) %collective-permute-start.5) | collective-permute-done | bytes 270368 | tf_op jit(solution)/shard_map/ppermute | solution.py:364
  22.4 2.0 %collective-permute-start.8 = (f32[264,256]{1,0:T(8,128)S(1)}, f32[264,256]{1,0:T(8,128)S(1)}, u32[]{:S(2)}, u32[]{:S(2)}) collective-permute-start(f32[264,256]{1,0:T(8,128)S(1)} %collective-permute-done.5.refs_7_), channel_id=1, source_target_pairs={{0,2},{1,5},{4,0},{5,9},{8,4},{9,13},{12,8},{13,15},{14,12},{15,11... | collective-permute-start | bytes 811016 | tf_op jit(solution)/shard_map/ppermute | solution.py:369
  24.3 1.4 collective-permute-done.6.refs_8_
  26.6 2.2 %collective-permute-done.8.refs_2_ = f32[264,256]{1,0:T(8,128)S(1)} collective-permute-done((f32[264,256]{1,0:T(8,128)S(1)}, f32[264,256]{1,0:T(8,128)S(1)}, u32[]{:S(2)}, u32[]{:S(2)}) %collective-permute-start.8) | collective-permute-done | bytes 270368 | tf_op jit(solution)/shard_map/ppermute | solution.py:369
  28.8 7.0 %collective-permute-start.11 = (f32[256,256]{1,0:T(8,128)S(1)}, f32[256,256]{1,0:T(8,128)S(1)}, u32[]{:S(2)}, u32[]{:S(2)}) collective-permute-start(f32[256,256]{1,0:T(8,128)S(1)} %get-tuple-element.49.refs_4_), channel_id=1, source_target_pairs={{0,15},{16,31}} | collective-permute-start | bytes 786440 | tf_op jit(solution)/shard_map/ppermute | solution.py:402
  35.9 1.3 collective-permute-start.10
  37.3 7.1 %shard_map.71 = (f32[256,256]{1,0:T(8,128)S(1)}, f32[1,256]{1,0:T(1,128)S(1)}) custom-call(f32[64]{0:T(128)S(1)} %dynamic-slice_bitcast_fusion.refs_0_.weight_ref, f32[264,256]{1,0:T(8,128)S(1)} %get-tuple-element.42.refs_0_, f32[264,256]{1,0:T(8,128)S(1)} %collective-permute-done.7.refs_1_, f32[264,256]{1,0:T(8,128)S(1)} %collective-permute-done.8.refs_2_, ...), custom_call_target="tpu_custom_call" | custom-call | flops 4026531840 | tf_op jit(solution)/shard_map/pallas_call | solution.py:407
  46.8 5.2 %collective-permute-done.12.refs_3_ = f32[256,256]{1,0:T(8,128)S(1)} collective-permute-done((f32[256,256]{1,0:T(8,128)S(1)}, f32[256,256]{1,0:T(8,128)S(1)}, u32[]{:S(2)}, u32[]{:S(2)}) %collective-permute-start.12) | collective-permute-done | bytes 262176 | tf_op jit(solution)/shard_map/ppermute | solution.py:364
  52.0 2.8 %collective-permute-done.14.refs_4_ = f32[256,256]{1,0:T(8,128)S(1)} collective-permute-done((f32[256,256]{1,0:T(8,128)S(1)}, f32[256,256]{1,0:T(8,128)S(1)}, u32[]{:S(2)}, u32[]{:S(2)}) %collective-permute-start.14) | collective-permute-done | bytes 262176 | tf_op jit(solution)/shard_map/ppermute | solution.py:365
  54.8 3.6 %collective-permute-done.15.refs_5_ = f32[256,256]{1,0:T(8,128)S(1)} collective-permute-done((f32[256,256]{1,0:T(8,128)S(1)}, f32[256,256]{1,0:T(8,128)S(1)}, u32[]{:S(2)}, u32[]{:S(2)}) %collective-permute-start.15) | collective-permute-done | bytes 262176 | tf_op jit(solution)/shard_map/ppermute | solution.py:364
  58.4 2.8 %collective-permute-done.16.refs_6_ = f32[256,256]{1,0:T(8,128)S(1)} collective-permute-done((f32[256,256]{1,0:T(8,128)S(1)}, f32[256,256]{1,0:T(8,128)S(1)}, u32[]{:S(2)}, u32[]{:S(2)}) %collective-permute-start.16) | collective-permute-done | bytes 262176 | tf_op jit(solution)/shard_map/ppermute | solution.py:365
  61.2 3.6 %collective-permute-done.17.refs_7_ = f32[256,256]{1,0:T(8,128)S(1)} collective-permute-done((f32[256,256]{1,0:T(8,128)S(1)}, f32[256,256]{1,0:T(8,128)S(1)}, u32[]{:S(2)}, u32[]{:S(2)}) %collective-permute-start.17) | collective-permute-done | bytes 262176 | tf_op jit(solution)/shard_map/ppermute | solution.py:364
  64.7 2.8 %collective-permute-done.18.refs_8_ = f32[256,256]{1,0:T(8,128)S(1)} collective-permute-done((f32[256,256]{1,0:T(8,128)S(1)}, f32[256,256]{1,0:T(8,128)S(1)}, u32[]{:S(2)}, u32[]{:S(2)}) %collective-permute-start.18) | collective-permute-done | bytes 262176 | tf_op jit(solution)/shard_map/ppermute | solution.py:365
  67.6 1.3 shard_map.72
  69.1 6.4 %collective-permute-done.20.refs_2_ = f32[256,256]{1,0:T(8,128)S(1)} collective-permute-done((f32[256,256]{1,0:T(8,128)S(1)}, f32[256,256]{1,0:T(8,128)S(1)}, u32[]{:S(2)}, u32[]{:S(2)}) %collective-permute-start.20) | collective-permute-done | bytes 262176 | tf_op jit(solution)/shard_map/ppermute | solution.py:369
  75.5 1.5 %collective-permute-done.21.refs_3_ = f32[256,256]{1,0:T(8,128)S(1)} collective-permute-done((f32[256,256]{1,0:T(8,128)S(1)}, f32[256,256]{1,0:T(8,128)S(1)}, u32[]{:S(2)}, u32[]{:S(2)}) %collective-permute-start.21) | collective-permute-done | bytes 262176 | tf_op jit(solution)/shard_map/ppermute | solution.py:378
  77.0 1.8 %shard_map.73.refs_1_ = f32[256,256]{1,0:T(8,128)S(1)} custom-call(f32[64]{0:T(128)S(1)} %dynamic-slice_bitcast_fusion.refs_0_.weight_ref, f32[256,768]{1,0:T(8,128)S(1)} %get-tuple-element.53.refs_0_, f32[256,768]{1,0:T(8,128)S(1)} %collective-permute-done.19.refs_1_, f32[256,256]{1,0:T(8,128)S(1)} %collective-permute-done.20.refs_2_, ...), custom_call_target="tpu_custom_call" | custom-call | tf_op jit(solution)/shard_map/pallas_call | solution.py:412
  79.0 1.4 collective-permute-done.23.refs_2_
  80.4 5.0 %collective-permute-done.22.refs_3_ = f32[256,256]{1,0:T(8,128)S(1)} collective-permute-done((f32[256,256]{1,0:T(8,128)S(1)}, f32[256,256]{1,0:T(8,128)S(1)}, u32[]{:S(2)}, u32[]{:S(2)}) %collective-permute-start.22) | collective-permute-done | bytes 262176 | tf_op jit(solution)/shard_map/ppermute | solution.py:364
  85.4 2.8 %collective-permute-done.24.refs_4_ = f32[256,256]{1,0:T(8,128)S(1)} collective-permute-done((f32[256,256]{1,0:T(8,128)S(1)}, f32[256,256]{1,0:T(8,128)S(1)}, u32[]{:S(2)}, u32[]{:S(2)}) %collective-permute-start.24) | collective-permute-done | bytes 262176 | tf_op jit(solution)/shard_map/ppermute | solution.py:365
  88.2 3.6 %collective-permute-done.25.refs_5_ = f32[256,256]{1,0:T(8,128)S(1)} collective-permute-done((f32[256,256]{1,0:T(8,128)S(1)}, f32[256,256]{1,0:T(8,128)S(1)}, u32[]{:S(2)}, u32[]{:S(2)}) %collective-permute-start.25) | collective-permute-done | bytes 262176 | tf_op jit(solution)/shard_map/ppermute | solution.py:364
  91.7 2.8 %collective-permute-done.26.refs_6_ = f32[256,256]{1,0:T(8,128)S(1)} collective-permute-done((f32[256,256]{1,0:T(8,128)S(1)}, f32[256,256]{1,0:T(8,128)S(1)}, u32[]{:S(2)}, u32[]{:S(2)}) %collective-permute-start.26) | collective-permute-done | bytes 262176 | tf_op jit(solution)/shard_map/ppermute | solution.py:365
  94.6 3.6 %collective-permute-done.27.refs_7_ = f32[256,256]{1,0:T(8,128)S(1)} collective-permute-done((f32[256,256]{1,0:T(8,128)S(1)}, f32[256,256]{1,0:T(8,128)S(1)}, u32[]{:S(2)}, u32[]{:S(2)}) %collective-permute-start.27) | collective-permute-done | bytes 262176 | tf_op jit(solution)/shard_map/ppermute | solution.py:364
  98.1 2.8 %collective-permute-done.28.refs_8_ = f32[256,256]{1,0:T(8,128)S(1)} collective-permute-done((f32[256,256]{1,0:T(8,128)S(1)}, f32[256,256]{1,0:T(8,128)S(1)}, u32[]{:S(2)}, u32[]{:S(2)}) %collective-permute-start.28) | collective-permute-done | bytes 262176 | tf_op jit(solution)/shard_map/ppermute | solution.py:365
  101.8 2.7 %collective-permute-done.30.refs_2_ = f32[256,256]{1,0:T(8,128)S(1)} collective-permute-done((f32[256,256]{1,0:T(8,128)S(1)}, f32[256,256]{1,0:T(8,128)S(1)}, u32[]{:S(2)}, u32[]{:S(2)}) %collective-permute-start.30) | collective-permute-done | bytes 262176 | tf_op jit(solution)/shard_map/ppermute | solution.py:369
  104.5 1.5 %collective-permute-done.31.refs_3_ = f32[256,256]{1,0:T(8,128)S(1)} collective-permute-done((f32[256,256]{1,0:T(8,128)S(1)}, f32[256,256]{1,0:T(8,128)S(1)}, u32[]{:S(2)}, u32[]{:S(2)}) %collective-permute-start.31) | collective-permute-done | bytes 262176 | tf_op jit(solution)/shard_map/ppermute | solution.py:378
  106.0 7.1 %shard_map.75.refs_1_ = f32[256,256]{1,0:T(8,128)S(1)} custom-call(f32[64]{0:T(128)S(1)} %dynamic-slice_bitcast_fusion.refs_0_.weight_ref, f32[256,256]{1,0:T(8,128)S(1)} %get-tuple-element.59.refs_0_, f32[256,256]{1,0:T(8,128)S(1)} %collective-permute-done.29.refs_1_, f32[256,256]{1,0:T(8,128)S(1)} %collective-permute-done.30.refs_2_, ...), custom_call_target="tpu_custom_call" | custom-call | flops 4026531840 | tf_op jit(solution)/shard_map/pallas_call | solution.py:414
  113.4 1.4 collective-permute-done.33.refs_2_
  114.8 4.9 %collective-permute-done.32.refs_3_ = f32[256,256]{1,0:T(8,128)S(1)} collective-permute-done((f32[256,256]{1,0:T(8,128)S(1)}, f32[256,256]{1,0:T(8,128)S(1)}, u32[]{:S(2)}, u32[]{:S(2)}) %collective-permute-start.32) | collective-permute-done | bytes 262176 | tf_op jit(solution)/shard_map/ppermute | solution.py:364
  119.7 2.7 %collective-permute-done.34.refs_4_ = f32[256,256]{1,0:T(8,128)S(1)} collective-permute-done((f32[256,256]{1,0:T(8,128)S(1)}, f32[256,256]{1,0:T(8,128)S(1)}, u32[]{:S(2)}, u32[]{:S(2)}) %collective-permute-start.34) | collective-permute-done | bytes 262176 | tf_op jit(solution)/shard_map/ppermute | solution.py:365
  122.6 3.5 %collective-permute-done.35.refs_5_ = f32[256,256]{1,0:T(8,128)S(1)} collective-permute-done((f32[256,256]{1,0:T(8,128)S(1)}, f32[256,256]{1,0:T(8,128)S(1)}, u32[]{:S(2)}, u32[]{:S(2)}) %collective-permute-start.35) | collective-permute-done | bytes 262176 | tf_op jit(solution)/shard_map/ppermute | solution.py:364
  126.1 2.7 %collective-permute-done.36.refs_6_ = f32[256,256]{1,0:T(8,128)S(1)} collective-permute-done((f32[256,256]{1,0:T(8,128)S(1)}, f32[256,256]{1,0:T(8,128)S(1)}, u32[]{:S(2)}, u32[]{:S(2)}) %collective-permute-start.36) | collective-permute-done | bytes 262176 | tf_op jit(solution)/shard_map/ppermute | solution.py:365
  128.9 3.5 %collective-permute-done.37.refs_7_ = f32[256,256]{1,0:T(8,128)S(1)} collective-permute-done((f32[256,256]{1,0:T(8,128)S(1)}, f32[256,256]{1,0:T(8,128)S(1)}, u32[]{:S(2)}, u32[]{:S(2)}) %collective-permute-start.37) | collective-permute-done | bytes 262176 | tf_op jit(solution)/shard_map/ppermute | solution.py:364
  132.4 2.8 %collective-permute-done.38.refs_8_ = f32[256,256]{1,0:T(8,128)S(1)} collective-permute-done((f32[256,256]{1,0:T(8,128)S(1)}, f32[256,256]{1,0:T(8,128)S(1)}, u32[]{:S(2)}, u32[]{:S(2)}) %collective-permute-start.38) | collective-permute-done | bytes 262176 | tf_op jit(solution)/shard_map/ppermute | solution.py:365
  135.2 1.3 shard_map.76
  136.8 6.3 %collective-permute-done.40.refs_2_ = f32[256,256]{1,0:T(8,128)S(1)} collective-permute-done((f32[256,256]{1,0:T(8,128)S(1)}, f32[256,256]{1,0:T(8,128)S(1)}, u32[]{:S(2)}, u32[]{:S(2)}) %collective-permute-start.40) | collective-permute-done | bytes 262176 | tf_op jit(solution)/shard_map/ppermute | solution.py:369
  143.1 1.5 %collective-permute-done.41.refs_3_ = f32[256,256]{1,0:T(8,128)S(1)} collective-permute-done((f32[256,256]{1,0:T(8,128)S(1)}, f32[256,256]{1,0:T(8,128)S(1)}, u32[]{:S(2)}, u32[]{:S(2)}) %collective-permute-start.41) | collective-permute-done | bytes 262176 | tf_op jit(solution)/shard_map/ppermute | solution.py:378
  144.6 2.5 %shard_map.77 = (f32[256,256]{1,0:T(8,128)}, f32[256,256]{1,0:T(8,128)}) custom-call(f32[64]{0:T(128)S(1)} %dynamic-slice_bitcast_fusion.refs_0_.weight_ref, f32[256,768]{1,0:T(8,128)S(1)} %get-tuple-element.64.refs_0_, f32[256,768]{1,0:T(8,128)S(1)} %collective-permute-done.39.refs_1_, f32[256,256]{1,0:T(8,128)S(1)} %collective-permute-done.40.refs_2_, ...), custom_call_target="tpu_custom_call" | custom-call | tf_op jit(solution)/shard_map/pallas_call | solution.py:416
  (55 shorter events, 8.4 us)
Async XLA Ops:
  0.6 4.3 %copy-start.1 = (f32[256,256]{1,0:T(8,128)S(1)}, f32[256,256]{1,0:T(8,128)}, u32[]{:S(2)}) copy-start(f32[256,256]{1,0:T(8,128)} %hop_x_ref.1) | copy-start | bytes 786436
  0.6 4.3 %copy-start.2 = (f32[256,256]{1,0:T(8,128)S(1)}, f32[256,256]{1,0:T(8,128)}, u32[]{:S(2)}) copy-start(f32[256,256]{1,0:T(8,128)} %hop_y_ref.1) | copy-start | bytes 786436
  1.8 4.5 %collective-permute-start.1 = (f32[264,256]{1,0:T(8,128)S(1)}, f32[264,256]{1,0:T(8,128)S(1)}, u32[]{:S(2)}, u32[]{:S(2)}) collective-permute-start(f32[264,256]{1,0:T(8,128)S(1)} %get-tuple-element.35.refs_1_), channel_id=1, source_target_pairs={{0,1},{1,0},{2,3},{3,2},{4,5},{5,4},{6,7},{7,6},{8,9},{9,8},{10,11... | collective-permute-start | bytes 811016 | tf_op jit(solution)/shard_map/ppermute | solution.py:361
  2.4 7.1 %collective-permute-start = (f32[264,256]{1,0:T(8,128)S(1)}, f32[264,256]{1,0:T(8,128)S(1)}, u32[]{:S(2)}, u32[]{:S(2)}) collective-permute-start(f32[264,256]{1,0:T(8,128)S(1)} %get-tuple-element.35.refs_1_), channel_id=1, source_target_pairs={{0,2},{1,5},{4,0},{5,9},{8,4},{9,13},{12,8},{13,15},{14,12},{15,11... | collective-permute-start | bytes 811016 | tf_op jit(solution)/shard_map/ppermute | solution.py:364
  6.3 6.5 %collective-permute-start.2 = (f32[264,256]{1,0:T(8,128)S(1)}, f32[264,256]{1,0:T(8,128)S(1)}, u32[]{:S(2)}, u32[]{:S(2)}) collective-permute-start(f32[264,256]{1,0:T(8,128)S(1)} %collective-permute-done.1.refs_2_), channel_id=1, source_target_pairs={{0,2},{1,5},{4,0},{5,9},{8,4},{9,13},{12,8},{13,15},{14,12},{15,11... | collective-permute-start | bytes 811016 | tf_op jit(solution)/shard_map/ppermute | solution.py:365
  9.4 6.5 %collective-permute-start.3 = (f32[264,256]{1,0:T(8,128)S(1)}, f32[264,256]{1,0:T(8,128)S(1)}, u32[]{:S(2)}, u32[]{:S(2)}) collective-permute-start(f32[264,256]{1,0:T(8,128)S(1)} %collective-permute-done.refs_3_), channel_id=1, source_target_pairs={{0,2},{1,5},{4,0},{5,9},{8,4},{9,13},{12,8},{13,15},{14,12},{15,11... | collective-permute-start | bytes 811016 | tf_op jit(solution)/shard_map/ppermute | solution.py:364
  12.8 6.5 %collective-permute-start.4 = (f32[264,256]{1,0:T(8,128)S(1)}, f32[264,256]{1,0:T(8,128)S(1)}, u32[]{:S(2)}, u32[]{:S(2)}) collective-permute-start(f32[264,256]{1,0:T(8,128)S(1)} %collective-permute-done.2.refs_4_), channel_id=1, source_target_pairs={{0,2},{1,5},{4,0},{5,9},{8,4},{9,13},{12,8},{13,15},{14,12},{15,11... | collective-permute-start | bytes 811016 | tf_op jit(solution)/shard_map/ppermute | solution.py:365
  15.9 6.5 %collective-permute-start.5 = (f32[264,256]{1,0:T(8,128)S(1)}, f32[264,256]{1,0:T(8,128)S(1)}, u32[]{:S(2)}, u32[]{:S(2)}) collective-permute-start(f32[264,256]{1,0:T(8,128)S(1)} %collective-permute-done.3.refs_5_), channel_id=1, source_target_pairs={{0,2},{1,5},{4,0},{5,9},{8,4},{9,13},{12,8},{13,15},{14,12},{15,11... | collective-permute-start | bytes 811016 | tf_op jit(solution)/shard_map/ppermute | solution.py:364
  19.2 6.5 %collective-permute-start.6 = (f32[264,256]{1,0:T(8,128)S(1)}, f32[264,256]{1,0:T(8,128)S(1)}, u32[]{:S(2)}, u32[]{:S(2)}) collective-permute-start(f32[264,256]{1,0:T(8,128)S(1)} %collective-permute-done.4.refs_6_), channel_id=1, source_target_pairs={{0,2},{1,5},{4,0},{5,9},{8,4},{9,13},{12,8},{13,15},{14,12},{15,11... | collective-permute-start | bytes 811016 | tf_op jit(solution)/shard_map/ppermute | solution.py:365
  22.4 6.5 %collective-permute-start.8 = (f32[264,256]{1,0:T(8,128)S(1)}, f32[264,256]{1,0:T(8,128)S(1)}, u32[]{:S(2)}, u32[]{:S(2)}) collective-permute-start(f32[264,256]{1,0:T(8,128)S(1)} %collective-permute-done.5.refs_7_), channel_id=1, source_target_pairs={{0,2},{1,5},{4,0},{5,9},{8,4},{9,13},{12,8},{13,15},{14,12},{15,11... | collective-permute-start | bytes 811016 | tf_op jit(solution)/shard_map/ppermute | solution.py:369
  26.5 10.7 %collective-permute-start.7 = (f32[264,256]{1,0:T(8,128)S(1)}, f32[264,256]{1,0:T(8,128)S(1)}, u32[]{:S(2)}, u32[]{:S(2)}) collective-permute-start(f32[264,256]{1,0:T(8,128)S(1)} %get-tuple-element.43), channel_id=1, source_target_pairs={{0,1},{1,0},{2,3},{3,2},{4,5},{5,4},{6,7},{7,6},{8,9},{9,8},{10,11... | collective-permute-start | bytes 811016 | tf_op jit(solution)/shard_map/ppermute | solution.py:377
  28.8 8.4 %collective-permute-start.9 = (f32[264,256]{1,0:T(8,128)S(1)}, f32[264,256]{1,0:T(8,128)S(1)}, u32[]{:S(2)}, u32[]{:S(2)}) collective-permute-start(f32[264,256]{1,0:T(8,128)S(1)} %collective-permute-done.8.refs_2_), channel_id=1, source_target_pairs={{0,1},{1,0},{2,3},{3,2},{4,5},{5,4},{6,7},{7,6},{8,9},{9,8},{10,11... | collective-permute-start | bytes 811016 | tf_op jit(solution)/shard_map/ppermute | solution.py:378
  28.8 15.6 %collective-permute-start.11 = (f32[256,256]{1,0:T(8,128)S(1)}, f32[256,256]{1,0:T(8,128)S(1)}, u32[]{:S(2)}, u32[]{:S(2)}) collective-permute-start(f32[256,256]{1,0:T(8,128)S(1)} %get-tuple-element.49.refs_4_), channel_id=1, source_target_pairs={{0,15},{16,31}} | collective-permute-start | bytes 786440 | tf_op jit(solution)/shard_map/ppermute | solution.py:402
  35.9 8.6 %collective-permute-start.10 = (f32[256,256]{1,0:T(8,128)S(1)}, f32[256,256]{1,0:T(8,128)S(1)}, u32[]{:S(2)}, u32[]{:S(2)}) collective-permute-start(f32[256,256]{1,0:T(8,128)S(1)} %get-tuple-element.49.refs_4_), channel_id=1, source_target_pairs={{1,0},{2,1},{3,2},{4,3},{5,4},{6,5},{7,6},{8,7},{9,8},{10,9},{11,1... | collective-permute-start | bytes 786440 | tf_op jit(solution)/shard_map/ppermute | solution.py:403
  44.4 2.4 %collective-permute-start.13 = (f32[256,256]{1,0:T(8,128)S(1)}, f32[256,256]{1,0:T(8,128)S(1)}, u32[]{:S(2)}, u32[]{:S(2)}) collective-permute-start(f32[256,256]{1,0:T(8,128)S(1)} %get-tuple-element.50.refs_1_.refs_10_), channel_id=1, source_target_pairs={{0,1},{1,0},{2,3},{3,2},{4,5},{5,4},{6,7},{7,6},{8,9},{9,8},{10,11... | collective-permute-start | bytes 786440 | tf_op jit(solution)/shard_map/ppermute | solution.py:361
  45.6 6.4 %collective-permute-start.12 = (f32[256,256]{1,0:T(8,128)S(1)}, f32[256,256]{1,0:T(8,128)S(1)}, u32[]{:S(2)}, u32[]{:S(2)}) collective-permute-start(f32[256,256]{1,0:T(8,128)S(1)} %get-tuple-element.50.refs_1_.refs_10_), channel_id=1, source_target_pairs={{0,2},{1,5},{4,0},{5,9},{8,4},{9,13},{12,8},{13,15},{14,12},{15,11... | collective-permute-start | bytes 786440 | tf_op jit(solution)/shard_map/ppermute | solution.py:364
  46.8 8.0 %collective-permute-start.14 = (f32[256,256]{1,0:T(8,128)S(1)}, f32[256,256]{1,0:T(8,128)S(1)}, u32[]{:S(2)}, u32[]{:S(2)}) collective-permute-start(f32[256,256]{1,0:T(8,128)S(1)} %collective-permute-done.13.refs_2_), channel_id=1, source_target_pairs={{0,2},{1,5},{4,0},{5,9},{8,4},{9,13},{12,8},{13,15},{14,12},{15,11... | collective-permute-start | bytes 786440 | tf_op jit(solution)/shard_map/ppermute | solution.py:365
  52.0 6.4 %collective-permute-start.15 = (f32[256,256]{1,0:T(8,128)S(1)}, f32[256,256]{1,0:T(8,128)S(1)}, u32[]{:S(2)}, u32[]{:S(2)}) collective-permute-start(f32[256,256]{1,0:T(8,128)S(1)} %collective-permute-done.12.refs_3_), channel_id=1, source_target_pairs={{0,2},{1,5},{4,0},{5,9},{8,4},{9,13},{12,8},{13,15},{14,12},{15,11... | collective-permute-start | bytes 786440 | tf_op jit(solution)/shard_map/ppermute | solution.py:364
  54.8 6.4 %collective-permute-start.16 = (f32[256,256]{1,0:T(8,128)S(1)}, f32[256,256]{1,0:T(8,128)S(1)}, u32[]{:S(2)}, u32[]{:S(2)}) collective-permute-start(f32[256,256]{1,0:T(8,128)S(1)} %collective-permute-done.14.refs_4_), channel_id=1, source_target_pairs={{0,2},{1,5},{4,0},{5,9},{8,4},{9,13},{12,8},{13,15},{14,12},{15,11... | collective-permute-start | bytes 786440 | tf_op jit(solution)/shard_map/ppermute | solution.py:365
  58.4 6.4 %collective-permute-start.17 = (f32[256,256]{1,0:T(8,128)S(1)}, f32[256,256]{1,0:T(8,128)S(1)}, u32[]{:S(2)}, u32[]{:S(2)}) collective-permute-start(f32[256,256]{1,0:T(8,128)S(1)} %collective-permute-done.15.refs_5_), channel_id=1, source_target_pairs={{0,2},{1,5},{4,0},{5,9},{8,4},{9,13},{12,8},{13,15},{14,12},{15,11... | collective-permute-start | bytes 786440 | tf_op jit(solution)/shard_map/ppermute | solution.py:364
  61.2 6.4 %collective-permute-start.18 = (f32[256,256]{1,0:T(8,128)S(1)}, f32[256,256]{1,0:T(8,128)S(1)}, u32[]{:S(2)}, u32[]{:S(2)}) collective-permute-start(f32[256,256]{1,0:T(8,128)S(1)} %collective-permute-done.16.refs_6_), channel_id=1, source_target_pairs={{0,2},{1,5},{4,0},{5,9},{8,4},{9,13},{12,8},{13,15},{14,12},{15,11... | collective-permute-start | bytes 786440 | tf_op jit(solution)/shard_map/ppermute | solution.py:365
  68.9 8.1 %copy-start = (f32[1,256,256]{2,1,0:T(8,128)S(1)}, f32[1,256,256]{2,1,0:T(8,128)}, u32[]{:S(2)}) copy-start(f32[1,256,256]{2,1,0:T(8,128)} %param.5) | copy-start | bytes 786436
  68.9 8.0 %collective-permute-start.19 = (f32[256,768]{1,0:T(8,128)S(1)}, f32[256,768]{1,0:T(8,128)S(1)}, u32[]{:S(2)}, u32[]{:S(2)}) collective-permute-start(f32[256,768]{1,0:T(8,128)S(1)} %get-tuple-element.54), channel_id=1, source_target_pairs={{0,1},{1,0},{2,3},{3,2},{4,5},{5,4},{6,7},{7,6},{8,9},{9,8},{10,11... | collective-permute-start | bytes 2359304 | tf_op jit(solution)/shard_map/ppermute | solution.py:377
  69.0 6.4 %collective-permute-start.20 = (f32[256,256]{1,0:T(8,128)S(1)}, f32[256,256]{1,0:T(8,128)S(1)}, u32[]{:S(2)}, u32[]{:S(2)}) collective-permute-start(f32[256,256]{1,0:T(8,128)S(1)} %collective-permute-done.17.refs_7_), channel_id=1, source_target_pairs={{0,2},{1,5},{4,0},{5,9},{8,4},{9,13},{12,8},{13,15},{14,12},{15,11... | collective-permute-start | bytes 786440 | tf_op jit(solution)/shard_map/ppermute | solution.py:369
  75.4 1.5 %collective-permute-start.21 = (f32[256,256]{1,0:T(8,128)S(1)}, f32[256,256]{1,0:T(8,128)S(1)}, u32[]{:S(2)}, u32[]{:S(2)}) collective-permute-start(f32[256,256]{1,0:T(8,128)S(1)} %collective-permute-done.20.refs_2_), channel_id=1, source_target_pairs={{0,1},{1,0},{2,3},{3,2},{4,5},{5,4},{6,7},{7,6},{8,9},{9,8},{10,11... | collective-permute-start | bytes 786440 | tf_op jit(solution)/shard_map/ppermute | solution.py:378
  78.8 1.6 %collective-permute-start.23 = (f32[256,256]{1,0:T(8,128)S(1)}, f32[256,256]{1,0:T(8,128)S(1)}, u32[]{:S(2)}, u32[]{:S(2)}) collective-permute-start(f32[256,256]{1,0:T(8,128)S(1)} %shard_map.73.refs_1_), channel_id=1, source_target_pairs={{0,1},{1,0},{2,3},{3,2},{4,5},{5,4},{6,7},{7,6},{8,9},{9,8},{10,11... | collective-permute-start | bytes 786440 | tf_op jit(solution)/shard_map/ppermute | solution.py:361
  79.0 6.4 %collective-permute-start.22 = (f32[256,256]{1,0:T(8,128)S(1)}, f32[256,256]{1,0:T(8,128)S(1)}, u32[]{:S(2)}, u32[]{:S(2)}) collective-permute-start(f32[256,256]{1,0:T(8,128)S(1)} %shard_map.73.refs_1_), channel_id=1, source_target_pairs={{0,2},{1,5},{4,0},{5,9},{8,4},{9,13},{12,8},{13,15},{14,12},{15,11... | collective-permute-start | bytes 786440 | tf_op jit(solution)/shard_map/ppermute | solution.py:364
  80.4 7.8 %collective-permute-start.24 = (f32[256,256]{1,0:T(8,128)S(1)}, f32[256,256]{1,0:T(8,128)S(1)}, u32[]{:S(2)}, u32[]{:S(2)}) collective-permute-start(f32[256,256]{1,0:T(8,128)S(1)} %collective-permute-done.23.refs_2_), channel_id=1, source_target_pairs={{0,2},{1,5},{4,0},{5,9},{8,4},{9,13},{12,8},{13,15},{14,12},{15,11... | collective-permute-start | bytes 786440 | tf_op jit(solution)/shard_map/ppermute | solution.py:365
  85.4 6.4 %collective-permute-start.25 = (f32[256,256]{1,0:T(8,128)S(1)}, f32[256,256]{1,0:T(8,128)S(1)}, u32[]{:S(2)}, u32[]{:S(2)}) collective-permute-start(f32[256,256]{1,0:T(8,128)S(1)} %collective-permute-done.22.refs_3_), channel_id=1, source_target_pairs={{0,2},{1,5},{4,0},{5,9},{8,4},{9,13},{12,8},{13,15},{14,12},{15,11... | collective-permute-start | bytes 786440 | tf_op jit(solution)/shard_map/ppermute | solution.py:364
  88.2 6.4 %collective-permute-start.26 = (f32[256,256]{1,0:T(8,128)S(1)}, f32[256,256]{1,0:T(8,128)S(1)}, u32[]{:S(2)}, u32[]{:S(2)}) collective-permute-start(f32[256,256]{1,0:T(8,128)S(1)} %collective-permute-done.24.refs_4_), channel_id=1, source_target_pairs={{0,2},{1,5},{4,0},{5,9},{8,4},{9,13},{12,8},{13,15},{14,12},{15,11... | collective-permute-start | bytes 786440 | tf_op jit(solution)/shard_map/ppermute | solution.py:365
  91.7 6.4 %collective-permute-start.27 = (f32[256,256]{1,0:T(8,128)S(1)}, f32[256,256]{1,0:T(8,128)S(1)}, u32[]{:S(2)}, u32[]{:S(2)}) collective-permute-start(f32[256,256]{1,0:T(8,128)S(1)} %collective-permute-done.25.refs_5_), channel_id=1, source_target_pairs={{0,2},{1,5},{4,0},{5,9},{8,4},{9,13},{12,8},{13,15},{14,12},{15,11... | collective-permute-start | bytes 786440 | tf_op jit(solution)/shard_map/ppermute | solution.py:364
  94.5 6.4 %collective-permute-start.28 = (f32[256,256]{1,0:T(8,128)S(1)}, f32[256,256]{1,0:T(8,128)S(1)}, u32[]{:S(2)}, u32[]{:S(2)}) collective-permute-start(f32[256,256]{1,0:T(8,128)S(1)} %collective-permute-done.26.refs_6_), channel_id=1, source_target_pairs={{0,2},{1,5},{4,0},{5,9},{8,4},{9,13},{12,8},{13,15},{14,12},{15,11... | collective-permute-start | bytes 786440 | tf_op jit(solution)/shard_map/ppermute | solution.py:365
  98.1 6.4 %collective-permute-start.30 = (f32[256,256]{1,0:T(8,128)S(1)}, f32[256,256]{1,0:T(8,128)S(1)}, u32[]{:S(2)}, u32[]{:S(2)}) collective-permute-start(f32[256,256]{1,0:T(8,128)S(1)} %collective-permute-done.27.refs_7_), channel_id=1, source_target_pairs={{0,2},{1,5},{4,0},{5,9},{8,4},{9,13},{12,8},{13,15},{14,12},{15,11... | collective-permute-start | bytes 786440 | tf_op jit(solution)/shard_map/ppermute | solution.py:369
  101.7 2.8 %collective-permute-start.29 = (f32[256,256]{1,0:T(8,128)S(1)}, f32[256,256]{1,0:T(8,128)S(1)}, u32[]{:S(2)}, u32[]{:S(2)}) collective-permute-start(f32[256,256]{1,0:T(8,128)S(1)} %get-tuple-element.60), channel_id=1, source_target_pairs={{0,1},{1,0},{2,3},{3,2},{4,5},{5,4},{6,7},{7,6},{8,9},{9,8},{10,11... | collective-permute-start | bytes 786440 | tf_op jit(solution)/shard_map/ppermute | solution.py:377
  104.5 1.5 %collective-permute-start.31 = (f32[256,256]{1,0:T(8,128)S(1)}, f32[256,256]{1,0:T(8,128)S(1)}, u32[]{:S(2)}, u32[]{:S(2)}) collective-permute-start(f32[256,256]{1,0:T(8,128)S(1)} %collective-permute-done.30.refs_2_), channel_id=1, source_target_pairs={{0,1},{1,0},{2,3},{3,2},{4,5},{5,4},{6,7},{7,6},{8,9},{9,8},{10,11... | collective-permute-start | bytes 786440 | tf_op jit(solution)/shard_map/ppermute | solution.py:378
  113.2 1.6 %collective-permute-start.33 = (f32[256,256]{1,0:T(8,128)S(1)}, f32[256,256]{1,0:T(8,128)S(1)}, u32[]{:S(2)}, u32[]{:S(2)}) collective-permute-start(f32[256,256]{1,0:T(8,128)S(1)} %shard_map.75.refs_1_), channel_id=1, source_target_pairs={{0,1},{1,0},{2,3},{3,2},{4,5},{5,4},{6,7},{7,6},{8,9},{9,8},{10,11... | collective-permute-start | bytes 786440 | tf_op jit(solution)/shard_map/ppermute | solution.py:361
  113.3 6.4 %collective-permute-start.32 = (f32[256,256]{1,0:T(8,128)S(1)}, f32[256,256]{1,0:T(8,128)S(1)}, u32[]{:S(2)}, u32[]{:S(2)}) collective-permute-start(f32[256,256]{1,0:T(8,128)S(1)} %shard_map.75.refs_1_), channel_id=1, source_target_pairs={{0,2},{1,5},{4,0},{5,9},{8,4},{9,13},{12,8},{13,15},{14,12},{15,11... | collective-permute-start | bytes 786440 | tf_op jit(solution)/shard_map/ppermute | solution.py:364
  114.8 7.7 %collective-permute-start.34 = (f32[256,256]{1,0:T(8,128)S(1)}, f32[256,256]{1,0:T(8,128)S(1)}, u32[]{:S(2)}, u32[]{:S(2)}) collective-permute-start(f32[256,256]{1,0:T(8,128)S(1)} %collective-permute-done.33.refs_2_), channel_id=1, source_target_pairs={{0,2},{1,5},{4,0},{5,9},{8,4},{9,13},{12,8},{13,15},{14,12},{15,11... | collective-permute-start | bytes 786440 | tf_op jit(solution)/shard_map/ppermute | solution.py:365
  119.7 6.4 %collective-permute-start.35 = (f32[256,256]{1,0:T(8,128)S(1)}, f32[256,256]{1,0:T(8,128)S(1)}, u32[]{:S(2)}, u32[]{:S(2)}) collective-permute-start(f32[256,256]{1,0:T(8,128)S(1)} %collective-permute-done.32.refs_3_), channel_id=1, source_target_pairs={{0,2},{1,5},{4,0},{5,9},{8,4},{9,13},{12,8},{13,15},{14,12},{15,11... | collective-permute-start | bytes 786440 | tf_op jit(solution)/shard_map/ppermute | solution.py:364
  122.5 6.4 %collective-permute-start.36 = (f32[256,256]{1,0:T(8,128)S(1)}, f32[256,256]{1,0:T(8,128)S(1)}, u32[]{:S(2)}, u32[]{:S(2)}) collective-permute-start(f32[256,256]{1,0:T(8,128)S(1)} %collective-permute-done.34.refs_4_), channel_id=1, source_target_pairs={{0,2},{1,5},{4,0},{5,9},{8,4},{9,13},{12,8},{13,15},{14,12},{15,11... | collective-permute-start | bytes 786440 | tf_op jit(solution)/shard_map/ppermute | solution.py:365
  126.0 6.4 %collective-permute-start.37 = (f32[256,256]{1,0:T(8,128)S(1)}, f32[256,256]{1,0:T(8,128)S(1)}, u32[]{:S(2)}, u32[]{:S(2)}) collective-permute-start(f32[256,256]{1,0:T(8,128)S(1)} %collective-permute-done.35.refs_5_), channel_id=1, source_target_pairs={{0,2},{1,5},{4,0},{5,9},{8,4},{9,13},{12,8},{13,15},{14,12},{15,11... | collective-permute-start | bytes 786440 | tf_op jit(solution)/shard_map/ppermute | solution.py:364
  128.9 6.4 %collective-permute-start.38 = (f32[256,256]{1,0:T(8,128)S(1)}, f32[256,256]{1,0:T(8,128)S(1)}, u32[]{:S(2)}, u32[]{:S(2)}) collective-permute-start(f32[256,256]{1,0:T(8,128)S(1)} %collective-permute-done.36.refs_6_), channel_id=1, source_target_pairs={{0,2},{1,5},{4,0},{5,9},{8,4},{9,13},{12,8},{13,15},{14,12},{15,11... | collective-permute-start | bytes 786440 | tf_op jit(solution)/shard_map/ppermute | solution.py:365
  136.6 8.0 %collective-permute-start.39 = (f32[256,768]{1,0:T(8,128)S(1)}, f32[256,768]{1,0:T(8,128)S(1)}, u32[]{:S(2)}, u32[]{:S(2)}) collective-permute-start(f32[256,768]{1,0:T(8,128)S(1)} %get-tuple-element.65), channel_id=1, source_target_pairs={{0,1},{1,0},{2,3},{3,2},{4,5},{5,4},{6,7},{7,6},{8,9},{9,8},{10,11... | collective-permute-start | bytes 2359304 | tf_op jit(solution)/shard_map/ppermute | solution.py:377
  136.7 6.4 %collective-permute-start.40 = (f32[256,256]{1,0:T(8,128)S(1)}, f32[256,256]{1,0:T(8,128)S(1)}, u32[]{:S(2)}, u32[]{:S(2)}) collective-permute-start(f32[256,256]{1,0:T(8,128)S(1)} %collective-permute-done.37.refs_7_), channel_id=1, source_target_pairs={{0,2},{1,5},{4,0},{5,9},{8,4},{9,13},{12,8},{13,15},{14,12},{15,11... | collective-permute-start | bytes 786440 | tf_op jit(solution)/shard_map/ppermute | solution.py:369
  143.1 1.5 %collective-permute-start.41 = (f32[256,256]{1,0:T(8,128)S(1)}, f32[256,256]{1,0:T(8,128)S(1)}, u32[]{:S(2)}, u32[]{:S(2)}) collective-permute-start(f32[256,256]{1,0:T(8,128)S(1)} %collective-permute-done.40.refs_2_), channel_id=1, source_target_pairs={{0,1},{1,0},{2,3},{3,2},{4,5},{5,4},{6,7},{7,6},{8,9},{9,8},{10,11... | collective-permute-start | bytes 786440 | tf_op jit(solution)/shard_map/ppermute | solution.py:378

commit v8 on v7

--- a/solution.py
+++ b/solution.py
@@ -114,11 +114,15 @@
 
 
 def joined(weight_ref, base, part, refs, window):
-    keep_ref, other_ref, last_ref, last_other_ref = refs
-    side_y = last_ref.shape[1]
+    keep_ref, other_ref, last, last_other = refs
+    side_y = last.shape[1]
     columns = slice(part * side_y, (part + 1) * side_y)
     total = keep_ref[window, columns] + other_ref[window, columns]
-    return total + (weight_ref[base + 2 * part] * last_ref[window] + weight_ref[base + 2 * part + 1] * last_other_ref[window])
+    return total + (weight_ref[base + 2 * part] * last[window] + weight_ref[base + 2 * part + 1] * last_other[window])
+
+
+def whole(refs):
+    return jnp.concatenate([ref[...] for ref in refs[:2]]), jnp.concatenate([ref[...] for ref in refs[2:]])
 
 
 def first_spectral_kernel(weight_ref, base, keep_ref, other_ref, last_ref, last_other_ref, cos_ref, *refs):
@@ -132,9 +136,9 @@
     out_ref[...] = chebyshev_sum(field, mean_level, cos_ref, hop_refs, row_ref)
 
 
-def next_spectral_kernel(weight_ref, base, keep_ref, other_ref, last_ref, last_other_ref, cos_ref, *refs):
-    hop_refs, (mean_ref, add_ref, out_ref, row_ref) = refs[:4], refs[4:]
-    field = joined(weight_ref, base, 0, (keep_ref, other_ref, last_ref, last_other_ref), slice(None))
+def next_spectral_kernel(weight_ref, base, keep_ref, other_ref, *refs):
+    cos_ref, hop_refs, (mean_ref, add_ref, out_ref, row_ref) = refs[4], refs[5:9], refs[9:]
+    field = joined(weight_ref, base, 0, (keep_ref, other_ref, *whole(refs[:4])), slice(None))
     out_ref[...] = chebyshev_sum(field, mean_ref[...], cos_ref, hop_refs, row_ref) + add_ref[...]
 
 
@@ -212,10 +216,47 @@
         send_ref[side_x:, :] = sum(extra[2:])
 
 
-def finish_kernel(weight_ref, base, keep_ref, other_ref, last_ref, last_other_ref, *refs):
-    damp_ref, damp_next_ref, noise_ref, xh_ref, xl_ref, yh_ref, yl_ref = refs[:7]
-    out_refs = refs[7:]
-    sources = keep_ref, other_ref, last_ref, last_other_ref
+def gather_chunks_kernel(*refs, outs, base):
+    weight_ref, keep_ref, send_ref = refs[0], refs[-2], refs[-1]
+    own_ref, partner_ref = refs[1:3]
+    hops = [refs[place : place + 3] for place in range(3, len(refs) - 2, 3)]
+    side_x, side_y = own_ref.shape
+    head = hops[0][0].shape[0]
+    rest = side_x - head
+    count = 2 + 2 * len(hops)
+    rows = 16
+
+    def body(index, carry):
+        start = pl.multiple_of(index * rows, rows)
+        window = pl.ds(start, rows)
+        fields = [own_ref[window, :], partner_ref[window, :]]
+        for first, middle, second in hops:
+            fields.append(first[window, :] if carry[0] else middle[pl.ds(start - head, rows), :])
+            fields.append(middle[pl.ds(start + rest, rows), :] if carry[1] else second[pl.ds(start - rest, rows), :])
+        for target, skip, begin in ((keep_ref, 0, base), (send_ref, 2, base + outs * count)):
+            for part in range(outs):
+                place = begin + part * (count - skip) - skip
+                total = weight_ref[place + skip] * fields[skip]
+                for index_in in range(skip + 1, count):
+                    total = total + weight_ref[place + index_in] * fields[index_in]
+                target[window, part * side_y : (part + 1) * side_y] = total
+
+    def run(low, high, in_first, in_middle):
+        def step(index, carry):
+            body(index, (in_first, in_middle))
+            return carry
+
+        lax.fori_loop(low // rows, high // rows, step, 0)
+
+    run(0, rest, True, True)
+    run(rest, head, True, False)
+    run(head, side_x, False, False)
+
+
+def finish_kernel(weight_ref, base, keep_ref, other_ref, *refs):
+    damp_ref, damp_next_ref, noise_ref, xh_ref, xl_ref, yh_ref, yl_ref = refs[4:11]
+    out_refs = refs[11:]
+    sources = keep_ref, other_ref, *whole(refs[:4])
     slices = [joined(weight_ref, base, part, sources, slice(None)) for part in range(3)]
     if len(out_refs) == 2:
         out_refs[1][...] = slices[1]
@@ -378,6 +419,30 @@
         last_other = lax.ppermute(last, "tm", swap)
         return (beside[0], keep, other, last, last_other), beside
 
+    def around_in_chunks(own, base, outs, weights):
+        head = (side_x * 11 // 16) // 16 * 16
+        rest = side_x - head
+        partner = lax.ppermute(own, "tm", swap)
+        chunks = [own[:head], jnp.concatenate([own[head:], partner[:rest]]), partner[rest:]]
+        fields = [own, partner]
+        for _ in range(1, reach):
+            first = lax.ppermute(chunks[0], "tm", hop)
+            chunks = [first] + [lax.ppermute(chunk, "tm", hop) for chunk in chunks[1:]]
+            fields += chunks
+        last = lax.ppermute(chunks[0], "tm", hop)
+        tail = lax.ppermute(chunks[1][:rest], "tm", hop)
+
+        def kernel(*refs):
+            gather_chunks_kernel(*refs, outs=outs, base=base[0])
+
+        wide = shape(side_x, outs * side_y)
+        adds = 4 * outs * len(fields) * side_x * side_y
+        keep, send = call(kernel, (wide, wide), len(fields), passes=adds, scalars=1)(weights, *fields)
+        other = lax.ppermute(send, "tm", swap)
+        last_other = lax.ppermute(last, "tm", swap)
+        tail_other = lax.ppermute(tail, "tm", swap)
+        return weights, keep, other, last, tail, last_other, tail_other
+
     def based(kernel, base):
         def run(weight_ref, *refs):
             kernel(weight_ref, base[1], *refs)
@@ -407,13 +472,12 @@
     first, mean_level = call(first_kernel, first_outs, 9, scratch, work, 1)(*parts, cosine, *hops)
     first, damp_next, damp_wrap = lax.optimization_barrier((first, damp_next, damp_wrap))
     damp_next = damp_next + damp_wrap
-    beside = (weights,)
-    parts, beside = around(first, back, 3, beside)
-    (second_residual,) = call(finish, (field_shape,), 11, scalars=1)(*parts, damp, damp_next, noise, *hops)
-    parts, beside = around(second_residual, forward, 1, beside)
-    total = call(next_kernel, field_shape, 11, scratch, work, 1)(*parts, cosine, *hops, mean_level, first)
-    parts, beside = around(total, back, 3, beside)
-    residual, result = call(finish, (field_shape,) * 2, 11, scalars=1)(*parts, damp, damp_next, noise, *hops)
+    parts = around_in_chunks(first, back, 3, weights)
+    (second_residual,) = call(finish, (field_shape,), 13, scalars=1)(*parts, damp, damp_next, noise, *hops)
+    parts = around_in_chunks(second_residual, forward, 1, weights)
+    total = call(next_kernel, field_shape, 13, scratch, work, 1)(*parts, cosine, *hops, mean_level, first)
+    parts = around_in_chunks(total, back, 3, weights)
+    residual, result = call(finish, (field_shape,) * 2, 13, scalars=1)(*parts, damp, damp_next, noise, *hops)
     return result, residual
 
 

time: 147 us -> 152 us (1.034)
  waiting for transfers between devices: 96.2 us -> 100 us
    ppermute x0 -> x45, waiting for transfers between devices: none -> 89.3 us  [the longest x18 33 us: around_in_chunks(): chunks = [first] + [lax.ppermute(chunk, 'tm', hop) for chunk in chunks[1:]]]
    ppermute x12 -> x3, waiting for transfers between devices: 40.9 us -> 4.65 us  [around(): own = lax.ppermute(own, 'tm', hop)]
    ppermute x12 -> x3, waiting for transfers between devices: 29.2 us -> 4.11 us  [around(): partner = lax.ppermute(partner, 'tm', hop)]
    ppermute x4 -> x1, waiting for transfers between devices: 17.5 us -> 2.21 us  [around(): last = lax.ppermute(own, 'tm', hop)]
    ppermute x4 -> x1, waiting for transfers between devices: 4.56 us -> 0.01 us  [around(): last_other = lax.ppermute(last, 'tm', swap)]
    ppermute x4 -> x1, waiting for transfers between devices: 3.95 us -> 0.01 us  [around(): partner = lax.ppermute(own, 'tm', swap)]
    pallas_call x3 -> x6, Pallas kernels: 11.5 us -> 15.2 us  [the longest x1 7.07 us: by_ring(): call(next_kernel, field_shape, 13, scratch, work, 1)]
    pallas_call x4 -> x1, Pallas kernels: 4.34 us -> 0.83 us  [around(): call(kernel, (wide, wide), len(fields), passes=adds, scalars=1)]
  transfers between devices with their start and end apart: 42 -> 57, of which waited for: 34 -> 43; matrix products, arithmetic and copies ran while one was open for 0% -> 1% of each run, Pallas kernels for 6% -> 6%
where the time goes in v8:
time: 152 us
  waiting for transfers between devices  100 us (66%)
  Pallas kernels  25 us (16%)
  starting transfers between devices  24.8 us (16%)
    ppermute x18, waiting for transfers between devices, around_in_chunks(): chunks = [first] + [lax.ppermute(chunk, 'tm', hop) for chunk in chunks[1:]]  33 us
    ppermute x9, waiting for transfers between devices, around_in_chunks(): first = lax.ppermute(chunks[0], 'tm', hop)  23.3 us
    ppermute x3, waiting for transfers between devices, around_in_chunks(): tail = lax.ppermute(chunks[1][:rest], 'tm', hop)  13.3 us
    ppermute x3, waiting for transfers between devices, around_in_chunks(): last = lax.ppermute(chunks[0], 'tm', hop)  11.9 us
    ppermute x1, starting transfers between devices, by_ring(): damp_wrap = lax.ppermute(damp, 'tm', [(0, length - 1)])  7.66 us
    pallas_call x1, Pallas kernels, by_ring(): call(first_kernel, first_outs, 9, scratch, work, 1)(*parts, cosine, *hops)  7.14 us
    pallas_call x1, Pallas kernels, by_ring(): call(next_kernel, field_shape, 13, scratch, work, 1)  7.07 us
    ppermute x3, starting transfers between devices, around(): own = lax.ppermute(own, 'tm', hop)  6.49 us
  transfers between devices with their start and end apart: 57, of which 43 were waited for; matrix products, arithmetic and copies ran while one was open for 1% of the time, Pallas kernels for 6%

profile of v8, /device:TPU:0, one launch (start us, length us, event | category | flops | bytes accessed | tf_op | source)
XLA Modules:
  0.0 152.1 jit_solution(16054767774003546155)
XLA Ops:
  2.4 2.6 %collective-permute-start = (f32[264,256]{1,0:T(8,128)S(1)}, f32[264,256]{1,0:T(8,128)S(1)}, u32[]{:S(2)}, u32[]{:S(2)}) collective-permute-start(f32[264,256]{1,0:T(8,128)S(1)} %get-tuple-element.29.refs_1_), channel_id=1, source_target_pairs={{0,2},{1,5},{4,0},{5,9},{8,4},{9,13},{12,8},{13,15},{14,12},{15,11... | collective-permute-start | bytes 811016 | tf_op jit(solution)/shard_map/ppermute | solution.py:405
  6.3 1.6 %collective-permute-start.2 = (f32[264,256]{1,0:T(8,128)S(1)}, f32[264,256]{1,0:T(8,128)S(1)}, u32[]{:S(2)}, u32[]{:S(2)}) collective-permute-start(f32[264,256]{1,0:T(8,128)S(1)} %collective-permute-done.1.refs_2_), channel_id=1, source_target_pairs={{0,2},{1,5},{4,0},{5,9},{8,4},{9,13},{12,8},{13,15},{14,12},{15,11... | collective-permute-start | bytes 811016 | tf_op jit(solution)/shard_map/ppermute | solution.py:406
  7.9 1.6 %collective-permute-done.refs_3_ = f32[264,256]{1,0:T(8,128)S(1)} collective-permute-done((f32[264,256]{1,0:T(8,128)S(1)}, f32[264,256]{1,0:T(8,128)S(1)}, u32[]{:S(2)}, u32[]{:S(2)}) %collective-permute-start) | collective-permute-done | bytes 270368 | tf_op jit(solution)/shard_map/ppermute | solution.py:405
  9.4 2.0 %collective-permute-start.3 = (f32[264,256]{1,0:T(8,128)S(1)}, f32[264,256]{1,0:T(8,128)S(1)}, u32[]{:S(2)}, u32[]{:S(2)}) collective-permute-start(f32[264,256]{1,0:T(8,128)S(1)} %collective-permute-done.refs_3_), channel_id=1, source_target_pairs={{0,2},{1,5},{4,0},{5,9},{8,4},{9,13},{12,8},{13,15},{14,12},{15,11... | collective-permute-start | bytes 811016 | tf_op jit(solution)/shard_map/ppermute | solution.py:405
  12.8 1.6 %collective-permute-start.4 = (f32[264,256]{1,0:T(8,128)S(1)}, f32[264,256]{1,0:T(8,128)S(1)}, u32[]{:S(2)}, u32[]{:S(2)}) collective-permute-start(f32[264,256]{1,0:T(8,128)S(1)} %collective-permute-done.2.refs_4_), channel_id=1, source_target_pairs={{0,2},{1,5},{4,0},{5,9},{8,4},{9,13},{12,8},{13,15},{14,12},{15,11... | collective-permute-start | bytes 811016 | tf_op jit(solution)/shard_map/ppermute | solution.py:406
  14.4 1.6 %collective-permute-done.3.refs_5_ = f32[264,256]{1,0:T(8,128)S(1)} collective-permute-done((f32[264,256]{1,0:T(8,128)S(1)}, f32[264,256]{1,0:T(8,128)S(1)}, u32[]{:S(2)}, u32[]{:S(2)}) %collective-permute-start.3) | collective-permute-done | bytes 270368 | tf_op jit(solution)/shard_map/ppermute | solution.py:405
  15.9 2.0 %collective-permute-start.5 = (f32[264,256]{1,0:T(8,128)S(1)}, f32[264,256]{1,0:T(8,128)S(1)}, u32[]{:S(2)}, u32[]{:S(2)}) collective-permute-start(f32[264,256]{1,0:T(8,128)S(1)} %collective-permute-done.3.refs_5_), channel_id=1, source_target_pairs={{0,2},{1,5},{4,0},{5,9},{8,4},{9,13},{12,8},{13,15},{14,12},{15,11... | collective-permute-start | bytes 811016 | tf_op jit(solution)/shard_map/ppermute | solution.py:405
  19.2 1.6 %collective-permute-start.6 = (f32[264,256]{1,0:T(8,128)S(1)}, f32[264,256]{1,0:T(8,128)S(1)}, u32[]{:S(2)}, u32[]{:S(2)}) collective-permute-start(f32[264,256]{1,0:T(8,128)S(1)} %collective-permute-done.4.refs_6_), channel_id=1, source_target_pairs={{0,2},{1,5},{4,0},{5,9},{8,4},{9,13},{12,8},{13,15},{14,12},{15,11... | collective-permute-start | bytes 811016 | tf_op jit(solution)/shard_map/ppermute | solution.py:406
  20.8 1.6 %collective-permute-done.5.refs_7_ = f32[264,256]{1,0:T(8,128)S(1)} collective-permute-done((f32[264,256]{1,0:T(8,128)S(1)}, f32[264,256]{1,0:T(8,128)S(1)}, u32[]{:S(2)}, u32[]{:S(2)}) %collective-permute-start.5) | collective-permute-done | bytes 270368 | tf_op jit(solution)/shard_map/ppermute | solution.py:405
  22.4 2.0 %collective-permute-start.8 = (f32[264,256]{1,0:T(8,128)S(1)}, f32[264,256]{1,0:T(8,128)S(1)}, u32[]{:S(2)}, u32[]{:S(2)}) collective-permute-start(f32[264,256]{1,0:T(8,128)S(1)} %collective-permute-done.5.refs_7_), channel_id=1, source_target_pairs={{0,2},{1,5},{4,0},{5,9},{8,4},{9,13},{12,8},{13,15},{14,12},{15,11... | collective-permute-start | bytes 811016 | tf_op jit(solution)/shard_map/ppermute | solution.py:410
  26.6 2.2 %collective-permute-done.8.refs_2_ = f32[264,256]{1,0:T(8,128)S(1)} collective-permute-done((f32[264,256]{1,0:T(8,128)S(1)}, f32[264,256]{1,0:T(8,128)S(1)}, u32[]{:S(2)}, u32[]{:S(2)}) %collective-permute-start.8) | collective-permute-done | bytes 270368 | tf_op jit(solution)/shard_map/ppermute | solution.py:410
  30.1 7.7 %collective-permute-start.11 = (f32[256,256]{1,0:T(8,128)S(1)}, f32[256,256]{1,0:T(8,128)S(1)}, u32[]{:S(2)}, u32[]{:S(2)}) collective-permute-start(f32[256,256]{1,0:T(8,128)S(1)} %get-tuple-element.43.refs_6_), channel_id=1, source_target_pairs={{0,15},{16,31}} | collective-permute-start | bytes 786440 | tf_op jit(solution)/shard_map/ppermute | solution.py:467
  37.9 7.1 %shard_map.71 = (f32[256,256]{1,0:T(8,128)S(1)}, f32[1,256]{1,0:T(1,128)S(1)}) custom-call(f32[64]{0:T(128)S(1)} %dynamic-slice_bitcast_fusion.refs_0_.weight_ref, f32[264,256]{1,0:T(8,128)S(1)} %get-tuple-element.36.refs_0_, f32[264,256]{1,0:T(8,128)S(1)} %collective-permute-done.7.refs_1_, f32[264,256]{1,0:T(8,128)S(1)} %collective-permute-done.8.refs_2_, ...), custom_call_target="tpu_custom_call" | custom-call | flops 4026531840 | tf_op jit(solution)/shard_map/pallas_call | solution.py:472
  45.3 1.4 collective-permute-done.12.refs_2_
  46.9 3.9 %collective-permute-done.13.refs_3_ = f32[176,256]{1,0:T(8,128)S(1)} collective-permute-done((f32[176,256]{1,0:T(8,128)S(1)}, f32[176,256]{1,0:T(8,128)S(1)}, u32[]{:S(2)}, u32[]{:S(2)}) %collective-permute-start.13) | collective-permute-done | bytes 180256 | tf_op jit(solution)/shard_map/ppermute | solution.py:429
  50.8 1.9 %collective-permute-done.15.refs_5_ = f32[176,256]{1,0:T(8,128)S(1)} collective-permute-done((f32[176,256]{1,0:T(8,128)S(1)}, f32[176,256]{1,0:T(8,128)S(1)}, u32[]{:S(2)}, u32[]{:S(2)}) %collective-permute-start.15) | collective-permute-done | bytes 180256 | tf_op jit(solution)/shard_map/ppermute | solution.py:430
  52.7 1.7 %collective-permute-done.14.refs_4_ = f32[160,256]{1,0:T(8,128)S(1)} collective-permute-done((f32[160,256]{1,0:T(8,128)S(1)}, f32[160,256]{1,0:T(8,128)S(1)}, u32[]{:S(2)}, u32[]{:S(2)}) %collective-permute-start.14) | collective-permute-done | bytes 163872 | tf_op jit(solution)/shard_map/ppermute | solution.py:430
  54.4 1.9 %collective-permute-done.16.refs_6_ = f32[176,256]{1,0:T(8,128)S(1)} collective-permute-done((f32[176,256]{1,0:T(8,128)S(1)}, f32[176,256]{1,0:T(8,128)S(1)}, u32[]{:S(2)}, u32[]{:S(2)}) %collective-permute-start.16) | collective-permute-done | bytes 180256 | tf_op jit(solution)/shard_map/ppermute | solution.py:429
  56.4 1.9 %collective-permute-done.18.refs_8_ = f32[176,256]{1,0:T(8,128)S(1)} collective-permute-done((f32[176,256]{1,0:T(8,128)S(1)}, f32[176,256]{1,0:T(8,128)S(1)}, u32[]{:S(2)}, u32[]{:S(2)}) %collective-permute-start.18) | collective-permute-done | bytes 180256 | tf_op jit(solution)/shard_map/ppermute | solution.py:430
  58.3 1.7 %collective-permute-done.17.refs_7_ = f32[160,256]{1,0:T(8,128)S(1)} collective-permute-done((f32[160,256]{1,0:T(8,128)S(1)}, f32[160,256]{1,0:T(8,128)S(1)}, u32[]{:S(2)}, u32[]{:S(2)}) %collective-permute-start.17) | collective-permute-done | bytes 163872 | tf_op jit(solution)/shard_map/ppermute | solution.py:430
  60.1 1.9 %collective-permute-done.19.refs_9_ = f32[176,256]{1,0:T(8,128)S(1)} collective-permute-done((f32[176,256]{1,0:T(8,128)S(1)}, f32[176,256]{1,0:T(8,128)S(1)}, u32[]{:S(2)}, u32[]{:S(2)}) %collective-permute-start.19) | collective-permute-done | bytes 180256 | tf_op jit(solution)/shard_map/ppermute | solution.py:429
  62.0 3.7 %collective-permute-done.20.refs_10_ = f32[160,256]{1,0:T(8,128)S(1)} collective-permute-done((f32[160,256]{1,0:T(8,128)S(1)}, f32[160,256]{1,0:T(8,128)S(1)}, u32[]{:S(2)}, u32[]{:S(2)}) %collective-permute-start.20) | collective-permute-done | bytes 163872 | tf_op jit(solution)/shard_map/ppermute | solution.py:430
  65.7 1.4 shard_map.72
  67.3 5.5 %collective-permute-done.23.refs_2_ = f32[176,256]{1,0:T(8,128)S(1)} collective-permute-done((f32[176,256]{1,0:T(8,128)S(1)}, f32[176,256]{1,0:T(8,128)S(1)}, u32[]{:S(2)}, u32[]{:S(2)}) %collective-permute-start.23) | collective-permute-done | bytes 180256 | tf_op jit(solution)/shard_map/ppermute | solution.py:432
  72.8 4.4 %collective-permute-done.24.refs_3_ = f32[80,256]{1,0:T(8,128)S(1)} collective-permute-done((f32[80,256]{1,0:T(8,128)S(1)}, f32[80,256]{1,0:T(8,128)S(1)}, u32[]{:S(2)}, u32[]{:S(2)}) %collective-permute-start.24) | collective-permute-done | bytes 81952 | tf_op jit(solution)/shard_map/ppermute | solution.py:433
  78.5 1.8 %shard_map.73.refs_1_ = f32[256,256]{1,0:T(8,128)S(1)} custom-call(f32[64]{0:T(128)S(1)} %dynamic-slice_bitcast_fusion.refs_0_.weight_ref, f32[256,768]{1,0:T(8,128)S(1)} %get-tuple-element.45.refs_0_, f32[256,768]{1,0:T(8,128)S(1)} %collective-permute-done.22.refs_1_, f32[176,256]{1,0:T(8,128)S(1)} %collective-permute-done.23.refs_2_, ...), custom_call_target="tpu_custom_call" | custom-call | tf_op jit(solution)/shard_map/pallas_call | solution.py:476
  82.2 4.0 %collective-permute-done.28.refs_3_ = f32[176,256]{1,0:T(8,128)S(1)} collective-permute-done((f32[176,256]{1,0:T(8,128)S(1)}, f32[176,256]{1,0:T(8,128)S(1)}, u32[]{:S(2)}, u32[]{:S(2)}) %collective-permute-start.28) | collective-permute-done | bytes 180256 | tf_op jit(solution)/shard_map/ppermute | solution.py:429
  86.2 1.9 %collective-permute-done.30.refs_5_ = f32[176,256]{1,0:T(8,128)S(1)} collective-permute-done((f32[176,256]{1,0:T(8,128)S(1)}, f32[176,256]{1,0:T(8,128)S(1)}, u32[]{:S(2)}, u32[]{:S(2)}) %collective-permute-start.30) | collective-permute-done | bytes 180256 | tf_op jit(solution)/shard_map/ppermute | solution.py:430
  88.1 1.7 %collective-permute-done.29.refs_4_ = f32[160,256]{1,0:T(8,128)S(1)} collective-permute-done((f32[160,256]{1,0:T(8,128)S(1)}, f32[160,256]{1,0:T(8,128)S(1)}, u32[]{:S(2)}, u32[]{:S(2)}) %collective-permute-start.29) | collective-permute-done | bytes 163872 | tf_op jit(solution)/shard_map/ppermute | solution.py:430
  89.8 1.9 %collective-permute-done.31.refs_6_ = f32[176,256]{1,0:T(8,128)S(1)} collective-permute-done((f32[176,256]{1,0:T(8,128)S(1)}, f32[176,256]{1,0:T(8,128)S(1)}, u32[]{:S(2)}, u32[]{:S(2)}) %collective-permute-start.31) | collective-permute-done | bytes 180256 | tf_op jit(solution)/shard_map/ppermute | solution.py:429
  91.8 1.9 %collective-permute-done.33.refs_8_ = f32[176,256]{1,0:T(8,128)S(1)} collective-permute-done((f32[176,256]{1,0:T(8,128)S(1)}, f32[176,256]{1,0:T(8,128)S(1)}, u32[]{:S(2)}, u32[]{:S(2)}) %collective-permute-start.33) | collective-permute-done | bytes 180256 | tf_op jit(solution)/shard_map/ppermute | solution.py:430
  93.7 1.7 %collective-permute-done.32.refs_7_ = f32[160,256]{1,0:T(8,128)S(1)} collective-permute-done((f32[160,256]{1,0:T(8,128)S(1)}, f32[160,256]{1,0:T(8,128)S(1)}, u32[]{:S(2)}, u32[]{:S(2)}) %collective-permute-start.32) | collective-permute-done | bytes 163872 | tf_op jit(solution)/shard_map/ppermute | solution.py:430
  95.5 1.9 %collective-permute-done.34.refs_9_ = f32[176,256]{1,0:T(8,128)S(1)} collective-permute-done((f32[176,256]{1,0:T(8,128)S(1)}, f32[176,256]{1,0:T(8,128)S(1)}, u32[]{:S(2)}, u32[]{:S(2)}) %collective-permute-start.34) | collective-permute-done | bytes 180256 | tf_op jit(solution)/shard_map/ppermute | solution.py:429
  97.4 3.7 %collective-permute-done.35.refs_10_ = f32[160,256]{1,0:T(8,128)S(1)} collective-permute-done((f32[160,256]{1,0:T(8,128)S(1)}, f32[160,256]{1,0:T(8,128)S(1)}, u32[]{:S(2)}, u32[]{:S(2)}) %collective-permute-start.35) | collective-permute-done | bytes 163872 | tf_op jit(solution)/shard_map/ppermute | solution.py:430
  103.3 4.4 %collective-permute-done.39.refs_3_ = f32[80,256]{1,0:T(8,128)S(1)} collective-permute-done((f32[80,256]{1,0:T(8,128)S(1)}, f32[80,256]{1,0:T(8,128)S(1)}, u32[]{:S(2)}, u32[]{:S(2)}) %collective-permute-start.39) | collective-permute-done | bytes 81952 | tf_op jit(solution)/shard_map/ppermute | solution.py:433
  109.0 7.1 %shard_map.75.refs_1_ = f32[256,256]{1,0:T(8,128)S(1)} custom-call(f32[64]{0:T(128)S(1)} %dynamic-slice_bitcast_fusion.refs_0_.weight_ref, f32[256,256]{1,0:T(8,128)S(1)} %get-tuple-element.49.refs_0_, f32[256,256]{1,0:T(8,128)S(1)} %collective-permute-done.37.refs_1_, f32[176,256]{1,0:T(8,128)S(1)} %collective-permute-done.38.refs_2_, ...), custom_call_target="tpu_custom_call" | custom-call | flops 4026531840 | tf_op jit(solution)/shard_map/pallas_call | solution.py:478
  117.9 4.0 %collective-permute-done.43.refs_3_ = f32[176,256]{1,0:T(8,128)S(1)} collective-permute-done((f32[176,256]{1,0:T(8,128)S(1)}, f32[176,256]{1,0:T(8,128)S(1)}, u32[]{:S(2)}, u32[]{:S(2)}) %collective-permute-start.43) | collective-permute-done | bytes 180256 | tf_op jit(solution)/shard_map/ppermute | solution.py:429
  121.8 1.9 %collective-permute-done.45.refs_5_ = f32[176,256]{1,0:T(8,128)S(1)} collective-permute-done((f32[176,256]{1,0:T(8,128)S(1)}, f32[176,256]{1,0:T(8,128)S(1)}, u32[]{:S(2)}, u32[]{:S(2)}) %collective-permute-start.45) | collective-permute-done | bytes 180256 | tf_op jit(solution)/shard_map/ppermute | solution.py:430
  123.8 1.7 %collective-permute-done.44.refs_4_ = f32[160,256]{1,0:T(8,128)S(1)} collective-permute-done((f32[160,256]{1,0:T(8,128)S(1)}, f32[160,256]{1,0:T(8,128)S(1)}, u32[]{:S(2)}, u32[]{:S(2)}) %collective-permute-start.44) | collective-permute-done | bytes 163872 | tf_op jit(solution)/shard_map/ppermute | solution.py:430
  125.5 1.9 %collective-permute-done.46.refs_6_ = f32[176,256]{1,0:T(8,128)S(1)} collective-permute-done((f32[176,256]{1,0:T(8,128)S(1)}, f32[176,256]{1,0:T(8,128)S(1)}, u32[]{:S(2)}, u32[]{:S(2)}) %collective-permute-start.46) | collective-permute-done | bytes 180256 | tf_op jit(solution)/shard_map/ppermute | solution.py:429
  127.5 1.9 %collective-permute-done.48.refs_8_ = f32[176,256]{1,0:T(8,128)S(1)} collective-permute-done((f32[176,256]{1,0:T(8,128)S(1)}, f32[176,256]{1,0:T(8,128)S(1)}, u32[]{:S(2)}, u32[]{:S(2)}) %collective-permute-start.48) | collective-permute-done | bytes 180256 | tf_op jit(solution)/shard_map/ppermute | solution.py:430
  129.4 1.7 %collective-permute-done.47.refs_7_ = f32[160,256]{1,0:T(8,128)S(1)} collective-permute-done((f32[160,256]{1,0:T(8,128)S(1)}, f32[160,256]{1,0:T(8,128)S(1)}, u32[]{:S(2)}, u32[]{:S(2)}) %collective-permute-start.47) | collective-permute-done | bytes 163872 | tf_op jit(solution)/shard_map/ppermute | solution.py:430
  131.1 1.9 %collective-permute-done.49.refs_9_ = f32[176,256]{1,0:T(8,128)S(1)} collective-permute-done((f32[176,256]{1,0:T(8,128)S(1)}, f32[176,256]{1,0:T(8,128)S(1)}, u32[]{:S(2)}, u32[]{:S(2)}) %collective-permute-start.49) | collective-permute-done | bytes 180256 | tf_op jit(solution)/shard_map/ppermute | solution.py:429
  133.1 3.7 %collective-permute-done.50.refs_10_ = f32[160,256]{1,0:T(8,128)S(1)} collective-permute-done((f32[160,256]{1,0:T(8,128)S(1)}, f32[160,256]{1,0:T(8,128)S(1)}, u32[]{:S(2)}, u32[]{:S(2)}) %collective-permute-start.50) | collective-permute-done | bytes 163872 | tf_op jit(solution)/shard_map/ppermute | solution.py:430
  136.8 1.4 shard_map.76
  138.3 5.5 %collective-permute-done.53.refs_2_ = f32[176,256]{1,0:T(8,128)S(1)} collective-permute-done((f32[176,256]{1,0:T(8,128)S(1)}, f32[176,256]{1,0:T(8,128)S(1)}, u32[]{:S(2)}, u32[]{:S(2)}) %collective-permute-start.53) | collective-permute-done | bytes 180256 | tf_op jit(solution)/shard_map/ppermute | solution.py:432
  143.9 4.4 %collective-permute-done.54.refs_3_ = f32[80,256]{1,0:T(8,128)S(1)} collective-permute-done((f32[80,256]{1,0:T(8,128)S(1)}, f32[80,256]{1,0:T(8,128)S(1)}, u32[]{:S(2)}, u32[]{:S(2)}) %collective-permute-start.54) | collective-permute-done | bytes 81952 | tf_op jit(solution)/shard_map/ppermute | solution.py:433
  149.6 2.5 %shard_map.77 = (f32[256,256]{1,0:T(8,128)}, f32[256,256]{1,0:T(8,128)}) custom-call(f32[64]{0:T(128)S(1)} %dynamic-slice_bitcast_fusion.refs_0_.weight_ref, f32[256,768]{1,0:T(8,128)S(1)} %get-tuple-element.52.refs_0_, f32[256,768]{1,0:T(8,128)S(1)} %collective-permute-done.52.refs_1_, f32[176,256]{1,0:T(8,128)S(1)} %collective-permute-done.53.refs_2_, ...), custom_call_target="tpu_custom_call" | custom-call | tf_op jit(solution)/shard_map/pallas_call | solution.py:480
  (103 shorter events, 19.9 us)
Async XLA Ops:
  2.4 7.1 %collective-permute-start = (f32[264,256]{1,0:T(8,128)S(1)}, f32[264,256]{1,0:T(8,128)S(1)}, u32[]{:S(2)}, u32[]{:S(2)}) collective-permute-start(f32[264,256]{1,0:T(8,128)S(1)} %get-tuple-element.29.refs_1_), channel_id=1, source_target_pairs={{0,2},{1,5},{4,0},{5,9},{8,4},{9,13},{12,8},{13,15},{14,12},{15,11... | collective-permute-start | bytes 811016 | tf_op jit(solution)/shard_map/ppermute | solution.py:405
  6.3 6.5 %collective-permute-start.2 = (f32[264,256]{1,0:T(8,128)S(1)}, f32[264,256]{1,0:T(8,128)S(1)}, u32[]{:S(2)}, u32[]{:S(2)}) collective-permute-start(f32[264,256]{1,0:T(8,128)S(1)} %collective-permute-done.1.refs_2_), channel_id=1, source_target_pairs={{0,2},{1,5},{4,0},{5,9},{8,4},{9,13},{12,8},{13,15},{14,12},{15,11... | collective-permute-start | bytes 811016 | tf_op jit(solution)/shard_map/ppermute | solution.py:406
  9.4 6.5 %collective-permute-start.3 = (f32[264,256]{1,0:T(8,128)S(1)}, f32[264,256]{1,0:T(8,128)S(1)}, u32[]{:S(2)}, u32[]{:S(2)}) collective-permute-start(f32[264,256]{1,0:T(8,128)S(1)} %collective-permute-done.refs_3_), channel_id=1, source_target_pairs={{0,2},{1,5},{4,0},{5,9},{8,4},{9,13},{12,8},{13,15},{14,12},{15,11... | collective-permute-start | bytes 811016 | tf_op jit(solution)/shard_map/ppermute | solution.py:405
  12.8 6.5 %collective-permute-start.4 = (f32[264,256]{1,0:T(8,128)S(1)}, f32[264,256]{1,0:T(8,128)S(1)}, u32[]{:S(2)}, u32[]{:S(2)}) collective-permute-start(f32[264,256]{1,0:T(8,128)S(1)} %collective-permute-done.2.refs_4_), channel_id=1, source_target_pairs={{0,2},{1,5},{4,0},{5,9},{8,4},{9,13},{12,8},{13,15},{14,12},{15,11... | collective-permute-start | bytes 811016 | tf_op jit(solution)/shard_map/ppermute | solution.py:406
  15.9 6.5 %collective-permute-start.5 = (f32[264,256]{1,0:T(8,128)S(1)}, f32[264,256]{1,0:T(8,128)S(1)}, u32[]{:S(2)}, u32[]{:S(2)}) collective-permute-start(f32[264,256]{1,0:T(8,128)S(1)} %collective-permute-done.3.refs_5_), channel_id=1, source_target_pairs={{0,2},{1,5},{4,0},{5,9},{8,4},{9,13},{12,8},{13,15},{14,12},{15,11... | collective-permute-start | bytes 811016 | tf_op jit(solution)/shard_map/ppermute | solution.py:405
  19.2 6.5 %collective-permute-start.6 = (f32[264,256]{1,0:T(8,128)S(1)}, f32[264,256]{1,0:T(8,128)S(1)}, u32[]{:S(2)}, u32[]{:S(2)}) collective-permute-start(f32[264,256]{1,0:T(8,128)S(1)} %collective-permute-done.4.refs_6_), channel_id=1, source_target_pairs={{0,2},{1,5},{4,0},{5,9},{8,4},{9,13},{12,8},{13,15},{14,12},{15,11... | collective-permute-start | bytes 811016 | tf_op jit(solution)/shard_map/ppermute | solution.py:406
  22.4 6.5 %collective-permute-start.8 = (f32[264,256]{1,0:T(8,128)S(1)}, f32[264,256]{1,0:T(8,128)S(1)}, u32[]{:S(2)}, u32[]{:S(2)}) collective-permute-start(f32[264,256]{1,0:T(8,128)S(1)} %collective-permute-done.5.refs_7_), channel_id=1, source_target_pairs={{0,2},{1,5},{4,0},{5,9},{8,4},{9,13},{12,8},{13,15},{14,12},{15,11... | collective-permute-start | bytes 811016 | tf_op jit(solution)/shard_map/ppermute | solution.py:410
  26.5 11.3 %collective-permute-start.7 = (f32[264,256]{1,0:T(8,128)S(1)}, f32[264,256]{1,0:T(8,128)S(1)}, u32[]{:S(2)}, u32[]{:S(2)}) collective-permute-start(f32[264,256]{1,0:T(8,128)S(1)} %get-tuple-element.37), channel_id=1, source_target_pairs={{0,1},{1,0},{2,3},{3,2},{4,5},{5,4},{6,7},{7,6},{8,9},{9,8},{10,11... | collective-permute-start | bytes 811016 | tf_op jit(solution)/shard_map/ppermute | solution.py:418
  28.8 9.1 %collective-permute-start.9 = (f32[264,256]{1,0:T(8,128)S(1)}, f32[264,256]{1,0:T(8,128)S(1)}, u32[]{:S(2)}, u32[]{:S(2)}) collective-permute-start(f32[264,256]{1,0:T(8,128)S(1)} %collective-permute-done.8.refs_2_), channel_id=1, source_target_pairs={{0,1},{1,0},{2,3},{3,2},{4,5},{5,4},{6,7},{7,6},{8,9},{9,8},{10,11... | collective-permute-start | bytes 811016 | tf_op jit(solution)/shard_map/ppermute | solution.py:419
  28.8 16.2 %collective-permute-start.10 = (f32[256,256]{1,0:T(8,128)S(1)}, f32[256,256]{1,0:T(8,128)S(1)}, u32[]{:S(2)}, u32[]{:S(2)}) collective-permute-start(f32[256,256]{1,0:T(8,128)S(1)} %get-tuple-element.43.refs_6_), channel_id=1, source_target_pairs={{1,0},{2,1},{3,2},{4,3},{5,4},{6,5},{7,6},{8,7},{9,8},{10,9},{11,1... | collective-permute-start | bytes 786440 | tf_op jit(solution)/shard_map/ppermute | solution.py:468
  30.1 15.0 %collective-permute-start.11 = (f32[256,256]{1,0:T(8,128)S(1)}, f32[256,256]{1,0:T(8,128)S(1)}, u32[]{:S(2)}, u32[]{:S(2)}) collective-permute-start(f32[256,256]{1,0:T(8,128)S(1)} %get-tuple-element.43.refs_6_), channel_id=1, source_target_pairs={{0,15},{16,31}} | collective-permute-start | bytes 786440 | tf_op jit(solution)/shard_map/ppermute | solution.py:467
  45.2 5.5 %collective-permute-start.13 = (f32[176,256]{1,0:T(8,128)S(1)}, f32[176,256]{1,0:T(8,128)S(1)}, u32[]{:S(2)}, u32[]{:S(2)}) collective-permute-start(f32[176,256]{1,0:T(8,128)S(1)} %slice.45), channel_id=1, source_target_pairs={{0,2},{1,5},{4,0},{5,9},{8,4},{9,13},{12,8},{13,15},{14,12},{15,11... | collective-permute-start | bytes 540680 | tf_op jit(solution)/shard_map/ppermute | solution.py:429
  46.7 6.0 %collective-permute-start.15 = (f32[176,256]{1,0:T(8,128)S(1)}, f32[176,256]{1,0:T(8,128)S(1)}, u32[]{:S(2)}, u32[]{:S(2)}) collective-permute-start(f32[176,256]{1,0:T(8,128)S(1)} %slice.61), channel_id=1, source_target_pairs={{0,2},{1,5},{4,0},{5,9},{8,4},{9,13},{12,8},{13,15},{14,12},{15,11... | collective-permute-start | bytes 540680 | tf_op jit(solution)/shard_map/ppermute | solution.py:430
  46.8 7.6 %collective-permute-start.14 = (f32[160,256]{1,0:T(8,128)S(1)}, f32[160,256]{1,0:T(8,128)S(1)}, u32[]{:S(2)}, u32[]{:S(2)}) collective-permute-start(f32[160,256]{1,0:T(8,128)S(1)} %pad_maximum_fusion), channel_id=1, source_target_pairs={{0,2},{1,5},{4,0},{5,9},{8,4},{9,13},{12,8},{13,15},{14,12},{15,11... | collective-permute-start | bytes 491528 | tf_op jit(solution)/shard_map/ppermute | solution.py:430
  50.8 5.6 %collective-permute-start.16 = (f32[176,256]{1,0:T(8,128)S(1)}, f32[176,256]{1,0:T(8,128)S(1)}, u32[]{:S(2)}, u32[]{:S(2)}) collective-permute-start(f32[176,256]{1,0:T(8,128)S(1)} %collective-permute-done.13.refs_3_), channel_id=1, source_target_pairs={{0,2},{1,5},{4,0},{5,9},{8,4},{9,13},{12,8},{13,15},{14,12},{15,11... | collective-permute-start | bytes 540680 | tf_op jit(solution)/shard_map/ppermute | solution.py:429
  52.7 5.6 %collective-permute-start.18 = (f32[176,256]{1,0:T(8,128)S(1)}, f32[176,256]{1,0:T(8,128)S(1)}, u32[]{:S(2)}, u32[]{:S(2)}) collective-permute-start(f32[176,256]{1,0:T(8,128)S(1)} %collective-permute-done.15.refs_5_), channel_id=1, source_target_pairs={{0,2},{1,5},{4,0},{5,9},{8,4},{9,13},{12,8},{13,15},{14,12},{15,11... | collective-permute-start | bytes 540680 | tf_op jit(solution)/shard_map/ppermute | solution.py:430
  54.4 5.6 %collective-permute-start.17 = (f32[160,256]{1,0:T(8,128)S(1)}, f32[160,256]{1,0:T(8,128)S(1)}, u32[]{:S(2)}, u32[]{:S(2)}) collective-permute-start(f32[160,256]{1,0:T(8,128)S(1)} %collective-permute-done.14.refs_4_), channel_id=1, source_target_pairs={{0,2},{1,5},{4,0},{5,9},{8,4},{9,13},{12,8},{13,15},{14,12},{15,11... | collective-permute-start | bytes 491528 | tf_op jit(solution)/shard_map/ppermute | solution.py:430
  56.4 5.6 %collective-permute-start.19 = (f32[176,256]{1,0:T(8,128)S(1)}, f32[176,256]{1,0:T(8,128)S(1)}, u32[]{:S(2)}, u32[]{:S(2)}) collective-permute-start(f32[176,256]{1,0:T(8,128)S(1)} %collective-permute-done.16.refs_6_), channel_id=1, source_target_pairs={{0,2},{1,5},{4,0},{5,9},{8,4},{9,13},{12,8},{13,15},{14,12},{15,11... | collective-permute-start | bytes 540680 | tf_op jit(solution)/shard_map/ppermute | solution.py:429
  58.3 7.4 %collective-permute-start.21 = (f32[176,256]{1,0:T(8,128)S(1)}, f32[176,256]{1,0:T(8,128)S(1)}, u32[]{:S(2)}, u32[]{:S(2)}) collective-permute-start(f32[176,256]{1,0:T(8,128)S(1)} %collective-permute-done.18.refs_8_), channel_id=1, source_target_pairs={{0,2},{1,5},{4,0},{5,9},{8,4},{9,13},{12,8},{13,15},{14,12},{15,11... | collective-permute-start | bytes 540680 | tf_op jit(solution)/shard_map/ppermute | solution.py:430
  60.1 5.6 %collective-permute-start.20 = (f32[160,256]{1,0:T(8,128)S(1)}, f32[160,256]{1,0:T(8,128)S(1)}, u32[]{:S(2)}, u32[]{:S(2)}) collective-permute-start(f32[160,256]{1,0:T(8,128)S(1)} %collective-permute-done.17.refs_7_), channel_id=1, source_target_pairs={{0,2},{1,5},{4,0},{5,9},{8,4},{9,13},{12,8},{13,15},{14,12},{15,11... | collective-permute-start | bytes 491528 | tf_op jit(solution)/shard_map/ppermute | solution.py:430
  67.1 11.4 %collective-permute-start.22 = (f32[256,768]{1,0:T(8,128)S(1)}, f32[256,768]{1,0:T(8,128)S(1)}, u32[]{:S(2)}, u32[]{:S(2)}) collective-permute-start(f32[256,768]{1,0:T(8,128)S(1)} %get-tuple-element.46), channel_id=1, source_target_pairs={{0,1},{1,0},{2,3},{3,2},{4,5},{5,4},{6,7},{7,6},{8,9},{9,8},{10,11... | collective-permute-start | bytes 2359304 | tf_op jit(solution)/shard_map/ppermute | solution.py:441
  67.2 5.5 %collective-permute-start.23 = (f32[176,256]{1,0:T(8,128)S(1)}, f32[176,256]{1,0:T(8,128)S(1)}, u32[]{:S(2)}, u32[]{:S(2)}) collective-permute-start(f32[176,256]{1,0:T(8,128)S(1)} %collective-permute-done.19.refs_9_), channel_id=1, source_target_pairs={{0,2},{1,5},{4,0},{5,9},{8,4},{9,13},{12,8},{13,15},{14,12},{15,11... | collective-permute-start | bytes 540680 | tf_op jit(solution)/shard_map/ppermute | solution.py:432
  72.7 4.6 %collective-permute-start.25 = (f32[176,256]{1,0:T(8,128)S(1)}, f32[176,256]{1,0:T(8,128)S(1)}, u32[]{:S(2)}, u32[]{:S(2)}) collective-permute-start(f32[176,256]{1,0:T(8,128)S(1)} %collective-permute-done.23.refs_2_), channel_id=1, source_target_pairs={{0,1},{1,0},{2,3},{3,2},{4,5},{5,4},{6,7},{7,6},{8,9},{9,8},{10,11... | collective-permute-start | bytes 540680 | tf_op jit(solution)/shard_map/ppermute | solution.py:442
  80.6 5.5 %collective-permute-start.28 = (f32[176,256]{1,0:T(8,128)S(1)}, f32[176,256]{1,0:T(8,128)S(1)}, u32[]{:S(2)}, u32[]{:S(2)}) collective-permute-start(f32[176,256]{1,0:T(8,128)S(1)} %slice.63), channel_id=1, source_target_pairs={{0,2},{1,5},{4,0},{5,9},{8,4},{9,13},{12,8},{13,15},{14,12},{15,11... | collective-permute-start | bytes 540680 | tf_op jit(solution)/shard_map/ppermute | solution.py:429
  82.0 6.1 %collective-permute-start.30 = (f32[176,256]{1,0:T(8,128)S(1)}, f32[176,256]{1,0:T(8,128)S(1)}, u32[]{:S(2)}, u32[]{:S(2)}) collective-permute-start(f32[176,256]{1,0:T(8,128)S(1)} %slice.66), channel_id=1, source_target_pairs={{0,2},{1,5},{4,0},{5,9},{8,4},{9,13},{12,8},{13,15},{14,12},{15,11... | collective-permute-start | bytes 540680 | tf_op jit(solution)/shard_map/ppermute | solution.py:430
  82.1 7.7 %collective-permute-start.29 = (f32[160,256]{1,0:T(8,128)S(1)}, f32[160,256]{1,0:T(8,128)S(1)}, u32[]{:S(2)}, u32[]{:S(2)}) collective-permute-start(f32[160,256]{1,0:T(8,128)S(1)} %pad_maximum_fusion.1), channel_id=1, source_target_pairs={{0,2},{1,5},{4,0},{5,9},{8,4},{9,13},{12,8},{13,15},{14,12},{15,11... | collective-permute-start | bytes 491528 | tf_op jit(solution)/shard_map/ppermute | solution.py:430
  86.2 5.6 %collective-permute-start.31 = (f32[176,256]{1,0:T(8,128)S(1)}, f32[176,256]{1,0:T(8,128)S(1)}, u32[]{:S(2)}, u32[]{:S(2)}) collective-permute-start(f32[176,256]{1,0:T(8,128)S(1)} %collective-permute-done.28.refs_3_), channel_id=1, source_target_pairs={{0,2},{1,5},{4,0},{5,9},{8,4},{9,13},{12,8},{13,15},{14,12},{15,11... | collective-permute-start | bytes 540680 | tf_op jit(solution)/shard_map/ppermute | solution.py:429
  88.1 5.6 %collective-permute-start.33 = (f32[176,256]{1,0:T(8,128)S(1)}, f32[176,256]{1,0:T(8,128)S(1)}, u32[]{:S(2)}, u32[]{:S(2)}) collective-permute-start(f32[176,256]{1,0:T(8,128)S(1)} %collective-permute-done.30.refs_5_), channel_id=1, source_target_pairs={{0,2},{1,5},{4,0},{5,9},{8,4},{9,13},{12,8},{13,15},{14,12},{15,11... | collective-permute-start | bytes 540680 | tf_op jit(solution)/shard_map/ppermute | solution.py:430
  89.8 5.6 %collective-permute-start.32 = (f32[160,256]{1,0:T(8,128)S(1)}, f32[160,256]{1,0:T(8,128)S(1)}, u32[]{:S(2)}, u32[]{:S(2)}) collective-permute-start(f32[160,256]{1,0:T(8,128)S(1)} %collective-permute-done.29.refs_4_), channel_id=1, source_target_pairs={{0,2},{1,5},{4,0},{5,9},{8,4},{9,13},{12,8},{13,15},{14,12},{15,11... | collective-permute-start | bytes 491528 | tf_op jit(solution)/shard_map/ppermute | solution.py:430
  91.8 5.6 %collective-permute-start.34 = (f32[176,256]{1,0:T(8,128)S(1)}, f32[176,256]{1,0:T(8,128)S(1)}, u32[]{:S(2)}, u32[]{:S(2)}) collective-permute-start(f32[176,256]{1,0:T(8,128)S(1)} %collective-permute-done.31.refs_6_), channel_id=1, source_target_pairs={{0,2},{1,5},{4,0},{5,9},{8,4},{9,13},{12,8},{13,15},{14,12},{15,11... | collective-permute-start | bytes 540680 | tf_op jit(solution)/shard_map/ppermute | solution.py:429
  93.7 7.4 %collective-permute-start.36 = (f32[176,256]{1,0:T(8,128)S(1)}, f32[176,256]{1,0:T(8,128)S(1)}, u32[]{:S(2)}, u32[]{:S(2)}) collective-permute-start(f32[176,256]{1,0:T(8,128)S(1)} %collective-permute-done.33.refs_8_), channel_id=1, source_target_pairs={{0,2},{1,5},{4,0},{5,9},{8,4},{9,13},{12,8},{13,15},{14,12},{15,11... | collective-permute-start | bytes 540680 | tf_op jit(solution)/shard_map/ppermute | solution.py:430
  95.5 5.6 %collective-permute-start.35 = (f32[160,256]{1,0:T(8,128)S(1)}, f32[160,256]{1,0:T(8,128)S(1)}, u32[]{:S(2)}, u32[]{:S(2)}) collective-permute-start(f32[160,256]{1,0:T(8,128)S(1)} %collective-permute-done.32.refs_7_), channel_id=1, source_target_pairs={{0,2},{1,5},{4,0},{5,9},{8,4},{9,13},{12,8},{13,15},{14,12},{15,11... | collective-permute-start | bytes 491528 | tf_op jit(solution)/shard_map/ppermute | solution.py:430
  97.4 5.6 %collective-permute-start.38 = (f32[176,256]{1,0:T(8,128)S(1)}, f32[176,256]{1,0:T(8,128)S(1)}, u32[]{:S(2)}, u32[]{:S(2)}) collective-permute-start(f32[176,256]{1,0:T(8,128)S(1)} %collective-permute-done.34.refs_9_), channel_id=1, source_target_pairs={{0,2},{1,5},{4,0},{5,9},{8,4},{9,13},{12,8},{13,15},{14,12},{15,11... | collective-permute-start | bytes 540680 | tf_op jit(solution)/shard_map/ppermute | solution.py:432
  102.0 7.0 %collective-permute-start.37 = (f32[256,256]{1,0:T(8,128)S(1)}, f32[256,256]{1,0:T(8,128)S(1)}, u32[]{:S(2)}, u32[]{:S(2)}) collective-permute-start(f32[256,256]{1,0:T(8,128)S(1)} %get-tuple-element.50), channel_id=1, source_target_pairs={{0,1},{1,0},{2,3},{3,2},{4,5},{5,4},{6,7},{7,6},{8,9},{9,8},{10,11... | collective-permute-start | bytes 786440 | tf_op jit(solution)/shard_map/ppermute | solution.py:441
  103.0 4.7 %collective-permute-start.40 = (f32[176,256]{1,0:T(8,128)S(1)}, f32[176,256]{1,0:T(8,128)S(1)}, u32[]{:S(2)}, u32[]{:S(2)}) collective-permute-start(f32[176,256]{1,0:T(8,128)S(1)} %collective-permute-done.38.refs_2_), channel_id=1, source_target_pairs={{0,1},{1,0},{2,3},{3,2},{4,5},{5,4},{6,7},{7,6},{8,9},{9,8},{10,11... | collective-permute-start | bytes 540680 | tf_op jit(solution)/shard_map/ppermute | solution.py:442
  103.0 4.7 %collective-permute-start.39 = (f32[80,256]{1,0:T(8,128)S(1)}, f32[80,256]{1,0:T(8,128)S(1)}, u32[]{:S(2)}, u32[]{:S(2)}) collective-permute-start(f32[80,256]{1,0:T(8,128)S(1)} %slice.67), channel_id=1, source_target_pairs={{0,2},{1,5},{4,0},{5,9},{8,4},{9,13},{12,8},{13,15},{14,12},{15,11... | collective-permute-start | bytes 245768 | tf_op jit(solution)/shard_map/ppermute | solution.py:433
  116.3 5.5 %collective-permute-start.43 = (f32[176,256]{1,0:T(8,128)S(1)}, f32[176,256]{1,0:T(8,128)S(1)}, u32[]{:S(2)}, u32[]{:S(2)}) collective-permute-start(f32[176,256]{1,0:T(8,128)S(1)} %slice.68), channel_id=1, source_target_pairs={{0,2},{1,5},{4,0},{5,9},{8,4},{9,13},{12,8},{13,15},{14,12},{15,11... | collective-permute-start | bytes 540680 | tf_op jit(solution)/shard_map/ppermute | solution.py:429
  117.7 6.1 %collective-permute-start.45 = (f32[176,256]{1,0:T(8,128)S(1)}, f32[176,256]{1,0:T(8,128)S(1)}, u32[]{:S(2)}, u32[]{:S(2)}) collective-permute-start(f32[176,256]{1,0:T(8,128)S(1)} %slice.71), channel_id=1, source_target_pairs={{0,2},{1,5},{4,0},{5,9},{8,4},{9,13},{12,8},{13,15},{14,12},{15,11... | collective-permute-start | bytes 540680 | tf_op jit(solution)/shard_map/ppermute | solution.py:430
  117.8 7.7 %collective-permute-start.44 = (f32[160,256]{1,0:T(8,128)S(1)}, f32[160,256]{1,0:T(8,128)S(1)}, u32[]{:S(2)}, u32[]{:S(2)}) collective-permute-start(f32[160,256]{1,0:T(8,128)S(1)} %pad_maximum_fusion.2), channel_id=1, source_target_pairs={{0,2},{1,5},{4,0},{5,9},{8,4},{9,13},{12,8},{13,15},{14,12},{15,11... | collective-permute-start | bytes 491528 | tf_op jit(solution)/shard_map/ppermute | solution.py:430
  121.8 5.6 %collective-permute-start.46 = (f32[176,256]{1,0:T(8,128)S(1)}, f32[176,256]{1,0:T(8,128)S(1)}, u32[]{:S(2)}, u32[]{:S(2)}) collective-permute-start(f32[176,256]{1,0:T(8,128)S(1)} %collective-permute-done.43.refs_3_), channel_id=1, source_target_pairs={{0,2},{1,5},{4,0},{5,9},{8,4},{9,13},{12,8},{13,15},{14,12},{15,11... | collective-permute-start | bytes 540680 | tf_op jit(solution)/shard_map/ppermute | solution.py:429
  123.8 5.6 %collective-permute-start.48 = (f32[176,256]{1,0:T(8,128)S(1)}, f32[176,256]{1,0:T(8,128)S(1)}, u32[]{:S(2)}, u32[]{:S(2)}) collective-permute-start(f32[176,256]{1,0:T(8,128)S(1)} %collective-permute-done.45.refs_5_), channel_id=1, source_target_pairs={{0,2},{1,5},{4,0},{5,9},{8,4},{9,13},{12,8},{13,15},{14,12},{15,11... | collective-permute-start | bytes 540680 | tf_op jit(solution)/shard_map/ppermute | solution.py:430
  125.5 5.6 %collective-permute-start.47 = (f32[160,256]{1,0:T(8,128)S(1)}, f32[160,256]{1,0:T(8,128)S(1)}, u32[]{:S(2)}, u32[]{:S(2)}) collective-permute-start(f32[160,256]{1,0:T(8,128)S(1)} %collective-permute-done.44.refs_4_), channel_id=1, source_target_pairs={{0,2},{1,5},{4,0},{5,9},{8,4},{9,13},{12,8},{13,15},{14,12},{15,11... | collective-permute-start | bytes 491528 | tf_op jit(solution)/shard_map/ppermute | solution.py:430
  127.4 5.6 %collective-permute-start.49 = (f32[176,256]{1,0:T(8,128)S(1)}, f32[176,256]{1,0:T(8,128)S(1)}, u32[]{:S(2)}, u32[]{:S(2)}) collective-permute-start(f32[176,256]{1,0:T(8,128)S(1)} %collective-permute-done.46.refs_6_), channel_id=1, source_target_pairs={{0,2},{1,5},{4,0},{5,9},{8,4},{9,13},{12,8},{13,15},{14,12},{15,11... | collective-permute-start | bytes 540680 | tf_op jit(solution)/shard_map/ppermute | solution.py:429
  129.4 7.4 %collective-permute-start.51 = (f32[176,256]{1,0:T(8,128)S(1)}, f32[176,256]{1,0:T(8,128)S(1)}, u32[]{:S(2)}, u32[]{:S(2)}) collective-permute-start(f32[176,256]{1,0:T(8,128)S(1)} %collective-permute-done.48.refs_8_), channel_id=1, source_target_pairs={{0,2},{1,5},{4,0},{5,9},{8,4},{9,13},{12,8},{13,15},{14,12},{15,11... | collective-permute-start | bytes 540680 | tf_op jit(solution)/shard_map/ppermute | solution.py:430
  131.1 5.6 %collective-permute-start.50 = (f32[160,256]{1,0:T(8,128)S(1)}, f32[160,256]{1,0:T(8,128)S(1)}, u32[]{:S(2)}, u32[]{:S(2)}) collective-permute-start(f32[160,256]{1,0:T(8,128)S(1)} %collective-permute-done.47.refs_7_), channel_id=1, source_target_pairs={{0,2},{1,5},{4,0},{5,9},{8,4},{9,13},{12,8},{13,15},{14,12},{15,11... | collective-permute-start | bytes 491528 | tf_op jit(solution)/shard_map/ppermute | solution.py:430
  138.2 11.4 %collective-permute-start.52 = (f32[256,768]{1,0:T(8,128)S(1)}, f32[256,768]{1,0:T(8,128)S(1)}, u32[]{:S(2)}, u32[]{:S(2)}) collective-permute-start(f32[256,768]{1,0:T(8,128)S(1)} %get-tuple-element.53), channel_id=1, source_target_pairs={{0,1},{1,0},{2,3},{3,2},{4,5},{5,4},{6,7},{7,6},{8,9},{9,8},{10,11... | collective-permute-start | bytes 2359304 | tf_op jit(solution)/shard_map/ppermute | solution.py:441
  138.3 5.5 %collective-permute-start.53 = (f32[176,256]{1,0:T(8,128)S(1)}, f32[176,256]{1,0:T(8,128)S(1)}, u32[]{:S(2)}, u32[]{:S(2)}) collective-permute-start(f32[176,256]{1,0:T(8,128)S(1)} %collective-permute-done.49.refs_9_), channel_id=1, source_target_pairs={{0,2},{1,5},{4,0},{5,9},{8,4},{9,13},{12,8},{13,15},{14,12},{15,11... | collective-permute-start | bytes 540680 | tf_op jit(solution)/shard_map/ppermute | solution.py:432
  143.8 4.5 %collective-permute-start.55 = (f32[176,256]{1,0:T(8,128)S(1)}, f32[176,256]{1,0:T(8,128)S(1)}, u32[]{:S(2)}, u32[]{:S(2)}) collective-permute-start(f32[176,256]{1,0:T(8,128)S(1)} %collective-permute-done.53.refs_2_), channel_id=1, source_target_pairs={{0,1},{1,0},{2,3},{3,2},{4,5},{5,4},{6,7},{7,6},{8,9},{9,8},{10,11... | collective-permute-start | bytes 540680 | tf_op jit(solution)/shard_map/ppermute | solution.py:442
  (12 other events, 36.5 us)

commit v9 on v8

--- a/solution.py
+++ b/solution.py
@@ -420,14 +420,16 @@
         return (beside[0], keep, other, last, last_other), beside
 
     def around_in_chunks(own, base, outs, weights):
-        head = (side_x * 11 // 16) // 16 * 16
+        head = (side_x * 3 // 4) // 16 * 16
         rest = side_x - head
         partner = lax.ppermute(own, "tm", swap)
         chunks = [own[:head], jnp.concatenate([own[head:], partner[:rest]]), partner[rest:]]
         fields = [own, partner]
         for _ in range(1, reach):
             first = lax.ppermute(chunks[0], "tm", hop)
-            chunks = [first] + [lax.ppermute(chunk, "tm", hop) for chunk in chunks[1:]]
+            middle = lax.ppermute(chunks[1], "tm", hop)
+            second = lax.ppermute(chunks[2], "tm", hop)
+            chunks = [first, middle, second]
             fields += chunks
         last = lax.ppermute(chunks[0], "tm", hop)
         tail = lax.ppermute(chunks[1][:rest], "tm", hop)

time: 152 us -> 161 us (1.059)
  waiting for transfers between devices: 100 us -> 108 us
    ppermute x18, waiting for transfers between devices: 33 us -> 44.1 us  [the longest x9 32.5 us: around_in_chunks(): middle = lax.ppermute(chunks[1], 'tm', hop)]
    ppermute x9, waiting for transfers between devices: 23.3 us -> 20.4 us  [around_in_chunks(): first = lax.ppermute(chunks[0], 'tm', hop)]
  transfers between devices with their start and end apart: 57 -> 57, of which waited for: 43 -> 40; matrix products, arithmetic and copies ran while one was open for 1% -> 1% of each run, Pallas kernels for 6% -> 6%
where the time goes in v9:
time: 161 us
  waiting for transfers between devices  108 us (67%)
  starting transfers between devices  25.3 us (16%)
  Pallas kernels  25.1 us (16%)
    ppermute x9, waiting for transfers between devices, around_in_chunks(): middle = lax.ppermute(chunks[1], 'tm', hop)  32.5 us
    ppermute x9, waiting for transfers between devices, around_in_chunks(): first = lax.ppermute(chunks[0], 'tm', hop)  20.4 us
    ppermute x3, waiting for transfers between devices, around_in_chunks(): tail = lax.ppermute(chunks[1][:rest], 'tm', hop)  12.8 us
    ppermute x3, waiting for transfers between devices, around_in_chunks(): last = lax.ppermute(chunks[0], 'tm', hop)  12.4 us
    ppermute x9, waiting for transfers between devices, around_in_chunks(): second = lax.ppermute(chunks[2], 'tm', hop)  11.6 us
    ppermute x1, starting transfers between devices, by_ring(): damp_wrap = lax.ppermute(damp, 'tm', [(0, length - 1)])  7.66 us
    pallas_call x1, Pallas kernels, by_ring(): call(first_kernel, first_outs, 9, scratch, work, 1)(*parts, cosine, *hops)  7.14 us
    pallas_call x1, Pallas kernels, by_ring(): call(next_kernel, field_shape, 13, scratch, work, 1)  7.13 us
  transfers between devices with their start and end apart: 57, of which 40 were waited for; matrix products, arithmetic and copies ran while one was open for 1% of the time, Pallas kernels for 6%

profile of v9, /device:TPU:0, one launch (start us, length us, event | category | flops | bytes accessed | tf_op | source)
XLA Modules:
  0.0 160.9 jit_solution(5065669333917447427)
XLA Ops:
  2.4 2.6 %collective-permute-start = (f32[264,256]{1,0:T(8,128)S(1)}, f32[264,256]{1,0:T(8,128)S(1)}, u32[]{:S(2)}, u32[]{:S(2)}) collective-permute-start(f32[264,256]{1,0:T(8,128)S(1)} %get-tuple-element.29.refs_1_), channel_id=1, source_target_pairs={{0,2},{1,5},{4,0},{5,9},{8,4},{9,13},{12,8},{13,15},{14,12},{15,11... | collective-permute-start | bytes 811016 | tf_op jit(solution)/shard_map/ppermute | solution.py:405
  6.3 1.6 collective-permute-start.2
  7.9 1.6 collective-permute-done.refs_3_
  9.4 2.0 %collective-permute-start.3 = (f32[264,256]{1,0:T(8,128)S(1)}, f32[264,256]{1,0:T(8,128)S(1)}, u32[]{:S(2)}, u32[]{:S(2)}) collective-permute-start(f32[264,256]{1,0:T(8,128)S(1)} %collective-permute-done.refs_3_), channel_id=1, source_target_pairs={{0,2},{1,5},{4,0},{5,9},{8,4},{9,13},{12,8},{13,15},{14,12},{15,11... | collective-permute-start | bytes 811016 | tf_op jit(solution)/shard_map/ppermute | solution.py:405
  11.4 1.4 collective-permute-done.2.refs_4_
  12.8 1.6 collective-permute-start.4
  14.4 1.6 collective-permute-done.3.refs_5_
  15.9 2.0 %collective-permute-start.5 = (f32[264,256]{1,0:T(8,128)S(1)}, f32[264,256]{1,0:T(8,128)S(1)}, u32[]{:S(2)}, u32[]{:S(2)}) collective-permute-start(f32[264,256]{1,0:T(8,128)S(1)} %collective-permute-done.3.refs_5_), channel_id=1, source_target_pairs={{0,2},{1,5},{4,0},{5,9},{8,4},{9,13},{12,8},{13,15},{14,12},{15,11... | collective-permute-start | bytes 811016 | tf_op jit(solution)/shard_map/ppermute | solution.py:405
  17.9 1.4 collective-permute-done.4.refs_6_
  19.2 1.6 collective-permute-start.6
  20.8 1.6 collective-permute-done.5.refs_7_
  22.4 2.0 %collective-permute-start.8 = (f32[264,256]{1,0:T(8,128)S(1)}, f32[264,256]{1,0:T(8,128)S(1)}, u32[]{:S(2)}, u32[]{:S(2)}) collective-permute-start(f32[264,256]{1,0:T(8,128)S(1)} %collective-permute-done.5.refs_7_), channel_id=1, source_target_pairs={{0,2},{1,5},{4,0},{5,9},{8,4},{9,13},{12,8},{13,15},{14,12},{15,11... | collective-permute-start | bytes 811016 | tf_op jit(solution)/shard_map/ppermute | solution.py:410
  24.3 1.4 collective-permute-done.6.refs_8_
  26.6 2.2 %collective-permute-done.8.refs_2_ = f32[264,256]{1,0:T(8,128)S(1)} collective-permute-done((f32[264,256]{1,0:T(8,128)S(1)}, f32[264,256]{1,0:T(8,128)S(1)}, u32[]{:S(2)}, u32[]{:S(2)}) %collective-permute-start.8) | collective-permute-done | bytes 270368 | tf_op jit(solution)/shard_map/ppermute | solution.py:410
  30.1 7.7 %collective-permute-start.11 = (f32[256,256]{1,0:T(8,128)S(1)}, f32[256,256]{1,0:T(8,128)S(1)}, u32[]{:S(2)}, u32[]{:S(2)}) collective-permute-start(f32[256,256]{1,0:T(8,128)S(1)} %get-tuple-element.43.refs_6_), channel_id=1, source_target_pairs={{0,15},{16,31}} | collective-permute-start | bytes 786440 | tf_op jit(solution)/shard_map/ppermute | solution.py:469
  37.9 7.1 %shard_map.71 = (f32[256,256]{1,0:T(8,128)S(1)}, f32[1,256]{1,0:T(1,128)S(1)}) custom-call(f32[64]{0:T(128)S(1)} %dynamic-slice_bitcast_fusion.refs_0_.weight_ref, f32[264,256]{1,0:T(8,128)S(1)} %get-tuple-element.36.refs_0_, f32[264,256]{1,0:T(8,128)S(1)} %collective-permute-done.7.refs_1_, f32[264,256]{1,0:T(8,128)S(1)} %collective-permute-done.8.refs_2_, ...), custom_call_target="tpu_custom_call" | custom-call | flops 4026531840 | tf_op jit(solution)/shard_map/pallas_call | solution.py:474
  45.3 1.4 collective-permute-done.12.refs_2_
  46.8 4.1 %collective-permute-done.13.refs_3_ = f32[192,256]{1,0:T(8,128)S(1)} collective-permute-done((f32[192,256]{1,0:T(8,128)S(1)}, f32[192,256]{1,0:T(8,128)S(1)}, u32[]{:S(2)}, u32[]{:S(2)}) %collective-permute-start.13) | collective-permute-done | bytes 196640 | tf_op jit(solution)/shard_map/ppermute | solution.py:429
  51.0 2.0 %collective-permute-done.15.refs_5_ = f32[192,256]{1,0:T(8,128)S(1)} collective-permute-done((f32[192,256]{1,0:T(8,128)S(1)}, f32[192,256]{1,0:T(8,128)S(1)}, u32[]{:S(2)}, u32[]{:S(2)}) %collective-permute-start.15) | collective-permute-done | bytes 196640 | tf_op jit(solution)/shard_map/ppermute | solution.py:431
  53.0 5.0 %collective-permute-done.14.refs_4_ = f32[128,256]{1,0:T(8,128)S(1)} collective-permute-done((f32[128,256]{1,0:T(8,128)S(1)}, f32[128,256]{1,0:T(8,128)S(1)}, u32[]{:S(2)}, u32[]{:S(2)}) %collective-permute-start.14) | collective-permute-done | bytes 131104 | tf_op jit(solution)/shard_map/ppermute | solution.py:430
  58.0 2.1 %collective-permute-done.18.refs_8_ = f32[192,256]{1,0:T(8,128)S(1)} collective-permute-done((f32[192,256]{1,0:T(8,128)S(1)}, f32[192,256]{1,0:T(8,128)S(1)}, u32[]{:S(2)}, u32[]{:S(2)}) %collective-permute-start.18) | collective-permute-done | bytes 196640 | tf_op jit(solution)/shard_map/ppermute | solution.py:431
  60.1 2.9 %collective-permute-done.17.refs_7_ = f32[128,256]{1,0:T(8,128)S(1)} collective-permute-done((f32[128,256]{1,0:T(8,128)S(1)}, f32[128,256]{1,0:T(8,128)S(1)}, u32[]{:S(2)}, u32[]{:S(2)}) %collective-permute-start.17) | collective-permute-done | bytes 131104 | tf_op jit(solution)/shard_map/ppermute | solution.py:430
  63.0 2.1 %collective-permute-done.19.refs_9_ = f32[192,256]{1,0:T(8,128)S(1)} collective-permute-done((f32[192,256]{1,0:T(8,128)S(1)}, f32[192,256]{1,0:T(8,128)S(1)}, u32[]{:S(2)}, u32[]{:S(2)}) %collective-permute-start.19) | collective-permute-done | bytes 196640 | tf_op jit(solution)/shard_map/ppermute | solution.py:429
  65.1 3.5 %collective-permute-done.20.refs_10_ = f32[128,256]{1,0:T(8,128)S(1)} collective-permute-done((f32[128,256]{1,0:T(8,128)S(1)}, f32[128,256]{1,0:T(8,128)S(1)}, u32[]{:S(2)}, u32[]{:S(2)}) %collective-permute-start.20) | collective-permute-done | bytes 131104 | tf_op jit(solution)/shard_map/ppermute | solution.py:430
  68.6 1.4 shard_map.72
  70.2 5.7 %collective-permute-done.23.refs_2_ = f32[192,256]{1,0:T(8,128)S(1)} collective-permute-done((f32[192,256]{1,0:T(8,128)S(1)}, f32[192,256]{1,0:T(8,128)S(1)}, u32[]{:S(2)}, u32[]{:S(2)}) %collective-permute-start.23) | collective-permute-done | bytes 196640 | tf_op jit(solution)/shard_map/ppermute | solution.py:434
  75.9 4.3 %collective-permute-done.24.refs_3_ = f32[64,256]{1,0:T(8,128)S(1)} collective-permute-done((f32[64,256]{1,0:T(8,128)S(1)}, f32[64,256]{1,0:T(8,128)S(1)}, u32[]{:S(2)}, u32[]{:S(2)}) %collective-permute-start.24) | collective-permute-done | bytes 65568 | tf_op jit(solution)/shard_map/ppermute | solution.py:435
  81.4 1.8 %shard_map.73.refs_1_ = f32[256,256]{1,0:T(8,128)S(1)} custom-call(f32[64]{0:T(128)S(1)} %dynamic-slice_bitcast_fusion.refs_0_.weight_ref, f32[256,768]{1,0:T(8,128)S(1)} %get-tuple-element.45.refs_0_, f32[256,768]{1,0:T(8,128)S(1)} %collective-permute-done.22.refs_1_, f32[192,256]{1,0:T(8,128)S(1)} %collective-permute-done.23.refs_2_, ...), custom_call_target="tpu_custom_call" | custom-call | tf_op jit(solution)/shard_map/pallas_call | solution.py:478
  84.9 4.3 %collective-permute-done.28.refs_3_ = f32[192,256]{1,0:T(8,128)S(1)} collective-permute-done((f32[192,256]{1,0:T(8,128)S(1)}, f32[192,256]{1,0:T(8,128)S(1)}, u32[]{:S(2)}, u32[]{:S(2)}) %collective-permute-start.28) | collective-permute-done | bytes 196640 | tf_op jit(solution)/shard_map/ppermute | solution.py:429
  89.3 2.0 %collective-permute-done.30.refs_5_ = f32[192,256]{1,0:T(8,128)S(1)} collective-permute-done((f32[192,256]{1,0:T(8,128)S(1)}, f32[192,256]{1,0:T(8,128)S(1)}, u32[]{:S(2)}, u32[]{:S(2)}) %collective-permute-start.30) | collective-permute-done | bytes 196640 | tf_op jit(solution)/shard_map/ppermute | solution.py:431
  91.3 3.6 %collective-permute-done.31.refs_6_ = f32[192,256]{1,0:T(8,128)S(1)} collective-permute-done((f32[192,256]{1,0:T(8,128)S(1)}, f32[192,256]{1,0:T(8,128)S(1)}, u32[]{:S(2)}, u32[]{:S(2)}) %collective-permute-start.31) | collective-permute-done | bytes 196640 | tf_op jit(solution)/shard_map/ppermute | solution.py:429
  94.9 1.4 collective-permute-done.29.refs_4_
  96.3 2.1 %collective-permute-done.33.refs_8_ = f32[192,256]{1,0:T(8,128)S(1)} collective-permute-done((f32[192,256]{1,0:T(8,128)S(1)}, f32[192,256]{1,0:T(8,128)S(1)}, u32[]{:S(2)}, u32[]{:S(2)}) %collective-permute-start.33) | collective-permute-done | bytes 196640 | tf_op jit(solution)/shard_map/ppermute | solution.py:431
  98.4 3.6 %collective-permute-done.32.refs_7_ = f32[128,256]{1,0:T(8,128)S(1)} collective-permute-done((f32[128,256]{1,0:T(8,128)S(1)}, f32[128,256]{1,0:T(8,128)S(1)}, u32[]{:S(2)}, u32[]{:S(2)}) %collective-permute-start.32) | collective-permute-done | bytes 131104 | tf_op jit(solution)/shard_map/ppermute | solution.py:430
  102.0 4.9 %collective-permute-done.35.refs_10_ = f32[128,256]{1,0:T(8,128)S(1)} collective-permute-done((f32[128,256]{1,0:T(8,128)S(1)}, f32[128,256]{1,0:T(8,128)S(1)}, u32[]{:S(2)}, u32[]{:S(2)}) %collective-permute-start.35) | collective-permute-done | bytes 131104 | tf_op jit(solution)/shard_map/ppermute | solution.py:430
  109.3 4.3 %collective-permute-done.39.refs_3_ = f32[64,256]{1,0:T(8,128)S(1)} collective-permute-done((f32[64,256]{1,0:T(8,128)S(1)}, f32[64,256]{1,0:T(8,128)S(1)}, u32[]{:S(2)}, u32[]{:S(2)}) %collective-permute-start.39) | collective-permute-done | bytes 65568 | tf_op jit(solution)/shard_map/ppermute | solution.py:435
  114.8 7.1 %shard_map.75.refs_1_ = f32[256,256]{1,0:T(8,128)S(1)} custom-call(f32[64]{0:T(128)S(1)} %dynamic-slice_bitcast_fusion.refs_0_.weight_ref, f32[256,256]{1,0:T(8,128)S(1)} %get-tuple-element.49.refs_0_, f32[256,256]{1,0:T(8,128)S(1)} %collective-permute-done.37.refs_1_, f32[192,256]{1,0:T(8,128)S(1)} %collective-permute-done.38.refs_2_, ...), custom_call_target="tpu_custom_call" | custom-call | flops 4026531840 | tf_op jit(solution)/shard_map/pallas_call | solution.py:480
  123.7 4.2 %collective-permute-done.43.refs_3_ = f32[192,256]{1,0:T(8,128)S(1)} collective-permute-done((f32[192,256]{1,0:T(8,128)S(1)}, f32[192,256]{1,0:T(8,128)S(1)}, u32[]{:S(2)}, u32[]{:S(2)}) %collective-permute-start.43) | collective-permute-done | bytes 196640 | tf_op jit(solution)/shard_map/ppermute | solution.py:429
  128.3 1.7 %collective-permute-done.45.refs_5_ = f32[192,256]{1,0:T(8,128)S(1)} collective-permute-done((f32[192,256]{1,0:T(8,128)S(1)}, f32[192,256]{1,0:T(8,128)S(1)}, u32[]{:S(2)}, u32[]{:S(2)}) %collective-permute-start.45) | collective-permute-done | bytes 196640 | tf_op jit(solution)/shard_map/ppermute | solution.py:431
  130.0 5.0 %collective-permute-done.44.refs_4_ = f32[128,256]{1,0:T(8,128)S(1)} collective-permute-done((f32[128,256]{1,0:T(8,128)S(1)}, f32[128,256]{1,0:T(8,128)S(1)}, u32[]{:S(2)}, u32[]{:S(2)}) %collective-permute-start.44) | collective-permute-done | bytes 131104 | tf_op jit(solution)/shard_map/ppermute | solution.py:430
  135.3 1.7 %collective-permute-done.48.refs_8_ = f32[192,256]{1,0:T(8,128)S(1)} collective-permute-done((f32[192,256]{1,0:T(8,128)S(1)}, f32[192,256]{1,0:T(8,128)S(1)}, u32[]{:S(2)}, u32[]{:S(2)}) %collective-permute-start.48) | collective-permute-done | bytes 196640 | tf_op jit(solution)/shard_map/ppermute | solution.py:431
  137.1 2.9 %collective-permute-done.47.refs_7_ = f32[128,256]{1,0:T(8,128)S(1)} collective-permute-done((f32[128,256]{1,0:T(8,128)S(1)}, f32[128,256]{1,0:T(8,128)S(1)}, u32[]{:S(2)}, u32[]{:S(2)}) %collective-permute-start.47) | collective-permute-done | bytes 131104 | tf_op jit(solution)/shard_map/ppermute | solution.py:430
  139.9 2.1 %collective-permute-done.49.refs_9_ = f32[192,256]{1,0:T(8,128)S(1)} collective-permute-done((f32[192,256]{1,0:T(8,128)S(1)}, f32[192,256]{1,0:T(8,128)S(1)}, u32[]{:S(2)}, u32[]{:S(2)}) %collective-permute-start.49) | collective-permute-done | bytes 196640 | tf_op jit(solution)/shard_map/ppermute | solution.py:429
  142.0 3.5 %collective-permute-done.50.refs_10_ = f32[128,256]{1,0:T(8,128)S(1)} collective-permute-done((f32[128,256]{1,0:T(8,128)S(1)}, f32[128,256]{1,0:T(8,128)S(1)}, u32[]{:S(2)}, u32[]{:S(2)}) %collective-permute-start.50) | collective-permute-done | bytes 131104 | tf_op jit(solution)/shard_map/ppermute | solution.py:430
  145.5 1.4 shard_map.76
  147.1 5.7 %collective-permute-done.53.refs_2_ = f32[192,256]{1,0:T(8,128)S(1)} collective-permute-done((f32[192,256]{1,0:T(8,128)S(1)}, f32[192,256]{1,0:T(8,128)S(1)}, u32[]{:S(2)}, u32[]{:S(2)}) %collective-permute-start.53) | collective-permute-done | bytes 196640 | tf_op jit(solution)/shard_map/ppermute | solution.py:434
  152.8 4.3 %collective-permute-done.54.refs_3_ = f32[64,256]{1,0:T(8,128)S(1)} collective-permute-done((f32[64,256]{1,0:T(8,128)S(1)}, f32[64,256]{1,0:T(8,128)S(1)}, u32[]{:S(2)}, u32[]{:S(2)}) %collective-permute-start.54) | collective-permute-done | bytes 65568 | tf_op jit(solution)/shard_map/ppermute | solution.py:435
  158.4 2.5 %shard_map.77 = (f32[256,256]{1,0:T(8,128)}, f32[256,256]{1,0:T(8,128)}) custom-call(f32[64]{0:T(128)S(1)} %dynamic-slice_bitcast_fusion.refs_0_.weight_ref, f32[256,768]{1,0:T(8,128)S(1)} %get-tuple-element.52.refs_0_, f32[256,768]{1,0:T(8,128)S(1)} %collective-permute-done.52.refs_1_, f32[192,256]{1,0:T(8,128)S(1)} %collective-permute-done.53.refs_2_, ...), custom_call_target="tpu_custom_call" | custom-call | tf_op jit(solution)/shard_map/pallas_call | solution.py:482
  (103 shorter events, 16.4 us)
Async XLA Ops:
  2.4 7.1 %collective-permute-start = (f32[264,256]{1,0:T(8,128)S(1)}, f32[264,256]{1,0:T(8,128)S(1)}, u32[]{:S(2)}, u32[]{:S(2)}) collective-permute-start(f32[264,256]{1,0:T(8,128)S(1)} %get-tuple-element.29.refs_1_), channel_id=1, source_target_pairs={{0,2},{1,5},{4,0},{5,9},{8,4},{9,13},{12,8},{13,15},{14,12},{15,11... | collective-permute-start | bytes 811016 | tf_op jit(solution)/shard_map/ppermute | solution.py:405
  6.3 6.5 %collective-permute-start.2 = (f32[264,256]{1,0:T(8,128)S(1)}, f32[264,256]{1,0:T(8,128)S(1)}, u32[]{:S(2)}, u32[]{:S(2)}) collective-permute-start(f32[264,256]{1,0:T(8,128)S(1)} %collective-permute-done.1.refs_2_), channel_id=1, source_target_pairs={{0,2},{1,5},{4,0},{5,9},{8,4},{9,13},{12,8},{13,15},{14,12},{15,11... | collective-permute-start | bytes 811016 | tf_op jit(solution)/shard_map/ppermute | solution.py:406
  9.4 6.5 %collective-permute-start.3 = (f32[264,256]{1,0:T(8,128)S(1)}, f32[264,256]{1,0:T(8,128)S(1)}, u32[]{:S(2)}, u32[]{:S(2)}) collective-permute-start(f32[264,256]{1,0:T(8,128)S(1)} %collective-permute-done.refs_3_), channel_id=1, source_target_pairs={{0,2},{1,5},{4,0},{5,9},{8,4},{9,13},{12,8},{13,15},{14,12},{15,11... | collective-permute-start | bytes 811016 | tf_op jit(solution)/shard_map/ppermute | solution.py:405
  12.8 6.5 %collective-permute-start.4 = (f32[264,256]{1,0:T(8,128)S(1)}, f32[264,256]{1,0:T(8,128)S(1)}, u32[]{:S(2)}, u32[]{:S(2)}) collective-permute-start(f32[264,256]{1,0:T(8,128)S(1)} %collective-permute-done.2.refs_4_), channel_id=1, source_target_pairs={{0,2},{1,5},{4,0},{5,9},{8,4},{9,13},{12,8},{13,15},{14,12},{15,11... | collective-permute-start | bytes 811016 | tf_op jit(solution)/shard_map/ppermute | solution.py:406
  15.9 6.5 %collective-permute-start.5 = (f32[264,256]{1,0:T(8,128)S(1)}, f32[264,256]{1,0:T(8,128)S(1)}, u32[]{:S(2)}, u32[]{:S(2)}) collective-permute-start(f32[264,256]{1,0:T(8,128)S(1)} %collective-permute-done.3.refs_5_), channel_id=1, source_target_pairs={{0,2},{1,5},{4,0},{5,9},{8,4},{9,13},{12,8},{13,15},{14,12},{15,11... | collective-permute-start | bytes 811016 | tf_op jit(solution)/shard_map/ppermute | solution.py:405
  19.2 6.5 %collective-permute-start.6 = (f32[264,256]{1,0:T(8,128)S(1)}, f32[264,256]{1,0:T(8,128)S(1)}, u32[]{:S(2)}, u32[]{:S(2)}) collective-permute-start(f32[264,256]{1,0:T(8,128)S(1)} %collective-permute-done.4.refs_6_), channel_id=1, source_target_pairs={{0,2},{1,5},{4,0},{5,9},{8,4},{9,13},{12,8},{13,15},{14,12},{15,11... | collective-permute-start | bytes 811016 | tf_op jit(solution)/shard_map/ppermute | solution.py:406
  22.4 6.5 %collective-permute-start.8 = (f32[264,256]{1,0:T(8,128)S(1)}, f32[264,256]{1,0:T(8,128)S(1)}, u32[]{:S(2)}, u32[]{:S(2)}) collective-permute-start(f32[264,256]{1,0:T(8,128)S(1)} %collective-permute-done.5.refs_7_), channel_id=1, source_target_pairs={{0,2},{1,5},{4,0},{5,9},{8,4},{9,13},{12,8},{13,15},{14,12},{15,11... | collective-permute-start | bytes 811016 | tf_op jit(solution)/shard_map/ppermute | solution.py:410
  26.5 11.3 %collective-permute-start.7 = (f32[264,256]{1,0:T(8,128)S(1)}, f32[264,256]{1,0:T(8,128)S(1)}, u32[]{:S(2)}, u32[]{:S(2)}) collective-permute-start(f32[264,256]{1,0:T(8,128)S(1)} %get-tuple-element.37), channel_id=1, source_target_pairs={{0,1},{1,0},{2,3},{3,2},{4,5},{5,4},{6,7},{7,6},{8,9},{9,8},{10,11... | collective-permute-start | bytes 811016 | tf_op jit(solution)/shard_map/ppermute | solution.py:418
  28.8 9.1 %collective-permute-start.9 = (f32[264,256]{1,0:T(8,128)S(1)}, f32[264,256]{1,0:T(8,128)S(1)}, u32[]{:S(2)}, u32[]{:S(2)}) collective-permute-start(f32[264,256]{1,0:T(8,128)S(1)} %collective-permute-done.8.refs_2_), channel_id=1, source_target_pairs={{0,1},{1,0},{2,3},{3,2},{4,5},{5,4},{6,7},{7,6},{8,9},{9,8},{10,11... | collective-permute-start | bytes 811016 | tf_op jit(solution)/shard_map/ppermute | solution.py:419
  28.8 16.2 %collective-permute-start.10 = (f32[256,256]{1,0:T(8,128)S(1)}, f32[256,256]{1,0:T(8,128)S(1)}, u32[]{:S(2)}, u32[]{:S(2)}) collective-permute-start(f32[256,256]{1,0:T(8,128)S(1)} %get-tuple-element.43.refs_6_), channel_id=1, source_target_pairs={{1,0},{2,1},{3,2},{4,3},{5,4},{6,5},{7,6},{8,7},{9,8},{10,9},{11,1... | collective-permute-start | bytes 786440 | tf_op jit(solution)/shard_map/ppermute | solution.py:470
  30.1 15.0 %collective-permute-start.11 = (f32[256,256]{1,0:T(8,128)S(1)}, f32[256,256]{1,0:T(8,128)S(1)}, u32[]{:S(2)}, u32[]{:S(2)}) collective-permute-start(f32[256,256]{1,0:T(8,128)S(1)} %get-tuple-element.43.refs_6_), channel_id=1, source_target_pairs={{0,15},{16,31}} | collective-permute-start | bytes 786440 | tf_op jit(solution)/shard_map/ppermute | solution.py:469
  45.2 5.7 %collective-permute-start.13 = (f32[192,256]{1,0:T(8,128)S(1)}, f32[192,256]{1,0:T(8,128)S(1)}, u32[]{:S(2)}, u32[]{:S(2)}) collective-permute-start(f32[192,256]{1,0:T(8,128)S(1)} %slice.45), channel_id=1, source_target_pairs={{0,2},{1,5},{4,0},{5,9},{8,4},{9,13},{12,8},{13,15},{14,12},{15,11... | collective-permute-start | bytes 589832 | tf_op jit(solution)/shard_map/ppermute | solution.py:429
  46.7 6.3 %collective-permute-start.15 = (f32[192,256]{1,0:T(8,128)S(1)}, f32[192,256]{1,0:T(8,128)S(1)}, u32[]{:S(2)}, u32[]{:S(2)}) collective-permute-start(f32[192,256]{1,0:T(8,128)S(1)} %slice.61), channel_id=1, source_target_pairs={{0,2},{1,5},{4,0},{5,9},{8,4},{9,13},{12,8},{13,15},{14,12},{15,11... | collective-permute-start | bytes 589832 | tf_op jit(solution)/shard_map/ppermute | solution.py:431
  50.9 7.1 %collective-permute-start.16 = (f32[192,256]{1,0:T(8,128)S(1)}, f32[192,256]{1,0:T(8,128)S(1)}, u32[]{:S(2)}, u32[]{:S(2)}) collective-permute-start(f32[192,256]{1,0:T(8,128)S(1)} %collective-permute-done.13.refs_3_), channel_id=1, source_target_pairs={{0,2},{1,5},{4,0},{5,9},{8,4},{9,13},{12,8},{13,15},{14,12},{15,11... | collective-permute-start | bytes 589832 | tf_op jit(solution)/shard_map/ppermute | solution.py:429
  50.9 7.0 %collective-permute-start.14 = (f32[128,256]{1,0:T(8,128)S(1)}, f32[128,256]{1,0:T(8,128)S(1)}, u32[]{:S(2)}, u32[]{:S(2)}) collective-permute-start(f32[128,256]{1,0:T(8,128)S(1)} %pad_maximum_fusion), channel_id=1, source_target_pairs={{0,2},{1,5},{4,0},{5,9},{8,4},{9,13},{12,8},{13,15},{14,12},{15,11... | collective-permute-start | bytes 393224 | tf_op jit(solution)/shard_map/ppermute | solution.py:430
  53.0 7.1 %collective-permute-start.18 = (f32[192,256]{1,0:T(8,128)S(1)}, f32[192,256]{1,0:T(8,128)S(1)}, u32[]{:S(2)}, u32[]{:S(2)}) collective-permute-start(f32[192,256]{1,0:T(8,128)S(1)} %collective-permute-done.15.refs_5_), channel_id=1, source_target_pairs={{0,2},{1,5},{4,0},{5,9},{8,4},{9,13},{12,8},{13,15},{14,12},{15,11... | collective-permute-start | bytes 589832 | tf_op jit(solution)/shard_map/ppermute | solution.py:431
  58.0 5.0 %collective-permute-start.17 = (f32[128,256]{1,0:T(8,128)S(1)}, f32[128,256]{1,0:T(8,128)S(1)}, u32[]{:S(2)}, u32[]{:S(2)}) collective-permute-start(f32[128,256]{1,0:T(8,128)S(1)} %collective-permute-done.14.refs_4_), channel_id=1, source_target_pairs={{0,2},{1,5},{4,0},{5,9},{8,4},{9,13},{12,8},{13,15},{14,12},{15,11... | collective-permute-start | bytes 393224 | tf_op jit(solution)/shard_map/ppermute | solution.py:430
  58.0 7.1 %collective-permute-start.19 = (f32[192,256]{1,0:T(8,128)S(1)}, f32[192,256]{1,0:T(8,128)S(1)}, u32[]{:S(2)}, u32[]{:S(2)}) collective-permute-start(f32[192,256]{1,0:T(8,128)S(1)} %collective-permute-done.16.refs_6_), channel_id=1, source_target_pairs={{0,2},{1,5},{4,0},{5,9},{8,4},{9,13},{12,8},{13,15},{14,12},{15,11... | collective-permute-start | bytes 589832 | tf_op jit(solution)/shard_map/ppermute | solution.py:429
  60.1 8.5 %collective-permute-start.21 = (f32[192,256]{1,0:T(8,128)S(1)}, f32[192,256]{1,0:T(8,128)S(1)}, u32[]{:S(2)}, u32[]{:S(2)}) collective-permute-start(f32[192,256]{1,0:T(8,128)S(1)} %collective-permute-done.18.refs_8_), channel_id=1, source_target_pairs={{0,2},{1,5},{4,0},{5,9},{8,4},{9,13},{12,8},{13,15},{14,12},{15,11... | collective-permute-start | bytes 589832 | tf_op jit(solution)/shard_map/ppermute | solution.py:431
  63.0 5.6 %collective-permute-start.20 = (f32[128,256]{1,0:T(8,128)S(1)}, f32[128,256]{1,0:T(8,128)S(1)}, u32[]{:S(2)}, u32[]{:S(2)}) collective-permute-start(f32[128,256]{1,0:T(8,128)S(1)} %collective-permute-done.17.refs_7_), channel_id=1, source_target_pairs={{0,2},{1,5},{4,0},{5,9},{8,4},{9,13},{12,8},{13,15},{14,12},{15,11... | collective-permute-start | bytes 393224 | tf_op jit(solution)/shard_map/ppermute | solution.py:430
  70.0 11.4 %collective-permute-start.22 = (f32[256,768]{1,0:T(8,128)S(1)}, f32[256,768]{1,0:T(8,128)S(1)}, u32[]{:S(2)}, u32[]{:S(2)}) collective-permute-start(f32[256,768]{1,0:T(8,128)S(1)} %get-tuple-element.46), channel_id=1, source_target_pairs={{0,1},{1,0},{2,3},{3,2},{4,5},{5,4},{6,7},{7,6},{8,9},{9,8},{10,11... | collective-permute-start | bytes 2359304 | tf_op jit(solution)/shard_map/ppermute | solution.py:443
  70.1 5.7 %collective-permute-start.23 = (f32[192,256]{1,0:T(8,128)S(1)}, f32[192,256]{1,0:T(8,128)S(1)}, u32[]{:S(2)}, u32[]{:S(2)}) collective-permute-start(f32[192,256]{1,0:T(8,128)S(1)} %collective-permute-done.19.refs_9_), channel_id=1, source_target_pairs={{0,2},{1,5},{4,0},{5,9},{8,4},{9,13},{12,8},{13,15},{14,12},{15,11... | collective-permute-start | bytes 589832 | tf_op jit(solution)/shard_map/ppermute | solution.py:434
  75.8 5.6 %collective-permute-start.25 = (f32[192,256]{1,0:T(8,128)S(1)}, f32[192,256]{1,0:T(8,128)S(1)}, u32[]{:S(2)}, u32[]{:S(2)}) collective-permute-start(f32[192,256]{1,0:T(8,128)S(1)} %collective-permute-done.23.refs_2_), channel_id=1, source_target_pairs={{0,1},{1,0},{2,3},{3,2},{4,5},{5,4},{6,7},{7,6},{8,9},{9,8},{10,11... | collective-permute-start | bytes 589832 | tf_op jit(solution)/shard_map/ppermute | solution.py:444
  83.5 5.7 %collective-permute-start.28 = (f32[192,256]{1,0:T(8,128)S(1)}, f32[192,256]{1,0:T(8,128)S(1)}, u32[]{:S(2)}, u32[]{:S(2)}) collective-permute-start(f32[192,256]{1,0:T(8,128)S(1)} %slice.63), channel_id=1, source_target_pairs={{0,2},{1,5},{4,0},{5,9},{8,4},{9,13},{12,8},{13,15},{14,12},{15,11... | collective-permute-start | bytes 589832 | tf_op jit(solution)/shard_map/ppermute | solution.py:429
  84.9 6.5 %collective-permute-start.30 = (f32[192,256]{1,0:T(8,128)S(1)}, f32[192,256]{1,0:T(8,128)S(1)}, u32[]{:S(2)}, u32[]{:S(2)}) collective-permute-start(f32[192,256]{1,0:T(8,128)S(1)} %slice.66), channel_id=1, source_target_pairs={{0,2},{1,5},{4,0},{5,9},{8,4},{9,13},{12,8},{13,15},{14,12},{15,11... | collective-permute-start | bytes 589832 | tf_op jit(solution)/shard_map/ppermute | solution.py:431
  89.2 5.7 %collective-permute-start.31 = (f32[192,256]{1,0:T(8,128)S(1)}, f32[192,256]{1,0:T(8,128)S(1)}, u32[]{:S(2)}, u32[]{:S(2)}) collective-permute-start(f32[192,256]{1,0:T(8,128)S(1)} %collective-permute-done.28.refs_3_), channel_id=1, source_target_pairs={{0,2},{1,5},{4,0},{5,9},{8,4},{9,13},{12,8},{13,15},{14,12},{15,11... | collective-permute-start | bytes 589832 | tf_op jit(solution)/shard_map/ppermute | solution.py:429
  89.3 7.0 %collective-permute-start.29 = (f32[128,256]{1,0:T(8,128)S(1)}, f32[128,256]{1,0:T(8,128)S(1)}, u32[]{:S(2)}, u32[]{:S(2)}) collective-permute-start(f32[128,256]{1,0:T(8,128)S(1)} %pad_maximum_fusion.1), channel_id=1, source_target_pairs={{0,2},{1,5},{4,0},{5,9},{8,4},{9,13},{12,8},{13,15},{14,12},{15,11... | collective-permute-start | bytes 393224 | tf_op jit(solution)/shard_map/ppermute | solution.py:430
  91.3 7.1 %collective-permute-start.33 = (f32[192,256]{1,0:T(8,128)S(1)}, f32[192,256]{1,0:T(8,128)S(1)}, u32[]{:S(2)}, u32[]{:S(2)}) collective-permute-start(f32[192,256]{1,0:T(8,128)S(1)} %collective-permute-done.30.refs_5_), channel_id=1, source_target_pairs={{0,2},{1,5},{4,0},{5,9},{8,4},{9,13},{12,8},{13,15},{14,12},{15,11... | collective-permute-start | bytes 589832 | tf_op jit(solution)/shard_map/ppermute | solution.py:431
  94.9 7.1 %collective-permute-start.34 = (f32[192,256]{1,0:T(8,128)S(1)}, f32[192,256]{1,0:T(8,128)S(1)}, u32[]{:S(2)}, u32[]{:S(2)}) collective-permute-start(f32[192,256]{1,0:T(8,128)S(1)} %collective-permute-done.31.refs_6_), channel_id=1, source_target_pairs={{0,2},{1,5},{4,0},{5,9},{8,4},{9,13},{12,8},{13,15},{14,12},{15,11... | collective-permute-start | bytes 589832 | tf_op jit(solution)/shard_map/ppermute | solution.py:429
  96.3 5.7 %collective-permute-start.32 = (f32[128,256]{1,0:T(8,128)S(1)}, f32[128,256]{1,0:T(8,128)S(1)}, u32[]{:S(2)}, u32[]{:S(2)}) collective-permute-start(f32[128,256]{1,0:T(8,128)S(1)} %collective-permute-done.29.refs_4_), channel_id=1, source_target_pairs={{0,2},{1,5},{4,0},{5,9},{8,4},{9,13},{12,8},{13,15},{14,12},{15,11... | collective-permute-start | bytes 393224 | tf_op jit(solution)/shard_map/ppermute | solution.py:430
  98.4 8.5 %collective-permute-start.36 = (f32[192,256]{1,0:T(8,128)S(1)}, f32[192,256]{1,0:T(8,128)S(1)}, u32[]{:S(2)}, u32[]{:S(2)}) collective-permute-start(f32[192,256]{1,0:T(8,128)S(1)} %collective-permute-done.33.refs_8_), channel_id=1, source_target_pairs={{0,2},{1,5},{4,0},{5,9},{8,4},{9,13},{12,8},{13,15},{14,12},{15,11... | collective-permute-start | bytes 589832 | tf_op jit(solution)/shard_map/ppermute | solution.py:431
  102.0 5.0 %collective-permute-start.35 = (f32[128,256]{1,0:T(8,128)S(1)}, f32[128,256]{1,0:T(8,128)S(1)}, u32[]{:S(2)}, u32[]{:S(2)}) collective-permute-start(f32[128,256]{1,0:T(8,128)S(1)} %collective-permute-done.32.refs_7_), channel_id=1, source_target_pairs={{0,2},{1,5},{4,0},{5,9},{8,4},{9,13},{12,8},{13,15},{14,12},{15,11... | collective-permute-start | bytes 393224 | tf_op jit(solution)/shard_map/ppermute | solution.py:430
  102.0 7.1 %collective-permute-start.38 = (f32[192,256]{1,0:T(8,128)S(1)}, f32[192,256]{1,0:T(8,128)S(1)}, u32[]{:S(2)}, u32[]{:S(2)}) collective-permute-start(f32[192,256]{1,0:T(8,128)S(1)} %collective-permute-done.34.refs_9_), channel_id=1, source_target_pairs={{0,2},{1,5},{4,0},{5,9},{8,4},{9,13},{12,8},{13,15},{14,12},{15,11... | collective-permute-start | bytes 589832 | tf_op jit(solution)/shard_map/ppermute | solution.py:434
  107.9 6.9 %collective-permute-start.37 = (f32[256,256]{1,0:T(8,128)S(1)}, f32[256,256]{1,0:T(8,128)S(1)}, u32[]{:S(2)}, u32[]{:S(2)}) collective-permute-start(f32[256,256]{1,0:T(8,128)S(1)} %get-tuple-element.50), channel_id=1, source_target_pairs={{0,1},{1,0},{2,3},{3,2},{4,5},{5,4},{6,7},{7,6},{8,9},{9,8},{10,11... | collective-permute-start | bytes 786440 | tf_op jit(solution)/shard_map/ppermute | solution.py:443
  109.0 5.8 %collective-permute-start.40 = (f32[192,256]{1,0:T(8,128)S(1)}, f32[192,256]{1,0:T(8,128)S(1)}, u32[]{:S(2)}, u32[]{:S(2)}) collective-permute-start(f32[192,256]{1,0:T(8,128)S(1)} %collective-permute-done.38.refs_2_), channel_id=1, source_target_pairs={{0,1},{1,0},{2,3},{3,2},{4,5},{5,4},{6,7},{7,6},{8,9},{9,8},{10,11... | collective-permute-start | bytes 589832 | tf_op jit(solution)/shard_map/ppermute | solution.py:444
  109.1 4.5 %collective-permute-start.39 = (f32[64,256]{1,0:T(8,128)S(1)}, f32[64,256]{1,0:T(8,128)S(1)}, u32[]{:S(2)}, u32[]{:S(2)}) collective-permute-start(f32[64,256]{1,0:T(8,128)S(1)} %slice.67), channel_id=1, source_target_pairs={{0,2},{1,5},{4,0},{5,9},{8,4},{9,13},{12,8},{13,15},{14,12},{15,11... | collective-permute-start | bytes 196616 | tf_op jit(solution)/shard_map/ppermute | solution.py:435
  122.1 5.7 %collective-permute-start.43 = (f32[192,256]{1,0:T(8,128)S(1)}, f32[192,256]{1,0:T(8,128)S(1)}, u32[]{:S(2)}, u32[]{:S(2)}) collective-permute-start(f32[192,256]{1,0:T(8,128)S(1)} %slice.68), channel_id=1, source_target_pairs={{0,2},{1,5},{4,0},{5,9},{8,4},{9,13},{12,8},{13,15},{14,12},{15,11... | collective-permute-start | bytes 589832 | tf_op jit(solution)/shard_map/ppermute | solution.py:429
  123.6 6.4 %collective-permute-start.45 = (f32[192,256]{1,0:T(8,128)S(1)}, f32[192,256]{1,0:T(8,128)S(1)}, u32[]{:S(2)}, u32[]{:S(2)}) collective-permute-start(f32[192,256]{1,0:T(8,128)S(1)} %slice.71), channel_id=1, source_target_pairs={{0,2},{1,5},{4,0},{5,9},{8,4},{9,13},{12,8},{13,15},{14,12},{15,11... | collective-permute-start | bytes 589832 | tf_op jit(solution)/shard_map/ppermute | solution.py:431
  127.9 7.1 %collective-permute-start.46 = (f32[192,256]{1,0:T(8,128)S(1)}, f32[192,256]{1,0:T(8,128)S(1)}, u32[]{:S(2)}, u32[]{:S(2)}) collective-permute-start(f32[192,256]{1,0:T(8,128)S(1)} %collective-permute-done.43.refs_3_), channel_id=1, source_target_pairs={{0,2},{1,5},{4,0},{5,9},{8,4},{9,13},{12,8},{13,15},{14,12},{15,11... | collective-permute-start | bytes 589832 | tf_op jit(solution)/shard_map/ppermute | solution.py:429
  127.9 7.0 %collective-permute-start.44 = (f32[128,256]{1,0:T(8,128)S(1)}, f32[128,256]{1,0:T(8,128)S(1)}, u32[]{:S(2)}, u32[]{:S(2)}) collective-permute-start(f32[128,256]{1,0:T(8,128)S(1)} %pad_maximum_fusion.2), channel_id=1, source_target_pairs={{0,2},{1,5},{4,0},{5,9},{8,4},{9,13},{12,8},{13,15},{14,12},{15,11... | collective-permute-start | bytes 393224 | tf_op jit(solution)/shard_map/ppermute | solution.py:430
  130.0 7.1 %collective-permute-start.48 = (f32[192,256]{1,0:T(8,128)S(1)}, f32[192,256]{1,0:T(8,128)S(1)}, u32[]{:S(2)}, u32[]{:S(2)}) collective-permute-start(f32[192,256]{1,0:T(8,128)S(1)} %collective-permute-done.45.refs_5_), channel_id=1, source_target_pairs={{0,2},{1,5},{4,0},{5,9},{8,4},{9,13},{12,8},{13,15},{14,12},{15,11... | collective-permute-start | bytes 589832 | tf_op jit(solution)/shard_map/ppermute | solution.py:431
  134.9 5.0 %collective-permute-start.47 = (f32[128,256]{1,0:T(8,128)S(1)}, f32[128,256]{1,0:T(8,128)S(1)}, u32[]{:S(2)}, u32[]{:S(2)}) collective-permute-start(f32[128,256]{1,0:T(8,128)S(1)} %collective-permute-done.44.refs_4_), channel_id=1, source_target_pairs={{0,2},{1,5},{4,0},{5,9},{8,4},{9,13},{12,8},{13,15},{14,12},{15,11... | collective-permute-start | bytes 393224 | tf_op jit(solution)/shard_map/ppermute | solution.py:430
  134.9 7.1 %collective-permute-start.49 = (f32[192,256]{1,0:T(8,128)S(1)}, f32[192,256]{1,0:T(8,128)S(1)}, u32[]{:S(2)}, u32[]{:S(2)}) collective-permute-start(f32[192,256]{1,0:T(8,128)S(1)} %collective-permute-done.46.refs_6_), channel_id=1, source_target_pairs={{0,2},{1,5},{4,0},{5,9},{8,4},{9,13},{12,8},{13,15},{14,12},{15,11... | collective-permute-start | bytes 589832 | tf_op jit(solution)/shard_map/ppermute | solution.py:429
  137.0 8.5 %collective-permute-start.51 = (f32[192,256]{1,0:T(8,128)S(1)}, f32[192,256]{1,0:T(8,128)S(1)}, u32[]{:S(2)}, u32[]{:S(2)}) collective-permute-start(f32[192,256]{1,0:T(8,128)S(1)} %collective-permute-done.48.refs_8_), channel_id=1, source_target_pairs={{0,2},{1,5},{4,0},{5,9},{8,4},{9,13},{12,8},{13,15},{14,12},{15,11... | collective-permute-start | bytes 589832 | tf_op jit(solution)/shard_map/ppermute | solution.py:431
  139.9 5.6 %collective-permute-start.50 = (f32[128,256]{1,0:T(8,128)S(1)}, f32[128,256]{1,0:T(8,128)S(1)}, u32[]{:S(2)}, u32[]{:S(2)}) collective-permute-start(f32[128,256]{1,0:T(8,128)S(1)} %collective-permute-done.47.refs_7_), channel_id=1, source_target_pairs={{0,2},{1,5},{4,0},{5,9},{8,4},{9,13},{12,8},{13,15},{14,12},{15,11... | collective-permute-start | bytes 393224 | tf_op jit(solution)/shard_map/ppermute | solution.py:430
  147.0 11.4 %collective-permute-start.52 = (f32[256,768]{1,0:T(8,128)S(1)}, f32[256,768]{1,0:T(8,128)S(1)}, u32[]{:S(2)}, u32[]{:S(2)}) collective-permute-start(f32[256,768]{1,0:T(8,128)S(1)} %get-tuple-element.53), channel_id=1, source_target_pairs={{0,1},{1,0},{2,3},{3,2},{4,5},{5,4},{6,7},{7,6},{8,9},{9,8},{10,11... | collective-permute-start | bytes 2359304 | tf_op jit(solution)/shard_map/ppermute | solution.py:443
  147.0 5.7 %collective-permute-start.53 = (f32[192,256]{1,0:T(8,128)S(1)}, f32[192,256]{1,0:T(8,128)S(1)}, u32[]{:S(2)}, u32[]{:S(2)}) collective-permute-start(f32[192,256]{1,0:T(8,128)S(1)} %collective-permute-done.49.refs_9_), channel_id=1, source_target_pairs={{0,2},{1,5},{4,0},{5,9},{8,4},{9,13},{12,8},{13,15},{14,12},{15,11... | collective-permute-start | bytes 589832 | tf_op jit(solution)/shard_map/ppermute | solution.py:434
  152.8 5.6 %collective-permute-start.55 = (f32[192,256]{1,0:T(8,128)S(1)}, f32[192,256]{1,0:T(8,128)S(1)}, u32[]{:S(2)}, u32[]{:S(2)}) collective-permute-start(f32[192,256]{1,0:T(8,128)S(1)} %collective-permute-done.53.refs_2_), channel_id=1, source_target_pairs={{0,1},{1,0},{2,3},{3,2},{4,5},{5,4},{6,7},{7,6},{8,9},{9,8},{10,11... | collective-permute-start | bytes 589832 | tf_op jit(solution)/shard_map/ppermute | solution.py:444
  (12 other events, 35.9 us)
